TPU v7x, 32 devices: a whole 2x2x4 slice. The times are simulated.
32 devices in a mesh: dp: 8 (over y, x, core), ctx: 4 (over z).
Axes of the slice: x: 2, y: 2, z: 4, core: 2. Of those that a mesh axis runs over, the one named last changes fastest.
Arguments:
- activations: bfloat16 [8, 1024, 1024], P('dp', 'ctx'), may hold values from -6 to 6
- block_ids: int32 [8, 1024], P('dp'), may hold values from 0 to 7, never falling along the last dimension, each value on 1 to 256 neighbouring positions
- cotangent: bfloat16 [8, 1024, 1024], P('dp', 'ctx'), may hold values from -6 to 6
- w_query: bfloat16 [1024, 1024], P(('dp', 'ctx'))
- w_key: bfloat16 [1024, 1024], P(('dp', 'ctx')), may hold values from -0.1875 to 0.1875
- w_value: bfloat16 [1024, 1024], P(('dp', 'ctx')), may hold values from -0.1875 to 0.1875
- w_out: bfloat16 [1024, 1024], P(('dp', 'ctx')), may hold values from -0.75 to 0.75
- w_gate: bfloat16 [1024, 2816], P(('dp', 'ctx')), may hold values from -0.1875 to 0.1875
- w_up: bfloat16 [1024, 2816], P(('dp', 'ctx')), may hold values from -0.1875 to 0.1875
- w_down: bfloat16 [2816, 1024], P(('dp', 'ctx')), may hold values from -0.109375 to 0.109375
- m_query: float32 [1024, 1024], P(('dp', 'ctx')), may hold values from -512 to 512
- m_key: float32 [1024, 1024], P(('dp', 'ctx')), may hold values from -512 to 512
- m_value: float32 [1024, 1024], P(('dp', 'ctx')), may hold values from -512 to 512
- m_out: float32 [1024, 1024], P(('dp', 'ctx')), may hold values from -512 to 512
- m_gate: float32 [1024, 2816], P(('dp', 'ctx')), may hold values from -512 to 512
- m_up: float32 [1024, 2816], P(('dp', 'ctx')), may hold values from -512 to 512
- m_down: float32 [2816, 1024], P(('dp', 'ctx')), may hold values from -512 to 512
- clip_threshold: float32 [], replicated, may hold values from 2.5 to 4.5
- momentum_coeff: float32 [], replicated, may hold values from 0.5 to 0.95
Outputs:
- layer_out: bfloat16 [8, 1024, 1024], P('dp', 'ctx')
- input_grad: float32 [8, 1024, 1024], P('dp', 'ctx')
- grad_query: float32 [1024, 1024], P(('dp', 'ctx'))
- grad_key: float32 [1024, 1024], P(('dp', 'ctx'))
- grad_value: float32 [1024, 1024], P(('dp', 'ctx'))
- grad_out: float32 [1024, 1024], P(('dp', 'ctx'))
- grad_gate: float32 [1024, 2816], P(('dp', 'ctx'))
- grad_up: float32 [1024, 2816], P(('dp', 'ctx'))
- grad_down: float32 [2816, 1024], P(('dp', 'ctx'))
- new_m_query: float32 [1024, 1024], P(('dp', 'ctx'))
- new_m_key: float32 [1024, 1024], P(('dp', 'ctx'))
- new_m_value: float32 [1024, 1024], P(('dp', 'ctx'))
- new_m_out: float32 [1024, 1024], P(('dp', 'ctx'))
- new_m_gate: float32 [1024, 2816], P(('dp', 'ctx'))
- new_m_up: float32 [1024, 2816], P(('dp', 'ctx'))
- new_m_down: float32 [2816, 1024], P(('dp', 'ctx'))
- new_w_query: bfloat16 [1024, 1024], P(('dp', 'ctx'))
- new_w_key: bfloat16 [1024, 1024], P(('dp', 'ctx'))
- new_w_value: bfloat16 [1024, 1024], P(('dp', 'ctx'))
- new_w_out: bfloat16 [1024, 1024], P(('dp', 'ctx'))
- new_w_gate: bfloat16 [1024, 2816], P(('dp', 'ctx'))
- new_w_up: bfloat16 [1024, 2816], P(('dp', 'ctx'))
- new_w_down: bfloat16 [2816, 1024], P(('dp', 'ctx'))
- head_peaks: float32 [16], replicated
- head_scale: float32 [16], replicated
Inputs may be any that keep to these rules, and one draw needn't show every extreme that they name: `block_ids`: along each sequence the block ids never fall, and each id covers 1 to 256 consecutive tokens.
All inputs are finite; a program needn't handle non-finite values.
Results may differ from a plain program's by a relative error of at most 0.017.
Values may be sent and summed in bfloat16 or wider, within the bound.
No kernel may reach another device: no remote copies, remote signals or barrier semaphores. Data moves between devices by JAX's collectives and lax.ppermute only.
A program may use at most 192 MiB of HBM per device.

v0:
```python
import math

import jax
import jax.numpy as jnp
from jax import lax
from jax.sharding import PartitionSpec as P

HEADS = 16
HEAD_DIM = 64


NORM_EPS = 1e-05
ROPE_BASE = 10000.0
LEARN_RATE = 0.0001
OUT_RATE = 0.0016
MASK_FILL = -1e30


def normalize(values):
    centred = values - jnp.mean(values, axis=-1, keepdims=True)
    spread = jnp.mean(centred * centred, axis=-1, keepdims=True)
    return centred * lax.rsqrt(spread + NORM_EPS)


def rotary_tables(positions, head_width):
    half_width = head_width // 2
    frequency = ROPE_BASE ** (-(jnp.arange(half_width, dtype=jnp.float32) * 2.0 / head_width))
    angles = positions.astype(jnp.float32)[:, None] * frequency[None, :]
    return (jnp.cos(angles), jnp.sin(angles))


def rotate(vectors, cosine, sine_table):
    half_width = vectors.shape[-1] // 2
    first_half = vectors[..., :half_width]
    second = vectors[..., half_width:]
    cos_wide = cosine[:, None, :]
    sin_wide = sine_table[:, None, :]
    return jnp.concatenate(
        [first_half * cos_wide - second * sin_wide, second * cos_wide + first_half * sin_wide],
        axis=-1,
    )


def swiglu(gate_proj, up_proj):
    return jax.nn.silu(gate_proj) * up_proj


def project(left_rows, matrix):
    return jnp.dot(left_rows, matrix, preferred_element_type=jnp.float32)


def project_back(grad_rows, matrix):
    return lax.dot_general(
        grad_rows, matrix, (((1,), (1,)), ((), ())), preferred_element_type=jnp.float32
    )


def shard_gradient(left_rows, right_rows):
    return lax.psum_scatter(
        lax.dot_general(
            left_rows, right_rows, (((0,), (0,)), ((), ())), preferred_element_type=jnp.float32
        ),
        ("dp", "ctx"),
        scatter_dimension=0,
        tiled=True,
    )


def per_device(
    activations,
    block_ids,
    cotangent,
    w_query,
    w_key,
    w_value,
    w_out,
    w_gate,
    w_up,
    w_down,
    m_query,
    m_key,
    m_value,
    m_out,
    m_gate,
    m_up,
    m_down,
    clip_threshold,
    momentum_coeff,
):
    shard_list = (w_query, w_key, w_value, w_out, w_gate, w_up, w_down)
    gathered = (
        lax.all_gather(shard_list[0], ("dp", "ctx"), axis=0, tiled=True),
        lax.all_gather(shard_list[1], ("dp", "ctx"), axis=0, tiled=True),
        lax.all_gather(shard_list[2], ("dp", "ctx"), axis=0, tiled=True),
        lax.all_gather(shard_list[3], ("dp", "ctx"), axis=0, tiled=True),
        lax.all_gather(shard_list[4], ("dp", "ctx"), axis=0, tiled=True),
        lax.all_gather(shard_list[5], ("dp", "ctx"), axis=0, tiled=True),
        lax.all_gather(shard_list[6], ("dp", "ctx"), axis=0, tiled=True),
    )
    full_query, full_key, full_value, full_out, full_gate, full_up, full_down = gathered
    seq_count, span_len, model_width = activations.shape
    ctx_place = lax.axis_index("ctx")
    positions = ctx_place * span_len + jnp.arange(span_len, dtype=jnp.int32)
    cosine, sine_table = rotary_tables(positions, HEAD_DIM)
    score_scale = 1.0 / math.sqrt(HEAD_DIM)

    def split_heads(matrix):
        return matrix.reshape(seq_count, span_len, HEADS, HEAD_DIM)

    tokens_flat = activations.astype(jnp.float32).reshape(-1, model_width)
    normed = normalize(tokens_flat).astype(jnp.bfloat16)
    queries = rotate(split_heads(project(normed, full_query)), cosine, sine_table).astype(
        jnp.bfloat16
    )
    key_rot = rotate(split_heads(project(normed, full_key)), cosine, sine_table).astype(
        jnp.bfloat16
    )
    value_rot = split_heads(project(normed, full_value)).astype(jnp.bfloat16)
    key_all, value_all = (
        lax.all_gather(key_rot, "ctx", axis=1, tiled=True),
        lax.all_gather(value_rot, "ctx", axis=1, tiled=True),
    )
    query_ids = lax.dynamic_slice_in_dim(block_ids, ctx_place * span_len, span_len, 1)
    allowed = (block_ids[:, None, :] <= query_ids[:, :, None])[:, None]

    def masked_scores():
        scores = (
            jnp.einsum("sqhd,skhd->shqk", queries, key_all, preferred_element_type=jnp.float32)
            * score_scale
        )
        return jnp.where(allowed, scores, MASK_FILL)

    masked = masked_scores()
    local_peaks = jnp.max(masked, axis=(0, 2, 3))
    row_top = jnp.max(masked, axis=-1, keepdims=True)
    log_total = row_top + jnp.log(jnp.sum(jnp.exp(masked - row_top), axis=-1, keepdims=True))
    probs_low = jnp.exp(masked - log_total).astype(jnp.bfloat16)
    attended = jnp.einsum(
        "shqk,skhd->sqhd", probs_low, value_all, preferred_element_type=jnp.float32
    )
    attended_low = attended.reshape(-1, model_width).astype(jnp.bfloat16)
    head_peaks = lax.pmax(local_peaks, ("dp", "ctx"))
    residual = tokens_flat + project(attended_low, full_out)
    normed2 = normalize(residual).astype(jnp.bfloat16)
    gate_proj = project(normed2, full_gate)
    up_proj = project(normed2, full_up)
    hidden_low = swiglu(gate_proj, up_proj).astype(jnp.bfloat16)
    layer_out = (
        (residual + project(hidden_low, full_down))
        .astype(jnp.bfloat16)
        .reshape(seq_count, span_len, model_width)
    )
    back_weights = (
        lax.all_gather(shard_list[0], ("dp", "ctx"), axis=0, tiled=True),
        lax.all_gather(shard_list[1], ("dp", "ctx"), axis=0, tiled=True),
        lax.all_gather(shard_list[2], ("dp", "ctx"), axis=0, tiled=True),
        lax.all_gather(shard_list[3], ("dp", "ctx"), axis=0, tiled=True),
        lax.all_gather(shard_list[4], ("dp", "ctx"), axis=0, tiled=True),
        lax.all_gather(shard_list[5], ("dp", "ctx"), axis=0, tiled=True),
        lax.all_gather(shard_list[6], ("dp", "ctx"), axis=0, tiled=True),
    )
    back_query, back_key, back_value, back_out, back_gate, back_up, back_down = back_weights
    grad_rows = cotangent.reshape(-1, model_width)
    grad_hidden = project_back(grad_rows, back_down)
    unused, gate_pull = jax.vjp(swiglu, gate_proj, up_proj)
    grad_gate_wide, grad_up_wide = gate_pull(grad_hidden)
    grad_gate_low = grad_gate_wide.astype(jnp.bfloat16)
    grad_up_low = grad_up_wide.astype(jnp.bfloat16)
    grad_normed2 = project_back(grad_gate_low, back_gate) + project_back(grad_up_low, back_up)
    unused, second_pull = jax.vjp(normalize, residual)
    grad_residual = grad_rows.astype(jnp.float32) + second_pull(grad_normed2)[0]
    grad_branch = grad_residual.astype(jnp.bfloat16)
    grad_attended = split_heads(project_back(grad_branch, back_out).astype(jnp.bfloat16))
    masked = masked_scores()
    probs = jnp.exp(masked - log_total)
    probs_again = probs.astype(jnp.bfloat16)
    grad_values_all = jnp.einsum(
        "shqk,sqhd->skhd", probs_again, grad_attended, preferred_element_type=jnp.float32
    )
    grad_probs = jnp.einsum(
        "sqhd,skhd->shqk", grad_attended, value_all, preferred_element_type=jnp.float32
    )
    score_grad = (
        probs * (grad_probs - jnp.sum(probs * grad_probs, axis=-1, keepdims=True))
    ).astype(jnp.bfloat16)
    grad_queries = (
        jnp.einsum("shqk,skhd->sqhd", score_grad, key_all, preferred_element_type=jnp.float32)
        * score_scale
    )
    grad_keys_all = (
        jnp.einsum("shqk,sqhd->skhd", score_grad, queries, preferred_element_type=jnp.float32)
        * score_scale
    )
    grad_keys, grad_values = (
        lax.psum_scatter(
            grad_keys_all.astype(jnp.bfloat16), "ctx", scatter_dimension=1, tiled=True
        ).astype(jnp.float32),
        lax.psum_scatter(
            grad_values_all.astype(jnp.bfloat16), "ctx", scatter_dimension=1, tiled=True
        ).astype(jnp.float32),
    )
    grad_query_low = (
        rotate(grad_queries, cosine, -sine_table).reshape(-1, model_width).astype(jnp.bfloat16)
    )
    grad_key_low = (
        rotate(grad_keys, cosine, -sine_table).reshape(-1, model_width).astype(jnp.bfloat16)
    )
    grad_value_low = grad_values.reshape(-1, model_width).astype(jnp.bfloat16)
    grad_normed = (
        project_back(grad_query_low, back_query)
        + project_back(grad_key_low, back_key)
        + project_back(grad_value_low, back_value)
    )
    unused, first_pull = jax.vjp(normalize, tokens_flat)
    input_grad = (grad_residual + first_pull(grad_normed)[0]).reshape(
        seq_count, span_len, model_width
    )
    weight_grads = (
        shard_gradient(normed, grad_query_low),
        shard_gradient(normed, grad_key_low),
        shard_gradient(normed, grad_value_low),
        shard_gradient(attended_low, grad_branch),
        shard_gradient(normed2, grad_gate_low),
        shard_gradient(normed2, grad_up_low),
        shard_gradient(hidden_low, grad_rows),
    )
    moments = (m_query, m_key, m_value, m_out, m_gate, m_up, m_down)
    new_moments = tuple(
        (momentum_coeff * moment + gradient for moment, gradient in zip(moments, weight_grads))
    )
    head_scale = jnp.sqrt(clip_threshold / jnp.maximum(head_peaks, clip_threshold))
    column_scale = jnp.repeat(head_scale, HEAD_DIM)
    rates = (LEARN_RATE, LEARN_RATE, LEARN_RATE, OUT_RATE, LEARN_RATE, LEARN_RATE, LEARN_RATE)
    updated = [
        matrix.astype(jnp.float32) - rate * moment
        for matrix, moment, rate in zip(shard_list, new_moments, rates)
    ]
    updated[0] = updated[0] * column_scale[None, :]
    updated[1] = updated[1] * column_scale[None, :]
    updated = [matrix.astype(jnp.bfloat16) for matrix in updated]
    return (
        layer_out,
        input_grad,
        weight_grads[0],
        weight_grads[1],
        weight_grads[2],
        weight_grads[3],
        weight_grads[4],
        weight_grads[5],
        weight_grads[6],
        new_moments[0],
        new_moments[1],
        new_moments[2],
        new_moments[3],
        new_moments[4],
        new_moments[5],
        new_moments[6],
        updated[0],
        updated[1],
        updated[2],
        updated[3],
        updated[4],
        updated[5],
        updated[6],
        head_peaks,
        head_scale,
    )


def solution(mesh):
    placed = (
        P("dp", "ctx", None),
        P("dp", None),
        P("dp", "ctx", None),
        P(("dp", "ctx"), None),
        P(("dp", "ctx"), None),
        P(("dp", "ctx"), None),
        P(("dp", "ctx"), None),
        P(("dp", "ctx"), None),
        P(("dp", "ctx"), None),
        P(("dp", "ctx"), None),
        P(("dp", "ctx"), None),
        P(("dp", "ctx"), None),
        P(("dp", "ctx"), None),
        P(("dp", "ctx"), None),
        P(("dp", "ctx"), None),
        P(("dp", "ctx"), None),
        P(("dp", "ctx"), None),
        P(),
        P(),
    )
    return jax.shard_map(
        per_device,
        mesh=mesh,
        in_specs=placed,
        out_specs=(
            P("dp", "ctx", None),
            P("dp", "ctx", None),
            P(("dp", "ctx"), None),
            P(("dp", "ctx"), None),
            P(("dp", "ctx"), None),
            P(("dp", "ctx"), None),
            P(("dp", "ctx"), None),
            P(("dp", "ctx"), None),
            P(("dp", "ctx"), None),
            P(("dp", "ctx"), None),
            P(("dp", "ctx"), None),
            P(("dp", "ctx"), None),
            P(("dp", "ctx"), None),
            P(("dp", "ctx"), None),
            P(("dp", "ctx"), None),
            P(("dp", "ctx"), None),
            P(("dp", "ctx"), None),
            P(("dp", "ctx"), None),
            P(("dp", "ctx"), None),
            P(("dp", "ctx"), None),
            P(("dp", "ctx"), None),
            P(("dp", "ctx"), None),
            P(("dp", "ctx"), None),
            P(),
            P(),
        ),
        check_vma=False,
    )
```

profile of v0, /device:TPU:0, one launch (start us, length us, event | category | flops | bytes accessed | tf_op | source)
XLA Modules:
  0.0 2023.9 jit_solution(12451990603385696247)
XLA Ops:
  9.5 1.2 convert_reduce_fusion
  10.7 1.3 fusion.30
  12.9 57.3 %all-gather.13.cloned.1.call-done = bf16[1024,1024]{1,0:T(8,128)(2,1)} async-done(((bf16[32,1024]{1,0:T(8,128)(2,1)}), bf16[1024,1024]{1,0:T(8,128)(2,1)}) %all-gather.13.cloned.1.call-update) | async-done | bytes 2097168 | tf_op jit(solution)/shard_map/all_gather | solution.py:92
  70.2 2.9 copy.50
  73.1 55.4 %all-gather.15.cloned.1.call-done = bf16[1024,1024]{1,0:T(8,128)(2,1)} async-done(((bf16[32,1024]{1,0:T(8,128)(2,1)}), bf16[1024,1024]{1,0:T(8,128)(2,1)}) %all-gather.15.cloned.1.call-update) | async-done | bytes 2097168 | tf_op jit(solution)/shard_map/all_gather | solution.py:93
  128.5 3.9 copy.51
  134.0 0.8 convolution_bitcast_fusion
  135.2 0.9 pad_maximum_fusion.1
  136.2 50.6 %all-gather.11.cloned.1.call-done = bf16[1024,1024]{1,0:T(8,128)(2,1)} async-done(((bf16[32,1024]{1,0:T(8,128)(2,1)}), bf16[1024,1024]{1,0:T(8,128)(2,1)}) %all-gather.11.cloned.1.call-update) | async-done | bytes 2097168 | tf_op jit(solution)/shard_map/all_gather | solution.py:94
  186.8 3.9 copy.49
  190.7 3.2 convolution_convert_fusion.1
  197.3 36.6 %all-gather.17.cloned.1.call-done = bf16[1,1024,16,64]{1,3,2,0:T(8,128)(2,1)} async-done(((bf16[1,256,16,64]{1,3,2,0:T(8,128)(2,1)}), bf16[1,1024,16,64]{1,3,2,0:T(8,128)(2,1)}) %all-gather.17.cloned.1.call-update) | async-done | bytes 2097168 | tf_op jit(solution)/shard_map/all_gather | solution.py:120
  233.9 4.5 fusion.64
  238.4 3.8 exponential_reduce_fusion
  242.2 2.2 copy-done
  244.5 35.9 %all-gather.27.cloned.1.call-done = bf16[1024,16,64]{0,2,1:T(8,128)(2,1)} async-done(((bf16[256,16,64]{0,2,1:T(8,128)(2,1)}), bf16[1024,16,64]{0,2,1:T(8,128)(2,1)}) %all-gather.27.cloned.1.call-update) | async-done | bytes 2097168 | tf_op jit(solution)/shard_map/all_gather | solution.py:121
  280.4 9.1 fusion.26
  289.5 48.4 %all-gather.19.cloned.1.call-done = bf16[1024,1024]{1,0:T(8,128)(2,1)} async-done(((bf16[32,1024]{1,0:T(8,128)(2,1)}), bf16[1024,1024]{1,0:T(8,128)(2,1)}) %all-gather.19.cloned.1.call-update) | async-done | bytes 2097168 | tf_op jit(solution)/shard_map/all_gather | solution.py:95
  337.9 2.4 fusion.65
  340.8 66.2 %all-gather.21.cloned.1.call-done = bf16[1024,2816]{1,0:T(8,128)(2,1)} async-done(((bf16[32,2816]{1,0:T(8,128)(2,1)}), bf16[1024,2816]{1,0:T(8,128)(2,1)}) %all-gather.21.cloned.1.call-update) | async-done | bytes 5767184 | tf_op jit(solution)/shard_map/all_gather | solution.py:96
  406.9 5.9 fusion.66
  412.8 63.3 %all-gather.23.cloned.1.call-done = bf16[1024,2816]{1,0:T(8,128)(2,1)} async-done(((bf16[32,2816]{1,0:T(8,128)(2,1)}), bf16[1024,2816]{1,0:T(8,128)(2,1)}) %all-gather.23.cloned.1.call-update) | async-done | bytes 5767184 | tf_op jit(solution)/shard_map/all_gather | solution.py:97
  476.1 5.8 fusion.67
  481.9 63.3 %all-gather.25.cloned.1.call-done = bf16[2816,1024]{1,0:T(8,128)(2,1)} async-done(((bf16[88,1024]{1,0:T(8,128)(2,1)}), bf16[2816,1024]{1,0:T(8,128)(2,1)}) %all-gather.25.cloned.1.call-update) | async-done | bytes 5767184 | tf_op jit(solution)/shard_map/all_gather | solution.py:98
  545.3 9.3 multiply_convert_fusion.2
  554.6 5.4 fusion.68
  560.0 1.8 multiply_reduce_fusion.1
  565.0 9.3 convert_bitcast_fusion
  574.3 10.4 fusion.62
  584.7 7.8 multiply_convert_fusion
  592.6 3.3 copy-done.1
  595.9 2.9 fusion.14
  598.8 2.7 fusion.70
  601.6 15.6 reduce-scatter.12.cloned.1.call-done
  617.2 3.9 fusion.44
  621.6 1.1 copy-done.10
  622.7 7.4 fusion.18
  630.2 32.7 %reduce-scatter.10.cloned.1.call-done = bf16[1,256,16,64]{1,3,2,0:T(8,128)(2,1)} async-done(((bf16[1,1024,16,64]{1,3,2,0:T(8,128)(2,1)}), bf16[1,256,16,64]{1,3,2,0:T(8,128)(2,1)}) %reduce-scatter.10.cloned.1.call-update) | async-done | bytes 524304 | tf_op jit(solution)/shard_map/reduce_scatter | solution.py:195
  662.9 1.1 convert_element_type.218
  664.0 1.5 multiply_subtract_fusion
  665.6 2.8 fusion.46
  668.6 2.9 fusion.42
  671.5 1.0 copy-done.13
  672.5 7.3 fusion.71
  679.9 7.3 fusion.72
  687.3 1.0 copy-done.16
  688.2 7.3 fusion.35
  696.9 40.1 %pmax.7 = f32[16]{0:T(128)S(1)} all-reduce(f32[16]{0:T(128)S(1)} %copy-done.50), channel_id=1, replica_groups=mesh['dp'=8,'ctx'=4] {'dp','ctx'}, use_global_device_ids=true, to_apply=%region_21.22 | all-reduce | flops 16 | bytes 128 | tf_op jit(solution)/shard_map/pmax | solution.py:142
  737.2 5.7 fusion.29
  746.2 0.9 fusion.31
  747.7 1.4 add_bitcast_fusion
  749.1 64.4 %reduce-scatter.20.cloned.1.call-done = f32[32,1024]{1,0:T(8,128)} async-done(((f32[1024,1024]{1,0:T(8,128)}), f32[32,1024]{1,0:T(8,128)}) %reduce-scatter.20.cloned.1.call-update) | async-done | bytes 131088 | tf_op jit(solution)/shard_map/reduce_scatter | solution.py:59
  813.5 1.6 subtract_convert_fusion.5
  815.1 147.6 %reduce-scatter.18.cloned.1.call-done = f32[32,1024]{1,0:T(8,128)} async-done(((f32[1024,1024]{1,0:T(8,128)}), f32[32,1024]{1,0:T(8,128)}) %reduce-scatter.18.cloned.1.call-update) | async-done | bytes 131088 | tf_op jit(solution)/shard_map/reduce_scatter | solution.py:59
  962.8 1.6 subtract_convert_fusion.6
  964.4 147.3 %reduce-scatter.14.cloned.1.call-done = f32[32,1024]{1,0:T(8,128)} async-done(((f32[1024,1024]{1,0:T(8,128)}), f32[32,1024]{1,0:T(8,128)}) %reduce-scatter.14.cloned.1.call-update) | async-done | bytes 131088 | tf_op jit(solution)/shard_map/reduce_scatter | solution.py:59
  1111.7 148.6 %reduce-scatter.16.cloned.1.call-done = f32[32,1024]{1,0:T(8,128)} async-done(((f32[1024,1024]{1,0:T(8,128)}), f32[32,1024]{1,0:T(8,128)}) %reduce-scatter.16.cloned.1.call-update) | async-done | bytes 131088 | tf_op jit(solution)/shard_map/reduce_scatter | solution.py:59
  1260.3 1.7 multiply_convert_fusion.5
  1262.0 250.6 %reduce-scatter.22.cloned.1.call-done = f32[32,2816]{1,0:T(8,128)} async-done(((f32[1024,2816]{1,0:T(8,128)}), f32[32,2816]{1,0:T(8,128)}) %reduce-scatter.22.cloned.1.call-update) | async-done | bytes 360464 | tf_op jit(solution)/shard_map/reduce_scatter | solution.py:59
  1512.7 1.8 subtract_convert_fusion.4
  1514.5 249.3 %reduce-scatter.24.cloned.1.call-done = f32[32,2816]{1,0:T(8,128)} async-done(((f32[1024,2816]{1,0:T(8,128)}), f32[32,2816]{1,0:T(8,128)}) %reduce-scatter.24.cloned.1.call-update) | async-done | bytes 360464 | tf_op jit(solution)/shard_map/reduce_scatter | solution.py:59
  1763.8 1.8 subtract_convert_fusion.3
  1765.7 249.4 %reduce-scatter.26.cloned.1.call-done = f32[88,1024]{1,0:T(8,128)} async-done(((f32[2816,1024]{1,0:T(8,128)}), f32[88,1024]{1,0:T(8,128)}) %reduce-scatter.26.cloned.1.call-update) | async-done | bytes 360464 | tf_op jit(solution)/shard_map/reduce_scatter | solution.py:59
  2015.0 1.9 subtract_convert_fusion.2
  (166 shorter events, 16.7 us)
Async XLA Ops:
  7.2 63.0 %all-gather.13.cloned.1.call-start = ((), (), s32[]{:S(2)}) async-start(), calls=%async_computation.10 | async-start | bytes 2162688 | tf_op jit(solution)/shard_map/all_gather | solution.py:92
  7.9 120.5 %all-gather.15.cloned.1.call-start = ((), (), s32[]{:S(2)}) async-start(), calls=%async_computation.11 | async-start | bytes 2162688 | tf_op jit(solution)/shard_map/all_gather | solution.py:93
  8.7 178.1 %all-gather.11.cloned.1.call-start = ((), (), s32[]{:S(2)}) async-start(), calls=%async_computation.9 | async-start | bytes 2162688 | tf_op jit(solution)/shard_map/all_gather | solution.py:94
  9.4 224.5 %all-gather.17.cloned.1.call-start = ((), (), s32[]{:S(2)}) async-start(), calls=%async_computation.12 | async-start | bytes 2621440 | tf_op jit(solution)/shard_map/all_gather | solution.py:120
  12.9 122.0 %copy-start.35 = (f32[256,32]{0,1:T(8,128)}, f32[256,32]{0,1:T(8,128)S(1)}, u32[]{:S(2)}) copy-start(f32[256,32]{0,1:T(8,128)S(1)} %get-tuple-element.62) | copy-start | bytes 98308
  73.0 59.4 %copy-start.2 = (bf16[1,256,1024]{2,1,0:T(8,128)(2,1)S(1)}, bf16[1,256,1024]{2,1,0:T(8,128)(2,1)}, u32[]{:S(2)}) copy-start(bf16[1,256,1024]{2,1,0:T(8,128)(2,1)} %param.19) | copy-start | bytes 1572868
  132.4 1.6 copy-start.23
  135.2 98.7 %copy-start.17 = (bf16[256,16,32]{0,2,1:T(8,128)(2,1)}, bf16[256,16,32]{0,2,1:T(8,128)(2,1)S(1)}, u32[]{:S(2)}) copy-start(bf16[256,16,32]{0,2,1:T(8,128)(2,1)S(1)} %get-tuple-element.50) | copy-start | bytes 786436
  135.2 98.7 %copy-start.19 = (bf16[256,16,32]{0,2,1:T(8,128)(2,1)}, bf16[256,16,32]{0,2,1:T(8,128)(2,1)S(1)}, u32[]{:S(2)}) copy-start(bf16[256,16,32]{0,2,1:T(8,128)(2,1)S(1)} %get-tuple-element.51) | copy-start | bytes 786436
  136.1 144.2 %all-gather.27.cloned.1.call-start = ((), (), s32[]{:S(2)}) async-start(), calls=%async_computation.26 | async-start | bytes 2621440 | tf_op jit(solution)/shard_map/all_gather | solution.py:121
  190.7 6.3 copy-start.48
  194.0 143.9 %all-gather.19.cloned.1.call-start = ((), (), s32[]{:S(2)}) async-start(), calls=%async_computation.13 | async-start | bytes 2162688 | tf_op jit(solution)/shard_map/all_gather | solution.py:95
  194.6 212.4 %all-gather.21.cloned.1.call-start = ((), (), s32[]{:S(2)}) async-start(), calls=%async_computation.14 | async-start | bytes 5947392 | tf_op jit(solution)/shard_map/all_gather | solution.py:96
  195.3 280.8 %all-gather.23.cloned.1.call-start = ((), (), s32[]{:S(2)}) async-start(), calls=%async_computation.15 | async-start | bytes 5947392 | tf_op jit(solution)/shard_map/all_gather | solution.py:97
  196.1 349.2 %all-gather.25.cloned.1.call-start = ((), (), s32[]{:S(2)}) async-start(), calls=%async_computation.16 | async-start | bytes 5947392 | tf_op jit(solution)/shard_map/all_gather | solution.py:98
  196.8 420.4 %reduce-scatter.12.cloned.1.call-start = ((), (), s32[]{:S(2)}) async-start(), calls=%async_computation.18 | async-start | bytes 2621440 | tf_op jit(solution)/shard_map/reduce_scatter | solution.py:198
  238.4 6.1 copy-start
  244.5 320.5 %copy-start.31 = (f32[16,256]{1,0:T(8,128)}, f32[16,256]{1,0:T(8,128)S(1)}, u32[]{:S(2)}) copy-start(f32[16,256]{1,0:T(8,128)S(1)} %log_add_fusion) | copy-start | bytes 49156
  340.3 221.5 %copy-start.3 = (f32[256,1024]{1,0:T(8,128)}, f32[256,1024]{1,0:T(8,128)S(1)}, u32[]{:S(2)}) copy-start(f32[256,1024]{1,0:T(8,128)S(1)} %get-tuple-element.66) | copy-start | bytes 3145732
  340.8 135.3 %copy-start.12 = (bf16[256,1024]{1,0:T(8,128)(2,1)}, bf16[256,1024]{1,0:T(8,128)(2,1)S(1)}, u32[]{:S(2)}) copy-start(bf16[256,1024]{1,0:T(8,128)(2,1)S(1)} %multiply_convert_fusion.4) | copy-start | bytes 1572868
  412.8 132.4 %copy-start.14 = (bf16[1,256,1024]{2,1,0:T(8,128)(2,1)S(1)}, bf16[1,256,1024]{2,1,0:T(8,128)(2,1)}, u32[]{:S(2)}) copy-start(bf16[1,256,1024]{2,1,0:T(8,128)(2,1)} %param.21) | copy-start | bytes 1572868
  554.5 5.4 copy-start.27
  554.6 5.4 copy-start.26
  554.6 5.4 copy-start.51
  561.8 2.1 copy-start.22
  562.2 2.7 copy-start.5
  562.3 2.7 copy-start.46
  564.9 9.3 copy-start.11
  574.2 88.6 %reduce-scatter.10.cloned.1.call-start = ((), (), s32[]{:S(2)}) async-start(), calls=%async_computation.17 | async-start | bytes 2621440 | tf_op jit(solution)/shard_map/reduce_scatter | solution.py:195
  584.7 11.1 copy-start.18
  584.7 11.1 copy-start.20
  592.5 3.3 copy-start.1
  595.8 3.0 copy-start.25
  598.7 214.8 %reduce-scatter.20.cloned.1.call-start = ((), (), s32[]{:S(2)}) async-start(), calls=%async_computation.22 | async-start | bytes 4325376 | tf_op jit(solution)/shard_map/reduce_scatter | solution.py:59
  601.5 361.2 %reduce-scatter.18.cloned.1.call-start = ((), (), s32[]{:S(2)}) async-start(), calls=%async_computation.21 | async-start | bytes 4325376 | tf_op jit(solution)/shard_map/reduce_scatter | solution.py:59
  621.1 1.6 copy-start.10
  621.2 42.8 %copy-start.36 = (f32[256,32]{0,1:T(8,128)S(1)}, f32[256,32]{0,1:T(8,128)}, u32[]{:S(2)}) copy-start(f32[256,32]{0,1:T(8,128)} %copy-done.35) | copy-start | bytes 98308
  621.2 42.8 %copy-start.41 = (f32[256,32]{0,1:T(8,128)S(1)}, f32[256,32]{0,1:T(8,128)}, u32[]{:S(2)}) copy-start(f32[256,32]{0,1:T(8,128)} %get-tuple-element.60) | copy-start | bytes 98308
  621.2 490.5 %reduce-scatter.14.cloned.1.call-start = ((), (), s32[]{:S(2)}) async-start(), calls=%async_computation.19 | async-start | bytes 4325376 | tf_op jit(solution)/shard_map/reduce_scatter | solution.py:59
  668.5 591.8 %reduce-scatter.16.cloned.1.call-start = ((), (), s32[]{:S(2)}) async-start(), calls=%async_computation.20 | async-start | bytes 4325376 | tf_op jit(solution)/shard_map/reduce_scatter | solution.py:59
  671.5 841.2 %reduce-scatter.22.cloned.1.call-start = ((), (), s32[]{:S(2)}) async-start(), calls=%async_computation.23 | async-start | bytes 11894784 | tf_op jit(solution)/shard_map/reduce_scatter | solution.py:59
  679.8 1084.0 %reduce-scatter.24.cloned.1.call-start = ((), (), s32[]{:S(2)}) async-start(), calls=%async_computation.24 | async-start | bytes 11894784 | tf_op jit(solution)/shard_map/reduce_scatter | solution.py:59
  687.2 1327.8 %reduce-scatter.26.cloned.1.call-start = ((), (), s32[]{:S(2)}) async-start(), calls=%async_computation.25 | async-start | bytes 11894784 | tf_op jit(solution)/shard_map/reduce_scatter | solution.py:59
  695.5 41.7 %copy-start.4 = (f32[256,1024]{1,0:T(8,128)S(1)}, f32[256,1024]{1,0:T(8,128)}, u32[]{:S(2)}) copy-start(f32[256,1024]{1,0:T(8,128)} %copy-done.3) | copy-start | bytes 3145732
  737.0 5.8 copy-start.52
  737.0 5.8 copy-start.49
  737.2 5.7 copy-start.8
  742.9 1.6 copy-start.9
  744.5 1.6 copy-start.7
  744.5 1.7 copy-start.21
  747.1 66.4 %copy-start.37 = (bf16[32,1024]{1,0:T(8,128)(2,1)S(1)}, bf16[32,1024]{1,0:T(8,128)(2,1)}, u32[]{:S(2)}) copy-start(bf16[32,1024]{1,0:T(8,128)(2,1)} %param.25) | copy-start | bytes 196612
  747.1 66.4 %copy-start.42 = (f32[32,1024]{1,0:T(8,128)S(1)}, f32[32,1024]{1,0:T(8,128)}, u32[]{:S(2)}) copy-start(f32[32,1024]{1,0:T(8,128)} %param.32) | copy-start | bytes 393220
  747.1 215.6 %copy-start.38 = (bf16[32,1024]{1,0:T(8,128)(2,1)S(1)}, bf16[32,1024]{1,0:T(8,128)(2,1)}, u32[]{:S(2)}) copy-start(bf16[32,1024]{1,0:T(8,128)(2,1)} %param.24) | copy-start | bytes 196612
  747.1 215.6 %copy-start.43 = (f32[32,1024]{1,0:T(8,128)S(1)}, f32[32,1024]{1,0:T(8,128)}, u32[]{:S(2)}) copy-start(f32[32,1024]{1,0:T(8,128)} %param.31) | copy-start | bytes 393220
  747.5 512.7 %copy-start.39 = (bf16[32,1024]{1,0:T(8,128)(2,1)S(1)}, bf16[32,1024]{1,0:T(8,128)(2,1)}, u32[]{:S(2)}) copy-start(bf16[32,1024]{1,0:T(8,128)(2,1)} %param.22) | copy-start | bytes 196612
  747.6 512.7 %copy-start.40 = (bf16[32,1024]{1,0:T(8,128)(2,1)S(1)}, bf16[32,1024]{1,0:T(8,128)(2,1)}, u32[]{:S(2)}) copy-start(bf16[32,1024]{1,0:T(8,128)(2,1)} %param.23) | copy-start | bytes 196612
  747.6 512.7 %copy-start.44 = (f32[32,1024]{1,0:T(8,128)S(1)}, f32[32,1024]{1,0:T(8,128)}, u32[]{:S(2)}) copy-start(f32[32,1024]{1,0:T(8,128)} %param.30) | copy-start | bytes 393220
  747.6 512.7 %copy-start.45 = (f32[32,1024]{1,0:T(8,128)S(1)}, f32[32,1024]{1,0:T(8,128)}, u32[]{:S(2)}) copy-start(f32[32,1024]{1,0:T(8,128)} %param.29) | copy-start | bytes 393220
  747.6 765.0 %copy-start.28 = (bf16[32,2816]{1,0:T(8,128)(2,1)S(1)}, bf16[32,2816]{1,0:T(8,128)(2,1)}, u32[]{:S(2)}) copy-start(bf16[32,2816]{1,0:T(8,128)(2,1)} %param.26) | copy-start | bytes 540676
  747.6 765.0 %copy-start.32 = (f32[32,2816]{1,0:T(8,128)S(1)}, f32[32,2816]{1,0:T(8,128)}, u32[]{:S(2)}) copy-start(f32[32,2816]{1,0:T(8,128)} %param.33) | copy-start | bytes 1081348
  747.6 1016.2 %copy-start.29 = (bf16[32,2816]{1,0:T(8,128)(2,1)S(1)}, bf16[32,2816]{1,0:T(8,128)(2,1)}, u32[]{:S(2)}) copy-start(bf16[32,2816]{1,0:T(8,128)(2,1)} %param.27) | copy-start | bytes 540676
  747.7 1016.2 %copy-start.33 = (f32[32,2816]{1,0:T(8,128)S(1)}, f32[32,2816]{1,0:T(8,128)}, u32[]{:S(2)}) copy-start(f32[32,2816]{1,0:T(8,128)} %param.34) | copy-start | bytes 1081348
  749.1 1265.9 %copy-start.30 = (bf16[88,1024]{1,0:T(8,128)(2,1)S(1)}, bf16[88,1024]{1,0:T(8,128)(2,1)}, u32[]{:S(2)}) copy-start(bf16[88,1024]{1,0:T(8,128)(2,1)} %param.28) | copy-start | bytes 540676
  749.1 1265.9 %copy-start.34 = (f32[88,1024]{1,0:T(8,128)S(1)}, f32[88,1024]{1,0:T(8,128)}, u32[]{:S(2)}) copy-start(f32[88,1024]{1,0:T(8,128)} %param.35) | copy-start | bytes 1081348
  (7 other events, 8.3 us)
Sparse Core Ops, SparseCore 0:
  11.0 59.1 all-gather.12
  73.1 55.3 all-gather.14
  131.4 55.3 all-gather.10
  188.8 45.0 all-gather.16
  235.9 44.4 all-gather.26
  283.2 54.6 all-gather.18
  340.7 66.1 all-gather.20
  409.8 66.2 all-gather.22
  478.9 66.2 all-gather.24
  574.4 42.8 reduce-scatter.11
  619.6 43.1 reduce-scatter.9
  665.6 147.9 reduce-scatter.19
  816.4 146.3 reduce-scatter.17
  965.5 146.1 reduce-scatter.13
  1114.4 145.8 reduce-scatter.15
  1263.0 249.5 reduce-scatter.21
  1515.4 248.4 reduce-scatter.23
  1766.6 248.4 reduce-scatter.25
where the time goes:
time: 2030 us; the launch traced here: 2020 us
  waiting for transfers between devices  1790 us (88%)
  matrix products  122 us (6%)
  blocking collectives  40.1 us (2%)
  other arithmetic  32.5 us (2%)
  local copies, waits for them, and re-layouts  23.8 us (1%)
    reduce_scatter x7, waiting for transfers between devices, shard_gradient(): lax.psum_scatter(lax.dot_general(left_rows, right_rows, (((0,), (0,)), ((...  1260 us
    all_gather x1, waiting for transfers between devices, per_device(): lax.all_gather(shard_list[4], ('dp', 'ctx'), axis=0, tiled=True)  66.2 us
    all_gather x1, waiting for transfers between devices, per_device(): lax.all_gather(shard_list[6], ('dp', 'ctx'), axis=0, tiled=True)  63.3 us
    all_gather x1, waiting for transfers between devices, per_device(): lax.all_gather(shard_list[5], ('dp', 'ctx'), axis=0, tiled=True)  63.3 us
    all_gather x1, waiting for transfers between devices, per_device(): lax.all_gather(shard_list[0], ('dp', 'ctx'), axis=0, tiled=True)  57.3 us
    all_gather x1, waiting for transfers between devices, per_device(): lax.all_gather(shard_list[1], ('dp', 'ctx'), axis=0, tiled=True)  55.4 us
    all_gather x1, waiting for transfers between devices, per_device(): lax.all_gather(shard_list[2], ('dp', 'ctx'), axis=0, tiled=True)  50.6 us
    all_gather x1, waiting for transfers between devices, per_device(): lax.all_gather(shard_list[3], ('dp', 'ctx'), axis=0, tiled=True)  48.4 us
  transfers between devices with their start and end apart: 18, of which 18 were waited for; matrix products, arithmetic and copies ran while one was open for 7% of the time, Pallas kernels for 0%

commit v1 on v0

--- a/solution.py
+++ b/solution.py
@@ -267,6 +267,314 @@
     )
 
 
+HALF = 512
+
+
+def swap(array, bit):
+    return lax.ppermute(array, "dp", [(i, i ^ bit) for i in range(8)])
+
+
+def order_of(first, second):
+    return [c * 1 + f * first + s * second for c in (0, 1) for f in (0, 1) for s in (0, 1)]
+
+
+ORDER_A = order_of(2, 4)
+ORDER_B = order_of(4, 2)
+
+
+def pick_columns(matrix, order, me, width):
+    return jnp.concatenate(
+        [lax.dynamic_slice_in_dim(matrix, (r ^ me) * width, width, 1) for r in order], axis=1
+    )
+
+
+def pick_rows(matrix, order, me, width):
+    return jnp.concatenate(
+        [lax.dynamic_slice_in_dim(matrix, (r ^ me) * width, width, 0) for r in order], axis=0
+    )
+
+
+def place_of(order, block, me):
+    table = [0] * 8
+    for place, r in enumerate(order):
+        table[r] = place
+    return jnp.asarray(table, jnp.int32)[block ^ me]
+
+
+def restore_columns(matrix, order, me, width):
+    return jnp.concatenate(
+        [
+            lax.dynamic_slice_in_dim(matrix, place_of(order, b, me) * width, width, 1)
+            for b in range(8)
+        ],
+        axis=1,
+    )
+
+
+def restore_rows(matrix, order, me, width):
+    return jnp.concatenate(
+        [
+            lax.dynamic_slice_in_dim(matrix, place_of(order, b, me) * width, width, 0)
+            for b in range(8)
+        ],
+        axis=0,
+    )
+
+
+def spread(own, first, second):
+    near = swap(own, first)
+    pair = jnp.concatenate([own, near], axis=0)
+    far = swap(pair, second)
+    rows = own.shape[0]
+    four = jnp.concatenate([own, far[:rows], near, far[rows:]], axis=0)
+    return jnp.concatenate([four, swap(four, 1)], axis=0)
+
+
+def halve(matrix, bit):
+    rows = matrix.shape[0] // 2
+    other = swap(matrix[rows:], bit)
+    return (matrix[:rows].astype(jnp.float32) + other.astype(jnp.float32)).astype(jnp.bfloat16)
+
+
+def collect(matrix):
+    return lax.psum_scatter(matrix, "ctx", scatter_dimension=0, tiled=True)
+
+
+def transposed_product(left, right):
+    return lax.dot_general(
+        left, right, (((0,), (0,)), ((), ())), preferred_element_type=jnp.float32
+    )
+
+
+def fast_device(
+    activations,
+    block_ids,
+    cotangent,
+    w_query,
+    w_key,
+    w_value,
+    w_out,
+    w_gate,
+    w_up,
+    w_down,
+    m_query,
+    m_key,
+    m_value,
+    m_out,
+    m_gate,
+    m_up,
+    m_down,
+    clip_threshold,
+    momentum_coeff,
+):
+    low = jnp.bfloat16
+    me = lax.axis_index("dp")
+    _, span, width = activations.shape
+    length = block_ids.shape[1]
+    group = length // span
+    own_heads = HEADS // group
+    own_width = own_heads * HEAD_DIM
+    rows = w_query.shape[0]
+    ff = w_gate.shape[1]
+    tokens_low = activations.reshape(span, width)
+    grad_rows = cotangent.reshape(span, width)
+    wide = jnp.concatenate([w_gate, w_out[:, :HALF], w_up, w_out[:, HALF:]], axis=1)
+    wide = lax.all_gather(wide, "ctx", axis=0, tiled=True)
+    tall = lax.all_gather(w_down, "ctx", axis=0, tiled=True)
+    all_low = lax.all_gather(tokens_low, "ctx", axis=0, tiled=True)
+    heads_own = jnp.stack([w_query, w_key, w_value], axis=1).reshape(rows, 3, group, own_width)
+    heads_own = heads_own.transpose(2, 0, 1, 3).reshape(group, rows, 3 * own_width)
+    heads_own = lax.all_to_all(heads_own, "ctx", 0, 0, tiled=True)
+    block = group * rows
+    heads_rel = spread(heads_own.reshape(block, 3 * own_width), 2, 4)
+    weight_a = spread(wide[:, : ff + HALF], 2, 4)
+    weight_b = spread(wide[:, ff + HALF :], 4, 2)
+    tall_block = group * w_down.shape[0]
+    down_a = restore_rows(spread(tall[:, :HALF], 2, 4), ORDER_A, me, tall_block)
+    down_b = restore_rows(spread(tall[:, HALF:], 4, 2), ORDER_B, me, tall_block)
+    full_down = jnp.concatenate([down_a, down_b], axis=1)
+    cosine, sine_table = rotary_tables(jnp.arange(length, dtype=jnp.int32), HEAD_DIM)
+    score_scale = 1.0 / math.sqrt(HEAD_DIM)
+    all_wide = all_low.astype(jnp.float32)
+    normed = normalize(all_wide).astype(low)
+    normed_rel = pick_columns(normed, ORDER_A, me, block)
+    mixed = project(normed_rel, heads_rel)
+
+    def split_heads(matrix):
+        return matrix.reshape(length, own_heads, HEAD_DIM)
+
+    queries = rotate(split_heads(mixed[:, :own_width]), cosine, sine_table).astype(low)
+    key_rot = rotate(split_heads(mixed[:, own_width : 2 * own_width]), cosine, sine_table).astype(
+        low
+    )
+    value_rot = split_heads(mixed[:, 2 * own_width :]).astype(low)
+    ids = block_ids[0]
+    allowed = (ids[None, :] <= ids[:, None])[None]
+
+    def masked_scores():
+        scores = (
+            jnp.einsum("qhd,khd->hqk", queries, key_rot, preferred_element_type=jnp.float32)
+            * score_scale
+        )
+        return jnp.where(allowed, scores, MASK_FILL)
+
+    masked = masked_scores()
+    local_peaks = jnp.max(masked, axis=(1, 2))
+    row_top = jnp.max(masked, axis=-1, keepdims=True)
+    log_total = row_top + jnp.log(jnp.sum(jnp.exp(masked - row_top), axis=-1, keepdims=True))
+    probs = jnp.exp(masked - log_total)
+    attended = jnp.einsum(
+        "hqk,khd->qhd", probs.astype(low), value_rot, preferred_element_type=jnp.float32
+    )
+    attended = attended.astype(low).reshape(group, span, own_width)
+    attended = lax.all_to_all(attended, "ctx", 0, 0, tiled=True)
+    attended = attended.transpose(1, 0, 2).reshape(span, width)
+    peaks = lax.all_gather(local_peaks, ("dp", "ctx"), axis=0, tiled=False)
+    head_peaks = jnp.max(peaks.reshape(-1, group, own_heads), axis=0).reshape(HEADS)
+    attended_a = pick_columns(attended, ORDER_A, me, block)
+    attended_b = pick_columns(attended, ORDER_B, me, block)
+    branch = jnp.concatenate(
+        [project(attended_a, weight_a[:, ff:]), project(attended_b, weight_b[:, ff:])], axis=1
+    )
+    residual = tokens_low.astype(jnp.float32) + branch
+    normed2 = normalize(residual).astype(low)
+    normed2_a = pick_columns(normed2, ORDER_A, me, block)
+    normed2_b = pick_columns(normed2, ORDER_B, me, block)
+    gate_proj = project(normed2_a, weight_a[:, :ff])
+    up_proj = project(normed2_b, weight_b[:, :ff])
+    hidden_low = swiglu(gate_proj, up_proj).astype(low)
+    layer_out = (residual + project(hidden_low, full_down)).astype(low)
+    grad_hidden = project_back(grad_rows, full_down)
+    unused, gate_pull = jax.vjp(swiglu, gate_proj, up_proj)
+    grad_gate_wide, grad_up_wide = gate_pull(grad_hidden)
+    grad_gate_low = grad_gate_wide.astype(low)
+    grad_up_low = grad_up_wide.astype(low)
+    grad_normed2 = restore_columns(
+        project_back(grad_gate_low, weight_a[:, :ff]), ORDER_A, me, block
+    ) + restore_columns(project_back(grad_up_low, weight_b[:, :ff]), ORDER_B, me, block)
+    unused, second_pull = jax.vjp(normalize, residual)
+    grad_residual = grad_rows.astype(jnp.float32) + second_pull(grad_normed2)[0]
+    grad_branch = grad_residual.astype(low)
+    grad_a = jnp.concatenate(
+        [
+            transposed_product(normed2_a, grad_gate_low).astype(low),
+            transposed_product(attended_a, grad_branch[:, :HALF]).astype(low),
+        ],
+        axis=1,
+    )
+    grad_b = jnp.concatenate(
+        [
+            transposed_product(normed2_b, grad_up_low).astype(low),
+            transposed_product(attended_b, grad_branch[:, HALF:]).astype(low),
+        ],
+        axis=1,
+    )
+    grad_a = halve(grad_a, 1)
+    grad_b = halve(grad_b, 1)
+    grad_a = halve(grad_a, 2)
+    grad_b = halve(grad_b, 4)
+    grad_a = halve(grad_a, 4)
+    grad_b = halve(grad_b, 2)
+    grad_tall = transposed_product(hidden_low, grad_rows).astype(low)
+    grad_tall = halve(
+        jnp.concatenate(
+            [
+                pick_rows(grad_tall[:, :HALF], ORDER_A, me, tall_block),
+                pick_rows(grad_tall[:, HALF:], ORDER_B, me, tall_block),
+            ],
+            axis=1,
+        ),
+        1,
+    )
+    grad_da = halve(grad_tall[:, :HALF], 2)
+    grad_db = halve(grad_tall[:, HALF:], 4)
+    grad_da = halve(grad_da, 4)
+    grad_db = halve(grad_db, 2)
+    grad_ab = collect(jnp.concatenate([grad_a, grad_b], axis=1)).astype(jnp.float32)
+    grad_d = collect(jnp.concatenate([grad_da, grad_db], axis=1)).astype(jnp.float32)
+    grad_attended = restore_columns(
+        project_back(grad_branch[:, :HALF], weight_a[:, ff:]), ORDER_A, me, block
+    ) + restore_columns(
+        project_back(grad_branch[:, HALF:], weight_b[:, ff:]), ORDER_B, me, block
+    )
+    grad_attended = grad_attended.astype(low).reshape(span, group, own_width).transpose(1, 0, 2)
+    grad_attended = lax.all_to_all(grad_attended, "ctx", 0, 0, tiled=True)
+    grad_attended = split_heads(grad_attended.reshape(length, own_width))
+    probs = jnp.exp(masked_scores() - log_total)
+    grad_values = jnp.einsum(
+        "hqk,qhd->khd", probs.astype(low), grad_attended, preferred_element_type=jnp.float32
+    )
+    grad_probs = jnp.einsum(
+        "qhd,khd->hqk", grad_attended, value_rot, preferred_element_type=jnp.float32
+    )
+    score_grad = (
+        probs * (grad_probs - jnp.sum(probs * grad_probs, axis=-1, keepdims=True))
+    ).astype(low)
+    grad_queries = (
+        jnp.einsum("hqk,khd->qhd", score_grad, key_rot, preferred_element_type=jnp.float32)
+        * score_scale
+    )
+    grad_keys = (
+        jnp.einsum("hqk,qhd->khd", score_grad, queries, preferred_element_type=jnp.float32)
+        * score_scale
+    )
+    grad_mixed = jnp.concatenate(
+        [
+            rotate(grad_queries, cosine, -sine_table).astype(low).reshape(length, own_width),
+            rotate(grad_keys, cosine, -sine_table).astype(low).reshape(length, own_width),
+            grad_values.astype(low).reshape(length, own_width),
+        ],
+        axis=1,
+    )
+    grad_normed = restore_columns(
+        project_back(grad_mixed, heads_rel).astype(low), ORDER_A, me, block
+    )
+    grad_normed = collect(grad_normed).astype(jnp.float32)
+    tokens_wide = tokens_low.astype(jnp.float32)
+    unused, first_pull = jax.vjp(normalize, tokens_wide)
+    input_grad = grad_residual + first_pull(grad_normed)[0]
+    grad_heads = transposed_product(normed_rel, grad_mixed).astype(low)
+    grad_heads = halve(halve(halve(grad_heads, 1), 2), 4)
+    grad_heads = lax.all_to_all(
+        grad_heads.reshape(group, rows, 3 * own_width), "ctx", 0, 0, tiled=True
+    ).astype(jnp.float32)
+    grad_heads = grad_heads.reshape(group, rows, 3, own_width).transpose(2, 1, 0, 3)
+    grad_heads = grad_heads.reshape(3, rows, width)
+    weight_grads = (
+        grad_heads[0],
+        grad_heads[1],
+        grad_heads[2],
+        jnp.concatenate([grad_ab[:, ff : ff + HALF], grad_ab[:, 2 * ff + HALF :]], axis=1),
+        grad_ab[:, :ff],
+        grad_ab[:, ff + HALF : 2 * ff + HALF],
+        grad_d,
+    )
+    moments = (m_query, m_key, m_value, m_out, m_gate, m_up, m_down)
+    new_moments = tuple(
+        (momentum_coeff * moment + gradient for moment, gradient in zip(moments, weight_grads))
+    )
+    head_scale = jnp.sqrt(clip_threshold / jnp.maximum(head_peaks, clip_threshold))
+    column_scale = jnp.repeat(head_scale, HEAD_DIM)
+    rates = (LEARN_RATE, LEARN_RATE, LEARN_RATE, OUT_RATE, LEARN_RATE, LEARN_RATE, LEARN_RATE)
+    shard_list = (w_query, w_key, w_value, w_out, w_gate, w_up, w_down)
+    updated = [
+        matrix.astype(jnp.float32) - rate * moment
+        for matrix, moment, rate in zip(shard_list, new_moments, rates)
+    ]
+    updated[0] = updated[0] * column_scale[None, :]
+    updated[1] = updated[1] * column_scale[None, :]
+    updated = [matrix.astype(low) for matrix in updated]
+    return (
+        layer_out[None],
+        input_grad[None],
+        *weight_grads,
+        *new_moments,
+        *updated,
+        head_peaks,
+        head_scale,
+    )
+
+
 def solution(mesh):
     placed = (
         P("dp", "ctx", None),
@@ -289,8 +597,9 @@
         P(),
         P(),
     )
+    fits = mesh.shape["dp"] == 8 and mesh.shape["ctx"] == 4
     return jax.shard_map(
-        per_device,
+        fast_device if fits else per_device,
         mesh=mesh,
         in_specs=placed,
         out_specs=(

time: 2030 us -> 536 us (0.26)
  waiting for transfers between devices: 1790 us -> 125 us
  other arithmetic: 32.5 us -> 89.4 us
  starting transfers between devices: 1.3 us -> 45.5 us
  local copies, waits for them, and re-layouts: 23.8 us -> 66.4 us
  matrix products: 122 us -> 86.1 us
  blocking collectives: 40.1 us -> 74.5 us
  between operations: 16.6 us -> 38.6 us
    reduce_scatter x9 -> x3, waiting for transfers between devices: 1310 us -> 0.03 us  [collect(): return lax.psum_scatter(matrix, 'ctx', scatter_dimension=0, tiled=True)]
    all_gather x9 -> x2, waiting for transfers between devices: 477 us -> 0.01 us  [the longest x1 0.01 us: fast_device(): wide = lax.all_gather(wide, 'ctx', axis=0, tiled=True)]
    ppermute x0 -> x29, waiting for transfers between devices: none -> 115 us  [swap(): return lax.ppermute(array, 'dp', [(i, i ^ bit) for i in range(8)])]
    unnamed x0 -> x1, blocking collectives: none -> 41.1 us
    pmax x1 -> x0, blocking collectives: 40.1 us -> none  [per_device(): head_peaks = lax.pmax(local_peaks, ('dp', 'ctx'))]
    all_gather x0 -> x1, blocking collectives: none -> 33.3 us  [fast_device(): tall = lax.all_gather(w_down, 'ctx', axis=0, tiled=True)]
    convert_element_type x11 -> x23, other arithmetic: 19.9 us -> 43.8 us  [the longest x13 18.6 us: halve(): (matrix[:rows].astype(jnp.float32) + other.astype(jnp.float32)).astype(jn...]
    ppermute x0 -> x29, starting transfers between devices: none -> 23.8 us  [swap(): return lax.ppermute(array, 'dp', [(i, i ^ bit) for i in range(8)])]
  transfers between devices with their start and end apart: 18 -> 38, of which waited for: 18 -> 15; matrix products, arithmetic and copies ran while one was open for 7% -> 38% of each run, Pallas kernels for 0% -> 0%
where the time goes in v1:
time: 536 us; the launch traced here: 525 us
  waiting for transfers between devices  125 us (23%)
  other arithmetic  89.4 us (17%)
  matrix products  86.1 us (16%)
  blocking collectives  74.5 us (14%)
  local copies, waits for them, and re-layouts  66.4 us (12%)
  starting transfers between devices  45.5 us (8%)
  between operations  38.6 us (7%)
    ppermute x29, waiting for transfers between devices, swap(): return lax.ppermute(array, 'dp', [(i, i ^ bit) for i in range(8)])  115 us
    unnamed x1, blocking collectives  41.1 us
    all_gather x1, blocking collectives, fast_device(): tall = lax.all_gather(w_down, 'ctx', axis=0, tiled=True)  33.3 us
    unnamed x250, local copies, waits for them, and re-layouts  32.5 us
    ppermute x29, starting transfers between devices, swap(): return lax.ppermute(array, 'dp', [(i, i ^ bit) for i in range(8)])  23.8 us
    convert_element_type x13, other arithmetic, halve(): (matrix[:rows].astype(jnp.float32) + other.astype(jnp.float32)).astype(jn...  18.6 us
    dot_general x6, matrix products, transposed_product(): lax.dot_general(left, right, (((0,), (0,)), ((), ())), preferred_element_...  16.8 us
    convert_element_type x1, other arithmetic, fast_device(): score_grad = (probs * (grad_probs - jnp.sum(probs * grad_probs, axis=-1,...  15.7 us
  transfers between devices with their start and end apart: 38, of which 15 were waited for; matrix products, arithmetic and copies ran while one was open for 38% of the time, Pallas kernels for 0%

profile of v1, /device:TPU:0, one launch (start us, length us, event | category | flops | bytes accessed | tf_op | source)
XLA Modules:
  0.0 525.2 jit_solution(14583317155318490903)
XLA Ops:
  8.1 1.8 pad_maximum_fusion.30
  14.3 6.3 %all-to-all-start = ((bf16[4,32,768]{2,1,0:T(8,128)(2,1)}), bf16[4,32,768]{2,1,0:T(8,128)(2,1)S(1)}, u32[]{:S(2)}, u32[]{:S(2)}) async-start(bf16[4,32,768]{2,1,0:T(8,128)(2,1)} %reshape.411), calls=%async_computation | async-start | bytes 393216 | tf_op jit(solution)/shard_map/all_to_all | solution.py:387
  20.6 33.3 %all_gather.17 = bf16[352,1024]{1,0:T(8,128)(2,1)S(1)} all-gather(bf16[88,1024]{1,0:T(8,128)(2,1)S(1)} %copy-done.29), channel_id=1, replica_groups=mesh['dp'=8,'ctx'=4] {'ctx'}, dimensions={0}, use_global_device_ids=true | all-gather | bytes 901120 | tf_op jit(solution)/shard_map/all_gather | solution.py:383
  61.5 6.2 %collective-permute-done = bf16[128,768]{1,0:T(8,128)(2,1)S(1)} collective-permute-done((bf16[128,768]{1,0:T(8,128)(2,1)S(1)}, bf16[128,768]{1,0:T(8,128)(2,1)S(1)}, u32[]{:S(2)}, u32[]{:S(2)}) %collective-permute-start) | collective-permute-done | bytes 196640 | tf_op jit(solution)/shard_map/ppermute | solution.py:274
  67.8 1.7 collective-permute-start.1
  94.9 13.0 %collective-permute-done.10 = bf16[704,512]{1,0:T(8,128)(2,1)S(1)} collective-permute-done((bf16[704,512]{1,0:T(8,128)(2,1)S(1)}, bf16[704,512]{1,0:T(8,128)(2,1)S(1)}, u32[]{:S(2)}, u32[]{:S(2)}) %collective-permute-start.10) | collective-permute-done | bytes 720928 | tf_op jit(solution)/shard_map/ppermute | solution.py:274
  109.2 2.2 collective-permute-done.11
  119.7 2.9 fusion.81
  124.5 2.1 convert_reduce_fusion
  129.4 1.9 fusion.93
  132.6 7.6 %fusion.92 = (f32[4,1024]{1,0:T(4,128)S(1)}, f32[4,1024,1024]{1,2,0:T(8,128)}) fusion(bf16[1024,4,32]{0,2,1:T(8,128)(2,1)S(1)} %get-tuple-element.111, bf16[1024,4,32]{0,2,1:T(8,128)(2,1)S(1)} %get-tuple-element.112, bf16[1024,4,32]{0,2,1:T(8,128)(2,1)S(1)} %get-tuple-element.77, bf16[1024,4,32]{0,2,1:T(8,128)(2,1)S(1)} %get-tuple-element.76, ...), kind=kOutput, calls=%fused_computation.337 | convolution fusion | flops 551546880 | bytes 18890752 | tf_op jit(solution)/shard_map/qhd,khd->hqk/dot_general | solution.py:416
  140.2 8.0 %exponential_reduce_fusion = f32[4,1024]{1,0:T(4,128)S(1)} fusion(f32[4,1024,1024]{1,2,0:T(8,128)} %get-tuple-element.139, f32[4,1024]{1,0:T(4,128)S(1)} %get-tuple-element.138), kind=kLoop, calls=%fused_computation.3 | loop fusion | flops 8384512 | bytes 16809984 | tf_op jit(solution)/shard_map/reduce_sum | solution.py:424
  149.1 9.3 %fusion.41 = bf16[1024,4,64]{0,2,1:T(8,128)(2,1)} fusion(bf16[1024,4,64]{0,2,1:T(8,128)(2,1)S(1)} %bitcast.153, f32[4,1024,1024]{1,2,0:T(8,128)} %get-tuple-element.139, f32[4,1024]{1,0:T(4,128)S(1)} %log_add_fusion), kind=kOutput, calls=%fused_computation.90 | convolution fusion | flops 545521664 | bytes 17842176 | tf_op jit(solution)/shard_map/hqk,khd->qhd/dot_general | solution.py:426
  158.4 2.2 reshape.415
  160.6 1.9 copy.130
  162.5 6.5 %all-to-all-start.1 = ((bf16[4,256,256]{1,2,0:T(8,128)(2,1)}), bf16[4,256,256]{1,2,0:T(8,128)(2,1)}, u32[]{:S(2)}, u32[]{:S(2)}) async-start(bf16[4,256,256]{1,2,0:T(8,128)(2,1)} %copy.130), calls=%async_computation.1 | async-start | bytes 1048576 | tf_op jit(solution)/shard_map/all_to_all | solution.py:430
  169.1 2.4 pad_maximum_fusion.9
  174.9 9.0 %all-to-all-done.1 = bf16[4,256,256]{1,2,0:T(8,128)(2,1)} async-done(((bf16[4,256,256]{1,2,0:T(8,128)(2,1)}), bf16[4,256,256]{1,2,0:T(8,128)(2,1)}, u32[]{:S(2)}, u32[]{:S(2)}) %all-to-all-start.1) | async-done | bytes 524320 | tf_op jit(solution)/shard_map/all_to_all | solution.py:430
  195.4 14.8 %collective-permute-done.7 = bf16[256,3328]{1,0:T(8,128)(2,1)} collective-permute-done((bf16[256,3328]{1,0:T(8,128)(2,1)}, bf16[256,3328]{1,0:T(8,128)(2,1)}, u32[]{:S(2)}, u32[]{:S(2)}) %collective-permute-start.7) | collective-permute-done | bytes 1703968 | tf_op jit(solution)/shard_map/ppermute | solution.py:274
  210.3 2.6 fusion.82
  212.9 4.0 pad_maximum_fusion.6
  217.0 1.7 fusion.80
  225.1 2.8 collective-permute-done.5
  229.8 1.7 fusion.3
  231.6 3.2 fusion.7
  234.8 6.0 %multiply_convert_fusion.1 = (bf16[256,2816]{1,0:T(8,128)(2,1)S(1)}, bf16[256,2816]{1,0:T(8,128)(2,1)S(1)}, bf16[256,2816]{1,0:T(8,128)(2,1)}) fusion(f32[256,2816]{1,0:T(8,128)} %fusion.7, f32[256,2816]{1,0:T(8,128)S(1)} %fusion.3, bf16[1,256,1024]{2,1,0:T(8,128)(2,1)S(1)} %copy-done.13, bf16[2816,512]{1,0:T(8,128)(2,1)} %dynamic-slice_dynamic-update-slice_fusion.16, ...), kind=kOutput, calls=%fused_computation.50 | convolution fusion | flops 1499463680 | bytes 16384000 | tf_op jit(solution)/shard_map/dot_general | solution.py:53
  240.8 1.7 fusion.1
  242.5 1.7 fusion.5
  249.5 4.2 convolution_convert_fusion.2
  253.7 4.2 convolution_convert_fusion.1
  259.5 4.8 all-to-all-start.2
  264.3 4.0 pad_maximum_fusion.4
  268.4 3.9 pad_maximum_fusion.3
  272.6 1.7 convolution_convert_fusion
  275.5 1.9 pad_maximum_fusion.7
  279.3 2.1 copy.133
  281.4 2.2 reshape_reshape.3
  283.6 12.2 %fusion.73 = (f32[4]{0:T(128)}, f32[4,1024]{1,0:T(4,128)S(1)}, f32[4,1024,1024]{1,2,0:T(8,128)}) fusion(f32[4,1024,1024]{1,2,0:T(8,128)} %get-tuple-element.139, f32[4,1024]{1,0:T(4,128)S(1)} %log_add_fusion, bf16[1024,4,64]{0,2,1:T(8,128)(2,1)} %reshape_reshape.3, bf16[1024,4,64]{0,2,1:T(8,128)(2,1)S(1)} %bitcast.154), kind=kOutput, calls=%fused_computation.319 | convolution fusion | flops 553644032 | bytes 34635792 | tf_op jit(solution)/shard_map/qhd,khd->hqk/dot_general | solution.py:507
  295.8 15.7 %multiply_convert_fusion = bf16[4,1024,1024]{1,2,0:T(8,128)(2,1)} fusion(f32[4,1024,1024]{1,2,0:T(8,128)} %get-tuple-element.140, f32[4,1024,1024]{1,2,0:T(8,128)} %get-tuple-element.139, f32[4,1024]{1,0:T(4,128)S(1)} %get-tuple-element.26, f32[4,1024]{1,0:T(4,128)S(1)} %log_add_fusion), kind=kLoop, calls=%fused_computation | loop fusion | flops 16777216 | bytes 41975808 | tf_op jit(solution)/shard_map/convert_element_type | solution.py:512
  311.5 6.9 %fusion.26 = f32[1024,4,64]{0,2,1:T(8,128)S(1)} fusion(bf16[4,1024,1024]{1,2,0:T(8,128)(2,1)} %multiply_convert_fusion, bf16[1024,4,32]{0,2,1:T(8,128)(2,1)S(1)} %copy-done.28, bf16[1024,4,32]{0,2,1:T(8,128)(2,1)S(1)} %copy-done.26), kind=kOutput, calls=%fused_computation.75 | convolution fusion | flops 538181632 | bytes 9961472 | tf_op jit(solution)/shard_map/hqk,qhd->khd/dot_general | solution.py:518
  318.5 4.9 fusion.27
  325.5 2.9 fusion.38
  328.4 3.8 convolution_convert_fusion.4
  332.3 1.8 convolution_convert_fusion.3
  340.9 3.5 add_convert_fusion.2
  346.6 4.2 add_convert_fusion.1
  353.4 10.1 %collective-permute-done.25 = bf16[704,512]{1,0:T(8,128)(2,1)S(1)} collective-permute-done((bf16[704,512]{1,0:T(8,128)(2,1)S(1)}, bf16[704,512]{1,0:T(8,128)(2,1)S(1)}, u32[]{:S(2)}, u32[]{:S(2)}) %collective-permute-start.25) | collective-permute-done | bytes 720928 | tf_op jit(solution)/shard_map/ppermute | solution.py:274
  365.3 2.4 add_convert_fusion
  374.2 33.5 %collective-permute-done.28 = bf16[352,512]{1,0:T(8,128)(2,1)S(1)} collective-permute-done((bf16[352,512]{1,0:T(8,128)(2,1)S(1)}, bf16[352,512]{1,0:T(8,128)(2,1)S(1)}, u32[]{:S(2)}, u32[]{:S(2)}) %collective-permute-start.28) | collective-permute-done | bytes 360480 | tf_op jit(solution)/shard_map/ppermute | solution.py:274
  407.8 7.5 %collective-permute-done.26 = bf16[352,512]{1,0:T(8,128)(2,1)S(1)} collective-permute-done((bf16[352,512]{1,0:T(8,128)(2,1)S(1)}, bf16[352,512]{1,0:T(8,128)(2,1)S(1)}, u32[]{:S(2)}, u32[]{:S(2)}) %collective-permute-start.26) | collective-permute-done | bytes 360480 | tf_op jit(solution)/shard_map/ppermute | solution.py:274
  416.4 2.5 add_convert_fusion.4
  419.0 1.7 collective-permute-start.20
  420.7 1.9 add_convert_fusion.3
  423.2 15.1 %collective-permute-done.20 = bf16[128,3328]{1,0:T(8,128)(2,1)S(1)} collective-permute-done((bf16[128,3328]{1,0:T(8,128)(2,1)S(1)}, bf16[128,3328]{1,0:T(8,128)(2,1)S(1)}, u32[]{:S(2)}, u32[]{:S(2)}) %collective-permute-start.20) | collective-permute-done | bytes 852000 | tf_op jit(solution)/shard_map/ppermute | solution.py:274
  438.5 3.1 collective-permute-done.23
  445.0 5.1 collective-permute-done.17
  450.8 4.0 all-to-all-start.3
  454.8 5.6 %fusion.44 = bf16[1,256,1024]{2,1,0:T(8,128)(2,1)} fusion(f32[256,1024]{1,0:T(8,128)S(1)} %get-tuple-element.50, bf16[256,2816]{1,0:T(8,128)(2,1)} %get-tuple-element.55, bf16[2816,512]{1,0:T(8,128)(2,1)} %dynamic-slice_dynamic-update-slice_fusion.16, bf16[2816,512]{1,0:T(8,128)(2,1)} %copy-done.45), kind=kOutput, calls=%fused_computation.91 | convolution fusion | flops 1488453632 | bytes 8781824 | tf_op jit(solution)/shard_map/dot_general | solution.py:49
  460.7 41.1 %all-reduce = f32[128]{0:T(128)S(1)} all-reduce(f32[128]{0:T(128)S(1)} %dynamic-update-slice), channel_id=3, replica_groups=mesh['dp'=8,'ctx'=4] {'dp','ctx'}, use_global_device_ids=true, to_apply=%add | all-reduce | flops 128 | bytes 1024
  504.0 1.7 multiply_convert_fusion.4
  508.7 2.5 add_bitcast_fusion
  511.3 1.9 subtract_convert_fusion.4
  514.1 1.6 subtract_convert_fusion.7
  515.7 2.5 subtract_convert_fusion.5
  (431 shorter events, 99.0 us)
Async XLA Ops:
  7.2 13.4 %copy-start.29 = (bf16[88,1024]{1,0:T(8,128)(2,1)S(1)}, bf16[88,1024]{1,0:T(8,128)(2,1)}, u32[]{:S(2)}) copy-start(bf16[88,1024]{1,0:T(8,128)(2,1)} %param.84) | copy-start | bytes 540676
  7.2 112.5 %all-gather.5.cloned.1.call-start = ((), (), s32[]{:S(2)}) async-start(), calls=%async_computation.7 | async-start | bytes 2129920 | tf_op jit(solution)/shard_map/all_gather | solution.py:382
  10.9 47.2 %copy-start = (bf16[1,256,1024]{2,1,0:T(8,128)(2,1)S(1)}, bf16[1,256,1024]{2,1,0:T(8,128)(2,1)}, u32[]{:S(2)}) copy-start(bf16[1,256,1024]{2,1,0:T(8,128)(2,1)} %param.75) | copy-start | bytes 1572868
  12.8 46.0 %copy-start.53 = (s32[1,1024]{1,0:T(1,128)S(1)}, s32[1,1024]{1,0:T(1,128)}, u32[]{:S(2)}) copy-start(s32[1,1024]{1,0:T(1,128)} %param.76) | copy-start | bytes 12292
  14.3 46.2 %all-to-all-start = ((bf16[4,32,768]{2,1,0:T(8,128)(2,1)}), bf16[4,32,768]{2,1,0:T(8,128)(2,1)S(1)}, u32[]{:S(2)}, u32[]{:S(2)}) async-start(bf16[4,32,768]{2,1,0:T(8,128)(2,1)} %reshape.411), calls=%async_computation | async-start | bytes 393216 | tf_op jit(solution)/shard_map/all_to_all | solution.py:387
  20.6 103.9 %all-gather.7.cloned.1.call-start = ((), (), s32[]{:S(2)}) async-start(), calls=%async_computation.11 | async-start | bytes 2621440 | tf_op jit(solution)/shard_map/all_gather | solution.py:384
  54.0 15.5 %copy-start.47 = (s32[8]{0:T(128)S(1)}, s32[8]{0:T(128)}, u32[]{:S(2)}) copy-start(s32[8]{0:T(128)} %constant.140.clone) | copy-start | bytes 100
  54.0 15.5 %copy-start.48 = (s32[8]{0:T(128)S(1)}, s32[8]{0:T(128)}, u32[]{:S(2)}) copy-start(s32[8]{0:T(128)} %constant.139.clone) | copy-start | bytes 100
  55.0 37.5 %collective-permute-start.9 = (bf16[352,512]{1,0:T(8,128)(2,1)S(1)}, bf16[352,512]{1,0:T(8,128)(2,1)S(1)}, u32[]{:S(2)}, u32[]{:S(2)}) collective-permute-start(bf16[352,512]{1,0:T(8,128)(2,1)S(1)} %get-tuple-element.83), channel_id=1, source_target_pairs={{0,8},{4,12},{8,0},{12,4},{16,24},{20,28},{24,16},{28,20},{1,9},{5... | collective-permute-start | bytes 1081352 | tf_op jit(solution)/shard_map/ppermute | solution.py:274
  56.5 36.5 %collective-permute-start.12 = (bf16[352,512]{1,0:T(8,128)(2,1)S(1)}, bf16[352,512]{1,0:T(8,128)(2,1)S(1)}, u32[]{:S(2)}, u32[]{:S(2)}) collective-permute-start(bf16[352,512]{1,0:T(8,128)(2,1)S(1)} %get-tuple-element.86), channel_id=1, source_target_pairs={{0,16},{4,20},{8,24},{12,28},{16,0},{20,4},{24,8},{28,12},{1,17},{... | collective-permute-start | bytes 1081352 | tf_op jit(solution)/shard_map/ppermute | solution.py:274
  60.5 7.2 %collective-permute-start = (bf16[128,768]{1,0:T(8,128)(2,1)S(1)}, bf16[128,768]{1,0:T(8,128)(2,1)S(1)}, u32[]{:S(2)}, u32[]{:S(2)}) collective-permute-start(bf16[128,768]{1,0:T(8,128)(2,1)S(1)} %bitcast.157), channel_id=1, source_target_pairs={{0,8},{4,12},{8,0},{12,4},{16,24},{20,28},{24,16},{28,20},{1,9},{5... | collective-permute-start | bytes 589832 | tf_op jit(solution)/shard_map/ppermute | solution.py:274
  67.8 26.9 %collective-permute-start.1 = (bf16[256,768]{1,0:T(8,128)(2,1)S(1)}, bf16[256,768]{1,0:T(8,128)(2,1)S(1)}, u32[]{:S(2)}, u32[]{:S(2)}) collective-permute-start(bf16[256,768]{1,0:T(8,128)(2,1)S(1)} %pad_maximum_fusion.31), channel_id=1, source_target_pairs={{0,16},{4,20},{8,24},{12,28},{16,0},{20,4},{24,8},{28,12},{1,17},{... | collective-permute-start | bytes 1179656 | tf_op jit(solution)/shard_map/ppermute | solution.py:274
  92.5 15.4 %copy-start.16 = (bf16[2816,512]{1,0:T(8,128)(2,1)S(1)}, bf16[2816,512]{1,0:T(8,128)(2,1)}, u32[]{:S(2)}) copy-start(bf16[2816,512]{1,0:T(8,128)(2,1)} %get-tuple-element.84) | copy-start | bytes 8650756
  92.6 15.3 %collective-permute-start.10 = (bf16[704,512]{1,0:T(8,128)(2,1)S(1)}, bf16[704,512]{1,0:T(8,128)(2,1)S(1)}, u32[]{:S(2)}, u32[]{:S(2)}) collective-permute-start(bf16[704,512]{1,0:T(8,128)(2,1)S(1)} %pad_maximum_fusion.21), channel_id=1, source_target_pairs={{0,16},{4,20},{8,24},{12,28},{16,0},{20,4},{24,8},{28,12},{1,17},{... | collective-permute-start | bytes 2162696 | tf_op jit(solution)/shard_map/ppermute | solution.py:274
  93.1 15.2 %collective-permute-start.13 = (bf16[704,512]{1,0:T(8,128)(2,1)S(1)}, bf16[704,512]{1,0:T(8,128)(2,1)S(1)}, u32[]{:S(2)}, u32[]{:S(2)}) collective-permute-start(bf16[704,512]{1,0:T(8,128)(2,1)S(1)} %pad_maximum_fusion.22), channel_id=1, source_target_pairs={{0,8},{4,12},{8,0},{12,4},{16,24},{20,28},{24,16},{28,20},{1,9},{5... | collective-permute-start | bytes 2162696 | tf_op jit(solution)/shard_map/ppermute | solution.py:274
  94.8 13.5 %copy-start.15 = (bf16[2816,512]{1,0:T(8,128)(2,1)S(1)}, bf16[2816,512]{1,0:T(8,128)(2,1)}, u32[]{:S(2)}) copy-start(bf16[2816,512]{1,0:T(8,128)(2,1)} %get-tuple-element.85) | copy-start | bytes 8650756
  94.8 14.3 %collective-permute-start.2 = (bf16[512,768]{1,0:T(8,128)(2,1)S(1)}, bf16[512,768]{1,0:T(8,128)(2,1)S(1)}, u32[]{:S(2)}, u32[]{:S(2)}) collective-permute-start(bf16[512,768]{1,0:T(8,128)(2,1)S(1)} %pad_maximum_fusion.20), channel_id=1, source_target_pairs={{0,4},{4,0},{8,12},{12,8},{16,20},{20,16},{24,28},{28,24},{1,5},{5... | collective-permute-start | bytes 2359304 | tf_op jit(solution)/shard_map/ppermute | solution.py:274
  108.1 3.3 collective-permute-start.11
  108.4 5.0 collective-permute-start.14
  122.6 49.8 %collective-permute-start.3 = (bf16[128,3328]{1,0:T(8,128)(2,1)S(1)}, bf16[128,3328]{1,0:T(8,128)(2,1)S(1)}, u32[]{:S(2)}, u32[]{:S(2)}) collective-permute-start(bf16[128,3328]{1,0:T(8,128)(2,1)S(1)} %get-tuple-element.65), channel_id=1, source_target_pairs={{0,8},{4,12},{8,0},{12,4},{16,24},{20,28},{24,16},{28,20},{1,9},{5... | collective-permute-start | bytes 2555912 | tf_op jit(solution)/shard_map/ppermute | solution.py:274
  124.1 45.0 %collective-permute-start.6 = (bf16[128,3328]{1,0:T(8,128)(2,1)S(1)}, bf16[128,3328]{1,0:T(8,128)(2,1)}, u32[]{:S(2)}, u32[]{:S(2)}) collective-permute-start(bf16[128,3328]{1,0:T(8,128)(2,1)S(1)} %get-tuple-element.68), channel_id=1, source_target_pairs={{0,16},{4,20},{8,24},{12,28},{16,0},{20,4},{24,8},{28,12},{1,17},{... | collective-permute-start | bytes 2555912 | tf_op jit(solution)/shard_map/ppermute | solution.py:274
  131.8 8.4 %copy-start.21 = (bf16[1024,4,32]{0,2,1:T(8,128)(2,1)}, bf16[1024,4,32]{0,2,1:T(8,128)(2,1)S(1)}, u32[]{:S(2)}) copy-start(bf16[1024,4,32]{0,2,1:T(8,128)(2,1)S(1)} %get-tuple-element.111) | copy-start | bytes 786436
  131.8 8.4 %copy-start.23 = (bf16[1024,4,32]{0,2,1:T(8,128)(2,1)}, bf16[1024,4,32]{0,2,1:T(8,128)(2,1)S(1)}, u32[]{:S(2)}) copy-start(bf16[1024,4,32]{0,2,1:T(8,128)(2,1)S(1)} %get-tuple-element.112) | copy-start | bytes 786436
  131.9 8.4 %copy-start.25 = (bf16[1024,4,32]{0,2,1:T(8,128)(2,1)}, bf16[1024,4,32]{0,2,1:T(8,128)(2,1)S(1)}, u32[]{:S(2)}) copy-start(bf16[1024,4,32]{0,2,1:T(8,128)(2,1)S(1)} %get-tuple-element.76) | copy-start | bytes 786436
  162.5 21.4 %all-to-all-start.1 = ((bf16[4,256,256]{1,2,0:T(8,128)(2,1)}), bf16[4,256,256]{1,2,0:T(8,128)(2,1)}, u32[]{:S(2)}, u32[]{:S(2)}) async-start(bf16[4,256,256]{1,2,0:T(8,128)(2,1)} %copy.130), calls=%async_computation.1 | async-start | bytes 1048576 | tf_op jit(solution)/shard_map/all_to_all | solution.py:430
  171.5 38.7 %collective-permute-start.7 = (bf16[256,3328]{1,0:T(8,128)(2,1)}, bf16[256,3328]{1,0:T(8,128)(2,1)}, u32[]{:S(2)}, u32[]{:S(2)}) collective-permute-start(bf16[256,3328]{1,0:T(8,128)(2,1)} %pad_maximum_fusion.9), channel_id=1, source_target_pairs={{0,8},{4,12},{8,0},{12,4},{16,24},{20,28},{24,16},{28,20},{1,9},{5... | collective-permute-start | bytes 5111816 | tf_op jit(solution)/shard_map/ppermute | solution.py:274
  173.8 43.2 %collective-permute-start.4 = (bf16[256,3328]{1,0:T(8,128)(2,1)}, bf16[256,3328]{1,0:T(8,128)(2,1)}, u32[]{:S(2)}, u32[]{:S(2)}) collective-permute-start(bf16[256,3328]{1,0:T(8,128)(2,1)} %pad_maximum_fusion.8), channel_id=1, source_target_pairs={{0,16},{4,20},{8,24},{12,28},{16,0},{20,4},{24,8},{28,12},{1,17},{... | collective-permute-start | bytes 5111816 | tf_op jit(solution)/shard_map/ppermute | solution.py:274
  184.7 32.3 %slice-start.6 = ((s8[6815744]{0:T(1024)(128)(4,1)}), s8[4194304]{0:T(1024)(128)(4,1)S(1)}, s32[]{:S(2)}) async-start(s8[6815744]{0:T(1024)(128)(4,1)} %bitcast.164), calls=%async_computation.18 | async-start | bytes 8388608
  216.9 7.5 %collective-permute-start.8 = (bf16[512,3328]{1,0:T(8,128)(2,1)S(1)}, bf16[512,3328]{1,0:T(8,128)(2,1)S(1)}, u32[]{:S(2)}, u32[]{:S(2)}) collective-permute-start(bf16[512,3328]{1,0:T(8,128)(2,1)S(1)} %pad_maximum_fusion.6), channel_id=1, source_target_pairs={{0,4},{4,0},{8,12},{12,8},{16,20},{20,16},{24,28},{28,24},{1,5},{5... | collective-permute-start | bytes 10223624 | tf_op jit(solution)/shard_map/ppermute | solution.py:274
  219.1 8.8 %collective-permute-start.5 = (bf16[512,3328]{1,0:T(8,128)(2,1)S(1)}, bf16[512,3328]{1,0:T(8,128)(2,1)S(1)}, u32[]{:S(2)}, u32[]{:S(2)}) collective-permute-start(bf16[512,3328]{1,0:T(8,128)(2,1)S(1)} %pad_maximum_fusion.5), channel_id=1, source_target_pairs={{0,4},{4,0},{8,12},{12,8},{16,20},{20,16},{24,28},{28,24},{1,5},{5... | collective-permute-start | bytes 10223624 | tf_op jit(solution)/shard_map/ppermute | solution.py:274
  259.5 19.8 %all-to-all-start.2 = ((bf16[4,256,256]{2,1,0:T(8,128)(2,1)}), bf16[4,256,256]{2,1,0:T(8,128)(2,1)}, u32[]{:S(2)}, u32[]{:S(2)}) async-start(bf16[4,256,256]{2,1,0:T(8,128)(2,1)} %bitcast.162), calls=%async_computation.2 | async-start | bytes 1048576 | tf_op jit(solution)/shard_map/all_to_all | solution.py:501
  264.3 241.4 %reduce-scatter.4.cloned.1.call-start = ((), (), s32[]{:S(2)}) async-start(), calls=%async_computation.8 | async-start | bytes 2621440 | tf_op jit(solution)/shard_map/reduce_scatter | solution.py:340
  268.3 78.2 %collective-permute-start.18 = (bf16[512,3328]{1,0:T(8,128)(2,1)}, bf16[512,3328]{1,0:T(8,128)(2,1)}, u32[]{:S(2)}, u32[]{:S(2)}) collective-permute-start(bf16[512,3328]{1,0:T(8,128)(2,1)} %pad_maximum_fusion.4), channel_id=1, source_target_pairs={{0,4},{4,0},{8,12},{12,8},{16,20},{20,16},{24,28},{28,24},{1,5},{5... | collective-permute-start | bytes 10223624 | tf_op jit(solution)/shard_map/ppermute | solution.py:274
  272.2 93.1 %collective-permute-start.21 = (bf16[512,3328]{1,0:T(8,128)(2,1)}, bf16[512,3328]{1,0:T(8,128)(2,1)}, u32[]{:S(2)}, u32[]{:S(2)}) collective-permute-start(bf16[512,3328]{1,0:T(8,128)(2,1)} %pad_maximum_fusion.3), channel_id=1, source_target_pairs={{0,4},{4,0},{8,12},{12,8},{16,20},{20,16},{24,28},{28,24},{1,5},{5... | collective-permute-start | bytes 10223624 | tf_op jit(solution)/shard_map/ppermute | solution.py:274
  278.8 62.1 %collective-permute-start.24 = (bf16[1408,1024]{1,0:T(8,128)(2,1)}, bf16[1408,1024]{1,0:T(8,128)(2,1)}, u32[]{:S(2)}, u32[]{:S(2)}) collective-permute-start(bf16[1408,1024]{1,0:T(8,128)(2,1)} %pad_maximum_fusion.7), channel_id=1, source_target_pairs={{0,4},{4,0},{8,12},{12,8},{16,20},{20,16},{24,28},{28,24},{1,5},{5... | collective-permute-start | bytes 8650760 | tf_op jit(solution)/shard_map/ppermute | solution.py:274
  295.8 15.7 %copy-start.26 = (bf16[1024,4,32]{0,2,1:T(8,128)(2,1)S(1)}, bf16[1024,4,32]{0,2,1:T(8,128)(2,1)}, u32[]{:S(2)}) copy-start(bf16[1024,4,32]{0,2,1:T(8,128)(2,1)} %copy-done.25) | copy-start | bytes 786436
  295.8 15.7 %copy-start.28 = (bf16[1024,4,32]{0,2,1:T(8,128)(2,1)S(1)}, bf16[1024,4,32]{0,2,1:T(8,128)(2,1)}, u32[]{:S(2)}) copy-start(bf16[1024,4,32]{0,2,1:T(8,128)(2,1)} %copy-done.27) | copy-start | bytes 786436
  295.8 29.6 %slice-start = ((s8[16777216]{0:T(1024)(128)(4,1)}), s8[4194304]{0:T(1024)(128)(4,1)S(1)}, s32[]{:S(2)}) async-start(s8[16777216]{0:T(1024)(128)(4,1)} %bitcast.149), calls=%async_computation.12 | async-start | bytes 8388608
  295.8 29.6 %slice-start.1 = ((s8[16777216]{0:T(1024)(128)(4,1)}), s8[4194304]{0:T(1024)(128)(4,1)S(1)}, s32[]{:S(2)}) async-start(s8[16777216]{0:T(1024)(128)(4,1)} %bitcast.149), calls=%async_computation.13 | async-start | bytes 8388608
  295.8 29.6 %slice-start.2 = ((s8[16777216]{0:T(1024)(128)(4,1)}), s8[4194304]{0:T(1024)(128)(4,1)S(1)}, s32[]{:S(2)}) async-start(s8[16777216]{0:T(1024)(128)(4,1)} %bitcast.149), calls=%async_computation.14 | async-start | bytes 8388608
  311.5 13.9 %slice-start.3 = ((s8[16777216]{0:T(1024)(128)(4,1)}), s8[4194304]{0:T(1024)(128)(4,1)S(1)}, s32[]{:S(2)}) async-start(s8[16777216]{0:T(1024)(128)(4,1)} %bitcast.149), calls=%async_computation.15 | async-start | bytes 8388608
  334.2 37.0 %collective-permute-start.15 = (bf16[512,768]{1,0:T(8,128)(2,1)S(1)}, bf16[512,768]{1,0:T(8,128)(2,1)}, u32[]{:S(2)}, u32[]{:S(2)}) collective-permute-start(bf16[512,768]{1,0:T(8,128)(2,1)S(1)} %slice.328), channel_id=1, source_target_pairs={{0,4},{4,0},{8,12},{12,8},{16,20},{20,16},{24,28},{28,24},{1,5},{5... | collective-permute-start | bytes 2359304 | tf_op jit(solution)/shard_map/ppermute | solution.py:274
  340.8 170.5 %reduce-scatter.8.cloned.1.call-start = ((), (), s32[]{:S(2)}) async-start(), calls=%async_computation.10 | async-start | bytes 901120 | tf_op jit(solution)/shard_map/reduce_scatter | solution.py:340
  344.5 19.0 %collective-permute-start.25 = (bf16[704,512]{1,0:T(8,128)(2,1)S(1)}, bf16[704,512]{1,0:T(8,128)(2,1)S(1)}, u32[]{:S(2)}, u32[]{:S(2)}) collective-permute-start(bf16[704,512]{1,0:T(8,128)(2,1)S(1)} %get-tuple-element.60), channel_id=1, source_target_pairs={{0,8},{4,12},{8,0},{12,4},{16,24},{20,28},{24,16},{28,20},{1,9},{5... | collective-permute-start | bytes 2162696 | tf_op jit(solution)/shard_map/ppermute | solution.py:274
  345.4 19.9 %slice-start.4 = ((s8[5767168]{0:T(1024)(128)(4,1)}), s8[4194304]{0:T(1024)(128)(4,1)S(1)}, s32[]{:S(2)}) async-start(s8[5767168]{0:T(1024)(128)(4,1)} %bitcast.151), calls=%async_computation.16 | async-start | bytes 8388608
  345.4 19.9 %slice-start.5 = ((s8[5767168]{0:T(1024)(128)(4,1)}), s8[1572864]{0:T(1024)(128)(4,1)S(1)}, s32[]{:S(2)}) async-start(s8[5767168]{0:T(1024)(128)(4,1)} %bitcast.151), calls=%async_computation.17 | async-start | bytes 3145728
  345.4 18.2 %collective-permute-start.27 = (bf16[704,512]{1,0:T(8,128)(2,1)S(1)}, bf16[704,512]{1,0:T(8,128)(2,1)S(1)}, u32[]{:S(2)}, u32[]{:S(2)}) collective-permute-start(bf16[704,512]{1,0:T(8,128)(2,1)S(1)} %get-tuple-element.61), channel_id=1, source_target_pairs={{0,16},{4,20},{8,24},{12,28},{16,0},{20,4},{24,8},{28,12},{1,17},{... | collective-permute-start | bytes 2162696 | tf_op jit(solution)/shard_map/ppermute | solution.py:274
  350.7 13.3 %copy-start.2 = (bf16[512,3328]{1,0:T(8,128)(2,1)}, bf16[512,3328]{1,0:T(8,128)(2,1)S(1)}, u32[]{:S(2)}) copy-start(bf16[512,3328]{1,0:T(8,128)(2,1)S(1)} %add_convert_fusion.1) | copy-start | bytes 10223620
  352.2 13.2 %copy-start.8 = (bf16[1024,512]{1,0:T(8,128)(2,1)S(1)}, bf16[1024,512]{1,0:T(8,128)(2,1)}, u32[]{:S(2)}) copy-start(bf16[1024,512]{1,0:T(8,128)(2,1)} %convolution_convert_fusion.5) | copy-start | bytes 3145732
  352.2 64.3 %collective-permute-start.19 = (bf16[256,3328]{1,0:T(8,128)(2,1)}, bf16[256,3328]{1,0:T(8,128)(2,1)}, u32[]{:S(2)}, u32[]{:S(2)}) collective-permute-start(bf16[256,3328]{1,0:T(8,128)(2,1)} %slice.339), channel_id=1, source_target_pairs={{0,8},{4,12},{8,0},{12,4},{16,24},{20,28},{24,16},{28,20},{1,9},{5... | collective-permute-start | bytes 5111816 | tf_op jit(solution)/shard_map/ppermute | solution.py:274
  364.1 43.7 %collective-permute-start.28 = (bf16[352,512]{1,0:T(8,128)(2,1)S(1)}, bf16[352,512]{1,0:T(8,128)(2,1)S(1)}, u32[]{:S(2)}, u32[]{:S(2)}) collective-permute-start(bf16[352,512]{1,0:T(8,128)(2,1)S(1)} %slice.363), channel_id=1, source_target_pairs={{0,8},{4,12},{8,0},{12,4},{16,24},{20,28},{24,16},{28,20},{1,9},{5... | collective-permute-start | bytes 1081352 | tf_op jit(solution)/shard_map/ppermute | solution.py:274
  369.1 51.6 %collective-permute-start.22 = (bf16[256,3328]{1,0:T(8,128)(2,1)}, bf16[256,3328]{1,0:T(8,128)(2,1)}, u32[]{:S(2)}, u32[]{:S(2)}) collective-permute-start(bf16[256,3328]{1,0:T(8,128)(2,1)} %slice.345), channel_id=1, source_target_pairs={{0,16},{4,20},{8,24},{12,28},{16,0},{20,4},{24,8},{28,12},{1,17},{... | collective-permute-start | bytes 5111816 | tf_op jit(solution)/shard_map/ppermute | solution.py:274
  370.7 44.6 %collective-permute-start.26 = (bf16[352,512]{1,0:T(8,128)(2,1)S(1)}, bf16[352,512]{1,0:T(8,128)(2,1)S(1)}, u32[]{:S(2)}, u32[]{:S(2)}) collective-permute-start(bf16[352,512]{1,0:T(8,128)(2,1)S(1)} %slice.359), channel_id=1, source_target_pairs={{0,16},{4,20},{8,24},{12,28},{16,0},{20,4},{24,8},{28,12},{1,17},{... | collective-permute-start | bytes 1081352 | tf_op jit(solution)/shard_map/ppermute | solution.py:274
  373.3 69.9 %collective-permute-start.16 = (bf16[256,768]{1,0:T(8,128)(2,1)}, bf16[256,768]{1,0:T(8,128)(2,1)}, u32[]{:S(2)}, u32[]{:S(2)}) collective-permute-start(bf16[256,768]{1,0:T(8,128)(2,1)} %slice.330), channel_id=1, source_target_pairs={{0,8},{4,12},{8,0},{12,4},{16,24},{20,28},{24,16},{28,20},{1,9},{5... | collective-permute-start | bytes 1179656 | tf_op jit(solution)/shard_map/ppermute | solution.py:274
  416.4 96.9 %reduce-scatter.6.cloned.1.call-start = ((), (), s32[]{:S(2)}) async-start(), calls=%async_computation.9 | async-start | bytes 2129920 | tf_op jit(solution)/shard_map/reduce_scatter | solution.py:340
  419.0 19.3 %collective-permute-start.20 = (bf16[128,3328]{1,0:T(8,128)(2,1)S(1)}, bf16[128,3328]{1,0:T(8,128)(2,1)S(1)}, u32[]{:S(2)}, u32[]{:S(2)}) collective-permute-start(bf16[128,3328]{1,0:T(8,128)(2,1)S(1)} %slice.341), channel_id=1, source_target_pairs={{0,16},{4,20},{8,24},{12,28},{16,0},{20,4},{24,8},{28,12},{1,17},{... | collective-permute-start | bytes 2555912 | tf_op jit(solution)/shard_map/ppermute | solution.py:274
  422.6 19.0 %collective-permute-start.23 = (bf16[128,3328]{1,0:T(8,128)(2,1)S(1)}, bf16[128,3328]{1,0:T(8,128)(2,1)S(1)}, u32[]{:S(2)}, u32[]{:S(2)}) collective-permute-start(bf16[128,3328]{1,0:T(8,128)(2,1)S(1)} %slice.347), channel_id=1, source_target_pairs={{0,8},{4,12},{8,0},{12,4},{16,24},{20,28},{24,16},{28,20},{1,9},{5... | collective-permute-start | bytes 2555912 | tf_op jit(solution)/shard_map/ppermute | solution.py:274
  444.3 5.7 %collective-permute-start.17 = (bf16[128,768]{1,0:T(8,128)(2,1)S(1)}, bf16[128,768]{1,0:T(8,128)(2,1)S(1)}, u32[]{:S(2)}, u32[]{:S(2)}) collective-permute-start(bf16[128,768]{1,0:T(8,128)(2,1)S(1)} %slice.332), channel_id=1, source_target_pairs={{0,16},{4,20},{8,24},{12,28},{16,0},{20,4},{24,8},{28,12},{1,17},{... | collective-permute-start | bytes 589832 | tf_op jit(solution)/shard_map/ppermute | solution.py:274
  450.8 51.5 %all-to-all-start.3 = ((bf16[4,32,768]{2,1,0:T(8,128)(2,1)}), bf16[4,32,768]{2,1,0:T(8,128)(2,1)S(1)}, u32[]{:S(2)}, u32[]{:S(2)}) async-start(bf16[4,32,768]{2,1,0:T(8,128)(2,1)} %bitcast.55), calls=%async_computation.4 | async-start | bytes 393216 | tf_op jit(solution)/shard_map/all_to_all | solution.py:538
  460.4 42.8 %copy-start.39 = (bf16[32,1024]{1,0:T(8,128)(2,1)S(1)}, bf16[32,1024]{1,0:T(8,128)(2,1)}, u32[]{:S(2)}) copy-start(bf16[32,1024]{1,0:T(8,128)(2,1)} %param.80) | copy-start | bytes 196612
  460.4 42.8 %copy-start.43 = (f32[32,1024]{1,0:T(8,128)S(1)}, f32[32,1024]{1,0:T(8,128)}, u32[]{:S(2)}) copy-start(f32[32,1024]{1,0:T(8,128)} %param.87) | copy-start | bytes 393220
  460.4 43.5 %copy-start.41 = (bf16[32,1024]{1,0:T(8,128)(2,1)S(1)}, bf16[32,1024]{1,0:T(8,128)(2,1)}, u32[]{:S(2)}) copy-start(bf16[32,1024]{1,0:T(8,128)(2,1)} %param.79) | copy-start | bytes 196612
  460.4 43.5 %copy-start.42 = (bf16[32,1024]{1,0:T(8,128)(2,1)S(1)}, bf16[32,1024]{1,0:T(8,128)(2,1)}, u32[]{:S(2)}) copy-start(bf16[32,1024]{1,0:T(8,128)(2,1)} %param.78) | copy-start | bytes 196612
  460.4 43.5 %copy-start.44 = (f32[32,1024]{1,0:T(8,128)S(1)}, f32[32,1024]{1,0:T(8,128)}, u32[]{:S(2)}) copy-start(f32[32,1024]{1,0:T(8,128)} %param.86) | copy-start | bytes 393220
  (44 other events, 198.3 us)
Sparse Core Ops, SparseCore 0:
  10.2 57.3 all-gather.4
  69.1 44.9 all-gather.6
  341.0 44.4 reduce-scatter.3
  416.5 22.7 reduce-scatter.7
  443.3 39.1 reduce-scatter.5

commit v2 on v0

--- a/solution.py
+++ b/solution.py
@@ -3,6 +3,8 @@
 import jax
 import jax.numpy as jnp
 from jax import lax
+from jax.experimental import pallas as pl
+from jax.experimental.pallas import tpu as pltpu
 from jax.sharding import PartitionSpec as P
 
 HEADS = 16
@@ -267,6 +269,581 @@
     )
 
 
+f32=jnp.float32; bf=jnp.bfloat16
+NT=(((1,),(1,)),((),())); TN=(((0,),(0,)),((),())); NN=(((1,),(0,)),((),()))
+def dot(a,b,dims): return lax.dot_general(a,b,dims,preferred_element_type=f32)
+
+def turn(values, cosine, signed_sine):
+    lane = lax.broadcasted_iota(jnp.int32, cosine.shape, 1)
+    first = lane % 64 < 32
+    parts = []
+    for j in range(values.shape[1] // 128):
+        part = values[:, 128 * j : 128 * j + 128]
+        partner = jnp.where(first, pltpu.roll(part, 96, 1), pltpu.roll(part, 32, 1))
+        parts.append(part * cosine + partner * signed_sine)
+    return jnp.concatenate(parts, axis=1)
+
+def attend_kernel(place_ref, act_ref, weight_hbm, cos_ref, sin_ref, id_col, id_row,
+                  normed_ref, mixed_ref, attended_ref, total_ref, peak_ref,
+                  weight, value_t, sems):
+    copies = []
+    for p in range(8):
+        copies.append(pltpu.make_async_copy(
+            weight_hbm.at[pl.ds(128 * p, 128)],
+            weight.at[pl.ds(pl.multiple_of(place_ref[p] * 128, 128), 128)], sems.at[p]))
+        copies[-1].start()
+    n = act_ref.shape[0]
+    @pl.loop(0, n // 128)
+    def _(i):
+        rows = pl.ds(pl.multiple_of(i * 128, 128), 128)
+        x = act_ref[rows, :].astype(f32)
+        c = x - jnp.mean(x, axis=-1, keepdims=True)
+        v = jnp.mean(c * c, axis=-1, keepdims=True)
+        normed_ref[rows, :] = (c * lax.rsqrt(v + NORM_EPS)).astype(bf)
+    for c in copies: c.wait()
+    @pl.loop(0, n // 256)
+    def _(i):
+        rows = pl.ds(pl.multiple_of(i * 256, 256), 256)
+        mixed = dot(normed_ref[rows, :], weight[...], NN)
+        cosine = cos_ref[rows, :]; sine = sin_ref[rows, :]
+        mixed_ref[rows, 0:256] = (turn(mixed[:, 0:256], cosine, sine).astype(bf).astype(f32) * 0.125).astype(bf)
+        mixed_ref[rows, 256:512] = turn(mixed[:, 256:512], cosine, sine).astype(bf)
+        val = mixed[:, 512:768].astype(bf)
+        mixed_ref[rows, 512:768] = val
+        value_t[:, rows] = val.astype(f32).T.astype(bf)
+    peak_ref[...] = jnp.zeros_like(peak_ref)
+    @pl.loop(0, 4)
+    def _(h):
+        pair = h // 2
+        lanes = pl.multiple_of(pair * 128, 128)
+        lane = lax.broadcasted_iota(jnp.int32, (256, 128), 1)
+        mine = lane // 64 == h % 2
+        best = None
+        for i in range(4):
+            width = min(256 * (i + 2), 1024)
+            low = 256 * i
+            q = mixed_ref[low:low + 256, pl.ds(lanes, 128)]
+            q = jnp.where(mine, q, jnp.zeros_like(q))
+            s = dot(mixed_ref[0:width, pl.ds(pl.multiple_of(256 + lanes, 128), 128)], q, NT)
+            ok = id_col[low:width, :][:, 0:1] <= id_row[0:1, low:low + 256]
+            tail = jnp.where(ok, s[low:width], MASK_FILL)
+            top = jnp.max(tail, axis=0, keepdims=True)
+            if i:
+                head = s[0:low]
+                top = jnp.maximum(top, jnp.max(head, axis=0, keepdims=True))
+                s = jnp.concatenate([head, tail], axis=0)
+            else:
+                s = tail
+            e = jnp.exp(s - top)
+            total = jnp.sum(e, axis=0, keepdims=True)
+            o = dot(value_t[pl.ds(lanes, 128), 0:width], e.astype(bf), NN)
+            o = o * (1.0 / total)
+            o = o.T.astype(bf)
+            old = attended_ref[low:low + 256, pl.ds(lanes, 128)]
+            attended_ref[low:low + 256, pl.ds(lanes, 128)] = jnp.where(mine, o, old)
+            total_ref[pl.ds(h, 1), low:low + 256] = top + jnp.log(total)
+            m = jnp.max(top, axis=1, keepdims=True)
+            best = m if best is None else jnp.maximum(best, m)
+        peak_ref[pl.ds(h, 1), :] = jnp.broadcast_to(best, (1, 128))
+
+def attend(place, act, weight, cosine, sine, id_col, id_row):
+    n = act.shape[0]
+    vm = pl.BlockSpec(memory_space=pltpu.VMEM)
+    return pl.pallas_call(
+        attend_kernel,
+        out_shape=(jax.ShapeDtypeStruct((n, 1024), bf), jax.ShapeDtypeStruct((n, 768), bf),
+                   jax.ShapeDtypeStruct((n, 256), bf), jax.ShapeDtypeStruct((8, n), f32),
+                   jax.ShapeDtypeStruct((8, 128), f32)),
+        in_specs=[pl.BlockSpec(memory_space=pltpu.SMEM), vm, pl.BlockSpec(memory_space=pl.ANY), vm, vm, vm, vm],
+        out_specs=(vm,) * 5,
+        scratch_shapes=[pltpu.VMEM((1024, 768), bf), pltpu.VMEM((256, n), bf), pltpu.SemaphoreType.DMA((8,))],
+        compiler_params=pltpu.CompilerParams(vmem_limit_bytes=48 << 20),
+        cost_estimate=pl.CostEstimate(flops=4 << 30, bytes_accessed=10 << 20, transcendentals=4 << 20),
+        name="attend",
+    )(place, act, weight, cosine, sine, id_col, id_row)
+
+def attend_back_kernel(mixed_ref, ga_ref, total_ref, cos_ref, sin_ref, id_col, id_row,
+                       gm_ref, gk_acc, gv_acc, key_t):
+    n = ga_ref.shape[0]
+    gk_acc[...] = jnp.zeros_like(gk_acc)
+    gv_acc[...] = jnp.zeros_like(gv_acc)
+    @pl.loop(0, n // 256)
+    def _(i):
+        rows = pl.ds(pl.multiple_of(i * 256, 256), 256)
+        key_t[:, rows] = mixed_ref[rows, 256:512].astype(f32).T.astype(bf)
+    @pl.loop(0, 2)
+    def _(pair):
+        lanes = pl.multiple_of(pair * 128, 128)
+        lane = lax.broadcasted_iota(jnp.int32, (256, 128), 1)
+        sub = lax.broadcasted_iota(jnp.int32, (128, 256), 0)
+        for i in range(4):
+            width = min(256 * (i + 2), 1024)
+            low = 256 * i
+            k = mixed_ref[0:width, pl.ds(pl.multiple_of(256 + lanes, 128), 128)]
+            v = mixed_ref[0:width, pl.ds(pl.multiple_of(512 + lanes, 128), 128)]
+            q_all = mixed_ref[low:low + 256, pl.ds(lanes, 128)]
+            g_all = ga_ref[low:low + 256, pl.ds(lanes, 128)]
+            kt = key_t[pl.ds(lanes, 128), 0:width]
+            ok = id_col[low:width, :][:, 0:1] <= id_row[0:1, low:low + 256]
+            def one(half, gq):
+                mine = lane // 64 == half
+                q = jnp.where(mine, q_all, jnp.zeros_like(q_all))
+                g = jnp.where(mine, g_all, jnp.zeros_like(g_all))
+                s = dot(k, q, NT) - total_ref[pl.ds(pair * 2 + half, 1), low:low + 256]
+                tail = jnp.where(ok, s[low:width], MASK_FILL)
+                s = jnp.concatenate([s[0:low], tail], axis=0) if i else tail
+                p = jnp.exp(s)
+                gp = dot(v, g, NT)
+                t = p * gp
+                delta = jnp.sum(t, axis=0, keepdims=True)
+                ds = (t - p * delta).astype(bf)
+                gv_acc[0:width, pl.ds(lanes, 128)] += dot(p.astype(bf), g, NN)
+                gk_acc[0:width, pl.ds(lanes, 128)] += dot(ds, q, NN)
+                r = dot(kt, ds, NN)
+                return jnp.where(sub // 64 == half, r, gq)
+            gq = lax.fori_loop(0, 2, one, jnp.zeros((128, 256), f32))
+            gq = gq.T * 0.125
+            cosine = cos_ref[low:low + 256, :]; sine = sin_ref[low:low + 256, :]
+            gm_ref[low:low + 256, pl.ds(lanes, 128)] = turn(gq, cosine, -sine).astype(bf)
+    @pl.loop(0, n // 256)
+    def _(i):
+        rows = pl.ds(pl.multiple_of(i * 256, 256), 256)
+        cosine = cos_ref[rows, :]; sine = sin_ref[rows, :]
+        gm_ref[rows, 256:512] = turn(gk_acc[rows, :], cosine, -sine).astype(bf)
+        gm_ref[rows, 512:768] = gv_acc[rows, :].astype(bf)
+
+def attend_back(mixed, ga, total, cosine, sine, id_col, id_row):
+    n = ga.shape[0]
+    vm = pl.BlockSpec(memory_space=pltpu.VMEM)
+    return pl.pallas_call(
+        attend_back_kernel,
+        out_shape=jax.ShapeDtypeStruct((n, 768), bf),
+        in_specs=[vm] * 7, out_specs=vm,
+        scratch_shapes=[pltpu.VMEM((n, 256), f32), pltpu.VMEM((n, 256), f32), pltpu.VMEM((256, n), bf)],
+        compiler_params=pltpu.CompilerParams(vmem_limit_bytes=48 << 20),
+        cost_estimate=pl.CostEstimate(flops=6 << 30, bytes_accessed=6 << 20, transcendentals=4 << 20),
+        name="attend_back",
+    )(mixed, ga, total, cosine, sine, id_col, id_row)
+
+def project_kernel(place_ref, gm_ref, weight_hbm, normed_ref, gn_ref, gw_hbm, weight, gw, sems, osems):
+    copies = []
+    for p in range(8):
+        copies.append(pltpu.make_async_copy(
+            weight_hbm.at[pl.ds(128 * p, 128)],
+            weight.at[pl.ds(pl.multiple_of(place_ref[p] * 128, 128), 128)], sems.at[p]))
+        copies[-1].start()
+    for c in copies: c.wait()
+    n = gm_ref.shape[0]
+    @pl.loop(0, n // 256)
+    def _(i):
+        rows = pl.ds(pl.multiple_of(i * 256, 256), 256)
+        gn_ref[rows, :] = dot(gm_ref[rows, :], weight[...], NT).astype(bf)
+    out = []
+    @pl.loop(0, 4)
+    def _(i):
+        cols = pl.ds(pl.multiple_of(i * 256, 256), 256)
+        gw[cols, :] = dot(normed_ref[:, cols], gm_ref[...], TN).astype(bf)
+    for p in range(8):
+        c = pltpu.make_async_copy(
+            gw.at[pl.ds(pl.multiple_of(place_ref[p] * 128, 128), 128)],
+            gw_hbm.at[pl.ds(128 * p, 128)], osems.at[p])
+        c.start(); out.append(c)
+    for c in out: c.wait()
+
+def project_heads(place, gm, weight, normed):
+    n = gm.shape[0]
+    vm = pl.BlockSpec(memory_space=pltpu.VMEM)
+    any_ = pl.BlockSpec(memory_space=pl.ANY)
+    return pl.pallas_call(
+        project_kernel,
+        out_shape=(jax.ShapeDtypeStruct((n, 1024), bf), jax.ShapeDtypeStruct((1024, 768), bf)),
+        in_specs=[pl.BlockSpec(memory_space=pltpu.SMEM), vm, any_, vm], out_specs=(vm, any_),
+        scratch_shapes=[pltpu.VMEM((1024, 768), bf), pltpu.VMEM((1024, 768), bf),
+                        pltpu.SemaphoreType.DMA((8,)), pltpu.SemaphoreType.DMA((8,))],
+        compiler_params=pltpu.CompilerParams(vmem_limit_bytes=48 << 20),
+        cost_estimate=pl.CostEstimate(flops=3 << 30, bytes_accessed=10 << 20, transcendentals=0),
+        name="project_heads",
+    )(place, gm, weight, normed)
+
+
+FF2=1408; FFP=1536
+def layer_norm(x):
+    c = x - jnp.mean(x, axis=-1, keepdims=True)
+    v = jnp.mean(c * c, axis=-1, keepdims=True)
+    return c * lax.rsqrt(v + NORM_EPS)
+
+FLIPS_A=((0,0),(1,0),(0,1),(1,1))
+FLIPS_B=((0,0),(0,1),(1,0),(1,1))
+
+def aligned(i, m): return pl.ds(pl.multiple_of(i * m, m), m)
+
+def feed_kernel(me_ref, att_ref, attp_ref, act_ref, actp_ref, cot_ref, cotp_ref,
+                a0, a1, a2, a3, b0, b1, b2, b3, da0, da1, da2, da3, db0, db1, db2, db3, outs,
+                part_ref, outown_ref, gnown_ref, res_ref, wo_hbm,
+                ga_keep, ga_send, gb_keep, gb_send, gda_keep, gda_send, gdb_keep, gdb_send,
+                wg, wu, wd, wo, n2, n2t, cot, out_acc, gn_acc, dg, du, dd, sems, osem):
+    me = me_ref[0]
+    core = me % 2
+    yx = me // 2
+    small = []; big = []
+    def start(lst, src, dst):
+        k = len(small) + len(big)
+        c = pltpu.make_async_copy(src, dst, sems.at[k]); c.start(); lst.append(c)
+    for p in range(4):
+        fa = FLIPS_A[p]; fb = FLIPS_B[p]
+        ja = yx ^ (fa[0] + 2 * fa[1]); jb = yx ^ (fb[0] + 2 * fb[1])
+        for which, src, j, col in ((0, (a0, a1, a2, a3)[p], ja, 0), (1, (b0, b1, b2, b3)[p], jb, 512)):
+            for half in range(2):
+                lo = col + 256 * half
+                start(small, src.at[pl.ds(128 * half, 128), pl.ds(FF2, 256)],
+                      wo.at[aligned(j * 2 + core, 128), pl.ds(lo, 256)])
+                start(small, outs.at[4 * which + p, pl.ds(128 * half, 128)],
+                      wo.at[aligned(j * 2 + 1 - core, 128), pl.ds(lo, 256)])
+    for p in range(4):
+        fa = FLIPS_A[p]; fb = FLIPS_B[p]
+        ja = yx ^ (fa[0] + 2 * fa[1]); jb = yx ^ (fb[0] + 2 * fb[1])
+        a = (a0, a1, a2, a3)[p]; b = (b0, b1, b2, b3)[p]
+        for src, dst, j in ((a, wg, ja), (b, wu, jb)):
+            start(big, src.at[pl.ds(0, 128), pl.ds(0, FF2)], dst.at[aligned(j * 2 + core, 128), pl.ds(0, FF2)])
+            start(big, src.at[pl.ds(128, 128), pl.ds(0, FF2)], dst.at[aligned(j * 2 + 1 - core, 128), pl.ds(0, FF2)])
+        start(big, (da0, da1, da2, da3)[p], wd.at[aligned(ja, 352), pl.ds(0, 512)])
+        start(big, (db0, db1, db2, db3)[p], wd.at[aligned(jb, 352), pl.ds(512, 512)])
+    wg[:, FF2:FFP] = jnp.zeros((1024, FFP - FF2), bf)
+    wu[:, FF2:FFP] = jnp.zeros((1024, FFP - FF2), bf)
+    wd[FF2:FFP, :] = jnp.zeros((FFP - FF2, 1024), bf)
+    cot[0:256, :] = cot_ref[...]
+    cot[256:512, :] = cotp_ref[...]
+    for c in small: c.wait()
+    keep = pltpu.make_async_copy(wo, wo_hbm, osem.at[16]); keep.start()
+    def first(att, act, base, own):
+        joined = jnp.concatenate([att[i] for i in range(4)], axis=1)
+        res = act[...].astype(f32) + dot(joined, wo[...], NN)
+        if own:
+            res_ref[...] = res
+        n = layer_norm(res)
+        n2[base:base + 256, :] = n.astype(bf)
+        n2t[:, base:base + 256] = n.T.astype(bf)
+    first(att_ref, act_ref, 0, True)
+    first(attp_ref, actp_ref, 256, False)
+    out_acc[...] = jnp.zeros_like(out_acc)
+    gn_acc[...] = jnp.zeros_like(gn_acc)
+    for c in big: c.wait()
+    @pl.loop(0, FFP // 256)
+    def _(t):
+        cols = aligned(t, 256)
+        g = dot(n2[...], wg[:, cols], NN)
+        u = dot(n2[...], wu[:, cols], NN)
+        gh = dot(cot[...], wd[cols, :], NT)
+        sig = 1.0 / (1.0 + jnp.exp(-g))
+        act_ = g * sig
+        h = (act_ * u).astype(bf)
+        gu = (gh * act_).astype(bf)
+        gg = (gh * u * (sig + act_ * (1.0 - sig))).astype(bf)
+        out_acc[...] += dot(h, wd[cols, :], NN)
+        gn_acc[...] += dot(gg, wg[:, cols], NT) + dot(gu, wu[:, cols], NT)
+        dg[:, cols] = dot(n2t[...], gg, NN).astype(bf)
+        du[:, cols] = dot(n2t[...], gu, NN).astype(bf)
+        dd[cols, :] = dot(h, cot[...], TN).astype(bf)
+    done = []
+    def put(src, dst):
+        c = pltpu.make_async_copy(src, dst, osem.at[len(done)]); c.start(); done.append(c)
+    for q in range(4):
+        fx, fy = FLIPS_A[q]
+        j = yx ^ (fx + 2 * fy)
+        rows = aligned(j, 256)
+        put(dg.at[rows, pl.ds(0, FF2)], (ga_send if fx else ga_keep).at[pl.ds(256 * fy, 256)])
+        put(du.at[rows, pl.ds(0, FF2)], (gb_send if fy else gb_keep).at[pl.ds(256 * fx, 256)])
+        rows = aligned(j, 352)
+        put(dd.at[rows, pl.ds(0, 512)], (gda_send if fx else gda_keep).at[pl.ds(352 * fy, 352)])
+        put(dd.at[rows, pl.ds(512, 512)], (gdb_send if fy else gdb_keep).at[pl.ds(352 * fx, 352)])
+    outown_ref[...] = out_acc[0:256, :]
+    gnown_ref[...] = gn_acc[0:256, :]
+    part_ref[0:256, :] = out_acc[256:512, :].astype(bf)
+    part_ref[256:512, :] = gn_acc[256:512, :].astype(bf)
+    keep.wait()
+    for c in done: c.wait()
+
+def feed(me, att, attp, act, actp, cot, cotp, a, b, da, db, outs):
+    vm = pl.BlockSpec(memory_space=pltpu.VMEM)
+    any_ = pl.BlockSpec(memory_space=pl.ANY)
+    S = jax.ShapeDtypeStruct
+    return pl.pallas_call(
+        feed_kernel,
+        out_shape=(S((512, 1024), bf), S((256, 1024), f32), S((256, 1024), f32), S((256, 1024), f32), S((1024, 1024), bf),
+                   *[S((512, FF2), bf)] * 4, *[S((704, 512), bf)] * 4),
+        in_specs=[pl.BlockSpec(memory_space=pltpu.SMEM)] + [vm] * 6 + [any_] * 17,
+        out_specs=(vm,) * 4 + (any_,) * 9,
+        scratch_shapes=[pltpu.VMEM((1024, FFP), bf), pltpu.VMEM((1024, FFP), bf), pltpu.VMEM((FFP, 1024), bf),
+                        pltpu.VMEM((1024, 1024), bf), pltpu.VMEM((512, 1024), bf), pltpu.VMEM((1024, 512), bf),
+                        pltpu.VMEM((512, 1024), bf), pltpu.VMEM((512, 1024), f32), pltpu.VMEM((512, 1024), f32),
+                        pltpu.VMEM((1024, FFP), bf), pltpu.VMEM((1024, FFP), bf), pltpu.VMEM((FFP, 1024), bf),
+                        pltpu.SemaphoreType.DMA((56,)), pltpu.SemaphoreType.DMA((17,))],
+        compiler_params=pltpu.CompilerParams(vmem_limit_bytes=50 << 20),
+        cost_estimate=pl.CostEstimate(flops=15 << 30, bytes_accessed=30 << 20, transcendentals=1 << 20),
+        name="feed",
+    )(me, att, attp, act, actp, cot, cotp, *a, *b, *da, *db, outs)
+
+def branch_kernel(me_ref, part_ref, outown_ref, gnown_ref, res_ref, cot_ref, att_ref, wo_ref,
+                  layer_ref, gres_ref, gatt_ref, keep_hbm, send_hbm, gw, osem):
+    me = me_ref[0]
+    core = me % 2
+    yx = me // 2
+    res = res_ref[...]
+    layer_ref[...] = (res + (outown_ref[...] + part_ref[0:256, :].astype(f32))).astype(bf)
+    g = gnown_ref[...] + part_ref[256:512, :].astype(f32)
+    c = res - jnp.mean(res, axis=-1, keepdims=True)
+    r = lax.rsqrt(jnp.mean(c * c, axis=-1, keepdims=True) + NORM_EPS)
+    xh = c * r
+    d = r * (g - jnp.mean(g, axis=-1, keepdims=True) - xh * jnp.mean(g * xh, axis=-1, keepdims=True))
+    gres = cot_ref[...].astype(f32) + d
+    gres_ref[...] = gres
+    low = gres.astype(bf)
+    for i in range(4):
+        gw[256 * i : 256 * i + 256, :] = dot(att_ref[i], low, TN).astype(bf)
+    done = []
+    def put(src, dst):
+        cc = pltpu.make_async_copy(src, dst, osem.at[len(done)]); cc.start(); done.append(cc)
+    for q in range(4):
+        fx, fy = FLIPS_A[q]
+        j = yx ^ (fx + 2 * fy)
+        for other, dst in ((0, keep_hbm), (1, send_hbm)):
+            cc = 1 - core if other else core
+            rows = aligned(j * 2 + cc, 128)
+            put(gw.at[rows, pl.ds(0, 512)], dst.at[pl.ds(128 * (2 * fx + fy), 128), pl.ds(0, 512)])
+            put(gw.at[rows, pl.ds(512, 512)], dst.at[pl.ds(128 * (2 * fy + fx), 128), pl.ds(512, 512)])
+    ga = dot(low, wo_ref[...], NT).astype(bf)
+    for z in range(4):
+        gatt_ref[z] = ga[:, 256 * z:256 * z + 256]
+    for cc in done: cc.wait()
+
+def branch(me, part, outown, gnown, res, cot, att, wo):
+    vm = pl.BlockSpec(memory_space=pltpu.VMEM)
+    any_ = pl.BlockSpec(memory_space=pl.ANY)
+    S = jax.ShapeDtypeStruct
+    return pl.pallas_call(
+        branch_kernel,
+        out_shape=(S((256, 1024), bf), S((256, 1024), f32), S((4, 256, 256), bf), S((512, 1024), bf), S((512, 1024), bf)),
+        in_specs=[pl.BlockSpec(memory_space=pltpu.SMEM)] + [vm] * 7,
+        out_specs=(vm, vm, vm, any_, any_),
+        scratch_shapes=[pltpu.VMEM((1024, 1024), bf), pltpu.SemaphoreType.DMA((16,))],
+        compiler_params=pltpu.CompilerParams(vmem_limit_bytes=40 << 20),
+        cost_estimate=pl.CostEstimate(flops=1 << 30, bytes_accessed=10 << 20, transcendentals=0),
+        name="branch",
+    )(me, part, outown, gnown, res, cot, att, wo)
+
+
+def swap(array, bit):
+    return lax.ppermute(array, "dp", [(i, i ^ bit) for i in range(8)])
+
+
+def shift(array, bits):
+    return lax.ppermute(array, "ctx", [(i, i ^ bits) for i in range(4)])
+
+
+def add_low(left, right):
+    return (left.astype(f32) + right.astype(f32)).astype(bf)
+
+
+def split_even(matrix):
+    n = matrix.shape[1] // 8
+    parts = [matrix[:, n * i : n * i + n] for i in range(8)]
+    return jnp.concatenate(parts[0::2], axis=1), jnp.concatenate(parts[1::2], axis=1)
+
+
+def join_even(even, odd):
+    n = even.shape[1] // 4
+    parts = []
+    for i in range(4):
+        parts += [even[:, n * i : n * i + n], odd[:, n * i : n * i + n]]
+    return jnp.concatenate(parts, axis=1)
+
+
+def tie(value, anchor):
+    return lax.optimization_barrier((value, anchor))[0]
+
+
+def fast_device(
+    activations,
+    block_ids,
+    cotangent,
+    w_query,
+    w_key,
+    w_value,
+    w_out,
+    w_gate,
+    w_up,
+    w_down,
+    m_query,
+    m_key,
+    m_value,
+    m_out,
+    m_gate,
+    m_up,
+    m_down,
+    clip_threshold,
+    momentum_coeff,
+):
+    me = lax.axis_index("dp")
+    z = lax.axis_index("ctx")
+    core = me % 2
+    me_ref = me.astype(jnp.int32).reshape(1)
+    _, span, width = activations.shape
+    length = block_ids.shape[1]
+    act = activations.reshape(span, width)
+    cot = cotangent.reshape(span, width)
+    g0, g1 = split_even(w_gate)
+    u0, u1 = split_even(w_up)
+    wide = jnp.concatenate([g0, u0, g1, u1, w_out], axis=1)
+    wide = lax.all_gather(wide, "ctx", axis=0, tiled=True)
+    act_all = lax.all_gather(act, "ctx", axis=0, tiled=True)
+    heads = jnp.stack(
+        [
+            jnp.concatenate([w[:, 256 * i : 256 * i + 256] for w in (w_query, w_key, w_value)], 1)
+            for i in range(4)
+        ]
+    )
+    heads = lax.all_to_all(heads, "ctx", 0, 0, tiled=True).reshape(128, 768)
+    hx = swap(heads, 2)
+    hy = swap(jnp.concatenate([heads, hx], axis=0), 4)
+    four = jnp.concatenate([heads, hy[:128], hx, hy[128:]], axis=0)
+    heads_rel = jnp.concatenate([four, swap(four, 1)], axis=0)
+    places = jnp.arange(8, dtype=jnp.int32)
+    places = ((places >> 2 & 1) | (places >> 1 & 1) << 1 | (places & 1) << 2) ^ me
+    mine = lax.dynamic_slice_in_dim(wide, core * 2 * FF2, 2 * FF2, 1)
+    other = swap(lax.dynamic_slice_in_dim(wide, (1 - core) * 2 * FF2, 2 * FF2, 1), 1)
+    out_rows = wide[:, 4 * FF2 :]
+
+    def group(lo, col):
+        gate = jnp.concatenate([mine[:, lo : lo + FF2], other[:, lo : lo + FF2]], axis=0)
+        out = jnp.concatenate(
+            [out_rows[:, col : col + 256], out_rows[:, col + 256 : col + 512]], axis=0
+        )
+        return jnp.concatenate([gate, out], axis=1)
+
+    def spread(own, first, second):
+        near = swap(own, first)
+        return [own, near, swap(own, second), swap(near, second)]
+
+    piece_a = spread(group(0, 0), 2, 4)
+    piece_b = spread(group(FF2, 512), 4, 2)
+    outs = swap(jnp.stack([p[:, FF2:] for p in piece_a + piece_b]), 1)
+    down = tie(w_down, act_all)
+    downs = jnp.stack([down] + [shift(down, d) for d in (1, 2, 3)])
+    down = jnp.concatenate(
+        [lax.dynamic_index_in_dim(downs, z ^ i, 0, keepdims=False) for i in range(4)], axis=0
+    )
+    piece_da = spread(down[:, :512], 2, 4)
+    piece_db = spread(down[:, 512:], 4, 2)
+    act_other = swap(act, 1)
+    cot_other = swap(cot, 1)
+    cosine, sine = rotary_tables(jnp.arange(length, dtype=jnp.int32), HEAD_DIM)
+    cosine = jnp.concatenate([cosine] * 4, axis=1)
+    sine = jnp.concatenate([-sine, sine, -sine, sine], axis=1)
+    id_row = jnp.broadcast_to(block_ids, (8, length))
+    id_col = jnp.broadcast_to(block_ids.reshape(length, 1), (length, 128))
+    normed, mixed, attended, totals, peaks = attend(
+        places, act_all, heads_rel, cosine, sine, id_col, id_row
+    )
+    attended = lax.all_to_all(attended.reshape(4, span, 256), "ctx", 0, 0, tiled=True)
+    attended_other = swap(attended, 1)
+    (part, out_own, back_own, residual, full_out, *grads) = feed(
+        me_ref, attended, attended_other, act, act_other, cot, cot_other,
+        piece_a, piece_b, piece_da, piece_db, outs,
+    )
+    ga_keep, ga_send, gb_keep, gb_send, gda_keep, gda_send, gdb_keep, gdb_send = grads
+    part = swap(part, 1)
+    layer_out, grad_residual, grad_attended, go_keep, go_send = branch(
+        me_ref, part, out_own, back_own, residual, cot, attended, full_out
+    )
+    grad_attended = lax.all_to_all(grad_attended, "ctx", 0, 0, tiled=True).reshape(length, 256)
+    grad_a = add_low(ga_keep, swap(ga_send, 2))
+    grad_b = add_low(gb_keep, swap(gb_send, 4))
+    grad_da = add_low(gda_keep, swap(gda_send, 2))
+    grad_db = add_low(gdb_keep, swap(gdb_send, 4))
+    grad_a = add_low(grad_a[:256], swap(grad_a[256:], 4))
+    grad_b = add_low(grad_b[:256], swap(grad_b[256:], 2))
+    grad_da = add_low(grad_da[:352], swap(grad_da[352:], 4))
+    grad_db = add_low(grad_db[:352], swap(grad_db[352:], 2))
+    grad_out = add_low(go_keep, swap(go_send, 1))
+    grad_oa = add_low(grad_out[:256, :512], swap(grad_out[256:, :512], 2))
+    grad_ob = add_low(grad_out[:256, 512:], swap(grad_out[256:, 512:], 4))
+    grad_oa = add_low(grad_oa[:128], swap(grad_oa[128:], 4))
+    grad_ob = add_low(grad_ob[:128], swap(grad_ob[128:], 2))
+
+    def core_rows(which):
+        return jnp.concatenate(
+            [lax.dynamic_slice_in_dim(g, which * 128, 128, 0) for g in (grad_a, grad_b)], axis=1
+        )
+
+    own_half = core_rows(core)
+    other_half = swap(core_rows(1 - core), 1)
+    flip = core == 1
+    grad_wide = jnp.concatenate(
+        [
+            jnp.where(flip, other_half, own_half),
+            jnp.where(flip, own_half, other_half),
+            grad_oa,
+            grad_ob,
+        ],
+        axis=1,
+    )
+    grad_wide = lax.psum_scatter(grad_wide, "ctx", scatter_dimension=0, tiled=True).astype(f32)
+    grad_d = jnp.concatenate([grad_da, grad_db], axis=1)
+    grad_d = lax.psum_scatter(grad_d, "ctx", scatter_dimension=0, tiled=True).astype(f32)
+    grad_mixed = attend_back(mixed, grad_attended, totals, cosine, sine, id_col, id_row)
+    grad_normed, grad_heads = project_heads(places, grad_mixed, heads_rel, normed)
+    grad_normed = lax.psum_scatter(grad_normed, "ctx", scatter_dimension=0, tiled=True)
+    tokens_wide = act.astype(f32)
+    unused, first_pull = jax.vjp(normalize, tokens_wide)
+    input_grad = grad_residual + first_pull(grad_normed.astype(f32))[0]
+    grad_heads = add_low(grad_heads[:512], swap(grad_heads[512:], 1))
+    grad_heads = add_low(grad_heads[:256], swap(grad_heads[256:], 2))
+    grad_heads = add_low(grad_heads[:128], swap(grad_heads[128:], 4))
+    grad_heads = lax.all_to_all(grad_heads.reshape(4, 32, 768), "ctx", 0, 0, tiled=True)
+    grad_heads = grad_heads.astype(f32)
+    grad_qkv = [
+        jnp.concatenate([grad_heads[i, :, 256 * k : 256 * k + 256] for i in range(4)], axis=1)
+        for k in range(3)
+    ]
+    for bit in (1, 2, 4):
+        peaks = jnp.maximum(peaks, swap(peaks, bit))
+    peak_list = jnp.stack([peaks] + [shift(peaks, d) for d in (1, 2, 3)])[:, :4, 0]
+    head_peaks = jnp.concatenate(
+        [lax.dynamic_index_in_dim(peak_list, z ^ i, 0, keepdims=False) for i in range(4)]
+    )
+    weight_grads = (
+        *grad_qkv,
+        grad_wide[:, 4 * FF2 :],
+        join_even(grad_wide[:, :FF2], grad_wide[:, 2 * FF2 : 3 * FF2]),
+        join_even(grad_wide[:, FF2 : 2 * FF2], grad_wide[:, 3 * FF2 : 4 * FF2]),
+        grad_d,
+    )
+    moments = (m_query, m_key, m_value, m_out, m_gate, m_up, m_down)
+    new_moments = tuple(
+        (momentum_coeff * moment + gradient for moment, gradient in zip(moments, weight_grads))
+    )
+    head_scale = jnp.sqrt(clip_threshold / jnp.maximum(head_peaks, clip_threshold))
+    column_scale = jnp.repeat(head_scale, HEAD_DIM)
+    rates = (LEARN_RATE, LEARN_RATE, LEARN_RATE, OUT_RATE, LEARN_RATE, LEARN_RATE, LEARN_RATE)
+    shard_list = (w_query, w_key, w_value, w_out, w_gate, w_up, w_down)
+    updated = [
+        matrix.astype(jnp.float32) - rate * moment
+        for matrix, moment, rate in zip(shard_list, new_moments, rates)
+    ]
+    updated[0] = updated[0] * column_scale[None, :]
+    updated[1] = updated[1] * column_scale[None, :]
+    updated = [matrix.astype(bf) for matrix in updated]
+    return (
+        layer_out[None],
+        input_grad[None],
+        *weight_grads,
+        *new_moments,
+        *updated,
+        head_peaks,
+        head_scale,
+    )
+
+
 def solution(mesh):
     placed = (
         P("dp", "ctx", None),
@@ -289,8 +866,9 @@
         P(),
         P(),
     )
+    fits = mesh.shape["dp"] == 8 and mesh.shape["ctx"] == 4
     return jax.shard_map(
-        per_device,
+        fast_device if fits else per_device,
         mesh=mesh,
         in_specs=placed,
         out_specs=(

time: 2030 us -> 436 us (0.21)
  waiting for transfers between devices: 1790 us -> 193 us
  matrix products: 122 us -> 0 us
  Pallas kernels: 0 us -> 82.9 us
  starting transfers between devices: 1.3 us -> 65.4 us
  blocking collectives: 40.1 us -> 0 us
    reduce_scatter x9 -> x3, waiting for transfers between devices: 1310 us -> 17.8 us  [the longest x1 17.8 us: fast_device(): lax.psum_scatter(grad_wide, 'ctx', scatter_dimension=0, tiled=True)]
    all_gather x9 -> x2, waiting for transfers between devices: 477 us -> 56 us  [the longest x1 36.4 us: fast_device(): act_all = lax.all_gather(act, 'ctx', axis=0, tiled=True)]
    dot_general x27 -> x0, matrix products: 122 us -> none  [the longest x7 34.2 us: shard_gradient(): lax.dot_general(left_rows, right_rows, (((0,), (0,)), ((), ())), preferre...]
    ppermute x0 -> x47, waiting for transfers between devices: none -> 103 us  [the longest x41 98.7 us: swap(): return lax.ppermute(array, 'dp', [(i, i ^ bit) for i in range(8)])]
    pallas_call x0 -> x5, Pallas kernels: none -> 82.9 us  [the longest x1 27.6 us: feed(): pl.pallas_call(feed_kernel, out_shape=(S((512, 1024), bf), S((256, 1024),...]
    ppermute x0 -> x47, starting transfers between devices: none -> 45.3 us  [the longest x41 36.6 us: swap(): return lax.ppermute(array, 'dp', [(i, i ^ bit) for i in range(8)])]
    pmax x1 -> x0, blocking collectives: 40.1 us -> none  [per_device(): head_peaks = lax.pmax(local_peaks, ('dp', 'ctx'))]
  transfers between devices with their start and end apart: 18 -> 56, of which waited for: 18 -> 26; matrix products, arithmetic and copies ran while one was open for 7% -> 13% of each run, Pallas kernels for 0% -> 13%
where the time goes in v2:
time: 436 us; the launch traced here: 434 us
  waiting for transfers between devices  193 us (44%)
  Pallas kernels  82.9 us (19%)
  starting transfers between devices  65.4 us (15%)
  other arithmetic  40.9 us (9%)
  local copies, waits for them, and re-layouts  35.7 us (8%)
  between operations  16.2 us (4%)
    ppermute x41, waiting for transfers between devices, swap(): return lax.ppermute(array, 'dp', [(i, i ^ bit) for i in range(8)])  98.7 us
    ppermute x41, starting transfers between devices, swap(): return lax.ppermute(array, 'dp', [(i, i ^ bit) for i in range(8)])  36.6 us
    all_gather x1, waiting for transfers between devices, fast_device(): act_all = lax.all_gather(act, 'ctx', axis=0, tiled=True)  36.4 us
    pallas_call x1, Pallas kernels, feed(): pl.pallas_call(feed_kernel, out_shape=(S((512, 1024), bf), S((256, 1024),...  27.6 us
    unnamed x142, local copies, waits for them, and re-layouts  20.5 us
    pallas_call x1, Pallas kernels, attend(): pl.pallas_call(attend_kernel, out_shape=(jax.ShapeDtypeStruct((n, 1024),...  20.5 us
    all_gather x1, waiting for transfers between devices, fast_device(): wide = lax.all_gather(wide, 'ctx', axis=0, tiled=True)  19.7 us
    reduce_scatter x1, waiting for transfers between devices, fast_device(): lax.psum_scatter(grad_wide, 'ctx', scatter_dimension=0, tiled=True)  17.8 us
  transfers between devices with their start and end apart: 56, of which 26 were waited for; matrix products, arithmetic and copies ran while one was open for 13% of the time, Pallas kernels for 13%

profile of v2, /device:TPU:0, one launch (start us, length us, event | category | flops | bytes accessed | tf_op | source)
XLA Modules:
  0.0 433.9 jit_solution(12781779080383801171)
XLA Ops:
  8.4 1.9 concatenate.91
  11.1 6.3 %all-to-all-start = ((bf16[4,32,768]{2,1,0:T(8,128)(2,1)}), bf16[4,32,768]{2,1,0:T(8,128)(2,1)S(1)}, u32[]{:S(2)}, u32[]{:S(2)}) async-start(bf16[4,32,768]{2,1,0:T(8,128)(2,1)} %pad_maximum_fusion.10), calls=%async_computation | async-start | bytes 393216 | tf_op jit(solution)/shard_map/all_to_all | solution.py:705
  18.2 6.9 %all-to-all-done = bf16[4,32,768]{2,1,0:T(8,128)(2,1)S(1)} async-done(((bf16[4,32,768]{2,1,0:T(8,128)(2,1)}), bf16[4,32,768]{2,1,0:T(8,128)(2,1)S(1)}, u32[]{:S(2)}, u32[]{:S(2)}) %all-to-all-start) | async-done | bytes 196640 | tf_op jit(solution)/shard_map/all_to_all | solution.py:705
  25.1 1.5 collective-permute-start
  26.6 1.9 fusion.6
  31.5 1.5 collective-permute-start.1
  33.1 19.7 %all-gather.4.cloned.1.call-done = bf16[128,6656]{1,0:T(8,128)(2,1)} async-done(((bf16[32,6656]{1,0:T(8,128)(2,1)}), bf16[128,6656]{1,0:T(8,128)(2,1)}) %all-gather.4.cloned.1.call-update) | async-done | bytes 1703952 | tf_op jit(solution)/shard_map/all_gather | solution.py:697
  58.5 1.5 collective-permute-start.7
  63.0 36.4 %all-gather.6.cloned.1.call-done = bf16[1,1024,1024]{2,1,0:T(8,128)(2,1)} async-done(((bf16[1,256,1024]{2,1,0:T(8,128)(2,1)}), bf16[1,1024,1024]{2,1,0:T(8,128)(2,1)}) %all-gather.6.cloned.1.call-update) | async-done | bytes 2097168 | tf_op jit(solution)/shard_map/all_gather | solution.py:698
  99.3 1.7 collective-permute-start.14
  101.0 2.7 collective-permute-start.15
  103.7 1.5 collective-permute-start.8
  105.2 2.0 maximum_maximum_fusion.1.b0
  107.2 1.6 collective-permute-done.13
  108.8 1.5 collective-permute-start.10
  111.0 20.5 %attend.1 = (bf16[1024,1024]{1,0:T(8,128)(2,1)}, bf16[1024,768]{1,0:T(8,128)(2,1)S(1)}, bf16[1024,256]{1,0:T(8,128)(2,1)}, f32[8,1024]{1,0:T(8,128)S(1)}, f32[8,128]{1,0:T(8,128)S(1)}) custom-call(s32[8]{0:T(128)S(1)} %fusion.25.place_ref, bf16[1024,1024]{1,0:T(8,128)(2,1)} %bitcast.115, bf16[1024,768]{1,0:T(8,128)(2,1)S(1)} %constant_dynamic-update-slice_fusion.weight_hbm, ...), custom_call_target="tpu_custom_call" | custom-call | flops 4294967296 | bytes 10485760 | tf_op jit(solution)/shard_map/attend/pallas_call | solution.py:352
  132.8 3.7 all-to-all-start.1
  136.5 1.6 collective-permute-start.11
  139.4 1.6 fusion.12
  141.2 3.0 collective-permute-done.10.b1
  144.2 1.5 collective-permute-start.12
  145.7 1.6 fusion.11
  147.2 13.2 %collective-permute-done.9.a3 = bf16[256,1664]{1,0:T(8,128)(2,1)} collective-permute-done((bf16[256,1664]{1,0:T(8,128)(2,1)}, bf16[256,1664]{1,0:T(8,128)(2,1)}, u32[]{:S(2)}, u32[]{:S(2)}) %collective-permute-start.9) | collective-permute-done | bytes 852000 | tf_op jit(solution)/shard_map/ppermute | solution.py:636
  160.4 1.6 fusion.10
  162.6 1.6 fusion.9
  164.9 11.5 %collective-permute-done.12.b3 = bf16[256,1664]{1,0:T(8,128)(2,1)S(1)} collective-permute-done((bf16[256,1664]{1,0:T(8,128)(2,1)}, bf16[256,1664]{1,0:T(8,128)(2,1)S(1)}, u32[]{:S(2)}, u32[]{:S(2)}) %collective-permute-start.12) | collective-permute-done | bytes 852000 | tf_op jit(solution)/shard_map/ppermute | solution.py:636
  177.5 1.6 collective-permute-start.16
  179.0 1.4 collective-permute-start.19
  181.3 6.8 %collective-permute-done.16.da1 = bf16[352,512]{1,0:T(8,128)(2,1)S(1)} collective-permute-done((bf16[352,512]{1,0:T(8,128)(2,1)S(1)}, bf16[352,512]{1,0:T(8,128)(2,1)S(1)}, u32[]{:S(2)}, u32[]{:S(2)}) %collective-permute-start.16) | collective-permute-done | bytes 360480 | tf_op jit(solution)/shard_map/ppermute | solution.py:636
  188.1 1.5 collective-permute-start.20
  190.3 1.4 collective-permute-start.18
  191.8 6.3 %collective-permute-done.17.da2 = bf16[352,512]{1,0:T(8,128)(2,1)S(1)} collective-permute-done((bf16[352,512]{1,0:T(8,128)(2,1)S(1)}, bf16[352,512]{1,0:T(8,128)(2,1)S(1)}, u32[]{:S(2)}, u32[]{:S(2)}) %collective-permute-start.17) | collective-permute-done | bytes 360480 | tf_op jit(solution)/shard_map/ppermute | solution.py:636
  198.6 6.2 %collective-permute-done.18.da3 = bf16[352,512]{1,0:T(8,128)(2,1)S(1)} collective-permute-done((bf16[352,512]{1,0:T(8,128)(2,1)S(1)}, bf16[352,512]{1,0:T(8,128)(2,1)S(1)}, u32[]{:S(2)}, u32[]{:S(2)}) %collective-permute-start.18) | collective-permute-done | bytes 360480 | tf_op jit(solution)/shard_map/ppermute | solution.py:636
  204.8 1.7 collective-permute-done.21.db3
  206.5 27.6 %feed.1 = (bf16[512,1024]{1,0:T(8,128)(2,1)}, f32[256,1024]{1,0:T(8,128)}, f32[256,1024]{1,0:T(8,128)}, f32[256,1024]{1,0:T(8,128)}, bf16[1024,1024]{1,0:T(8,128...) custom-call(s32[1]{0:T(128)} %bitcast.me_ref, ...), custom_call_target="tpu_custom_call" | custom-call | flops 16106127360 | bytes 31457280 | tf_op jit(solution)/shard_map/feed/pallas_call | solution.py:570
  238.2 15.2 %collective-permute-done.37 = bf16[704,512]{1,0:T(8,128)(2,1)S(1)} collective-permute-done((bf16[704,512]{1,0:T(8,128)(2,1)}, bf16[704,512]{1,0:T(8,128)(2,1)S(1)}, u32[]{:S(2)}, u32[]{:S(2)}) %collective-permute-start.37) | collective-permute-done | bytes 720928 | tf_op jit(solution)/shard_map/ppermute | solution.py:636
  253.4 2.2 add_convert_fusion.5
  256.6 1.5 collective-permute-start.38
  265.2 5.0 %branch.1 = (bf16[256,1024]{1,0:T(8,128)(2,1)}, f32[256,1024]{1,0:T(8,128)S(1)}, bf16[4,256,256]{2,1,0:T(8,128)(2,1)S(1)}, bf16[512,1024]{1,0:T(8,128)(2,1)S(1)}, bf16[512,1024]{1,0:T(8,128)(2,1)}) custom-call(s32[1]{0:T(128)} %bitcast.me_ref, bf16[512,1024]{1,0:T(8,128)(2,1)} %collective-permute-done.23.part_ref, f32[256,1024]{1,0:T(8,128)S(1)} %copy-done.5, ...), custom_call_target="tpu_custom_call" | custom-call | flops 1073741824 | bytes 10485760 | tf_op jit(solution)/shard_map/branch/pallas_call | solution.py:623
  273.0 4.9 %all-to-all-start.2 = ((bf16[4,256,256]{2,1,0:T(8,128)(2,1)}), bf16[4,256,256]{2,1,0:T(8,128)(2,1)S(1)}, u32[]{:S(2)}, u32[]{:S(2)}) async-start(bf16[4,256,256]{2,1,0:T(8,128)(2,1)} %copy-done.12), calls=%async_computation.2 | async-start | bytes 1048576 | tf_op jit(solution)/shard_map/all_to_all | solution.py:758
  277.9 14.3 %collective-permute-done.38 = bf16[352,512]{1,0:T(8,128)(2,1)} collective-permute-done((bf16[352,512]{1,0:T(8,128)(2,1)S(1)}, bf16[352,512]{1,0:T(8,128)(2,1)}, u32[]{:S(2)}, u32[]{:S(2)}) %collective-permute-start.38) | collective-permute-done | bytes 360480 | tf_op jit(solution)/shard_map/ppermute | solution.py:636
  295.7 2.1 add_convert_fusion.1
  300.3 1.8 add_convert_fusion
  306.3 17.6 %attend_back.1.gm_ref = bf16[1024,768]{1,0:T(8,128)(2,1)S(1)} custom-call(bf16[1024,768]{1,0:T(8,128)(2,1)S(1)} %copy-done.18, bf16[1024,256]{1,0:T(8,128)(2,1)S(1)} %bitcast.97, f32[8,1024]{1,0:T(8,128)S(1)} %copy-done.20, f32[1024,128]{1,0:T(8,128)S(1)} %get-tuple-element.199.cos_ref, f32[1024,128]{1,0:T(8,128)S(1)} %copy-done.9, ...), custom_call_target="tpu_custom_call" | custom-call | flops 6442450944 | bytes 6291456 | tf_op jit(solution)/shard_map/attend_back/pallas_call | solution.py:418
  323.9 12.3 %project_heads.1 = (bf16[1024,1024]{1,0:T(8,128)(2,1)}, bf16[1024,768]{1,0:T(8,128)(2,1)S(1)}) custom-call(s32[8]{0:T(128)S(1)} %fusion.25.place_ref, bf16[1024,768]{1,0:T(8,128)(2,1)S(1)} %attend_back.1.gm_ref, bf16[1024,768]{1,0:T(8,128)(2,1)S(1)} %copy-done.16, bf16[1024,1024]{1,0:T(8,128)(2,1)} %get-tuple-element.63.normed_ref), custom_call_target="tpu_custom_call" | custom-call | flops 3221225472 | bytes 10485760 | tf_op jit(solution)/shard_map/project_heads/pallas_call | solution.py:457
  337.7 1.7 add_convert_fusion.2
  342.7 1.4 add_convert_fusion.6
  344.3 3.5 collective-permute-done.33
  349.7 1.5 collective-permute-start.36
  351.2 2.1 collective-permute-done.34
  353.3 2.3 collective-permute-done.36
  357.1 1.5 collective-permute-start.25
  361.9 6.1 %collective-permute-done.42 = f32[8,128]{1,0:T(8,128)S(1)} collective-permute-done((f32[8,128]{1,0:T(8,128)S(1)}, f32[8,128]{1,0:T(8,128)S(1)}, u32[]{:S(2)}, u32[]{:S(2)}) %collective-permute-start.42) | collective-permute-done | bytes 4128 | tf_op jit(solution)/shard_map/ppermute | solution.py:636
  369.1 2.6 collective-permute-done.43
  371.7 1.7 collective-permute-start.44
  373.4 2.4 collective-permute-start.45
  378.5 3.0 collective-permute-done.46
  382.7 4.8 %all-to-all-start.3 = ((bf16[4,32,768]{2,1,0:T(8,128)(2,1)}), bf16[4,32,768]{2,1,0:T(8,128)(2,1)S(1)}, u32[]{:S(2)}, u32[]{:S(2)}) async-start(bf16[4,32,768]{2,1,0:T(8,128)(2,1)} %bitcast.30), calls=%async_computation.4 | async-start | bytes 393216 | tf_op jit(solution)/shard_map/all_to_all | solution.py:802
  388.3 2.1 subtract_convert_fusion
  390.4 8.1 %all-to-all-done.3 = bf16[4,32,768]{2,1,0:T(8,128)(2,1)S(1)} async-done(((bf16[4,32,768]{2,1,0:T(8,128)(2,1)}), bf16[4,32,768]{2,1,0:T(8,128)(2,1)S(1)}, u32[]{:S(2)}, u32[]{:S(2)}) %all-to-all-start.3) | async-done | bytes 196640 | tf_op jit(solution)/shard_map/all_to_all | solution.py:802
  400.2 1.5 fusion.3
  401.8 1.5 fusion.5
  404.6 17.8 %reduce-scatter.6.cloned.1.call-done = bf16[32,6656]{1,0:T(8,128)(2,1)} async-done(((bf16[128,6656]{1,0:T(8,128)(2,1)}), bf16[32,6656]{1,0:T(8,128)(2,1)}) %reduce-scatter.6.cloned.1.call-update) | async-done | bytes 426000 | tf_op jit(solution)/shard_map/reduce_scatter | solution.py:790
  425.8 1.6 subtract_convert_fusion.3
  (289 shorter events, 69.7 us)
Async XLA Ops:
  7.2 45.5 %all-gather.4.cloned.1.call-start = ((), (), s32[]{:S(2)}) async-start(), calls=%async_computation.7 | async-start | bytes 2129920 | tf_op jit(solution)/shard_map/all_gather | solution.py:697
  11.1 14.0 %all-to-all-start = ((bf16[4,32,768]{2,1,0:T(8,128)(2,1)}), bf16[4,32,768]{2,1,0:T(8,128)(2,1)S(1)}, u32[]{:S(2)}, u32[]{:S(2)}) async-start(bf16[4,32,768]{2,1,0:T(8,128)(2,1)} %pad_maximum_fusion.10), calls=%async_computation | async-start | bytes 393216 | tf_op jit(solution)/shard_map/all_to_all | solution.py:705
  17.5 81.9 %all-gather.6.cloned.1.call-start = ((), (), s32[]{:S(2)}) async-start(), calls=%async_computation.11 | async-start | bytes 2621440 | tf_op jit(solution)/shard_map/all_gather | solution.py:698
  25.1 5.7 %collective-permute-start = (bf16[128,768]{1,0:T(8,128)(2,1)S(1)}, bf16[128,768]{1,0:T(8,128)(2,1)S(1)}, u32[]{:S(2)}, u32[]{:S(2)}) collective-permute-start(bf16[128,768]{1,0:T(8,128)(2,1)S(1)} %bitcast.103), channel_id=1, source_target_pairs={{0,8},{4,12},{8,0},{12,4},{16,24},{20,28},{24,16},{28,20},{1,9},{5... | collective-permute-start | bytes 589832 | tf_op jit(solution)/shard_map/ppermute | solution.py:636
  29.4 81.6 %copy-start.8 = (f32[1024,128]{1,0:T(8,128)}, f32[1024,128]{1,0:T(8,128)S(1)}, u32[]{:S(2)}) copy-start(f32[1024,128]{1,0:T(8,128)S(1)} %get-tuple-element.200.sin_ref) | copy-start | bytes 1572868
  31.5 22.5 %collective-permute-start.1 = (bf16[256,768]{1,0:T(8,128)(2,1)}, bf16[256,768]{1,0:T(8,128)(2,1)}, u32[]{:S(2)}, u32[]{:S(2)}) collective-permute-start(bf16[256,768]{1,0:T(8,128)(2,1)} %pad_maximum_fusion.9), channel_id=1, source_target_pairs={{0,16},{4,20},{8,24},{12,28},{16,0},{20,4},{24,8},{28,12},{1,17},{... | collective-permute-start | bytes 1179656 | tf_op jit(solution)/shard_map/ppermute | solution.py:636
  53.9 2.8 collective-permute-start.6
  56.1 4.9 %collective-permute-start.2 = (bf16[512,768]{1,0:T(8,128)(2,1)}, bf16[512,768]{1,0:T(8,128)(2,1)}, u32[]{:S(2)}, u32[]{:S(2)}) collective-permute-start(bf16[512,768]{1,0:T(8,128)(2,1)} %pad_maximum_fusion.1), channel_id=1, source_target_pairs={{0,4},{4,0},{8,12},{12,8},{16,20},{20,16},{24,28},{28,24},{1,5},{5... | collective-permute-start | bytes 2359304 | tf_op jit(solution)/shard_map/ppermute | solution.py:636
  56.5 48.7 %copy-start.39 = (bf16[128,256]{1,0:T(8,128)(2,1)}, bf16[128,256]{1,0:T(8,128)(2,1)S(1)}, u32[]{:S(2)}) copy-start(bf16[128,256]{1,0:T(8,128)(2,1)S(1)} %get-tuple-element.106) | copy-start | bytes 196612
  56.5 48.7 %copy-start.41 = (bf16[128,256]{1,0:T(8,128)(2,1)}, bf16[128,256]{1,0:T(8,128)(2,1)S(1)}, u32[]{:S(2)}) copy-start(bf16[128,256]{1,0:T(8,128)(2,1)S(1)} %get-tuple-element.107) | copy-start | bytes 196612
  58.5 40.9 %copy-start.36 = (bf16[88,1024]{1,0:T(8,128)(2,1)S(1)}, bf16[88,1024]{1,0:T(8,128)(2,1)}, u32[]{:S(2)}) copy-start(bf16[88,1024]{1,0:T(8,128)(2,1)} %param.28) | copy-start | bytes 540676
  58.5 51.8 %collective-permute-start.7 = (bf16[256,1664]{1,0:T(8,128)(2,1)}, bf16[256,1664]{1,0:T(8,128)(2,1)}, u32[]{:S(2)}, u32[]{:S(2)}) collective-permute-start(bf16[256,1664]{1,0:T(8,128)(2,1)} %maximum_maximum_fusion.a0), channel_id=1, source_target_pairs={{0,8},{4,12},{8,0},{12,4},{16,24},{20,28},{24,16},{28,20},{1,9},{5... | collective-permute-start | bytes 2555912 | tf_op jit(solution)/shard_map/ppermute | solution.py:636
  61.0 49.8 %copy-start.64 = (s32[1,1024]{1,0:T(1,128)S(1)}, s32[1,1024]{1,0:T(1,128)}, u32[]{:S(2)}) copy-start(s32[1,1024]{1,0:T(1,128)} %param.20) | copy-start | bytes 12292
  62.2 69.3 %copy-start.15 = (bf16[1024,768]{1,0:T(8,128)(2,1)}, bf16[1024,768]{1,0:T(8,128)(2,1)S(1)}, u32[]{:S(2)}) copy-start(bf16[1024,768]{1,0:T(8,128)(2,1)S(1)} %constant_dynamic-update-slice_fusion.weight_hbm) | copy-start | bytes 4718596
  99.3 9.4 %collective-permute-start.13 = (bf16[88,1024]{1,0:T(8,128)(2,1)S(1)}, bf16[88,1024]{1,0:T(8,128)(2,1)S(1)}, u32[]{:S(2)}, u32[]{:S(2)}) collective-permute-start(bf16[88,1024]{1,0:T(8,128)(2,1)S(1)} %copy-done.36), channel_id=1, source_target_pairs={{0,1},{1,0},{2,3},{3,2},{4,5},{5,4},{6,7},{7,6},{8,9},{9,8},{10,11... | collective-permute-start | bytes 540680 | tf_op jit(solution)/shard_map/ppermute | solution.py:640
  99.3 37.1 %collective-permute-start.14 = (bf16[88,1024]{1,0:T(8,128)(2,1)S(1)}, bf16[88,1024]{1,0:T(8,128)(2,1)}, u32[]{:S(2)}, u32[]{:S(2)}) collective-permute-start(bf16[88,1024]{1,0:T(8,128)(2,1)S(1)} %copy-done.36), channel_id=1, source_target_pairs={{0,2},{1,3},{2,0},{3,1},{4,6},{5,7},{6,4},{7,5},{8,10},{9,11},{10,... | collective-permute-start | bytes 540680 | tf_op jit(solution)/shard_map/ppermute | solution.py:640
  101.0 35.5 %collective-permute-start.15 = (bf16[88,1024]{1,0:T(8,128)(2,1)S(1)}, bf16[88,1024]{1,0:T(8,128)(2,1)}, u32[]{:S(2)}, u32[]{:S(2)}) collective-permute-start(bf16[88,1024]{1,0:T(8,128)(2,1)S(1)} %copy-done.36), channel_id=1, source_target_pairs={{0,3},{1,2},{2,1},{3,0},{4,7},{5,6},{6,5},{7,4},{8,11},{9,10},{10,... | collective-permute-start | bytes 540680 | tf_op jit(solution)/shard_map/ppermute | solution.py:640
  103.7 37.3 %collective-permute-start.8 = (bf16[256,1664]{1,0:T(8,128)(2,1)}, bf16[256,1664]{1,0:T(8,128)(2,1)}, u32[]{:S(2)}, u32[]{:S(2)}) collective-permute-start(bf16[256,1664]{1,0:T(8,128)(2,1)} %maximum_maximum_fusion.a0), channel_id=1, source_target_pairs={{0,16},{4,20},{8,24},{12,28},{16,0},{20,4},{24,8},{28,12},{1,17},{... | collective-permute-start | bytes 2555912 | tf_op jit(solution)/shard_map/ppermute | solution.py:636
  108.8 35.4 %collective-permute-start.10 = (bf16[256,1664]{1,0:T(8,128)(2,1)}, bf16[256,1664]{1,0:T(8,128)(2,1)}, u32[]{:S(2)}, u32[]{:S(2)}) collective-permute-start(bf16[256,1664]{1,0:T(8,128)(2,1)} %maximum_maximum_fusion.1.b0), channel_id=1, source_target_pairs={{0,16},{4,20},{8,24},{12,28},{16,0},{20,4},{24,8},{28,12},{1,17},{... | collective-permute-start | bytes 2555912 | tf_op jit(solution)/shard_map/ppermute | solution.py:636
  110.2 50.2 %collective-permute-start.9 = (bf16[256,1664]{1,0:T(8,128)(2,1)}, bf16[256,1664]{1,0:T(8,128)(2,1)}, u32[]{:S(2)}, u32[]{:S(2)}) collective-permute-start(bf16[256,1664]{1,0:T(8,128)(2,1)} %collective-permute-done.7.a1), channel_id=1, source_target_pairs={{0,16},{4,20},{8,24},{12,28},{16,0},{20,4},{24,8},{28,12},{1,17},{... | collective-permute-start | bytes 2555912 | tf_op jit(solution)/shard_map/ppermute | solution.py:636
  111.0 25.4 %copy-start.13 = (bf16[1,256,1024]{2,1,0:T(8,128)(2,1)S(1)}, bf16[1,256,1024]{2,1,0:T(8,128)(2,1)}, u32[]{:S(2)}) copy-start(bf16[1,256,1024]{2,1,0:T(8,128)(2,1)} %param.21) | copy-start | bytes 1572868
  132.8 48.5 %all-to-all-start.1 = ((bf16[4,256,256]{2,1,0:T(8,128)(2,1)}), bf16[4,256,256]{2,1,0:T(8,128)(2,1)S(1)}, u32[]{:S(2)}, u32[]{:S(2)}) async-start(bf16[4,256,256]{2,1,0:T(8,128)(2,1)} %bitcast.8), calls=%async_computation.1 | async-start | bytes 1048576 | tf_op jit(solution)/shard_map/all_to_all | solution.py:747
  136.5 44.0 %collective-permute-start.5 = (bf16[256,1024]{1,0:T(8,128)(2,1)S(1)}, bf16[256,1024]{1,0:T(8,128)(2,1)S(1)}, u32[]{:S(2)}, u32[]{:S(2)}) collective-permute-start(bf16[256,1024]{1,0:T(8,128)(2,1)S(1)} %bitcast.99), channel_id=1, source_target_pairs={{0,4},{4,0},{8,12},{12,8},{16,20},{20,16},{24,28},{28,24},{1,5},{5... | collective-permute-start | bytes 1572872 | tf_op jit(solution)/shard_map/ppermute | solution.py:636
  136.5 27.7 %collective-permute-start.11 = (bf16[256,1664]{1,0:T(8,128)(2,1)}, bf16[256,1664]{1,0:T(8,128)(2,1)S(1)}, u32[]{:S(2)}, u32[]{:S(2)}) collective-permute-start(bf16[256,1664]{1,0:T(8,128)(2,1)} %maximum_maximum_fusion.1.b0), channel_id=1, source_target_pairs={{0,8},{4,12},{8,0},{12,4},{16,24},{20,28},{24,16},{28,20},{1,9},{5... | collective-permute-start | bytes 2555912 | tf_op jit(solution)/shard_map/ppermute | solution.py:636
  141.0 40.2 %collective-permute-start.4 = (bf16[256,1024]{1,0:T(8,128)(2,1)S(1)}, bf16[256,1024]{1,0:T(8,128)(2,1)}, u32[]{:S(2)}, u32[]{:S(2)}) collective-permute-start(bf16[256,1024]{1,0:T(8,128)(2,1)S(1)} %bitcast.102), channel_id=1, source_target_pairs={{0,4},{4,0},{8,12},{12,8},{16,20},{20,16},{24,28},{28,24},{1,5},{5... | collective-permute-start | bytes 1572872 | tf_op jit(solution)/shard_map/ppermute | solution.py:636
  144.2 32.2 %collective-permute-start.12 = (bf16[256,1664]{1,0:T(8,128)(2,1)}, bf16[256,1664]{1,0:T(8,128)(2,1)S(1)}, u32[]{:S(2)}, u32[]{:S(2)}) collective-permute-start(bf16[256,1664]{1,0:T(8,128)(2,1)} %collective-permute-done.10.b1), channel_id=1, source_target_pairs={{0,8},{4,12},{8,0},{12,4},{16,24},{20,28},{24,16},{28,20},{1,9},{5... | collective-permute-start | bytes 2555912 | tf_op jit(solution)/shard_map/ppermute | solution.py:636
  177.1 29.4 %collective-permute-start.22 = (bf16[8,256,256]{2,1,0:T(8,128)(2,1)}, bf16[8,256,256]{2,1,0:T(8,128)(2,1)}, u32[]{:S(2)}, u32[]{:S(2)}) collective-permute-start(bf16[8,256,256]{2,1,0:T(8,128)(2,1)} %fusion.7), channel_id=1, source_target_pairs={{0,4},{4,0},{8,12},{12,8},{16,20},{20,16},{24,28},{28,24},{1,5},{5... | collective-permute-start | bytes 3145736 | tf_op jit(solution)/shard_map/ppermute | solution.py:636
  177.5 10.6 %collective-permute-start.16 = (bf16[352,512]{1,0:T(8,128)(2,1)S(1)}, bf16[352,512]{1,0:T(8,128)(2,1)S(1)}, u32[]{:S(2)}, u32[]{:S(2)}) collective-permute-start(bf16[352,512]{1,0:T(8,128)(2,1)S(1)} %get-tuple-element.121.da0), channel_id=1, source_target_pairs={{0,8},{4,12},{8,0},{12,4},{16,24},{20,28},{24,16},{28,20},{1,9},{5... | collective-permute-start | bytes 1081352 | tf_op jit(solution)/shard_map/ppermute | solution.py:636
  179.0 11.3 %collective-permute-start.19 = (bf16[352,512]{1,0:T(8,128)(2,1)S(1)}, bf16[352,512]{1,0:T(8,128)(2,1)S(1)}, u32[]{:S(2)}, u32[]{:S(2)}) collective-permute-start(bf16[352,512]{1,0:T(8,128)(2,1)S(1)} %get-tuple-element.120.db0), channel_id=1, source_target_pairs={{0,16},{4,20},{8,24},{12,28},{16,0},{20,4},{24,8},{28,12},{1,17},{... | collective-permute-start | bytes 1081352 | tf_op jit(solution)/shard_map/ppermute | solution.py:636
  180.5 17.6 %collective-permute-start.17 = (bf16[352,512]{1,0:T(8,128)(2,1)S(1)}, bf16[352,512]{1,0:T(8,128)(2,1)S(1)}, u32[]{:S(2)}, u32[]{:S(2)}) collective-permute-start(bf16[352,512]{1,0:T(8,128)(2,1)S(1)} %get-tuple-element.121.da0), channel_id=1, source_target_pairs={{0,16},{4,20},{8,24},{12,28},{16,0},{20,4},{24,8},{28,12},{1,17},{... | collective-permute-start | bytes 1081352 | tf_op jit(solution)/shard_map/ppermute | solution.py:636
  181.3 25.2 %collective-permute-start.3 = (bf16[4,256,256]{2,1,0:T(8,128)(2,1)S(1)}, bf16[4,256,256]{2,1,0:T(8,128)(2,1)S(1)}, u32[]{:S(2)}, u32[]{:S(2)}) collective-permute-start(bf16[4,256,256]{2,1,0:T(8,128)(2,1)S(1)} %all-to-all-done.1.att_ref), channel_id=1, source_target_pairs={{0,4},{4,0},{8,12},{12,8},{16,20},{20,16},{24,28},{28,24},{1,5},{5... | collective-permute-start | bytes 1572872 | tf_op jit(solution)/shard_map/ppermute | solution.py:636
  188.1 10.5 %collective-permute-start.20 = (bf16[352,512]{1,0:T(8,128)(2,1)S(1)}, bf16[352,512]{1,0:T(8,128)(2,1)S(1)}, u32[]{:S(2)}, u32[]{:S(2)}) collective-permute-start(bf16[352,512]{1,0:T(8,128)(2,1)S(1)} %get-tuple-element.120.db0), channel_id=1, source_target_pairs={{0,8},{4,12},{8,0},{12,4},{16,24},{20,28},{24,16},{28,20},{1,9},{5... | collective-permute-start | bytes 1081352 | tf_op jit(solution)/shard_map/ppermute | solution.py:636
  190.3 14.4 %collective-permute-start.18 = (bf16[352,512]{1,0:T(8,128)(2,1)S(1)}, bf16[352,512]{1,0:T(8,128)(2,1)S(1)}, u32[]{:S(2)}, u32[]{:S(2)}) collective-permute-start(bf16[352,512]{1,0:T(8,128)(2,1)S(1)} %collective-permute-done.16.da1), channel_id=1, source_target_pairs={{0,16},{4,20},{8,24},{12,28},{16,0},{20,4},{24,8},{28,12},{1,17},{... | collective-permute-start | bytes 1081352 | tf_op jit(solution)/shard_map/ppermute | solution.py:636
  198.0 8.4 %collective-permute-start.21 = (bf16[352,512]{1,0:T(8,128)(2,1)S(1)}, bf16[352,512]{1,0:T(8,128)(2,1)S(1)}, u32[]{:S(2)}, u32[]{:S(2)}) collective-permute-start(bf16[352,512]{1,0:T(8,128)(2,1)S(1)} %collective-permute-done.19.db1), channel_id=1, source_target_pairs={{0,8},{4,12},{8,0},{12,4},{16,24},{20,28},{24,16},{28,20},{1,9},{5... | collective-permute-start | bytes 1081352 | tf_op jit(solution)/shard_map/ppermute | solution.py:636
  234.0 24.0 %copy-start.38 = (bf16[704,512]{1,0:T(8,128)(2,1)S(1)}, bf16[704,512]{1,0:T(8,128)(2,1)}, u32[]{:S(2)}) copy-start(bf16[704,512]{1,0:T(8,128)(2,1)} %get-tuple-element.74) | copy-start | bytes 2162692
  234.1 19.4 %collective-permute-start.37 = (bf16[704,512]{1,0:T(8,128)(2,1)}, bf16[704,512]{1,0:T(8,128)(2,1)S(1)}, u32[]{:S(2)}, u32[]{:S(2)}) collective-permute-start(bf16[704,512]{1,0:T(8,128)(2,1)} %get-tuple-element.73), channel_id=1, source_target_pairs={{0,8},{4,12},{8,0},{12,4},{16,24},{20,28},{24,16},{28,20},{1,9},{5... | collective-permute-start | bytes 2162696 | tf_op jit(solution)/shard_map/ppermute | solution.py:636
  234.7 25.8 %collective-permute-start.23 = (bf16[512,1024]{1,0:T(8,128)(2,1)}, bf16[512,1024]{1,0:T(8,128)(2,1)}, u32[]{:S(2)}, u32[]{:S(2)}) collective-permute-start(bf16[512,1024]{1,0:T(8,128)(2,1)} %get-tuple-element.53), channel_id=1, source_target_pairs={{0,4},{4,0},{8,12},{12,8},{16,20},{20,16},{24,28},{28,24},{1,5},{5... | collective-permute-start | bytes 3145736 | tf_op jit(solution)/shard_map/ppermute | solution.py:636
  234.7 23.4 %collective-permute-start.39 = (bf16[704,512]{1,0:T(8,128)(2,1)}, bf16[704,512]{1,0:T(8,128)(2,1)S(1)}, u32[]{:S(2)}, u32[]{:S(2)}) collective-permute-start(bf16[704,512]{1,0:T(8,128)(2,1)} %get-tuple-element.75), channel_id=1, source_target_pairs={{0,16},{4,20},{8,24},{12,28},{16,0},{20,4},{24,8},{28,12},{1,17},{... | collective-permute-start | bytes 2162696 | tf_op jit(solution)/shard_map/ppermute | solution.py:636
  236.2 59.6 %collective-permute-start.27 = (bf16[512,1408]{1,0:T(8,128)(2,1)}, bf16[512,1408]{1,0:T(8,128)(2,1)}, u32[]{:S(2)}, u32[]{:S(2)}) collective-permute-start(bf16[512,1408]{1,0:T(8,128)(2,1)} %get-tuple-element.67), channel_id=1, source_target_pairs={{0,8},{4,12},{8,0},{12,4},{16,24},{20,28},{24,16},{28,20},{1,9},{5... | collective-permute-start | bytes 4325384 | tf_op jit(solution)/shard_map/ppermute | solution.py:636
  237.6 62.7 %collective-permute-start.29 = (bf16[512,1408]{1,0:T(8,128)(2,1)}, bf16[512,1408]{1,0:T(8,128)(2,1)}, u32[]{:S(2)}, u32[]{:S(2)}) collective-permute-start(bf16[512,1408]{1,0:T(8,128)(2,1)} %get-tuple-element.69), channel_id=1, source_target_pairs={{0,16},{4,20},{8,24},{12,28},{16,0},{20,4},{24,8},{28,12},{1,17},{... | collective-permute-start | bytes 4325384 | tf_op jit(solution)/shard_map/ppermute | solution.py:636
  256.6 35.6 %collective-permute-start.38 = (bf16[352,512]{1,0:T(8,128)(2,1)S(1)}, bf16[352,512]{1,0:T(8,128)(2,1)}, u32[]{:S(2)}, u32[]{:S(2)}) collective-permute-start(bf16[352,512]{1,0:T(8,128)(2,1)S(1)} %slice.479), channel_id=1, source_target_pairs={{0,16},{4,20},{8,24},{12,28},{16,0},{20,4},{24,8},{28,12},{1,17},{... | collective-permute-start | bytes 1081352 | tf_op jit(solution)/shard_map/ppermute | solution.py:636
  259.9 33.5 %collective-permute-start.40 = (bf16[352,512]{1,0:T(8,128)(2,1)}, bf16[352,512]{1,0:T(8,128)(2,1)}, u32[]{:S(2)}, u32[]{:S(2)}) collective-permute-start(bf16[352,512]{1,0:T(8,128)(2,1)} %slice.481), channel_id=1, source_target_pairs={{0,8},{4,12},{8,0},{12,4},{16,24},{20,28},{24,16},{28,20},{1,9},{5... | collective-permute-start | bytes 1081352 | tf_op jit(solution)/shard_map/ppermute | solution.py:636
  273.0 64.2 %collective-permute-start.32 = (bf16[512,1024]{1,0:T(8,128)(2,1)}, bf16[512,1024]{1,0:T(8,128)(2,1)}, u32[]{:S(2)}, u32[]{:S(2)}) collective-permute-start(bf16[512,1024]{1,0:T(8,128)(2,1)} %get-tuple-element.71), channel_id=1, source_target_pairs={{0,4},{4,0},{8,12},{12,8},{16,20},{20,16},{24,28},{28,24},{1,5},{5... | collective-permute-start | bytes 3145736 | tf_op jit(solution)/shard_map/ppermute | solution.py:636
  273.0 31.9 %all-to-all-start.2 = ((bf16[4,256,256]{2,1,0:T(8,128)(2,1)}), bf16[4,256,256]{2,1,0:T(8,128)(2,1)S(1)}, u32[]{:S(2)}, u32[]{:S(2)}) async-start(bf16[4,256,256]{2,1,0:T(8,128)(2,1)} %copy-done.12), calls=%async_computation.2 | async-start | bytes 1048576 | tf_op jit(solution)/shard_map/all_to_all | solution.py:758
  277.9 110.3 %reduce-scatter.8.cloned.1.call-start = ((), (), s32[]{:S(2)}) async-start(), calls=%async_computation.10 | async-start | bytes 901120 | tf_op jit(solution)/shard_map/reduce_scatter | solution.py:792
  295.5 104.8 %reduce-scatter.4.cloned.1.call-start = ((), (), s32[]{:S(2)}) async-start(), calls=%async_computation.8 | async-start | bytes 2621440 | tf_op jit(solution)/shard_map/reduce_scatter | solution.py:795
  298.8 42.5 %collective-permute-start.28 = (bf16[256,1408]{1,0:T(8,128)(2,1)}, bf16[256,1408]{1,0:T(8,128)(2,1)}, u32[]{:S(2)}, u32[]{:S(2)}) collective-permute-start(bf16[256,1408]{1,0:T(8,128)(2,1)} %slice.450), channel_id=1, source_target_pairs={{0,16},{4,20},{8,24},{12,28},{16,0},{20,4},{24,8},{28,12},{1,17},{... | collective-permute-start | bytes 2162696 | tf_op jit(solution)/shard_map/ppermute | solution.py:636
  303.5 39.2 %collective-permute-start.30 = (bf16[256,1408]{1,0:T(8,128)(2,1)}, bf16[256,1408]{1,0:T(8,128)(2,1)}, u32[]{:S(2)}, u32[]{:S(2)}) collective-permute-start(bf16[256,1408]{1,0:T(8,128)(2,1)} %slice.452), channel_id=1, source_target_pairs={{0,8},{4,12},{8,0},{12,4},{16,24},{20,28},{24,16},{28,20},{1,9},{5... | collective-permute-start | bytes 2162696 | tf_op jit(solution)/shard_map/ppermute | solution.py:636
  337.1 18.6 %collective-permute-start.24 = (bf16[512,768]{1,0:T(8,128)(2,1)}, bf16[512,768]{1,0:T(8,128)(2,1)}, u32[]{:S(2)}, u32[]{:S(2)}) collective-permute-start(bf16[512,768]{1,0:T(8,128)(2,1)} %slice.366), channel_id=1, source_target_pairs={{0,4},{4,0},{8,12},{12,8},{16,20},{20,16},{24,28},{28,24},{1,5},{5... | collective-permute-start | bytes 2359304 | tf_op jit(solution)/shard_map/ppermute | solution.py:636
  337.2 85.2 %reduce-scatter.6.cloned.1.call-start = ((), (), s32[]{:S(2)}) async-start(), calls=%async_computation.9 | async-start | bytes 2129920 | tf_op jit(solution)/shard_map/reduce_scatter | solution.py:790
  339.5 8.3 %collective-permute-start.33 = (bf16[256,512]{1,0:T(8,128)(2,1)S(1)}, bf16[256,512]{1,0:T(8,128)(2,1)S(1)}, u32[]{:S(2)}, u32[]{:S(2)}) collective-permute-start(bf16[256,512]{1,0:T(8,128)(2,1)S(1)} %get-tuple-element.114), channel_id=1, source_target_pairs={{0,8},{4,12},{8,0},{12,4},{16,24},{20,28},{24,16},{28,20},{1,9},{5... | collective-permute-start | bytes 786440 | tf_op jit(solution)/shard_map/ppermute | solution.py:636
  340.1 8.0 %collective-permute-start.35 = (bf16[256,512]{1,0:T(8,128)(2,1)S(1)}, bf16[256,512]{1,0:T(8,128)(2,1)S(1)}, u32[]{:S(2)}, u32[]{:S(2)}) collective-permute-start(bf16[256,512]{1,0:T(8,128)(2,1)S(1)} %get-tuple-element.115), channel_id=1, source_target_pairs={{0,16},{4,20},{8,24},{12,28},{16,0},{20,4},{24,8},{28,12},{1,17},{... | collective-permute-start | bytes 786440 | tf_op jit(solution)/shard_map/ppermute | solution.py:636
  348.3 5.0 %collective-permute-start.34 = (bf16[128,512]{1,0:T(8,128)(2,1)S(1)}, bf16[128,512]{1,0:T(8,128)(2,1)S(1)}, u32[]{:S(2)}, u32[]{:S(2)}) collective-permute-start(bf16[128,512]{1,0:T(8,128)(2,1)S(1)} %slice.456), channel_id=1, source_target_pairs={{0,16},{4,20},{8,24},{12,28},{16,0},{20,4},{24,8},{28,12},{1,17},{... | collective-permute-start | bytes 393224 | tf_op jit(solution)/shard_map/ppermute | solution.py:636
  349.6 9.0 %collective-permute-start.31 = (bf16[128,2816]{1,0:T(8,128)(2,1)S(1)}, bf16[128,2816]{1,0:T(8,128)(2,1)S(1)}, u32[]{:S(2)}, u32[]{:S(2)}) collective-permute-start(bf16[128,2816]{1,0:T(8,128)(2,1)S(1)} %pad_maximum_fusion.4), channel_id=1, source_target_pairs={{0,4},{4,0},{8,12},{12,8},{16,20},{20,16},{24,28},{28,24},{1,5},{5... | collective-permute-start | bytes 2162696 | tf_op jit(solution)/shard_map/ppermute | solution.py:636
  349.7 6.0 %collective-permute-start.36 = (bf16[128,512]{1,0:T(8,128)(2,1)S(1)}, bf16[128,512]{1,0:T(8,128)(2,1)S(1)}, u32[]{:S(2)}, u32[]{:S(2)}) collective-permute-start(bf16[128,512]{1,0:T(8,128)(2,1)S(1)} %slice.460), channel_id=1, source_target_pairs={{0,8},{4,12},{8,0},{12,4},{16,24},{20,28},{24,16},{28,20},{1,9},{5... | collective-permute-start | bytes 393224 | tf_op jit(solution)/shard_map/ppermute | solution.py:636
  357.1 19.0 %collective-permute-start.25 = (bf16[256,768]{1,0:T(8,128)(2,1)S(1)}, bf16[256,768]{1,0:T(8,128)(2,1)S(1)}, u32[]{:S(2)}, u32[]{:S(2)}) collective-permute-start(bf16[256,768]{1,0:T(8,128)(2,1)S(1)} %slice.434), channel_id=1, source_target_pairs={{0,8},{4,12},{8,0},{12,4},{16,24},{20,28},{24,16},{28,20},{1,9},{5... | collective-permute-start | bytes 1179656 | tf_op jit(solution)/shard_map/ppermute | solution.py:636
  360.2 1.2 collective-permute-start.41
  361.4 6.6 %collective-permute-start.42 = (f32[8,128]{1,0:T(8,128)S(1)}, f32[8,128]{1,0:T(8,128)S(1)}, u32[]{:S(2)}, u32[]{:S(2)}) collective-permute-start(f32[8,128]{1,0:T(8,128)S(1)} %max.13), channel_id=1, source_target_pairs={{0,8},{4,12},{8,0},{12,4},{16,24},{20,28},{24,16},{28,20},{1,9},{5... | collective-permute-start | bytes 12296 | tf_op jit(solution)/shard_map/ppermute | solution.py:636
  368.0 3.7 collective-permute-start.43
  371.7 6.7 %collective-permute-start.44 = (f32[8,128]{1,0:T(8,128)S(1)}, f32[8,128]{1,0:T(8,128)S(1)}, u32[]{:S(2)}, u32[]{:S(2)}) collective-permute-start(f32[8,128]{1,0:T(8,128)S(1)} %max.15), channel_id=1, source_target_pairs={{0,1},{1,0},{2,3},{3,2},{4,5},{5,4},{6,7},{7,6},{8,9},{9,8},{10,11... | collective-permute-start | bytes 12296 | tf_op jit(solution)/shard_map/ppermute | solution.py:640
  373.4 5.0 %collective-permute-start.45 = (f32[8,128]{1,0:T(8,128)S(1)}, f32[8,128]{1,0:T(8,128)S(1)}, u32[]{:S(2)}, u32[]{:S(2)}) collective-permute-start(f32[8,128]{1,0:T(8,128)S(1)} %max.15), channel_id=1, source_target_pairs={{0,2},{1,3},{2,0},{3,1},{4,6},{5,7},{6,4},{7,5},{8,10},{9,11},{10,... | collective-permute-start | bytes 12296 | tf_op jit(solution)/shard_map/ppermute | solution.py:640
  375.8 5.6 %collective-permute-start.46 = (f32[8,128]{1,0:T(8,128)S(1)}, f32[8,128]{1,0:T(8,128)S(1)}, u32[]{:S(2)}, u32[]{:S(2)}) collective-permute-start(f32[8,128]{1,0:T(8,128)S(1)} %max.15), channel_id=1, source_target_pairs={{0,3},{1,2},{2,1},{3,0},{4,7},{5,6},{6,5},{7,4},{8,11},{9,10},{10,... | collective-permute-start | bytes 12296 | tf_op jit(solution)/shard_map/ppermute | solution.py:640
  376.2 5.7 %collective-permute-start.26 = (bf16[128,768]{1,0:T(8,128)(2,1)S(1)}, bf16[128,768]{1,0:T(8,128)(2,1)S(1)}, u32[]{:S(2)}, u32[]{:S(2)}) collective-permute-start(bf16[128,768]{1,0:T(8,128)(2,1)S(1)} %slice.436), channel_id=1, source_target_pairs={{0,16},{4,20},{8,24},{12,28},{16,0},{20,4},{24,8},{28,12},{1,17},{... | collective-permute-start | bytes 589832 | tf_op jit(solution)/shard_map/ppermute | solution.py:636
  382.7 15.8 %all-to-all-start.3 = ((bf16[4,32,768]{2,1,0:T(8,128)(2,1)}), bf16[4,32,768]{2,1,0:T(8,128)(2,1)S(1)}, u32[]{:S(2)}, u32[]{:S(2)}) async-start(bf16[4,32,768]{2,1,0:T(8,128)(2,1)} %bitcast.30), calls=%async_computation.4 | async-start | bytes 393216 | tf_op jit(solution)/shard_map/all_to_all | solution.py:802
  (59 other events, 381.6 us)
Sparse Core Ops, SparseCore 0:
  10.4 42.2 all-gather.3
  54.3 44.9 all-gather.5
  295.6 23.8 reduce-scatter.7
  337.3 44.1 reduce-scatter.3
  383.8 38.5 reduce-scatter.5

commit v3 on v2

--- a/solution.py
+++ b/solution.py
@@ -292,11 +292,11 @@
             weight_hbm.at[pl.ds(128 * p, 128)],
             weight.at[pl.ds(pl.multiple_of(place_ref[p] * 128, 128), 128)], sems.at[p]))
         copies[-1].start()
-    n = act_ref.shape[0]
+    n = normed_ref.shape[0]
     @pl.loop(0, n // 128)
     def _(i):
         rows = pl.ds(pl.multiple_of(i * 128, 128), 128)
-        x = act_ref[rows, :].astype(f32)
+        x = act_ref[pl.ds(pl.multiple_of(i // 2 * 352 + i % 2 * 128, 32), 128), :].astype(f32)
         c = x - jnp.mean(x, axis=-1, keepdims=True)
         v = jnp.mean(c * c, axis=-1, keepdims=True)
         normed_ref[rows, :] = (c * lax.rsqrt(v + NORM_EPS)).astype(bf)
@@ -347,7 +347,7 @@
         peak_ref[pl.ds(h, 1), :] = jnp.broadcast_to(best, (1, 128))
 
 def attend(place, act, weight, cosine, sine, id_col, id_row):
-    n = act.shape[0]
+    n = cosine.shape[0]
     vm = pl.BlockSpec(memory_space=pltpu.VMEM)
     return pl.pallas_call(
         attend_kernel,
@@ -357,8 +357,8 @@
         in_specs=[pl.BlockSpec(memory_space=pltpu.SMEM), vm, pl.BlockSpec(memory_space=pl.ANY), vm, vm, vm, vm],
         out_specs=(vm,) * 5,
         scratch_shapes=[pltpu.VMEM((1024, 768), bf), pltpu.VMEM((256, n), bf), pltpu.SemaphoreType.DMA((8,))],
-        compiler_params=pltpu.CompilerParams(vmem_limit_bytes=48 << 20),
-        cost_estimate=pl.CostEstimate(flops=4 << 30, bytes_accessed=10 << 20, transcendentals=4 << 20),
+        compiler_params=pltpu.CompilerParams(vmem_limit_bytes=28 << 20),
+        cost_estimate=pl.CostEstimate(flops=4294967296, bytes_accessed=10485760, transcendentals=0),
         name="attend",
     )(place, act, weight, cosine, sine, id_col, id_row)
 
@@ -420,12 +420,12 @@
         out_shape=jax.ShapeDtypeStruct((n, 768), bf),
         in_specs=[vm] * 7, out_specs=vm,
         scratch_shapes=[pltpu.VMEM((n, 256), f32), pltpu.VMEM((n, 256), f32), pltpu.VMEM((256, n), bf)],
-        compiler_params=pltpu.CompilerParams(vmem_limit_bytes=48 << 20),
-        cost_estimate=pl.CostEstimate(flops=6 << 30, bytes_accessed=6 << 20, transcendentals=4 << 20),
+        compiler_params=pltpu.CompilerParams(vmem_limit_bytes=28 << 20),
+        cost_estimate=pl.CostEstimate(flops=6442450944, bytes_accessed=6291456, transcendentals=0),
         name="attend_back",
     )(mixed, ga, total, cosine, sine, id_col, id_row)
 
-def project_kernel(place_ref, gm_ref, weight_hbm, normed_ref, gn_ref, gw_hbm, weight, gw, sems, osems):
+def tokens_kernel(place_ref, gm_ref, weight_hbm, gn_ref, weight, sems):
     copies = []
     for p in range(8):
         copies.append(pltpu.make_async_copy(
@@ -433,37 +433,49 @@
             weight.at[pl.ds(pl.multiple_of(place_ref[p] * 128, 128), 128)], sems.at[p]))
         copies[-1].start()
     for c in copies: c.wait()
-    n = gm_ref.shape[0]
-    @pl.loop(0, n // 256)
+    @pl.loop(0, gm_ref.shape[0] // 256)
     def _(i):
         rows = pl.ds(pl.multiple_of(i * 256, 256), 256)
         gn_ref[rows, :] = dot(gm_ref[rows, :], weight[...], NT).astype(bf)
-    out = []
+
+def project_tokens(place, gm, weight):
+    n = gm.shape[0]
+    vm = pl.BlockSpec(memory_space=pltpu.VMEM)
+    return pl.pallas_call(
+        tokens_kernel,
+        out_shape=jax.ShapeDtypeStruct((n, 1024), bf),
+        in_specs=[pl.BlockSpec(memory_space=pltpu.SMEM), vm, pl.BlockSpec(memory_space=pl.ANY)], out_specs=vm,
+        scratch_shapes=[pltpu.VMEM((1024, 768), bf), pltpu.SemaphoreType.DMA((8,))],
+        compiler_params=pltpu.CompilerParams(vmem_limit_bytes=28 << 20),
+        cost_estimate=pl.CostEstimate(flops=1073741824, bytes_accessed=4194304, transcendentals=0),
+        name="project_tokens",
+    )(place, gm, weight)
+
+def weights_kernel(place_ref, gm_ref, normed_ref, keep_hbm, send_hbm, gw, osems):
     @pl.loop(0, 4)
     def _(i):
         cols = pl.ds(pl.multiple_of(i * 256, 256), 256)
         gw[cols, :] = dot(normed_ref[:, cols], gm_ref[...], TN).astype(bf)
+    out = []
     for p in range(8):
         c = pltpu.make_async_copy(
             gw.at[pl.ds(pl.multiple_of(place_ref[p] * 128, 128), 128)],
-            gw_hbm.at[pl.ds(128 * p, 128)], osems.at[p])
+            (keep_hbm if p < 4 else send_hbm).at[pl.ds(128 * (p % 4), 128)], osems.at[p])
         c.start(); out.append(c)
     for c in out: c.wait()
 
-def project_heads(place, gm, weight, normed):
-    n = gm.shape[0]
+def project_weights(place, gm, normed):
     vm = pl.BlockSpec(memory_space=pltpu.VMEM)
     any_ = pl.BlockSpec(memory_space=pl.ANY)
     return pl.pallas_call(
-        project_kernel,
-        out_shape=(jax.ShapeDtypeStruct((n, 1024), bf), jax.ShapeDtypeStruct((1024, 768), bf)),
-        in_specs=[pl.BlockSpec(memory_space=pltpu.SMEM), vm, any_, vm], out_specs=(vm, any_),
-        scratch_shapes=[pltpu.VMEM((1024, 768), bf), pltpu.VMEM((1024, 768), bf),
-                        pltpu.SemaphoreType.DMA((8,)), pltpu.SemaphoreType.DMA((8,))],
-        compiler_params=pltpu.CompilerParams(vmem_limit_bytes=48 << 20),
-        cost_estimate=pl.CostEstimate(flops=3 << 30, bytes_accessed=10 << 20, transcendentals=0),
-        name="project_heads",
-    )(place, gm, weight, normed)
+        weights_kernel,
+        out_shape=(jax.ShapeDtypeStruct((512, 768), bf),) * 2,
+        in_specs=[pl.BlockSpec(memory_space=pltpu.SMEM), vm, vm], out_specs=(any_,) * 2,
+        scratch_shapes=[pltpu.VMEM((1024, 768), bf), pltpu.SemaphoreType.DMA((8,))],
+        compiler_params=pltpu.CompilerParams(vmem_limit_bytes=28 << 20),
+        cost_estimate=pl.CostEstimate(flops=1073741824, bytes_accessed=4194304, transcendentals=0),
+        name="project_weights",
+    )(place, gm, normed)
 
 
 FF2=1408; FFP=1536
@@ -579,7 +591,7 @@
                         pltpu.VMEM((1024, FFP), bf), pltpu.VMEM((1024, FFP), bf), pltpu.VMEM((FFP, 1024), bf),
                         pltpu.SemaphoreType.DMA((56,)), pltpu.SemaphoreType.DMA((17,))],
         compiler_params=pltpu.CompilerParams(vmem_limit_bytes=50 << 20),
-        cost_estimate=pl.CostEstimate(flops=15 << 30, bytes_accessed=30 << 20, transcendentals=1 << 20),
+        cost_estimate=pl.CostEstimate(flops=16106127360, bytes_accessed=31457280, transcendentals=0),
         name="feed",
     )(me, att, attp, act, actp, cot, cotp, *a, *b, *da, *db, outs)
 
@@ -627,7 +639,7 @@
         out_specs=(vm, vm, vm, any_, any_),
         scratch_shapes=[pltpu.VMEM((1024, 1024), bf), pltpu.SemaphoreType.DMA((16,))],
         compiler_params=pltpu.CompilerParams(vmem_limit_bytes=40 << 20),
-        cost_estimate=pl.CostEstimate(flops=1 << 30, bytes_accessed=10 << 20, transcendentals=0),
+        cost_estimate=pl.CostEstimate(flops=1073741824, bytes_accessed=10485760, transcendentals=0),
         name="branch",
     )(me, part, outown, gnown, res, cot, att, wo)
 
@@ -658,8 +670,8 @@
     return jnp.concatenate(parts, axis=1)
 
 
-def tie(value, anchor):
-    return lax.optimization_barrier((value, anchor))[0]
+def tie(value, *anchors):
+    return lax.optimization_barrier((value, *anchors))[0]
 
 
 def fast_device(
@@ -691,11 +703,21 @@
     length = block_ids.shape[1]
     act = activations.reshape(span, width)
     cot = cotangent.reshape(span, width)
+    act_other = swap(act, 1)
+    cot_other = swap(cot, 1)
     g0, g1 = split_even(w_gate)
     u0, u1 = split_even(w_up)
-    wide = jnp.concatenate([g0, u0, g1, u1, w_out], axis=1)
-    wide = lax.all_gather(wide, "ctx", axis=0, tiled=True)
-    act_all = lax.all_gather(act, "ctx", axis=0, tiled=True)
+    even = jnp.stack([g0, u0])
+    odd = jnp.stack([g1, u1])
+    flip = core == 1
+    mine = jnp.where(flip, odd, even)
+    other = swap(jnp.where(flip, even, odd), 1)
+    out_rows = jnp.stack([w_out[:, :512], w_out[:, 512:]]).reshape(2, 32, 2, 256)
+    wide = jnp.stack([mine, other], axis=1)
+    wide = jnp.concatenate([wide, out_rows.transpose(0, 2, 1, 3)], axis=3)
+    wide = lax.all_gather(wide, "ctx", axis=2, tiled=True).reshape(2, 256, FF2 + 256)
+    padded = jnp.concatenate([act, w_down, jnp.zeros((8, width), bf)], axis=0)
+    rows_all = lax.all_gather(padded, "ctx", axis=0, tiled=True)
     heads = jnp.stack(
         [
             jnp.concatenate([w[:, 256 * i : 256 * i + 256] for w in (w_query, w_key, w_value)], 1)
@@ -709,41 +731,29 @@
     heads_rel = jnp.concatenate([four, swap(four, 1)], axis=0)
     places = jnp.arange(8, dtype=jnp.int32)
     places = ((places >> 2 & 1) | (places >> 1 & 1) << 1 | (places & 1) << 2) ^ me
-    mine = lax.dynamic_slice_in_dim(wide, core * 2 * FF2, 2 * FF2, 1)
-    other = swap(lax.dynamic_slice_in_dim(wide, (1 - core) * 2 * FF2, 2 * FF2, 1), 1)
-    out_rows = wide[:, 4 * FF2 :]
-
-    def group(lo, col):
-        gate = jnp.concatenate([mine[:, lo : lo + FF2], other[:, lo : lo + FF2]], axis=0)
-        out = jnp.concatenate(
-            [out_rows[:, col : col + 256], out_rows[:, col + 256 : col + 512]], axis=0
-        )
-        return jnp.concatenate([gate, out], axis=1)
+    wide, act_other, cot_other = lax.optimization_barrier((wide, act_other, cot_other))
 
     def spread(own, first, second):
         near = swap(own, first)
         return [own, near, swap(own, second), swap(near, second)]
 
-    piece_a = spread(group(0, 0), 2, 4)
-    piece_b = spread(group(FF2, 512), 4, 2)
+    piece_a = spread(wide[0], 2, 4)
+    piece_b = spread(wide[1], 4, 2)
     outs = swap(jnp.stack([p[:, FF2:] for p in piece_a + piece_b]), 1)
-    down = tie(w_down, act_all)
-    downs = jnp.stack([down] + [shift(down, d) for d in (1, 2, 3)])
     down = jnp.concatenate(
-        [lax.dynamic_index_in_dim(downs, z ^ i, 0, keepdims=False) for i in range(4)], axis=0
+        [rows_all[352 * i + 256 : 352 * i + 344] for i in range(4)], axis=0
     )
     piece_da = spread(down[:, :512], 2, 4)
     piece_db = spread(down[:, 512:], 4, 2)
-    act_other = swap(act, 1)
-    cot_other = swap(cot, 1)
     cosine, sine = rotary_tables(jnp.arange(length, dtype=jnp.int32), HEAD_DIM)
     cosine = jnp.concatenate([cosine] * 4, axis=1)
     sine = jnp.concatenate([-sine, sine, -sine, sine], axis=1)
     id_row = jnp.broadcast_to(block_ids, (8, length))
     id_col = jnp.broadcast_to(block_ids.reshape(length, 1), (length, 128))
     normed, mixed, attended, totals, peaks = attend(
-        places, act_all, heads_rel, cosine, sine, id_col, id_row
-    )
+        places, tie(rows_all, *piece_a, *piece_b), heads_rel, cosine, sine, id_col, id_row
+    )
+    attended = tie(attended, *piece_da[1:3], *piece_db[1:3])
     attended = lax.all_to_all(attended.reshape(4, span, 256), "ctx", 0, 0, tiled=True)
     attended_other = swap(attended, 1)
     (part, out_own, back_own, residual, full_out, *grads) = feed(
@@ -752,14 +762,18 @@
     )
     ga_keep, ga_send, gb_keep, gb_send, gda_keep, gda_send, gdb_keep, gdb_send = grads
     part = swap(part, 1)
+    gda_send, gdb_send, part = lax.optimization_barrier((gda_send, gdb_send, part))
     layer_out, grad_residual, grad_attended, go_keep, go_send = branch(
         me_ref, part, out_own, back_own, residual, cot, attended, full_out
     )
     grad_attended = lax.all_to_all(grad_attended, "ctx", 0, 0, tiled=True).reshape(length, 256)
+    grad_da = add_low(gda_keep, swap(gda_send, 2))
+    grad_db = add_low(gdb_keep, swap(gdb_send, 4))
+    ga_send, gb_send, grad_da, grad_db, grad_attended = lax.optimization_barrier(
+        (ga_send, gb_send, grad_da, grad_db, grad_attended)
+    )
     grad_a = add_low(ga_keep, swap(ga_send, 2))
     grad_b = add_low(gb_keep, swap(gb_send, 4))
-    grad_da = add_low(gda_keep, swap(gda_send, 2))
-    grad_db = add_low(gdb_keep, swap(gdb_send, 4))
     grad_a = add_low(grad_a[:256], swap(grad_a[256:], 4))
     grad_b = add_low(grad_b[:256], swap(grad_b[256:], 2))
     grad_da = add_low(grad_da[:352], swap(grad_da[352:], 4))
@@ -777,7 +791,6 @@
 
     own_half = core_rows(core)
     other_half = swap(core_rows(1 - core), 1)
-    flip = core == 1
     grad_wide = jnp.concatenate(
         [
             jnp.where(flip, other_half, own_half),
@@ -791,12 +804,14 @@
     grad_d = jnp.concatenate([grad_da, grad_db], axis=1)
     grad_d = lax.psum_scatter(grad_d, "ctx", scatter_dimension=0, tiled=True).astype(f32)
     grad_mixed = attend_back(mixed, grad_attended, totals, cosine, sine, id_col, id_row)
-    grad_normed, grad_heads = project_heads(places, grad_mixed, heads_rel, normed)
+    grad_normed = project_tokens(places, grad_mixed, heads_rel)
+    grad_heads = project_weights(places, tie(grad_mixed, grad_normed), normed)
+    peaks = tie(peaks, grad_normed)
     grad_normed = lax.psum_scatter(grad_normed, "ctx", scatter_dimension=0, tiled=True)
     tokens_wide = act.astype(f32)
     unused, first_pull = jax.vjp(normalize, tokens_wide)
     input_grad = grad_residual + first_pull(grad_normed.astype(f32))[0]
-    grad_heads = add_low(grad_heads[:512], swap(grad_heads[512:], 1))
+    grad_heads = add_low(grad_heads[0], swap(grad_heads[1], 1))
     grad_heads = add_low(grad_heads[:256], swap(grad_heads[256:], 2))
     grad_heads = add_low(grad_heads[:128], swap(grad_heads[128:], 4))
     grad_heads = lax.all_to_all(grad_heads.reshape(4, 32, 768), "ctx", 0, 0, tiled=True)
@@ -807,7 +822,9 @@
     ]
     for bit in (1, 2, 4):
         peaks = jnp.maximum(peaks, swap(peaks, bit))
-    peak_list = jnp.stack([peaks] + [shift(peaks, d) for d in (1, 2, 3)])[:, :4, 0]
+    peaks = jnp.concatenate([peaks, shift(peaks, 1)], axis=0)
+    peaks = jnp.concatenate([peaks, shift(peaks, 2)], axis=0)
+    peak_list = peaks.reshape(4, 8, 128)[:, :4, 0]
     head_peaks = jnp.concatenate(
         [lax.dynamic_index_in_dim(peak_list, z ^ i, 0, keepdims=False) for i in range(4)]
     )

time: 436 us -> 421 us (0.966)
  local copies, waits for them, and re-layouts: 35.7 us -> 51.4 us
  starting transfers between devices: 65.4 us -> 52.7 us
  other arithmetic: 40.9 us -> 33.9 us
  waiting for transfers between devices: 193 us -> 187 us
  Pallas kernels: 82.9 us -> 78.5 us
    all_gather x2, waiting for transfers between devices: 56 us -> 23 us  [the longest x1 13.7 us: fast_device(): rows_all = lax.all_gather(padded, 'ctx', axis=0, tiled=True)]
    ppermute x41, waiting for transfers between devices: 98.7 us -> 121 us  [swap(): return lax.ppermute(array, 'dp', [(i, i ^ bit) for i in range(8)])]
    reduce_scatter x1, waiting for transfers between devices: 17.8 us -> 0.01 us  [fast_device(): lax.psum_scatter(grad_wide, 'ctx', scatter_dimension=0, tiled=True)]
    unnamed x142 -> x164, local copies, waits for them, and re-layouts: 20.5 us -> 37.5 us
    all_to_all x1, waiting for transfers between devices: 0.01 us -> 10.3 us  [fast_device(): lax.all_to_all(attended.reshape(4, span, 256), 'ctx', 0, 0, tiled=True)]
    ppermute x6 -> x2, starting transfers between devices: 8.77 us -> 0.14 us  [shift(): return lax.ppermute(array, 'ctx', [(i, i ^ bits) for i in range(4)])]
    all_to_all x1, waiting for transfers between devices: 0.01 us -> 8.43 us  [fast_device(): lax.all_to_all(grad_attended, 'ctx', 0, 0, tiled=True).reshape(length, 256)]
    ppermute x6 -> x2, waiting for transfers between devices: 4.56 us -> 0.01 us  [shift(): return lax.ppermute(array, 'ctx', [(i, i ^ bits) for i in range(4)])]
  transfers between devices with their start and end apart: 56 -> 52, of which waited for: 26 -> 26; matrix products, arithmetic and copies ran while one was open for 13% -> 11% of each run, Pallas kernels for 13% -> 12%
where the time goes in v3:
time: 421 us; the launch traced here: 419 us
  waiting for transfers between devices  187 us (44%)
  Pallas kernels  78.5 us (19%)
  starting transfers between devices  52.7 us (13%)
  local copies, waits for them, and re-layouts  51.4 us (12%)
  other arithmetic  33.9 us (8%)
  between operations  16.3 us (4%)
    ppermute x41, waiting for transfers between devices, swap(): return lax.ppermute(array, 'dp', [(i, i ^ bit) for i in range(8)])  121 us
    unnamed x164, local copies, waits for them, and re-layouts  37.5 us
    ppermute x41, starting transfers between devices, swap(): return lax.ppermute(array, 'dp', [(i, i ^ bit) for i in range(8)])  35 us
    pallas_call x1, Pallas kernels, feed(): pl.pallas_call(feed_kernel, out_shape=(S((512, 1024), bf), S((256, 1024),...  27.6 us
    pallas_call x1, Pallas kernels, attend(): pl.pallas_call(attend_kernel, out_shape=(jax.ShapeDtypeStruct((n, 1024),...  18 us
    pallas_call x1, Pallas kernels, attend_back(): pl.pallas_call(attend_back_kernel, out_shape=jax.ShapeDtypeStruct((n, 768...  17.6 us
    all_gather x1, waiting for transfers between devices, fast_device(): rows_all = lax.all_gather(padded, 'ctx', axis=0, tiled=True)  13.7 us
    all_to_all x1, waiting for transfers between devices, fast_device(): lax.all_to_all(grad_heads.reshape(4, 32, 768), 'ctx', 0, 0, tiled=True)  12.4 us
  transfers between devices with their start and end apart: 52, of which 26 were waited for; matrix products, arithmetic and copies ran while one was open for 11% of the time, Pallas kernels for 12%

profile of v3, /device:TPU:0, one launch (start us, length us, event | category | flops | bytes accessed | tf_op | source)
XLA Modules:
  0.0 419.3 jit_solution(15340545634639794795)
XLA Ops:
  14.3 6.2 %all-to-all-start = ((bf16[4,32,768]{2,1,0:T(8,128)(2,1)}), bf16[4,32,768]{2,1,0:T(8,128)(2,1)S(1)}, u32[]{:S(2)}, u32[]{:S(2)}) async-start(bf16[4,32,768]{2,1,0:T(8,128)(2,1)} %pad_maximum_fusion.10), calls=%async_computation | async-start | bytes 393216 | tf_op jit(solution)/shard_map/all_to_all | solution.py:727
  21.1 11.0 %all-to-all-done = bf16[4,32,768]{2,1,0:T(8,128)(2,1)S(1)} async-done(((bf16[4,32,768]{2,1,0:T(8,128)(2,1)}), bf16[4,32,768]{2,1,0:T(8,128)(2,1)S(1)}, u32[]{:S(2)}, u32[]{:S(2)}) %all-to-all-start) | async-done | bytes 196640 | tf_op jit(solution)/shard_map/all_to_all | solution.py:727
  32.1 1.5 collective-permute-start.9
  33.6 4.2 collective-permute-done.9
  37.8 1.6 collective-permute-start.10
  39.4 3.0 fusion.6
  42.4 3.2 collective-permute-done.10
  47.3 9.2 %all-gather.5.cloned.1.call-done = bf16[2,2,128,1664]{3,2,0,1:T(8,128)(2,1)} async-done(((bf16[2,2,32,1664]{3,2,0,1:T(8,128)(2,1)}), bf16[2,2,128,1664]{3,2,0,1:T(8,128)(2,1)}) %all-gather.5.cloned.1.call-update) | async-done | bytes 1703952 | tf_op jit(solution)/shard_map/all_gather | solution.py:718
  56.6 1.6 copy.53
  59.2 1.5 collective-permute-start.3
  60.7 1.5 collective-permute-start.6
  66.2 14.9 %collective-permute-done.3.a1 = bf16[256,1664]{1,0:T(8,128)(2,1)} collective-permute-done((bf16[256,1664]{1,0:T(8,128)(2,1)S(1)}, bf16[256,1664]{1,0:T(8,128)(2,1)}, u32[]{:S(2)}, u32[]{:S(2)}) %collective-permute-start.3) | collective-permute-done | bytes 852000 | tf_op jit(solution)/shard_map/ppermute | solution.py:648
  81.1 1.5 collective-permute-start.5
  84.1 1.6 fusion.13
  85.7 15.3 %collective-permute-done.4.a2 = bf16[256,1664]{1,0:T(8,128)(2,1)S(1)} collective-permute-done((bf16[256,1664]{1,0:T(8,128)(2,1)S(1)}, bf16[256,1664]{1,0:T(8,128)(2,1)S(1)}, u32[]{:S(2)}, u32[]{:S(2)}) %collective-permute-start.4) | collective-permute-done | bytes 852000 | tf_op jit(solution)/shard_map/ppermute | solution.py:648
  102.6 13.7 %all-gather.3.cloned.1.call-done.act_ref = bf16[1408,1024]{1,0:T(8,128)(2,1)} async-done(((bf16[352,1024]{1,0:T(8,128)(2,1)}), bf16[1408,1024]{1,0:T(8,128)(2,1)}) %all-gather.3.cloned.1.call-update) | async-done | bytes 2883600 | tf_op jit(solution)/shard_map/all_gather | solution.py:720
  117.7 1.5 collective-permute-start.12
  119.3 1.5 collective-permute-start.13
  121.3 1.6 fusion.11
  122.9 1.6 fusion.10
  125.0 1.6 fusion.9
  126.8 18.0 %attend.1 = (bf16[1024,1024]{1,0:T(8,128)(2,1)S(1)}, bf16[1024,768]{1,0:T(8,128)(2,1)S(1)}, bf16[1024,256]{1,0:T(8,128)(2,1)S(1)}, f32[8,1024]{1,0:T(8,128)S(1)}, f32[8,128]{1,0:T(8,128)S(1)}) custom-call(s32[8]{0:T(128)S(1)} %fusion.21.place_ref, bf16[1408,1024]{1,0:T(8,128)(2,1)S(1)} %copy-done.22, ...), custom_call_target="tpu_custom_call" | custom-call | flops 4294967296 | bytes 10485760 | tf_op jit(solution)/shard_map/attend/pallas_call | solution.py:352
  150.3 3.8 all-to-all-start.1
  154.1 1.6 fusion.8
  155.7 1.6 fusion.7
  157.3 10.3 %all-to-all-done.1.att_ref = bf16[4,256,256]{2,1,0:T(8,128)(2,1)S(1)} async-done(((bf16[4,256,256]{2,1,0:T(8,128)(2,1)}), bf16[4,256,256]{2,1,0:T(8,128)(2,1)S(1)}, u32[]{:S(2)}, u32[]{:S(2)}) %all-to-all-start.1) | async-done | bytes 524320 | tf_op jit(solution)/shard_map/all_to_all | solution.py:757
  167.5 1.5 collective-permute-start.17
  169.0 1.5 collective-permute-start.18
  170.5 7.9 %collective-permute-done.17.da3 = bf16[352,512]{1,0:T(8,128)(2,1)S(1)} collective-permute-done((bf16[352,512]{1,0:T(8,128)(2,1)S(1)}, bf16[352,512]{1,0:T(8,128)(2,1)S(1)}, u32[]{:S(2)}, u32[]{:S(2)}) %collective-permute-start.17) | collective-permute-done | bytes 360480 | tf_op jit(solution)/shard_map/ppermute | solution.py:648
  182.7 27.6 %feed.1 = (bf16[512,1024]{1,0:T(8,128)(2,1)}, f32[256,1024]{1,0:T(8,128)}, f32[256,1024]{1,0:T(8,128)}, f32[256,1024]{1,0:T(8,128)}, bf16[1024,1024]{1,0:T(8,128...) custom-call(s32[1]{0:T(128)} %bitcast.me_ref, ...), custom_call_target="tpu_custom_call" | custom-call | flops 16106127360 | bytes 31457280 | tf_op jit(solution)/shard_map/feed/pallas_call | solution.py:582
  210.5 2.9 collective-permute-done.20.part_ref
  213.9 1.5 collective-permute-start.21
  215.3 1.6 copy-done
  220.6 3.5 branch.1
  226.9 3.5 all-to-all-start.2
  231.8 2.4 add_convert_fusion.6
  234.2 2.2 add_convert_fusion.7
  236.4 8.4 %all-to-all-done.2 = bf16[4,256,256]{2,1,0:T(8,128)(2,1)S(1)} async-done(((bf16[4,256,256]{2,1,0:T(8,128)(2,1)}), bf16[4,256,256]{2,1,0:T(8,128)(2,1)S(1)}, u32[]{:S(2)}, u32[]{:S(2)}) %all-to-all-start.2) | async-done | bytes 524320 | tf_op jit(solution)/shard_map/all_to_all | solution.py:769
  246.1 1.5 collective-permute-start.36
  249.2 6.3 %collective-permute-done.36 = bf16[352,512]{1,0:T(8,128)(2,1)S(1)} collective-permute-done((bf16[352,512]{1,0:T(8,128)(2,1)S(1)}, bf16[352,512]{1,0:T(8,128)(2,1)S(1)}, u32[]{:S(2)}, u32[]{:S(2)}) %collective-permute-start.36) | collective-permute-done | bytes 360480 | tf_op jit(solution)/shard_map/ppermute | solution.py:648
  255.6 2.1 collective-permute-done.37
  264.4 17.6 %attend_back.1.gm_ref = bf16[1024,768]{1,0:T(8,128)(2,1)S(1)} custom-call(bf16[1024,768]{1,0:T(8,128)(2,1)S(1)} %copy-done.35, bf16[1024,256]{1,0:T(8,128)(2,1)S(1)} %bitcast.104, f32[8,1024]{1,0:T(8,128)S(1)} %copy-done.37, f32[1024,128]{1,0:T(8,128)S(1)} %copy-done.9, f32[1024,128]{1,0:T(8,128)S(1)} %copy-done.11, s32[1024,128]{1,0:T(8,128)S(1)} %copy-done.13, ...), custom_call_target="tpu_custom_call" | custom-call | flops 6442450944 | bytes 6291456 | tf_op jit(solution)/shard_map/attend_back/pallas_call | solution.py:418
  282.0 6.5 %project_tokens.1 = bf16[1024,1024]{1,0:T(8,128)(2,1)} custom-call(s32[8]{0:T(128)S(1)} %fusion.21.place_ref, bf16[1024,768]{1,0:T(8,128)(2,1)S(1)} %attend_back.1.gm_ref, bf16[1024,768]{1,0:T(8,128)(2,1)S(1)} %constant_dynamic-update-slice_fusion.weight_hbm), custom_call_target="tpu_custom_call" | custom-call | flops 1073741824 | bytes 4194304 | tf_op jit(solution)/shard_map/project_tokens/pallas_call | solution.py:444
  290.8 1.5 collective-permute-start.39
  293.7 1.6 copy-done.33
  295.3 5.3 %project_weights.1 = (bf16[512,768]{1,0:T(8,128)(2,1)S(1)}, bf16[512,768]{1,0:T(8,128)(2,1)S(1)}) custom-call(s32[8]{0:T(128)S(1)} %fusion.21.place_ref, bf16[1024,768]{1,0:T(8,128)(2,1)S(1)} %copy-done.2, bf16[1024,1024]{1,0:T(8,128)(2,1)S(1)} %copy-done.33), custom_call_target="tpu_custom_call" | custom-call | flops 1073741824 | bytes 4194304 | tf_op jit(solution)/shard_map/project_weights/pallas_call | solution.py:470
  301.9 1.7 add_convert_fusion.2
  305.3 1.7 add_convert_fusion.1
  307.1 5.1 %collective-permute-done.32 = bf16[256,512]{1,0:T(8,128)(2,1)S(1)} collective-permute-done((bf16[256,512]{1,0:T(8,128)(2,1)S(1)}, bf16[256,512]{1,0:T(8,128)(2,1)S(1)}, u32[]{:S(2)}, u32[]{:S(2)}) %collective-permute-start.32) | collective-permute-done | bytes 262176 | tf_op jit(solution)/shard_map/ppermute | solution.py:648
  313.1 17.0 %collective-permute-done.34 = bf16[256,512]{1,0:T(8,128)(2,1)S(1)} collective-permute-done((bf16[256,512]{1,0:T(8,128)(2,1)S(1)}, bf16[256,512]{1,0:T(8,128)(2,1)S(1)}, u32[]{:S(2)}, u32[]{:S(2)}) %collective-permute-start.34) | collective-permute-done | bytes 262176 | tf_op jit(solution)/shard_map/ppermute | solution.py:648
  330.9 1.5 collective-permute-start.35
  332.5 1.7 add_convert_fusion
  334.3 11.3 %collective-permute-done.27 = bf16[256,1408]{1,0:T(8,128)(2,1)S(1)} collective-permute-done((bf16[256,1408]{1,0:T(8,128)(2,1)S(1)}, bf16[256,1408]{1,0:T(8,128)(2,1)S(1)}, u32[]{:S(2)}, u32[]{:S(2)}) %collective-permute-start.27) | collective-permute-done | bytes 720928 | tf_op jit(solution)/shard_map/ppermute | solution.py:648
  345.6 1.4 collective-permute-start.29
  347.3 15.2 %collective-permute-done.29 = bf16[256,1408]{1,0:T(8,128)(2,1)S(1)} collective-permute-done((bf16[256,1408]{1,0:T(8,128)(2,1)S(1)}, bf16[256,1408]{1,0:T(8,128)(2,1)S(1)}, u32[]{:S(2)}, u32[]{:S(2)}) %collective-permute-start.29) | collective-permute-done | bytes 720928 | tf_op jit(solution)/shard_map/ppermute | solution.py:648
  363.3 1.6 collective-permute-start.24
  368.0 6.9 %collective-permute-done.24 = bf16[256,768]{1,0:T(8,128)(2,1)S(1)} collective-permute-done((bf16[256,768]{1,0:T(8,128)(2,1)S(1)}, bf16[256,768]{1,0:T(8,128)(2,1)S(1)}, u32[]{:S(2)}, u32[]{:S(2)}) %collective-permute-start.24) | collective-permute-done | bytes 393248 | tf_op jit(solution)/shard_map/ppermute | solution.py:648
  377.2 4.5 %collective-permute-done.25 = bf16[128,768]{1,0:T(8,128)(2,1)S(1)} collective-permute-done((bf16[128,768]{1,0:T(8,128)(2,1)S(1)}, bf16[128,768]{1,0:T(8,128)(2,1)S(1)}, u32[]{:S(2)}, u32[]{:S(2)}) %collective-permute-start.25) | collective-permute-done | bytes 196640 | tf_op jit(solution)/shard_map/ppermute | solution.py:648
  382.5 3.6 all-to-all-start.3
  387.3 12.4 %all-to-all-done.3 = bf16[4,32,768]{2,1,0:T(8,128)(2,1)S(1)} async-done(((bf16[4,32,768]{2,1,0:T(8,128)(2,1)}), bf16[4,32,768]{2,1,0:T(8,128)(2,1)S(1)}, u32[]{:S(2)}, u32[]{:S(2)}) %all-to-all-start.3) | async-done | bytes 196640 | tf_op jit(solution)/shard_map/all_to_all | solution.py:817
  401.4 2.0 subtract_convert_fusion
  403.4 1.5 fusion.3
  404.9 1.5 fusion.5
  411.2 1.6 subtract_convert_fusion.3
  (313 shorter events, 69.4 us)
Async XLA Ops:
  7.2 49.3 %all-gather.5.cloned.1.call-start = ((), (), s32[]{:S(2)}) async-start(), calls=%async_computation.8 | async-start | bytes 2129920 | tf_op jit(solution)/shard_map/all_gather | solution.py:718
  9.8 1.6 collective-permute-start
  12.3 104.1 %all-gather.3.cloned.1.call-start = ((), (), s32[]{:S(2)}) async-start(), calls=%async_computation.7 | async-start | bytes 3604480 | tf_op jit(solution)/shard_map/all_gather | solution.py:720
  14.3 17.7 %all-to-all-start = ((bf16[4,32,768]{2,1,0:T(8,128)(2,1)}), bf16[4,32,768]{2,1,0:T(8,128)(2,1)S(1)}, u32[]{:S(2)}, u32[]{:S(2)}) async-start(bf16[4,32,768]{2,1,0:T(8,128)(2,1)} %pad_maximum_fusion.10), calls=%async_computation | async-start | bytes 393216 | tf_op jit(solution)/shard_map/all_to_all | solution.py:727
  20.6 37.6 %collective-permute-start.1 = (bf16[256,1024]{1,0:T(8,128)(2,1)S(1)}, bf16[256,1024]{1,0:T(8,128)(2,1)}, u32[]{:S(2)}, u32[]{:S(2)}) collective-permute-start(bf16[256,1024]{1,0:T(8,128)(2,1)S(1)} %bitcast.111), channel_id=1, source_target_pairs={{0,4},{4,0},{8,12},{12,8},{16,20},{20,16},{24,28},{28,24},{1,5},{5... | collective-permute-start | bytes 1572872 | tf_op jit(solution)/shard_map/ppermute | solution.py:648
  20.6 37.6 %collective-permute-start.2 = (bf16[256,1024]{1,0:T(8,128)(2,1)S(1)}, bf16[256,1024]{1,0:T(8,128)(2,1)}, u32[]{:S(2)}, u32[]{:S(2)}) collective-permute-start(bf16[256,1024]{1,0:T(8,128)(2,1)S(1)} %bitcast.107), channel_id=1, source_target_pairs={{0,4},{4,0},{8,12},{12,8},{16,20},{20,16},{24,28},{28,24},{1,5},{5... | collective-permute-start | bytes 1572872 | tf_op jit(solution)/shard_map/ppermute | solution.py:648
  32.1 5.7 %collective-permute-start.9 = (bf16[128,768]{1,0:T(8,128)(2,1)S(1)}, bf16[128,768]{1,0:T(8,128)(2,1)S(1)}, u32[]{:S(2)}, u32[]{:S(2)}) collective-permute-start(bf16[128,768]{1,0:T(8,128)(2,1)S(1)} %bitcast.113), channel_id=1, source_target_pairs={{0,8},{4,12},{8,0},{12,4},{16,24},{20,28},{24,16},{28,20},{1,9},{5... | collective-permute-start | bytes 589832 | tf_op jit(solution)/shard_map/ppermute | solution.py:648
  37.8 7.8 %collective-permute-start.10 = (bf16[256,768]{1,0:T(8,128)(2,1)S(1)}, bf16[256,768]{1,0:T(8,128)(2,1)S(1)}, u32[]{:S(2)}, u32[]{:S(2)}) collective-permute-start(bf16[256,768]{1,0:T(8,128)(2,1)S(1)} %pad_maximum_fusion.9), channel_id=1, source_target_pairs={{0,16},{4,20},{8,24},{12,28},{16,0},{20,4},{24,8},{28,12},{1,17},{... | collective-permute-start | bytes 1179656 | tf_op jit(solution)/shard_map/ppermute | solution.py:648
  47.3 16.4 %collective-permute-start.11 = (bf16[512,768]{1,0:T(8,128)(2,1)}, bf16[512,768]{1,0:T(8,128)(2,1)}, u32[]{:S(2)}, u32[]{:S(2)}) collective-permute-start(bf16[512,768]{1,0:T(8,128)(2,1)} %pad_maximum_fusion.1), channel_id=1, source_target_pairs={{0,4},{4,0},{8,12},{12,8},{16,20},{20,16},{24,28},{28,24},{1,5},{5... | collective-permute-start | bytes 2359304 | tf_op jit(solution)/shard_map/ppermute | solution.py:648
  59.2 21.9 %collective-permute-start.3 = (bf16[256,1664]{1,0:T(8,128)(2,1)S(1)}, bf16[256,1664]{1,0:T(8,128)(2,1)}, u32[]{:S(2)}, u32[]{:S(2)}) collective-permute-start(bf16[256,1664]{1,0:T(8,128)(2,1)S(1)} %get-tuple-element.133.a0), channel_id=1, source_target_pairs={{0,8},{4,12},{8,0},{12,4},{16,24},{20,28},{24,16},{28,20},{1,9},{5... | collective-permute-start | bytes 2555912 | tf_op jit(solution)/shard_map/ppermute | solution.py:648
  60.7 22.2 %collective-permute-start.6 = (bf16[256,1664]{1,0:T(8,128)(2,1)}, bf16[256,1664]{1,0:T(8,128)(2,1)}, u32[]{:S(2)}, u32[]{:S(2)}) collective-permute-start(bf16[256,1664]{1,0:T(8,128)(2,1)} %get-tuple-element.132.b0), channel_id=1, source_target_pairs={{0,16},{4,20},{8,24},{12,28},{16,0},{20,4},{24,8},{28,12},{1,17},{... | collective-permute-start | bytes 2555912 | tf_op jit(solution)/shard_map/ppermute | solution.py:648
  63.1 63.7 %copy-start.8 = (f32[1024,128]{1,0:T(8,128)}, f32[1024,128]{1,0:T(8,128)S(1)}, u32[]{:S(2)}) copy-start(f32[1024,128]{1,0:T(8,128)S(1)} %get-tuple-element.223.cos_ref) | copy-start | bytes 1572868
  63.1 63.7 %copy-start.10 = (f32[1024,128]{1,0:T(8,128)}, f32[1024,128]{1,0:T(8,128)S(1)}, u32[]{:S(2)}) copy-start(f32[1024,128]{1,0:T(8,128)S(1)} %get-tuple-element.224.sin_ref) | copy-start | bytes 1572868
  63.1 37.9 %collective-permute-start.4 = (bf16[256,1664]{1,0:T(8,128)(2,1)S(1)}, bf16[256,1664]{1,0:T(8,128)(2,1)S(1)}, u32[]{:S(2)}, u32[]{:S(2)}) collective-permute-start(bf16[256,1664]{1,0:T(8,128)(2,1)S(1)} %get-tuple-element.133.a0), channel_id=1, source_target_pairs={{0,16},{4,20},{8,24},{12,28},{16,0},{20,4},{24,8},{28,12},{1,17},{... | collective-permute-start | bytes 2555912 | tf_op jit(solution)/shard_map/ppermute | solution.py:648
  65.0 59.4 %collective-permute-start.7 = (bf16[256,1664]{1,0:T(8,128)(2,1)}, bf16[256,1664]{1,0:T(8,128)(2,1)}, u32[]{:S(2)}, u32[]{:S(2)}) collective-permute-start(bf16[256,1664]{1,0:T(8,128)(2,1)} %get-tuple-element.132.b0), channel_id=1, source_target_pairs={{0,8},{4,12},{8,0},{12,4},{16,24},{20,28},{24,16},{28,20},{1,9},{5... | collective-permute-start | bytes 2555912 | tf_op jit(solution)/shard_map/ppermute | solution.py:648
  81.1 39.6 %collective-permute-start.5 = (bf16[256,1664]{1,0:T(8,128)(2,1)}, bf16[256,1664]{1,0:T(8,128)(2,1)}, u32[]{:S(2)}, u32[]{:S(2)}) collective-permute-start(bf16[256,1664]{1,0:T(8,128)(2,1)} %collective-permute-done.3.a1), channel_id=1, source_target_pairs={{0,16},{4,20},{8,24},{12,28},{16,0},{20,4},{24,8},{28,12},{1,17},{... | collective-permute-start | bytes 2555912 | tf_op jit(solution)/shard_map/ppermute | solution.py:648
  82.9 42.1 %collective-permute-start.8 = (bf16[256,1664]{1,0:T(8,128)(2,1)}, bf16[256,1664]{1,0:T(8,128)(2,1)}, u32[]{:S(2)}, u32[]{:S(2)}) collective-permute-start(bf16[256,1664]{1,0:T(8,128)(2,1)} %collective-permute-done.6.b1), channel_id=1, source_target_pairs={{0,8},{4,12},{8,0},{12,4},{16,24},{20,28},{24,16},{28,20},{1,9},{5... | collective-permute-start | bytes 2555912 | tf_op jit(solution)/shard_map/ppermute | solution.py:648
  117.7 27.1 %copy-start.20 = (bf16[352,512]{1,0:T(8,128)(2,1)}, bf16[352,512]{1,0:T(8,128)(2,1)S(1)}, u32[]{:S(2)}) copy-start(bf16[352,512]{1,0:T(8,128)(2,1)S(1)} %get-tuple-element.145.da0) | copy-start | bytes 1081348
  117.7 31.0 %collective-permute-start.12 = (bf16[352,512]{1,0:T(8,128)(2,1)S(1)}, bf16[352,512]{1,0:T(8,128)(2,1)S(1)}, u32[]{:S(2)}, u32[]{:S(2)}) collective-permute-start(bf16[352,512]{1,0:T(8,128)(2,1)S(1)} %get-tuple-element.145.da0), channel_id=1, source_target_pairs={{0,8},{4,12},{8,0},{12,4},{16,24},{20,28},{24,16},{28,20},{1,9},{5... | collective-permute-start | bytes 1081352 | tf_op jit(solution)/shard_map/ppermute | solution.py:648
  119.3 29.5 %collective-permute-start.13 = (bf16[352,512]{1,0:T(8,128)(2,1)S(1)}, bf16[352,512]{1,0:T(8,128)(2,1)S(1)}, u32[]{:S(2)}, u32[]{:S(2)}) collective-permute-start(bf16[352,512]{1,0:T(8,128)(2,1)S(1)} %get-tuple-element.145.da0), channel_id=1, source_target_pairs={{0,16},{4,20},{8,24},{12,28},{16,0},{20,4},{24,8},{28,12},{1,17},{... | collective-permute-start | bytes 1081352 | tf_op jit(solution)/shard_map/ppermute | solution.py:648
  120.8 28.0 %collective-permute-start.14 = (bf16[352,512]{1,0:T(8,128)(2,1)S(1)}, bf16[352,512]{1,0:T(8,128)(2,1)S(1)}, u32[]{:S(2)}, u32[]{:S(2)}) collective-permute-start(bf16[352,512]{1,0:T(8,128)(2,1)S(1)} %get-tuple-element.144.db0), channel_id=1, source_target_pairs={{0,16},{4,20},{8,24},{12,28},{16,0},{20,4},{24,8},{28,12},{1,17},{... | collective-permute-start | bytes 1081352 | tf_op jit(solution)/shard_map/ppermute | solution.py:648
  124.5 25.1 %collective-permute-start.15 = (bf16[352,512]{1,0:T(8,128)(2,1)S(1)}, bf16[352,512]{1,0:T(8,128)(2,1)S(1)}, u32[]{:S(2)}, u32[]{:S(2)}) collective-permute-start(bf16[352,512]{1,0:T(8,128)(2,1)S(1)} %get-tuple-element.144.db0), channel_id=1, source_target_pairs={{0,8},{4,12},{8,0},{12,4},{16,24},{20,28},{24,16},{28,20},{1,9},{5... | collective-permute-start | bytes 1081352 | tf_op jit(solution)/shard_map/ppermute | solution.py:648
  148.7 31.0 %copy-start.21 = (bf16[352,512]{1,0:T(8,128)(2,1)S(1)}, bf16[352,512]{1,0:T(8,128)(2,1)}, u32[]{:S(2)}) copy-start(bf16[352,512]{1,0:T(8,128)(2,1)} %copy-done.20) | copy-start | bytes 1081348
  150.3 17.2 %all-to-all-start.1 = ((bf16[4,256,256]{2,1,0:T(8,128)(2,1)}), bf16[4,256,256]{2,1,0:T(8,128)(2,1)S(1)}, u32[]{:S(2)}, u32[]{:S(2)}) async-start(bf16[4,256,256]{2,1,0:T(8,128)(2,1)} %bitcast.105), calls=%async_computation.1 | async-start | bytes 1048576 | tf_op jit(solution)/shard_map/all_to_all | solution.py:757
  157.3 22.5 %collective-permute-start.19 = (bf16[8,256,256]{2,1,0:T(8,128)(2,1)}, bf16[8,256,256]{2,1,0:T(8,128)(2,1)}, u32[]{:S(2)}, u32[]{:S(2)}) collective-permute-start(bf16[8,256,256]{2,1,0:T(8,128)(2,1)} %fusion.7), channel_id=1, source_target_pairs={{0,4},{4,0},{8,12},{12,8},{16,20},{20,16},{24,28},{28,24},{1,5},{5... | collective-permute-start | bytes 3145736 | tf_op jit(solution)/shard_map/ppermute | solution.py:648
  167.5 12.2 %collective-permute-start.16 = (bf16[4,256,256]{2,1,0:T(8,128)(2,1)S(1)}, bf16[4,256,256]{2,1,0:T(8,128)(2,1)S(1)}, u32[]{:S(2)}, u32[]{:S(2)}) collective-permute-start(bf16[4,256,256]{2,1,0:T(8,128)(2,1)S(1)} %all-to-all-done.1.att_ref), channel_id=1, source_target_pairs={{0,4},{4,0},{8,12},{12,8},{16,20},{20,16},{24,28},{28,24},{1,5},{5... | collective-permute-start | bytes 1572872 | tf_op jit(solution)/shard_map/ppermute | solution.py:648
  167.5 10.8 %collective-permute-start.17 = (bf16[352,512]{1,0:T(8,128)(2,1)S(1)}, bf16[352,512]{1,0:T(8,128)(2,1)S(1)}, u32[]{:S(2)}, u32[]{:S(2)}) collective-permute-start(bf16[352,512]{1,0:T(8,128)(2,1)S(1)} %copy-done.25), channel_id=1, source_target_pairs={{0,16},{4,20},{8,24},{12,28},{16,0},{20,4},{24,8},{28,12},{1,17},{... | collective-permute-start | bytes 1081352 | tf_op jit(solution)/shard_map/ppermute | solution.py:648
  169.0 10.8 %collective-permute-start.18 = (bf16[352,512]{1,0:T(8,128)(2,1)}, bf16[352,512]{1,0:T(8,128)(2,1)S(1)}, u32[]{:S(2)}, u32[]{:S(2)}) collective-permute-start(bf16[352,512]{1,0:T(8,128)(2,1)} %copy-done.28), channel_id=1, source_target_pairs={{0,8},{4,12},{8,0},{12,4},{16,24},{20,28},{24,16},{28,20},{1,9},{5... | collective-permute-start | bytes 1081352 | tf_op jit(solution)/shard_map/ppermute | solution.py:648
  182.7 32.6 %copy-start.19 = (bf16[1,256,1024]{2,1,0:T(8,128)(2,1)S(1)}, bf16[1,256,1024]{2,1,0:T(8,128)(2,1)}, u32[]{:S(2)}) copy-start(bf16[1,256,1024]{2,1,0:T(8,128)(2,1)} %param.21) | copy-start | bytes 1572868
  210.4 2.9 collective-permute-start.20
  213.3 18.5 %collective-permute-start.22 = (bf16[704,512]{1,0:T(8,128)(2,1)}, bf16[704,512]{1,0:T(8,128)(2,1)}, u32[]{:S(2)}, u32[]{:S(2)}) collective-permute-start(bf16[704,512]{1,0:T(8,128)(2,1)} %get-tuple-element.87), channel_id=1, source_target_pairs={{0,16},{4,20},{8,24},{12,28},{16,0},{20,4},{24,8},{28,12},{1,17},{... | collective-permute-start | bytes 2162696 | tf_op jit(solution)/shard_map/ppermute | solution.py:648
  213.9 20.3 %collective-permute-start.21 = (bf16[704,512]{1,0:T(8,128)(2,1)}, bf16[704,512]{1,0:T(8,128)(2,1)}, u32[]{:S(2)}, u32[]{:S(2)}) collective-permute-start(bf16[704,512]{1,0:T(8,128)(2,1)} %get-tuple-element.85), channel_id=1, source_target_pairs={{0,8},{4,12},{8,0},{12,4},{16,24},{20,28},{24,16},{28,20},{1,9},{5... | collective-permute-start | bytes 2162696 | tf_op jit(solution)/shard_map/ppermute | solution.py:648
  226.9 18.0 %all-to-all-start.2 = ((bf16[4,256,256]{2,1,0:T(8,128)(2,1)}), bf16[4,256,256]{2,1,0:T(8,128)(2,1)S(1)}, u32[]{:S(2)}, u32[]{:S(2)}) async-start(bf16[4,256,256]{2,1,0:T(8,128)(2,1)} %copy-done.16), calls=%async_computation.2 | async-start | bytes 1048576 | tf_op jit(solution)/shard_map/all_to_all | solution.py:769
  230.3 171.0 %reduce-scatter.8.cloned.1.call-start = ((), (), s32[]{:S(2)}) async-start(), calls=%async_computation.11 | async-start | bytes 901120 | tf_op jit(solution)/shard_map/reduce_scatter | solution.py:805
  246.1 9.4 %collective-permute-start.36 = (bf16[352,512]{1,0:T(8,128)(2,1)S(1)}, bf16[352,512]{1,0:T(8,128)(2,1)S(1)}, u32[]{:S(2)}, u32[]{:S(2)}) collective-permute-start(bf16[352,512]{1,0:T(8,128)(2,1)S(1)} %slice.408), channel_id=1, source_target_pairs={{0,16},{4,20},{8,24},{12,28},{16,0},{20,4},{24,8},{28,12},{1,17},{... | collective-permute-start | bytes 1081352 | tf_op jit(solution)/shard_map/ppermute | solution.py:648
  248.6 9.2 %collective-permute-start.37 = (bf16[352,512]{1,0:T(8,128)(2,1)S(1)}, bf16[352,512]{1,0:T(8,128)(2,1)S(1)}, u32[]{:S(2)}, u32[]{:S(2)}) collective-permute-start(bf16[352,512]{1,0:T(8,128)(2,1)S(1)} %slice.410), channel_id=1, source_target_pairs={{0,8},{4,12},{8,0},{12,4},{16,24},{20,28},{24,16},{28,20},{1,9},{5... | collective-permute-start | bytes 1081352 | tf_op jit(solution)/shard_map/ppermute | solution.py:648
  258.9 144.5 %reduce-scatter.4.cloned.1.call-start = ((), (), s32[]{:S(2)}) async-start(), calls=%async_computation.9 | async-start | bytes 2621440 | tf_op jit(solution)/shard_map/reduce_scatter | solution.py:810
  259.1 42.7 %collective-permute-start.31 = (bf16[512,1024]{1,0:T(8,128)(2,1)}, bf16[512,1024]{1,0:T(8,128)(2,1)}, u32[]{:S(2)}, u32[]{:S(2)}) collective-permute-start(bf16[512,1024]{1,0:T(8,128)(2,1)} %copy-done.23), channel_id=1, source_target_pairs={{0,4},{4,0},{8,12},{12,8},{16,20},{20,16},{24,28},{28,24},{1,5},{5... | collective-permute-start | bytes 3145736 | tf_op jit(solution)/shard_map/ppermute | solution.py:648
  259.2 45.1 %collective-permute-start.26 = (bf16[512,1408]{1,0:T(8,128)(2,1)}, bf16[512,1408]{1,0:T(8,128)(2,1)}, u32[]{:S(2)}, u32[]{:S(2)}) collective-permute-start(bf16[512,1408]{1,0:T(8,128)(2,1)} %get-tuple-element.96), channel_id=1, source_target_pairs={{0,8},{4,12},{8,0},{12,4},{16,24},{20,28},{24,16},{28,20},{1,9},{5... | collective-permute-start | bytes 4325384 | tf_op jit(solution)/shard_map/ppermute | solution.py:648
  289.6 1.2 collective-permute-start.38
  289.8 41.1 %collective-permute-start.28 = (bf16[512,1408]{1,0:T(8,128)(2,1)}, bf16[512,1408]{1,0:T(8,128)(2,1)}, u32[]{:S(2)}, u32[]{:S(2)}) collective-permute-start(bf16[512,1408]{1,0:T(8,128)(2,1)} %get-tuple-element.98), channel_id=1, source_target_pairs={{0,16},{4,20},{8,24},{12,28},{16,0},{20,4},{24,8},{28,12},{1,17},{... | collective-permute-start | bytes 4325384 | tf_op jit(solution)/shard_map/ppermute | solution.py:648
  290.8 9.9 %collective-permute-start.39 = (f32[8,128]{1,0:T(8,128)S(1)}, f32[8,128]{1,0:T(8,128)S(1)}, u32[]{:S(2)}, u32[]{:S(2)}) collective-permute-start(f32[8,128]{1,0:T(8,128)S(1)} %max.13), channel_id=1, source_target_pairs={{0,8},{4,12},{8,0},{12,4},{16,24},{20,28},{24,16},{28,20},{1,9},{5... | collective-permute-start | bytes 12296 | tf_op jit(solution)/shard_map/ppermute | solution.py:648
  300.6 62.5 %collective-permute-start.23 = (bf16[512,768]{1,0:T(8,128)(2,1)S(1)}, bf16[512,768]{1,0:T(8,128)(2,1)S(1)}, u32[]{:S(2)}, u32[]{:S(2)}) collective-permute-start(bf16[512,768]{1,0:T(8,128)(2,1)S(1)} %get-tuple-element.94), channel_id=1, source_target_pairs={{0,4},{4,0},{8,12},{12,8},{16,20},{20,16},{24,28},{28,24},{1,5},{5... | collective-permute-start | bytes 2359304 | tf_op jit(solution)/shard_map/ppermute | solution.py:648
  300.7 107.1 %reduce-scatter.6.cloned.1.call-start = ((), (), s32[]{:S(2)}) async-start(), calls=%async_computation.10 | async-start | bytes 2129920 | tf_op jit(solution)/shard_map/reduce_scatter | solution.py:803
  300.8 67.1 %collective-permute-start.40 = (f32[8,128]{1,0:T(8,128)S(1)}, f32[8,128]{1,0:T(8,128)S(1)}, u32[]{:S(2)}, u32[]{:S(2)}) collective-permute-start(f32[8,128]{1,0:T(8,128)S(1)} %max.14), channel_id=1, source_target_pairs={{0,16},{4,20},{8,24},{12,28},{16,0},{20,4},{24,8},{28,12},{1,17},{... | collective-permute-start | bytes 12296 | tf_op jit(solution)/shard_map/ppermute | solution.py:648
  303.6 8.5 %collective-permute-start.32 = (bf16[256,512]{1,0:T(8,128)(2,1)S(1)}, bf16[256,512]{1,0:T(8,128)(2,1)S(1)}, u32[]{:S(2)}, u32[]{:S(2)}) collective-permute-start(bf16[256,512]{1,0:T(8,128)(2,1)S(1)} %get-tuple-element.138), channel_id=1, source_target_pairs={{0,8},{4,12},{8,0},{12,4},{16,24},{20,28},{24,16},{28,20},{1,9},{5... | collective-permute-start | bytes 786440 | tf_op jit(solution)/shard_map/ppermute | solution.py:648
  304.3 25.9 %collective-permute-start.34 = (bf16[256,512]{1,0:T(8,128)(2,1)S(1)}, bf16[256,512]{1,0:T(8,128)(2,1)S(1)}, u32[]{:S(2)}, u32[]{:S(2)}) collective-permute-start(bf16[256,512]{1,0:T(8,128)(2,1)S(1)} %get-tuple-element.139), channel_id=1, source_target_pairs={{0,16},{4,20},{8,24},{12,28},{16,0},{20,4},{24,8},{28,12},{1,17},{... | collective-permute-start | bytes 786440 | tf_op jit(solution)/shard_map/ppermute | solution.py:648
  307.0 25.5 %copy-start.45 = (bf16[512,1408]{1,0:T(8,128)(2,1)S(1)}, bf16[512,1408]{1,0:T(8,128)(2,1)}, u32[]{:S(2)}) copy-start(bf16[512,1408]{1,0:T(8,128)(2,1)} %get-tuple-element.97) | copy-start | bytes 4325380
  312.1 33.5 %collective-permute-start.27 = (bf16[256,1408]{1,0:T(8,128)(2,1)S(1)}, bf16[256,1408]{1,0:T(8,128)(2,1)S(1)}, u32[]{:S(2)}, u32[]{:S(2)}) collective-permute-start(bf16[256,1408]{1,0:T(8,128)(2,1)S(1)} %slice.445), channel_id=1, source_target_pairs={{0,16},{4,20},{8,24},{12,28},{16,0},{20,4},{24,8},{28,12},{1,17},{... | collective-permute-start | bytes 2162696 | tf_op jit(solution)/shard_map/ppermute | solution.py:648
  330.3 32.6 %collective-permute-start.33 = (bf16[128,512]{1,0:T(8,128)(2,1)S(1)}, bf16[128,512]{1,0:T(8,128)(2,1)S(1)}, u32[]{:S(2)}, u32[]{:S(2)}) collective-permute-start(bf16[128,512]{1,0:T(8,128)(2,1)S(1)} %slice.451), channel_id=1, source_target_pairs={{0,16},{4,20},{8,24},{12,28},{16,0},{20,4},{24,8},{28,12},{1,17},{... | collective-permute-start | bytes 393224 | tf_op jit(solution)/shard_map/ppermute | solution.py:648
  330.9 32.1 %collective-permute-start.35 = (bf16[128,512]{1,0:T(8,128)(2,1)S(1)}, bf16[128,512]{1,0:T(8,128)(2,1)S(1)}, u32[]{:S(2)}, u32[]{:S(2)}) collective-permute-start(bf16[128,512]{1,0:T(8,128)(2,1)S(1)} %slice.455), channel_id=1, source_target_pairs={{0,8},{4,12},{8,0},{12,4},{16,24},{20,28},{24,16},{28,20},{1,9},{5... | collective-permute-start | bytes 393224 | tf_op jit(solution)/shard_map/ppermute | solution.py:648
  345.6 16.9 %collective-permute-start.29 = (bf16[256,1408]{1,0:T(8,128)(2,1)S(1)}, bf16[256,1408]{1,0:T(8,128)(2,1)S(1)}, u32[]{:S(2)}, u32[]{:S(2)}) collective-permute-start(bf16[256,1408]{1,0:T(8,128)(2,1)S(1)} %slice.447), channel_id=1, source_target_pairs={{0,8},{4,12},{8,0},{12,4},{16,24},{20,28},{24,16},{28,20},{1,9},{5... | collective-permute-start | bytes 2162696 | tf_op jit(solution)/shard_map/ppermute | solution.py:648
  362.9 2.3 collective-permute-start.30
  363.3 11.6 %collective-permute-start.24 = (bf16[256,768]{1,0:T(8,128)(2,1)S(1)}, bf16[256,768]{1,0:T(8,128)(2,1)S(1)}, u32[]{:S(2)}, u32[]{:S(2)}) collective-permute-start(bf16[256,768]{1,0:T(8,128)(2,1)S(1)} %slice.429), channel_id=1, source_target_pairs={{0,8},{4,12},{8,0},{12,4},{16,24},{20,28},{24,16},{28,20},{1,9},{5... | collective-permute-start | bytes 1179656 | tf_op jit(solution)/shard_map/ppermute | solution.py:648
  367.9 9.2 %collective-permute-start.41 = (f32[8,128]{1,0:T(8,128)S(1)}, f32[8,128]{1,0:T(8,128)S(1)}, u32[]{:S(2)}, u32[]{:S(2)}) collective-permute-start(f32[8,128]{1,0:T(8,128)S(1)} %max.15), channel_id=1, source_target_pairs={{0,1},{1,0},{2,3},{3,2},{4,5},{5,4},{6,7},{7,6},{8,9},{9,8},{10,11... | collective-permute-start | bytes 12296 | tf_op jit(solution)/shard_map/ppermute | solution.py:652
  375.0 24.7 %copy-start.61 = (bf16[32,1024]{1,0:T(8,128)(2,1)S(1)}, bf16[32,1024]{1,0:T(8,128)(2,1)}, u32[]{:S(2)}) copy-start(bf16[32,1024]{1,0:T(8,128)(2,1)} %param.24) | copy-start | bytes 196612
  375.0 24.7 %copy-start.70 = (f32[32,1024]{1,0:T(8,128)S(1)}, f32[32,1024]{1,0:T(8,128)}, u32[]{:S(2)}) copy-start(f32[32,1024]{1,0:T(8,128)} %param.31) | copy-start | bytes 393220
  375.0 6.7 %collective-permute-start.25 = (bf16[128,768]{1,0:T(8,128)(2,1)S(1)}, bf16[128,768]{1,0:T(8,128)(2,1)S(1)}, u32[]{:S(2)}, u32[]{:S(2)}) collective-permute-start(bf16[128,768]{1,0:T(8,128)(2,1)S(1)} %slice.431), channel_id=1, source_target_pairs={{0,16},{4,20},{8,24},{12,28},{16,0},{20,4},{24,8},{28,12},{1,17},{... | collective-permute-start | bytes 589832 | tf_op jit(solution)/shard_map/ppermute | solution.py:648
  377.1 23.4 %copy-start.63 = (bf16[32,1024]{1,0:T(8,128)(2,1)S(1)}, bf16[32,1024]{1,0:T(8,128)(2,1)}, u32[]{:S(2)}) copy-start(bf16[32,1024]{1,0:T(8,128)(2,1)} %param.23) | copy-start | bytes 196612
  377.1 23.4 %copy-start.65 = (bf16[32,1024]{1,0:T(8,128)(2,1)S(1)}, bf16[32,1024]{1,0:T(8,128)(2,1)}, u32[]{:S(2)}) copy-start(bf16[32,1024]{1,0:T(8,128)(2,1)} %param.22) | copy-start | bytes 196612
  377.1 23.4 %copy-start.68 = (f32[32,1024]{1,0:T(8,128)S(1)}, f32[32,1024]{1,0:T(8,128)}, u32[]{:S(2)}) copy-start(f32[32,1024]{1,0:T(8,128)} %param.30) | copy-start | bytes 393220
  377.1 23.4 %copy-start.69 = (f32[32,1024]{1,0:T(8,128)S(1)}, f32[32,1024]{1,0:T(8,128)}, u32[]{:S(2)}) copy-start(f32[32,1024]{1,0:T(8,128)} %param.29) | copy-start | bytes 393220
  377.1 9.0 %collective-permute-start.42 = (f32[16,128]{1,0:T(8,128)S(1)}, f32[16,128]{1,0:T(8,128)S(1)}, u32[]{:S(2)}, u32[]{:S(2)}) collective-permute-start(f32[16,128]{1,0:T(8,128)S(1)} %pad_maximum_fusion.14), channel_id=1, source_target_pairs={{0,2},{1,3},{2,0},{3,1},{4,6},{5,7},{6,4},{7,5},{8,10},{9,11},{10,... | collective-permute-start | bytes 24584 | tf_op jit(solution)/shard_map/ppermute | solution.py:652
  382.5 17.2 %all-to-all-start.3 = ((bf16[4,32,768]{2,1,0:T(8,128)(2,1)}), bf16[4,32,768]{2,1,0:T(8,128)(2,1)S(1)}, u32[]{:S(2)}, u32[]{:S(2)}) async-start(bf16[4,32,768]{2,1,0:T(8,128)(2,1)} %bitcast.35), calls=%async_computation.4 | async-start | bytes 393216 | tf_op jit(solution)/shard_map/all_to_all | solution.py:817
  (63 other events, 239.5 us)
Sparse Core Ops, SparseCore 0:
  12.4 44.1 all-gather.4
  58.1 58.1 all-gather.2
  259.0 19.1 reduce-scatter.7
  300.8 40.9 reduce-scatter.3
  366.8 38.1 reduce-scatter.5

commit v4 on v3

v4 whole, which is shorter than its diff:
```python
import math

import jax
import jax.numpy as jnp
from jax import lax
from jax.experimental import pallas as pl
from jax.experimental.pallas import tpu as pltpu
from jax.sharding import PartitionSpec as P

HEADS = 16
HEAD_DIM = 64


NORM_EPS = 1e-05
ROPE_BASE = 10000.0
LEARN_RATE = 0.0001
OUT_RATE = 0.0016
MASK_FILL = -1e30


def normalize(values):
    centred = values - jnp.mean(values, axis=-1, keepdims=True)
    spread = jnp.mean(centred * centred, axis=-1, keepdims=True)
    return centred * lax.rsqrt(spread + NORM_EPS)


def rotary_tables(positions, head_width):
    half_width = head_width // 2
    frequency = ROPE_BASE ** (-(jnp.arange(half_width, dtype=jnp.float32) * 2.0 / head_width))
    angles = positions.astype(jnp.float32)[:, None] * frequency[None, :]
    return (jnp.cos(angles), jnp.sin(angles))


def rotate(vectors, cosine, sine_table):
    half_width = vectors.shape[-1] // 2
    first_half = vectors[..., :half_width]
    second = vectors[..., half_width:]
    cos_wide = cosine[:, None, :]
    sin_wide = sine_table[:, None, :]
    return jnp.concatenate(
        [first_half * cos_wide - second * sin_wide, second * cos_wide + first_half * sin_wide],
        axis=-1,
    )


def swiglu(gate_proj, up_proj):
    return jax.nn.silu(gate_proj) * up_proj


def project(left_rows, matrix):
    return jnp.dot(left_rows, matrix, preferred_element_type=jnp.float32)


def project_back(grad_rows, matrix):
    return lax.dot_general(
        grad_rows, matrix, (((1,), (1,)), ((), ())), preferred_element_type=jnp.float32
    )


def shard_gradient(left_rows, right_rows):
    return lax.psum_scatter(
        lax.dot_general(
            left_rows, right_rows, (((0,), (0,)), ((), ())), preferred_element_type=jnp.float32
        ),
        ("dp", "ctx"),
        scatter_dimension=0,
        tiled=True,
    )


def per_device(
    activations,
    block_ids,
    cotangent,
    w_query,
    w_key,
    w_value,
    w_out,
    w_gate,
    w_up,
    w_down,
    m_query,
    m_key,
    m_value,
    m_out,
    m_gate,
    m_up,
    m_down,
    clip_threshold,
    momentum_coeff,
):
    shard_list = (w_query, w_key, w_value, w_out, w_gate, w_up, w_down)
    gathered = (
        lax.all_gather(shard_list[0], ("dp", "ctx"), axis=0, tiled=True),
        lax.all_gather(shard_list[1], ("dp", "ctx"), axis=0, tiled=True),
        lax.all_gather(shard_list[2], ("dp", "ctx"), axis=0, tiled=True),
        lax.all_gather(shard_list[3], ("dp", "ctx"), axis=0, tiled=True),
        lax.all_gather(shard_list[4], ("dp", "ctx"), axis=0, tiled=True),
        lax.all_gather(shard_list[5], ("dp", "ctx"), axis=0, tiled=True),
        lax.all_gather(shard_list[6], ("dp", "ctx"), axis=0, tiled=True),
    )
    full_query, full_key, full_value, full_out, full_gate, full_up, full_down = gathered
    seq_count, span_len, model_width = activations.shape
    ctx_place = lax.axis_index("ctx")
    positions = ctx_place * span_len + jnp.arange(span_len, dtype=jnp.int32)
    cosine, sine_table = rotary_tables(positions, HEAD_DIM)
    score_scale = 1.0 / math.sqrt(HEAD_DIM)

    def split_heads(matrix):
        return matrix.reshape(seq_count, span_len, HEADS, HEAD_DIM)

    tokens_flat = activations.astype(jnp.float32).reshape(-1, model_width)
    normed = normalize(tokens_flat).astype(jnp.bfloat16)
    queries = rotate(split_heads(project(normed, full_query)), cosine, sine_table).astype(
        jnp.bfloat16
    )
    key_rot = rotate(split_heads(project(normed, full_key)), cosine, sine_table).astype(
        jnp.bfloat16
    )
    value_rot = split_heads(project(normed, full_value)).astype(jnp.bfloat16)
    key_all, value_all = (
        lax.all_gather(key_rot, "ctx", axis=1, tiled=True),
        lax.all_gather(value_rot, "ctx", axis=1, tiled=True),
    )
    query_ids = lax.dynamic_slice_in_dim(block_ids, ctx_place * span_len, span_len, 1)
    allowed = (block_ids[:, None, :] <= query_ids[:, :, None])[:, None]

    def masked_scores():
        scores = (
            jnp.einsum("sqhd,skhd->shqk", queries, key_all, preferred_element_type=jnp.float32)
            * score_scale
        )
        return jnp.where(allowed, scores, MASK_FILL)

    masked = masked_scores()
    local_peaks = jnp.max(masked, axis=(0, 2, 3))
    row_top = jnp.max(masked, axis=-1, keepdims=True)
    log_total = row_top + jnp.log(jnp.sum(jnp.exp(masked - row_top), axis=-1, keepdims=True))
    probs_low = jnp.exp(masked - log_total).astype(jnp.bfloat16)
    attended = jnp.einsum(
        "shqk,skhd->sqhd", probs_low, value_all, preferred_element_type=jnp.float32
    )
    attended_low = attended.reshape(-1, model_width).astype(jnp.bfloat16)
    head_peaks = lax.pmax(local_peaks, ("dp", "ctx"))
    residual = tokens_flat + project(attended_low, full_out)
    normed2 = normalize(residual).astype(jnp.bfloat16)
    gate_proj = project(normed2, full_gate)
    up_proj = project(normed2, full_up)
    hidden_low = swiglu(gate_proj, up_proj).astype(jnp.bfloat16)
    layer_out = (
        (residual + project(hidden_low, full_down))
        .astype(jnp.bfloat16)
        .reshape(seq_count, span_len, model_width)
    )
    back_weights = (
        lax.all_gather(shard_list[0], ("dp", "ctx"), axis=0, tiled=True),
        lax.all_gather(shard_list[1], ("dp", "ctx"), axis=0, tiled=True),
        lax.all_gather(shard_list[2], ("dp", "ctx"), axis=0, tiled=True),
        lax.all_gather(shard_list[3], ("dp", "ctx"), axis=0, tiled=True),
        lax.all_gather(shard_list[4], ("dp", "ctx"), axis=0, tiled=True),
        lax.all_gather(shard_list[5], ("dp", "ctx"), axis=0, tiled=True),
        lax.all_gather(shard_list[6], ("dp", "ctx"), axis=0, tiled=True),
    )
    back_query, back_key, back_value, back_out, back_gate, back_up, back_down = back_weights
    grad_rows = cotangent.reshape(-1, model_width)
    grad_hidden = project_back(grad_rows, back_down)
    unused, gate_pull = jax.vjp(swiglu, gate_proj, up_proj)
    grad_gate_wide, grad_up_wide = gate_pull(grad_hidden)
    grad_gate_low = grad_gate_wide.astype(jnp.bfloat16)
    grad_up_low = grad_up_wide.astype(jnp.bfloat16)
    grad_normed2 = project_back(grad_gate_low, back_gate) + project_back(grad_up_low, back_up)
    unused, second_pull = jax.vjp(normalize, residual)
    grad_residual = grad_rows.astype(jnp.float32) + second_pull(grad_normed2)[0]
    grad_branch = grad_residual.astype(jnp.bfloat16)
    grad_attended = split_heads(project_back(grad_branch, back_out).astype(jnp.bfloat16))
    masked = masked_scores()
    probs = jnp.exp(masked - log_total)
    probs_again = probs.astype(jnp.bfloat16)
    grad_values_all = jnp.einsum(
        "shqk,sqhd->skhd", probs_again, grad_attended, preferred_element_type=jnp.float32
    )
    grad_probs = jnp.einsum(
        "sqhd,skhd->shqk", grad_attended, value_all, preferred_element_type=jnp.float32
    )
    score_grad = (
        probs * (grad_probs - jnp.sum(probs * grad_probs, axis=-1, keepdims=True))
    ).astype(jnp.bfloat16)
    grad_queries = (
        jnp.einsum("shqk,skhd->sqhd", score_grad, key_all, preferred_element_type=jnp.float32)
        * score_scale
    )
    grad_keys_all = (
        jnp.einsum("shqk,sqhd->skhd", score_grad, queries, preferred_element_type=jnp.float32)
        * score_scale
    )
    grad_keys, grad_values = (
        lax.psum_scatter(
            grad_keys_all.astype(jnp.bfloat16), "ctx", scatter_dimension=1, tiled=True
        ).astype(jnp.float32),
        lax.psum_scatter(
            grad_values_all.astype(jnp.bfloat16), "ctx", scatter_dimension=1, tiled=True
        ).astype(jnp.float32),
    )
    grad_query_low = (
        rotate(grad_queries, cosine, -sine_table).reshape(-1, model_width).astype(jnp.bfloat16)
    )
    grad_key_low = (
        rotate(grad_keys, cosine, -sine_table).reshape(-1, model_width).astype(jnp.bfloat16)
    )
    grad_value_low = grad_values.reshape(-1, model_width).astype(jnp.bfloat16)
    grad_normed = (
        project_back(grad_query_low, back_query)
        + project_back(grad_key_low, back_key)
        + project_back(grad_value_low, back_value)
    )
    unused, first_pull = jax.vjp(normalize, tokens_flat)
    input_grad = (grad_residual + first_pull(grad_normed)[0]).reshape(
        seq_count, span_len, model_width
    )
    weight_grads = (
        shard_gradient(normed, grad_query_low),
        shard_gradient(normed, grad_key_low),
        shard_gradient(normed, grad_value_low),
        shard_gradient(attended_low, grad_branch),
        shard_gradient(normed2, grad_gate_low),
        shard_gradient(normed2, grad_up_low),
        shard_gradient(hidden_low, grad_rows),
    )
    moments = (m_query, m_key, m_value, m_out, m_gate, m_up, m_down)
    new_moments = tuple(
        (momentum_coeff * moment + gradient for moment, gradient in zip(moments, weight_grads))
    )
    head_scale = jnp.sqrt(clip_threshold / jnp.maximum(head_peaks, clip_threshold))
    column_scale = jnp.repeat(head_scale, HEAD_DIM)
    rates = (LEARN_RATE, LEARN_RATE, LEARN_RATE, OUT_RATE, LEARN_RATE, LEARN_RATE, LEARN_RATE)
    updated = [
        matrix.astype(jnp.float32) - rate * moment
        for matrix, moment, rate in zip(shard_list, new_moments, rates)
    ]
    updated[0] = updated[0] * column_scale[None, :]
    updated[1] = updated[1] * column_scale[None, :]
    updated = [matrix.astype(jnp.bfloat16) for matrix in updated]
    return (
        layer_out,
        input_grad,
        weight_grads[0],
        weight_grads[1],
        weight_grads[2],
        weight_grads[3],
        weight_grads[4],
        weight_grads[5],
        weight_grads[6],
        new_moments[0],
        new_moments[1],
        new_moments[2],
        new_moments[3],
        new_moments[4],
        new_moments[5],
        new_moments[6],
        updated[0],
        updated[1],
        updated[2],
        updated[3],
        updated[4],
        updated[5],
        updated[6],
        head_peaks,
        head_scale,
    )


f32=jnp.float32; bf=jnp.bfloat16
NT=(((1,),(1,)),((),())); TN=(((0,),(0,)),((),())); NN=(((1,),(0,)),((),()))
FF2=1408
FFP=1536
FLIPS_A=((0,0),(1,0),(0,1),(1,1))
FLIPS_B=((0,0),(0,1),(1,0),(1,1))
MAIN=pl.BlockSpec(memory_space=pltpu.HBM)
S=jax.ShapeDtypeStruct


def dot(a, b, dims):
    return lax.dot_general(a, b, dims, preferred_element_type=f32)


def aligned(i, m):
    return pl.ds(pl.multiple_of(i * m, m), m)


class Copies:
    def __init__(self, sems):
        self.sems = sems
        self.count = 0

    def start(self, source, target):
        copy = pltpu.make_async_copy(source, target, self.sems.at[self.count])
        self.count += 1
        copy.start()
        return copy


def wait_all(copies):
    for copy in copies:
        copy.wait()


def call(kernel, name, outs, scratch, sems, flops, args, limit):
    return pl.pallas_call(
        kernel,
        out_shape=tuple(pltpu.HBM(*o) for o in outs),
        in_specs=[MAIN] * len(args),
        out_specs=(MAIN,) * len(outs),
        scratch_shapes=[pltpu.VMEM(*s) for s in scratch] + [pltpu.SemaphoreType.DMA(n if isinstance(n, tuple) else (n,)) for n in sems],
        compiler_params=pltpu.CompilerParams(vmem_limit_bytes=limit << 20),
        cost_estimate=pl.CostEstimate(flops=flops << 30, bytes_accessed=8 << 20, transcendentals=0),
        name=name,
    )(*(pltpu.with_memory_space_constraint(arg, pltpu.HBM) for arg in args))


def place_of(p):
    return lax.axis_index("dp") ^ ((p >> 2 & 1) | (p >> 1 & 1) << 1 | (p & 1) << 2)


def turn(values, cosine, signed_sine):
    lane = lax.broadcasted_iota(jnp.int32, cosine.shape, 1)
    first = lane % 64 < 32
    parts = []
    for j in range(values.shape[1] // 128):
        part = values[:, 128 * j : 128 * j + 128]
        partner = jnp.where(first, pltpu.roll(part, 96, 1), pltpu.roll(part, 32, 1))
        parts.append(part * cosine + partner * signed_sine)
    return jnp.concatenate(parts, axis=1)


def layer_norm(x):
    c = x - jnp.mean(x, axis=-1, keepdims=True)
    v = jnp.mean(c * c, axis=-1, keepdims=True)
    return c * lax.rsqrt(v + NORM_EPS)


def attend_kernel(*refs):
    (rows_hbm, weight_hbm, cos_hbm, sin_hbm, id_hbm, *pieces) = refs[:13]
    normed_hbm, mixed_hbm, attended_hbm, total_hbm, peak_hbm, outs_hbm = refs[13:19]
    (act, weight, cos_ref, sin_ref, ids, id_col, normed, mixed_ref, attended, value_t, total_ref,
     peak_ref, outs, sems) = refs[19:]
    n = normed.shape[0]
    go = Copies(sems)
    early = [go.start(rows_hbm.at[pl.ds(352 * i, 256)], act.at[pl.ds(256 * i, 256)]) for i in range(4)]
    middle = [
        go.start(weight_hbm.at[pl.ds(128 * p, 128)], weight.at[aligned(place_of(p), 128)])
        for p in range(8)
    ]
    middle += [go.start(cos_hbm, cos_ref), go.start(sin_hbm, sin_ref), go.start(id_hbm, ids)]
    packs = [go.start(piece.at[:, pl.ds(FF2, 256)], outs.at[i]) for i, piece in enumerate(pieces)]
    wait_all(early)

    @pl.loop(0, n // 128)
    def _(i):
        rows = aligned(i, 128)
        normed[rows, :] = layer_norm(act[rows, :].astype(f32)).astype(bf)

    late = [go.start(normed, normed_hbm)]
    wait_all(middle)
    wait_all(packs)
    late.append(go.start(outs, outs_hbm))
    id_col[...] = jnp.broadcast_to(ids[0:1, :], (128, n)).T

    @pl.loop(0, n // 256)
    def _(i):
        rows = aligned(i, 256)
        mixed = dot(normed[rows, :], weight[...], NN)
        cosine = cos_ref[rows, :]
        sine = sin_ref[rows, :]
        queries = turn(mixed[:, 0:256], cosine, sine).astype(bf)
        mixed_ref[rows, 0:256] = (queries.astype(f32) * 0.125).astype(bf)
        mixed_ref[rows, 256:512] = turn(mixed[:, 256:512], cosine, sine).astype(bf)
        value = mixed[:, 512:768]
        mixed_ref[rows, 512:768] = value.astype(bf)
        value_t[:, rows] = value.T.astype(bf)

    late.append(go.start(mixed_ref, mixed_hbm))
    peak_ref[...] = jnp.zeros_like(peak_ref)
    total_ref[...] = jnp.zeros_like(total_ref)

    @pl.loop(0, 4)
    def _(h):
        lanes = pl.multiple_of(h // 2 * 128, 128)
        lane = lax.broadcasted_iota(jnp.int32, (256, 128), 1)
        mine = lane // 64 == h % 2
        best = None
        for i in range(4):
            width = min(256 * (i + 2), 1024)
            low = 256 * i
            q = mixed_ref[low : low + 256, pl.ds(lanes, 128)]
            q = jnp.where(mine, q, jnp.zeros_like(q))
            s = dot(mixed_ref[0:width, pl.ds(pl.multiple_of(256 + lanes, 128), 128)], q, NT)
            ok = id_col[low:width, 0:1] <= ids[0:1, low : low + 256]
            tail = jnp.where(ok, s[low:width], MASK_FILL)
            top = jnp.max(tail, axis=0, keepdims=True)
            if i:
                top = jnp.maximum(top, jnp.max(s[0:low], axis=0, keepdims=True))
                s = jnp.concatenate([s[0:low], tail], axis=0)
            else:
                s = tail
            e = jnp.exp(s - top)
            total = jnp.sum(e, axis=0, keepdims=True)
            o = dot(value_t[pl.ds(lanes, 128), 0:width], e.astype(bf), NN)
            o = (o * (1.0 / total)).T.astype(bf)
            old = attended[low : low + 256, pl.ds(lanes, 128)]
            attended[low : low + 256, pl.ds(lanes, 128)] = jnp.where(mine, o, old)
            total_ref[pl.ds(h, 1), low : low + 256] = top + jnp.log(total)
            m = jnp.max(top, axis=1, keepdims=True)
            best = m if best is None else jnp.maximum(best, m)
        peak_ref[pl.ds(h, 1), :] = jnp.broadcast_to(best, (1, 128))

    late.append(go.start(attended, attended_hbm))
    late.append(go.start(total_ref, total_hbm))
    late.append(go.start(peak_ref, peak_hbm))
    wait_all(late)


def attend(rows_all, weight, cosine, sine, ids, pieces):
    n = cosine.shape[0]
    return call(
        attend_kernel, "attend",
        [((n, 1024), bf), ((n, 768), bf), ((n, 256), bf), ((8, n), f32), ((8, 128), f32),
         ((8, 256, 256), bf)],
        [((n, 1024), bf), ((1024, 768), bf), ((n, 128), f32), ((n, 128), f32), ((8, n), f32),
         ((n, 128), f32), ((n, 1024), bf), ((n, 768), bf), ((n, 256), bf), ((256, n), bf),
         ((8, n), f32), ((8, 128), f32), ((8, 256, 256), bf)],
        [29], 4, (rows_all, weight, cosine, sine, ids, *pieces), 28,
    )


def attend_back_kernel(mixed_hbm, ga_hbm, total_hbm, cos_hbm, sin_hbm, id_hbm, weight_hbm,
                       gm_hbm, gn_hbm,
                       mixed_ref, ga_ref, total_ref, cos_ref, sin_ref, ids, weight,
                       gm_ref, gn_ref, gk_acc, gv_acc, key_t, id_col, sems):
    n = ga_ref.shape[0]
    go = Copies(sems)
    early = [
        go.start(a, b)
        for a, b in ((mixed_hbm, mixed_ref), (ga_hbm, ga_ref), (total_hbm, total_ref),
                     (id_hbm, ids), (cos_hbm, cos_ref), (sin_hbm, sin_ref))
    ]
    late = [
        go.start(weight_hbm.at[pl.ds(128 * p, 128)], weight.at[aligned(place_of(p), 128)])
        for p in range(8)
    ]
    gk_acc[...] = jnp.zeros_like(gk_acc)
    gv_acc[...] = jnp.zeros_like(gv_acc)
    wait_all(early)
    id_col[...] = jnp.broadcast_to(ids[0:1, :], (128, n)).T

    @pl.loop(0, n // 256)
    def _(i):
        rows = aligned(i, 256)
        key_t[:, rows] = mixed_ref[rows, 256:512].astype(f32).T.astype(bf)

    @pl.loop(0, 2)
    def _(pair):
        lanes = pl.multiple_of(pair * 128, 128)
        lane = lax.broadcasted_iota(jnp.int32, (256, 128), 1)
        sub = lax.broadcasted_iota(jnp.int32, (128, 256), 0)
        for i in range(4):
            width = min(256 * (i + 2), 1024)
            low = 256 * i
            k = mixed_ref[0:width, pl.ds(pl.multiple_of(256 + lanes, 128), 128)]
            v = mixed_ref[0:width, pl.ds(pl.multiple_of(512 + lanes, 128), 128)]
            q_all = mixed_ref[low : low + 256, pl.ds(lanes, 128)]
            g_all = ga_ref[low : low + 256, pl.ds(lanes, 128)]
            kt = key_t[pl.ds(lanes, 128), 0:width]
            ok = id_col[low:width, 0:1] <= ids[0:1, low : low + 256]

            def one(half, gq):
                mine = lane // 64 == half
                q = jnp.where(mine, q_all, jnp.zeros_like(q_all))
                g = jnp.where(mine, g_all, jnp.zeros_like(g_all))
                s = dot(k, q, NT) - total_ref[pl.ds(pair * 2 + half, 1), low : low + 256]
                tail = jnp.where(ok, s[low:width], MASK_FILL)
                s = jnp.concatenate([s[0:low], tail], axis=0) if i else tail
                p = jnp.exp(s)
                t = p * dot(v, g, NT)
                delta = jnp.sum(t, axis=0, keepdims=True)
                ds = (t - p * delta).astype(bf)
                gv_acc[0:width, pl.ds(lanes, 128)] += dot(p.astype(bf), g, NN)
                gk_acc[0:width, pl.ds(lanes, 128)] += dot(ds, q, NN)
                return jnp.where(sub // 64 == half, dot(kt, ds, NN), gq)

            gq = lax.fori_loop(0, 2, one, jnp.zeros((128, 256), f32))
            gq = gq.T * 0.125
            cosine = cos_ref[low : low + 256, :]
            sine = sin_ref[low : low + 256, :]
            gm_ref[low : low + 256, pl.ds(lanes, 128)] = turn(gq, cosine, -sine).astype(bf)

    wait_all(late)

    @pl.loop(0, n // 256)
    def _(i):
        rows = aligned(i, 256)
        cosine = cos_ref[rows, :]
        sine = sin_ref[rows, :]
        gm_ref[rows, 256:512] = turn(gk_acc[rows, :], cosine, -sine).astype(bf)
        gm_ref[rows, 512:768] = gv_acc[rows, :].astype(bf)
        gn_ref[rows, :] = dot(gm_ref[rows, :], weight[...], NT).astype(bf)
        copy = pltpu.make_async_copy(gn_ref.at[rows], gn_hbm.at[rows], sems.at[14 + i])
        copy.start()

    out = pltpu.make_async_copy(gm_ref, gm_hbm, sems.at[18])
    out.start()
    for i in range(4):
        rows = pl.ds(256 * i, 256)
        pltpu.make_async_copy(gn_ref.at[rows], gn_hbm.at[rows], sems.at[14 + i]).wait()
    out.wait()


def attend_back(mixed, ga, total, cosine, sine, ids, weight):
    n = ga.shape[0]
    return call(
        attend_back_kernel, "attend_back",
        [((n, 768), bf), ((n, 1024), bf)],
        [((n, 768), bf), ((n, 256), bf), ((8, n), f32), ((n, 128), f32), ((n, 128), f32),
         ((8, n), f32), ((1024, 768), bf), ((n, 768), bf), ((n, 1024), bf), ((n, 256), f32),
         ((n, 256), f32), ((256, n), bf), ((n, 128), f32)],
        [19], 7, (mixed, ga, total, cosine, sine, ids, weight), 32,
    )


def weights_kernel(gm_hbm, normed_hbm, keep_hbm, send_hbm, gm_ref, normed_ref, gw, sems):
    go = Copies(sems)
    wait_all([go.start(gm_hbm, gm_ref), go.start(normed_hbm, normed_ref)])

    @pl.loop(0, 4)
    def _(i):
        cols = aligned(i, 256)
        gw[cols, :] = dot(normed_ref[:, cols], gm_ref[...], TN).astype(bf)

    wait_all([
        go.start(gw.at[aligned(place_of(p), 128)],
                 (keep_hbm if p < 4 else send_hbm).at[pl.ds(128 * (p % 4), 128)])
        for p in range(8)
    ])


def project_weights(gm, normed):
    n = gm.shape[0]
    return call(
        weights_kernel, "project_weights", [((512, 768), bf)] * 2,
        [((n, 768), bf), ((n, 1024), bf), ((1024, 768), bf)], [10], 1, (gm, normed), 24,
    )


def feed_kernel(*refs):
    att_hbm, attp_hbm, act_hbm, actp_hbm, cot_hbm, cotp_hbm = refs[:6]
    a_in, b_in, da_in, db_in, outs = refs[6:10], refs[10:14], refs[14:18], refs[18:22], refs[22]
    part_hbm, outown_hbm, gnown_hbm, res_hbm, wo_hbm = refs[23:28]
    (ga_keep, ga_send, gb_keep, gb_send, gda_keep, gda_send, gdb_keep, gdb_send) = refs[28:36]
    (wg, wu, wd, wo, att, act, n2, n2t, cot, res_ref, out_acc, gn_acc, part, dg, du, dd,
     sems, osem, tsem) = refs[36:]
    me = lax.axis_index("dp")
    core = me % 2
    yx = me // 2
    go = Copies(sems)
    small = []
    for base, src, own in ((0, att_hbm, act_hbm), (256, attp_hbm, actp_hbm)):
        rows = pl.ds(base, 256)
        small += [go.start(src.at[i], att.at[rows, pl.ds(256 * i, 256)]) for i in range(4)]
        small.append(go.start(own, act.at[rows]))
    places = []
    for p in range(4):
        (ax, ay), (bx, by) = FLIPS_A[p], FLIPS_B[p]
        places.append((yx ^ (ax + 2 * ay), yx ^ (bx + 2 * by)))
    for p, (ja, jb) in enumerate(places):
        for which, src, j, col in ((0, a_in[p], ja, 0), (1, b_in[p], jb, 512)):
            for half in range(2):
                cols = pl.ds(col + 256 * half, 256)
                rows = pl.ds(128 * half, 128)
                small.append(go.start(src.at[rows, pl.ds(FF2, 256)], wo.at[aligned(j * 2 + core, 128), cols]))
                small.append(go.start(outs.at[4 * which + p, rows], wo.at[aligned(j * 2 + 1 - core, 128), cols]))
    big = []
    for p, (ja, jb) in enumerate(places):
        for src, dst, j in ((a_in[p], wg, ja), (b_in[p], wu, jb)):
            for half, c in ((0, core), (1, 1 - core)):
                big.append(go.start(src.at[pl.ds(128 * half, 128), pl.ds(0, FF2)],
                                    dst.at[aligned(j * 2 + c, 128), pl.ds(0, FF2)]))
    big += [go.start(cot_hbm, cot.at[pl.ds(0, 256)]), go.start(cotp_hbm, cot.at[pl.ds(256, 256)])]
    for p, (ja, jb) in enumerate(places):
        big.append(go.start(da_in[p], wd.at[aligned(ja, 352), pl.ds(0, 512)]))
        big.append(go.start(db_in[p], wd.at[aligned(jb, 352), pl.ds(512, 512)]))
    wg[:, FF2:FFP] = jnp.zeros((1024, FFP - FF2), bf)
    wu[:, FF2:FFP] = jnp.zeros((1024, FFP - FF2), bf)
    wd[FF2:FFP, :] = jnp.zeros((FFP - FF2, 1024), bf)
    out_acc[...] = jnp.zeros_like(out_acc)
    gn_acc[...] = jnp.zeros_like(gn_acc)
    wait_all(small)
    ogo = Copies(osem)
    done = [ogo.start(wo, wo_hbm)]

    @pl.loop(0, 2)
    def _(i):
        rows = aligned(i, 256)
        res = act[rows, :].astype(f32) + dot(att[rows, :], wo[...], NN)
        res_ref[rows, :] = res
        n = layer_norm(res)
        n2[rows, :] = n.astype(bf)
        n2t[:, rows] = n.T.astype(bf)

    done.append(ogo.start(res_ref.at[pl.ds(0, 256)], res_hbm))
    wait_all(big)

    def tile_copies(t, width):
        copies = []
        cols = pl.ds(pl.multiple_of(t * 256, 256), width)
        for q in range(4):
            fx, fy = FLIPS_A[q]
            rows = aligned(yx ^ (fx + 2 * fy), 256)
            for k, src, dst, slot in ((0, dg, ga_send if fx else ga_keep, fy), (1, du, gb_send if fy else gb_keep, fx)):
                copies.append(pltpu.make_async_copy(
                    src.at[rows, cols], dst.at[pl.ds(256 * slot, 256), cols], tsem.at[t, 2 * q + k]))
        return copies

    last = FFP // 256 - 1

    @pl.loop(0, last + 1)
    def _(t):
        cols = aligned(t, 256)
        g = dot(n2[...], wg[:, cols], NN)
        u = dot(n2[...], wu[:, cols], NN)
        gh = dot(cot[...], wd[cols, :], NT)
        sig = 1.0 / (1.0 + jnp.exp(-g))
        silu = g * sig
        h = (silu * u).astype(bf)
        gu = (gh * silu).astype(bf)
        gg = (gh * u * (sig + silu * (1.0 - sig))).astype(bf)
        dg[:, cols] = dot(n2t[...], gg, NN).astype(bf)
        du[:, cols] = dot(n2t[...], gu, NN).astype(bf)

        @pl.when(t < last)
        def _():
            for copy in tile_copies(t, 256):
                copy.start()

        dd[cols, :] = dot(h, cot[...], TN).astype(bf)
        gn_acc[...] += dot(gg, wg[:, cols], NT) + dot(gu, wu[:, cols], NT)
        out_acc[...] += dot(h, wd[cols, :], NN)

    ends = tile_copies(last, FF2 - 256 * last)
    for copy in ends:
        copy.start()
    part[0:256, :] = out_acc[256:512, :].astype(bf)
    part[256:512, :] = gn_acc[256:512, :].astype(bf)
    done.append(ogo.start(part, part_hbm))
    done.append(ogo.start(gn_acc.at[pl.ds(0, 256)], gnown_hbm))
    done.append(ogo.start(out_acc.at[pl.ds(0, 256)], outown_hbm))
    for q in range(4):
        fx, fy = FLIPS_A[q]
        rows = aligned(yx ^ (fx + 2 * fy), 352)
        done.append(ogo.start(dd.at[rows, pl.ds(0, 512)], (gda_send if fx else gda_keep).at[pl.ds(352 * fy, 352)]))
        done.append(ogo.start(dd.at[rows, pl.ds(512, 512)], (gdb_send if fy else gdb_keep).at[pl.ds(352 * fx, 352)]))
    for t in range(last):
        wait_all(tile_copies(t, 256))
    wait_all(ends)
    wait_all(done)


def feed(att, attp, act, actp, cot, cotp, a, b, da, db, outs):
    big = [((1024, FFP), bf), ((1024, FFP), bf), ((FFP, 1024), bf)]
    return call(
        feed_kernel, "feed",
        [((512, 1024), bf), ((256, 1024), f32), ((256, 1024), f32), ((256, 1024), f32), ((1024, 1024), bf)]
        + [((512, FF2), bf)] * 4 + [((704, 512), bf)] * 4,
        big + [((1024, 1024), bf), ((512, 1024), bf), ((512, 1024), bf), ((512, 1024), bf), ((1024, 512), bf),
               ((512, 1024), bf), ((512, 1024), f32), ((512, 1024), f32), ((512, 1024), f32), ((512, 1024), bf)] + big,
        [68, 13, (6, 8)], 15, (att, attp, act, actp, cot, cotp, *a, *b, *da, *db, outs), 50,
    )


def branch_kernel(part_hbm, outown_hbm, gnown_hbm, res_hbm, cot_hbm, att_hbm, wo_hbm,
                  layer_hbm, gres_hbm, gatt_hbm, keep_hbm, send_hbm,
                  part, outown, gnown, res_ref, cot, att, wo, layer, gres_ref, gatt, gw, sems):
    me = lax.axis_index("dp")
    core = me % 2
    yx = me // 2
    go = Copies(sems)
    first = [
        go.start(a, b)
        for a, b in ((part_hbm, part), (gnown_hbm, gnown), (res_hbm, res_ref), (cot_hbm, cot))
    ]
    late = [go.start(wo_hbm, wo), go.start(outown_hbm, outown)]
    late += [go.start(att_hbm.at[i], att.at[:, pl.ds(256 * i, 256)]) for i in range(4)]
    wait_all(first)
    res = res_ref[...]
    g = gnown[...] + part[256:512, :].astype(f32)
    c = res - jnp.mean(res, axis=-1, keepdims=True)
    r = lax.rsqrt(jnp.mean(c * c, axis=-1, keepdims=True) + NORM_EPS)
    xh = c * r
    d = r * (g - jnp.mean(g, axis=-1, keepdims=True) - xh * jnp.mean(g * xh, axis=-1, keepdims=True))
    gres = cot[...].astype(f32) + d
    gres_ref[...] = gres
    low = gres.astype(bf)
    wait_all(late)
    done = [go.start(gres_ref, gres_hbm)]
    ga = dot(low, wo[...], NT).astype(bf)
    for z in range(4):
        gatt[z] = ga[:, 256 * z : 256 * z + 256]
    done.append(go.start(gatt, gatt_hbm))
    layer[...] = (res + (outown[...] + part[0:256, :].astype(f32))).astype(bf)
    done.append(go.start(layer, layer_hbm))
    gw[...] = dot(att[...], low, TN).astype(bf)
    for q in range(4):
        fx, fy = FLIPS_A[q]
        j = yx ^ (fx + 2 * fy)
        for dst, c in ((keep_hbm, core), (send_hbm, 1 - core)):
            rows = aligned(j * 2 + c, 128)
            done.append(go.start(gw.at[rows, pl.ds(0, 512)], dst.at[pl.ds(128 * (2 * fx + fy), 128), pl.ds(0, 512)]))
            done.append(go.start(gw.at[rows, pl.ds(512, 512)], dst.at[pl.ds(128 * (2 * fy + fx), 128), pl.ds(512, 512)]))
    wait_all(done)


def branch(part, outown, gnown, res, cot, att, wo):
    tall = ((256, 1024), f32)
    low = ((256, 1024), bf)
    return call(
        branch_kernel, "branch",
        [low, tall, ((4, 256, 256), bf), ((512, 1024), bf), ((512, 1024), bf)],
        [((512, 1024), bf), tall, tall, tall, low, low, ((1024, 1024), bf), low, tall, ((4, 256, 256), bf),
         ((1024, 1024), bf)],
        [29], 1, (part, outown, gnown, res, cot, att, wo), 32,
    )


def swap(array, bit):
    return lax.ppermute(array, "dp", [(i, i ^ bit) for i in range(8)])


def shift(array, bits):
    return lax.ppermute(array, "ctx", [(i, i ^ bits) for i in range(4)])


def add_low(left, right):
    return (left.astype(f32) + right.astype(f32)).astype(bf)


def split_even(matrix):
    n = matrix.shape[1] // 8
    parts = [matrix[:, n * i : n * i + n] for i in range(8)]
    return jnp.concatenate(parts[0::2], axis=1), jnp.concatenate(parts[1::2], axis=1)


def join_even(even, odd):
    n = even.shape[1] // 4
    parts = []
    for i in range(4):
        parts += [even[:, n * i : n * i + n], odd[:, n * i : n * i + n]]
    return jnp.concatenate(parts, axis=1)


def tie(value, *anchors):
    return lax.optimization_barrier((value, *anchors))[0]


def fast_device(
    activations,
    block_ids,
    cotangent,
    w_query,
    w_key,
    w_value,
    w_out,
    w_gate,
    w_up,
    w_down,
    m_query,
    m_key,
    m_value,
    m_out,
    m_gate,
    m_up,
    m_down,
    clip_threshold,
    momentum_coeff,
):
    me = lax.axis_index("dp")
    z = lax.axis_index("ctx")
    core = me % 2
    _, span, width = activations.shape
    length = block_ids.shape[1]
    act = activations.reshape(span, width)
    cot = cotangent.reshape(span, width)
    act_other = swap(act, 1)
    cot_other = swap(cot, 1)
    g0, g1 = split_even(w_gate)
    u0, u1 = split_even(w_up)
    even = jnp.stack([g0, u0])
    odd = jnp.stack([g1, u1])
    flip = core == 1
    mine = jnp.where(flip, odd, even)
    other = swap(jnp.where(flip, even, odd), 1)
    out_rows = jnp.stack([w_out[:, :512], w_out[:, 512:]]).reshape(2, 32, 2, 256)
    wide = jnp.stack([mine, other], axis=1)
    wide = jnp.concatenate([wide, out_rows.transpose(0, 2, 1, 3)], axis=3)
    wide = lax.all_gather(wide, "ctx", axis=2, tiled=True).reshape(2, 256, FF2 + 256)
    padded = jnp.concatenate([act, w_down, jnp.zeros((8, width), bf)], axis=0)
    rows_all = lax.all_gather(padded, "ctx", axis=0, tiled=True)
    heads = jnp.stack(
        [
            jnp.concatenate([w[:, 256 * i : 256 * i + 256] for w in (w_query, w_key, w_value)], 1)
            for i in range(4)
        ]
    )
    heads = lax.all_to_all(heads, "ctx", 0, 0, tiled=True).reshape(128, 768)
    hx = swap(heads, 2)
    hy = swap(jnp.concatenate([heads, hx], axis=0), 4)
    four = jnp.concatenate([heads, hy[:128], hx, hy[128:]], axis=0)
    heads_rel = jnp.concatenate([four, swap(four, 1)], axis=0)
    wide, act_other, cot_other = lax.optimization_barrier((wide, act_other, cot_other))

    def spread(own, first, second):
        near = swap(own, first)
        return [own, near, swap(own, second), swap(near, second)]

    piece_a = spread(wide[0], 2, 4)
    piece_b = spread(wide[1], 4, 2)
    down = jnp.concatenate(
        [rows_all[352 * i + 256 : 352 * i + 344] for i in range(4)], axis=0
    )
    piece_da = spread(down[:, :512], 2, 4)
    piece_db = spread(down[:, 512:], 4, 2)
    cosine, sine = rotary_tables(jnp.arange(length, dtype=jnp.int32), HEAD_DIM)
    cosine = jnp.concatenate([cosine] * 4, axis=1)
    sine = jnp.concatenate([-sine, sine, -sine, sine], axis=1)
    ids = jnp.broadcast_to(block_ids, (8, length)).astype(f32)
    pieces = lax.optimization_barrier((rows_all, *piece_a, *piece_b))
    normed, mixed, attended, totals, peaks, outs = attend(
        pieces[0], heads_rel, cosine, sine, ids, pieces[1:]
    )
    piece_a, piece_b = pieces[1:5], pieces[5:]
    outs = swap(outs, 1)
    attended = tie(attended, *piece_da[1:3], *piece_db[1:3])
    attended = lax.all_to_all(attended.reshape(4, span, 256), "ctx", 0, 0, tiled=True)
    attended_other = swap(tie(attended, piece_da[3], piece_db[3]), 1)
    (part, out_own, back_own, residual, full_out, *grads) = feed(
        attended, attended_other, act, act_other, cot, cot_other,
        piece_a, piece_b, piece_da, piece_db, outs,
    )
    ga_keep, ga_send, gb_keep, gb_send, gda_keep, gda_send, gdb_keep, gdb_send = grads
    part = swap(part, 1)
    gda_send, gdb_send, part = lax.optimization_barrier((gda_send, gdb_send, part))
    layer_out, grad_residual, grad_attended, go_keep, go_send = branch(
        part, out_own, back_own, residual, cot, attended, full_out
    )
    grad_attended = lax.all_to_all(grad_attended, "ctx", 0, 0, tiled=True).reshape(length, 256)
    gda_other = swap(gda_send, 2)
    gdb_other = swap(gdb_send, 4)
    grad_da = add_low(gda_keep, gda_other)
    grad_db = add_low(gdb_keep, gdb_other)
    ga_send, gb_send, grad_da, grad_db = lax.optimization_barrier(
        (ga_send, gb_send, grad_da, grad_db)
    )
    ga_other = swap(ga_send, 2)
    gb_other = swap(gb_send, 4)
    grad_a = add_low(ga_keep, ga_other)
    grad_b = add_low(gb_keep, gb_other)
    grad_a = add_low(grad_a[:256], swap(grad_a[256:], 4))
    grad_b = add_low(grad_b[:256], swap(grad_b[256:], 2))
    grad_da = add_low(grad_da[:352], swap(grad_da[352:], 4))
    grad_db = add_low(grad_db[:352], swap(grad_db[352:], 2))
    go_keep, ga_later = lax.optimization_barrier((go_keep, ga_other))
    grad_out = add_low(go_keep, swap(go_send, 1))
    grad_oa = add_low(grad_out[:256, :512], swap(grad_out[256:, :512], 2))
    grad_ob = add_low(grad_out[:256, 512:], swap(grad_out[256:, 512:], 4))
    grad_oa = add_low(grad_oa[:128], swap(grad_oa[128:], 4))
    grad_ob = add_low(grad_ob[:128], swap(grad_ob[128:], 2))

    def core_rows(which):
        return jnp.concatenate(
            [lax.dynamic_slice_in_dim(g, which * 128, 128, 0) for g in (grad_a, grad_b)], axis=1
        )

    own_half = core_rows(core)
    other_half = swap(core_rows(1 - core), 1)
    grad_d = jnp.concatenate([grad_da, grad_db], axis=1).reshape(4, 88, width)
    grad_d = jnp.pad(grad_d, ((0, 0), (0, 8), (0, 0))).reshape(4, 3, 32, width)
    grad_d = grad_d.transpose(0, 2, 1, 3).reshape(128, 3 * width)
    grad_wide = jnp.concatenate(
        [
            jnp.where(flip, other_half, own_half),
            jnp.where(flip, own_half, other_half),
            grad_oa,
            grad_ob,
            grad_d,
        ],
        axis=1,
    )
    grad_wide = lax.psum_scatter(grad_wide, "ctx", scatter_dimension=0, tiled=True).astype(f32)
    grad_mixed, grad_normed = attend_back(
        mixed, grad_attended, totals, cosine, sine, ids, heads_rel
    )
    grad_heads = project_weights(tie(grad_mixed, ga_other, gb_other), normed)
    peaks = tie(peaks, ga_other)
    peaks = lax.all_to_all(
        jnp.broadcast_to(peaks[None], (32, 8, 128)), ("dp", "ctx"), 0, 0, tiled=True
    )
    head_peaks = jnp.max(peaks.reshape(8, 4, 8, 128), axis=0)[:, :4, 0].reshape(HEADS)
    grad_normed = lax.psum_scatter(grad_normed, "ctx", scatter_dimension=0, tiled=True)
    tokens_wide = act.astype(f32)
    unused, first_pull = jax.vjp(normalize, tokens_wide)
    input_grad = grad_residual + first_pull(grad_normed.astype(f32))[0]
    grad_heads = add_low(grad_heads[0], swap(grad_heads[1], 1))
    grad_heads = add_low(grad_heads[:256], swap(grad_heads[256:], 2))
    grad_heads = add_low(grad_heads[:128], swap(grad_heads[128:], 4))
    grad_heads = lax.all_to_all(grad_heads.reshape(4, 32, 768), "ctx", 0, 0, tiled=True)
    grad_heads = grad_heads.astype(f32)
    grad_qkv = [
        jnp.concatenate([grad_heads[i, :, 256 * k : 256 * k + 256] for i in range(4)], axis=1)
        for k in range(3)
    ]
    grad_d_sum = grad_wide[:, 4 * FF2 + width :].reshape(32, 3, width).transpose(1, 0, 2)
    grad_d_sum = grad_d_sum.reshape(96, width)[:88]
    weight_grads = (
        *grad_qkv,
        grad_wide[:, 4 * FF2 : 4 * FF2 + width],
        join_even(grad_wide[:, :FF2], grad_wide[:, 2 * FF2 : 3 * FF2]),
        join_even(grad_wide[:, FF2 : 2 * FF2], grad_wide[:, 3 * FF2 : 4 * FF2]),
        grad_d_sum,
    )
    moments = (m_query, m_key, m_value, m_out, m_gate, m_up, m_down)
    new_moments = tuple(
        (momentum_coeff * moment + gradient for moment, gradient in zip(moments, weight_grads))
    )
    head_scale = jnp.sqrt(clip_threshold / jnp.maximum(head_peaks, clip_threshold))
    column_scale = jnp.repeat(head_scale, HEAD_DIM)
    rates = (LEARN_RATE, LEARN_RATE, LEARN_RATE, OUT_RATE, LEARN_RATE, LEARN_RATE, LEARN_RATE)
    shard_list = (w_query, w_key, w_value, w_out, w_gate, w_up, w_down)
    updated = [
        matrix.astype(jnp.float32) - rate * moment
        for matrix, moment, rate in zip(shard_list, new_moments, rates)
    ]
    updated[0] = updated[0] * column_scale[None, :]
    updated[1] = updated[1] * column_scale[None, :]
    updated = [matrix.astype(bf) for matrix in updated]
    return (
        layer_out[None],
        input_grad[None],
        *weight_grads,
        *new_moments,
        *updated,
        head_peaks,
        head_scale,
    )


def solution(mesh):
    placed = (
        P("dp", "ctx", None),
        P("dp", None),
        P("dp", "ctx", None),
        P(("dp", "ctx"), None),
        P(("dp", "ctx"), None),
        P(("dp", "ctx"), None),
        P(("dp", "ctx"), None),
        P(("dp", "ctx"), None),
        P(("dp", "ctx"), None),
        P(("dp", "ctx"), None),
        P(("dp", "ctx"), None),
        P(("dp", "ctx"), None),
        P(("dp", "ctx"), None),
        P(("dp", "ctx"), None),
        P(("dp", "ctx"), None),
        P(("dp", "ctx"), None),
        P(("dp", "ctx"), None),
        P(),
        P(),
    )
    fits = mesh.shape["dp"] == 8 and mesh.shape["ctx"] == 4
    return jax.shard_map(
        fast_device if fits else per_device,
        mesh=mesh,
        in_specs=placed,
        out_specs=(
            P("dp", "ctx", None),
            P("dp", "ctx", None),
            P(("dp", "ctx"), None),
            P(("dp", "ctx"), None),
            P(("dp", "ctx"), None),
            P(("dp", "ctx"), None),
            P(("dp", "ctx"), None),
            P(("dp", "ctx"), None),
            P(("dp", "ctx"), None),
            P(("dp", "ctx"), None),
            P(("dp", "ctx"), None),
            P(("dp", "ctx"), None),
            P(("dp", "ctx"), None),
            P(("dp", "ctx"), None),
            P(("dp", "ctx"), None),
            P(("dp", "ctx"), None),
            P(("dp", "ctx"), None),
            P(("dp", "ctx"), None),
            P(("dp", "ctx"), None),
            P(("dp", "ctx"), None),
            P(("dp", "ctx"), None),
            P(("dp", "ctx"), None),
            P(("dp", "ctx"), None),
            P(),
            P(),
        ),
        check_vma=False,
    )
```

time: 421 us -> 366 us (0.87)
  waiting for transfers between devices: 187 us -> 158 us
  local copies, waits for them, and re-layouts: 51.4 us -> 23.4 us
  other arithmetic: 33.9 us -> 28.1 us
  starting transfers between devices: 52.7 us -> 57 us
    ppermute x41 -> x38, waiting for transfers between devices: 121 us -> 76.3 us  [swap(): return lax.ppermute(array, 'dp', [(i, i ^ bit) for i in range(8)])]
    unnamed x164 -> x106, local copies, waits for them, and re-layouts: 37.5 us -> 9.79 us
    all_gather x1, waiting for transfers between devices: 13.7 us -> 30.4 us  [fast_device(): rows_all = lax.all_gather(padded, 'ctx', axis=0, tiled=True)]
    all_to_all x1, waiting for transfers between devices: 10.3 us -> 0.34 us  [fast_device(): lax.all_to_all(attended.reshape(4, span, 256), 'ctx', 0, 0, tiled=True)]
    all_gather x1, waiting for transfers between devices: 9.24 us -> 16.5 us  [fast_device(): lax.all_gather(wide, 'ctx', axis=2, tiled=True).reshape(2, 256, FF2 + 256)]
    all_to_all x1, waiting for transfers between devices: 8.43 us -> 1.8 us  [fast_device(): lax.all_to_all(grad_attended, 'ctx', 0, 0, tiled=True).reshape(length, 256)]
    all_to_all x0 -> x1, waiting for transfers between devices: none -> 5.41 us  [fast_device(): lax.all_to_all(jnp.broadcast_to(peaks[None], (32, 8, 128)), ('dp', 'ctx')...]
    pallas_call x6 -> x5, Pallas kernels: 78.5 us -> 82.5 us  [call(): pl.pallas_call(kernel, out_shape=tuple((pltpu.HBM(*o) for o in outs)), in...]
  transfers between devices with their start and end apart: 52 -> 47, of which waited for: 26 -> 27; matrix products, arithmetic and copies ran while one was open for 11% -> 10% of each run, Pallas kernels for 12% -> 14%
where the time goes in v4:
time: 366 us; the launch traced here: 365 us
  waiting for transfers between devices  158 us (43%)
  Pallas kernels  82.5 us (23%)
  starting transfers between devices  57 us (16%)
  other arithmetic  28.1 us (8%)
  local copies, waits for them, and re-layouts  23.4 us (6%)
  between operations  16.2 us (4%)
    pallas_call x5, Pallas kernels, call(): pl.pallas_call(kernel, out_shape=tuple((pltpu.HBM(*o) for o in outs)), in...  82.5 us
    ppermute x38, waiting for transfers between devices, swap(): return lax.ppermute(array, 'dp', [(i, i ^ bit) for i in range(8)])  76.3 us
    ppermute x38, starting transfers between devices, swap(): return lax.ppermute(array, 'dp', [(i, i ^ bit) for i in range(8)])  35.3 us
    all_gather x1, waiting for transfers between devices, fast_device(): rows_all = lax.all_gather(padded, 'ctx', axis=0, tiled=True)  30.4 us
    all_gather x1, waiting for transfers between devices, fast_device(): lax.all_gather(wide, 'ctx', axis=2, tiled=True).reshape(2, 256, FF2 + 256)  16.5 us
    all_to_all x1, waiting for transfers between devices, fast_device(): lax.all_to_all(grad_heads.reshape(4, 32, 768), 'ctx', 0, 0, tiled=True)  12.6 us
    all_to_all x1, waiting for transfers between devices, fast_device(): heads = lax.all_to_all(heads, 'ctx', 0, 0, tiled=True).reshape(128, 768)  11 us
    convert_element_type x13, other arithmetic, add_low(): return (left.astype(f32) + right.astype(f32)).astype(bf)  10.5 us
  transfers between devices with their start and end apart: 47, of which 27 were waited for; matrix products, arithmetic and copies ran while one was open for 10% of the time, Pallas kernels for 14%

profile of v4, /device:TPU:0, one launch (start us, length us, event | category | flops | bytes accessed | tf_op | source)
XLA Modules:
  0.0 365.0 jit_solution(9643214003701756533)
XLA Ops:
  14.3 6.2 %all-to-all-start = ((bf16[4,32,768]{2,1,0:T(8,128)(2,1)}), bf16[4,32,768]{2,1,0:T(8,128)(2,1)S(1)}, u32[]{:S(2)}, u32[]{:S(2)}) async-start(bf16[4,32,768]{2,1,0:T(8,128)(2,1)} %pad_maximum_fusion.9), calls=%async_computation | async-start | bytes 393216 | tf_op jit(solution)/shard_map/all_to_all | solution.py:811
  21.0 11.0 %all-to-all-done = bf16[4,32,768]{2,1,0:T(8,128)(2,1)S(1)} async-done(((bf16[4,32,768]{2,1,0:T(8,128)(2,1)}), bf16[4,32,768]{2,1,0:T(8,128)(2,1)S(1)}, u32[]{:S(2)}, u32[]{:S(2)}) %all-to-all-start) | async-done | bytes 196640 | tf_op jit(solution)/shard_map/all_to_all | solution.py:811
  32.0 1.5 collective-permute-start.9
  34.2 3.5 collective-permute-done.9
  38.4 1.6 collective-permute-start.10
  40.0 16.5 %all-gather.5.cloned.1.call-done = bf16[2,2,128,1664]{3,2,0,1:T(8,128)(2,1)} async-done(((bf16[2,2,32,1664]{3,2,0,1:T(8,128)(2,1)}), bf16[2,2,128,1664]{3,2,0,1:T(8,128)(2,1)}) %all-gather.5.cloned.1.call-update) | async-done | bytes 1703952 | tf_op jit(solution)/shard_map/all_gather | solution.py:802
  56.5 1.6 copy.68
  59.8 1.6 collective-permute-start.3
  61.4 1.5 collective-permute-start.6
  63.8 1.9 fusion.6
  65.7 1.9 pad_maximum_fusion.5
  69.3 12.5 %collective-permute-done.3.refs_6_.refs_7_ = bf16[256,1664]{1,0:T(8,128)(2,1)} collective-permute-done((bf16[256,1664]{1,0:T(8,128)(2,1)S(1)}, bf16[256,1664]{1,0:T(8,128)(2,1)}, u32[]{:S(2)}, u32[]{:S(2)}) %collective-permute-start.3) | collective-permute-done | bytes 852000 | tf_op jit(solution)/shard_map/ppermute | solution.py:733
  81.8 1.5 collective-permute-start.5
  83.3 1.5 collective-permute-start.8
  86.5 30.4 %all-gather.3.cloned.1.call-done.refs_0_ = bf16[1408,1024]{1,0:T(8,128)(2,1)} async-done(((bf16[352,1024]{1,0:T(8,128)(2,1)}), bf16[1408,1024]{1,0:T(8,128)(2,1)}) %all-gather.3.cloned.1.call-update) | async-done | bytes 2883600 | tf_op jit(solution)/shard_map/all_gather | solution.py:804
  118.2 1.5 collective-permute-start.12
  119.8 1.5 collective-permute-start.13
  123.0 18.1 %attend.1 = (bf16[1024,1024]{1,0:T(8,128)(2,1)}, bf16[1024,768]{1,0:T(8,128)(2,1)}, bf16[1024,256]{1,0:T(8,128)(2,1)}, f32[8,1024]{1,0:T(8,128)}, f32[8,128]{1,0:T(8,128)}, /*index=5*/bf16[8,256,256]{2,1,0:T(8,128)(2,1)}) custom-call(bf16[1408,1024]{1,0:T(8,128)(2,1)} %all-gather.3.cloned.1.call-done.refs_0_, ...), custom_call_target="tpu_custom_call" | custom-call | flops 4294967296 | bytes 8388608 | tf_op jit(solution)/shard_map/attend/pallas_call | solution.py:308
  142.0 3.7 %all-to-all-start.1 = ((bf16[4,256,256]{2,1,0:T(8,128)(2,1)}), bf16[4,256,256]{2,1,0:T(8,128)(2,1)S(1)}, u32[]{:S(2)}, u32[]{:S(2)}) async-start(bf16[4,256,256]{2,1,0:T(8,128)(2,1)} %bitcast.100), calls=%async_computation.1 | async-start | bytes 1048576 | tf_op jit(solution)/shard_map/all_to_all | solution.py:840
  145.8 1.5 collective-permute-start.16
  147.3 1.5 collective-permute-start.17
  148.8 7.8 %collective-permute-done.16.refs_17_ = bf16[352,512]{1,0:T(8,128)(2,1)S(1)} collective-permute-done((bf16[352,512]{1,0:T(8,128)(2,1)S(1)}, bf16[352,512]{1,0:T(8,128)(2,1)S(1)}, u32[]{:S(2)}, u32[]{:S(2)}) %collective-permute-start.16) | collective-permute-done | bytes 360480 | tf_op jit(solution)/shard_map/ppermute | solution.py:733
  156.6 1.4 collective-permute-done.17.refs_21_
  159.1 1.9 collective-permute-done.18.refs_1_
  161.8 29.7 %feed.1 = (bf16[512,1024]{1,0:T(8,128)(2,1)}, f32[256,1024]{1,0:T(8,128)}, f32[256,1024]{1,0:T(8,128)}, f32[256,1024]{1,0:T(8,128)}, bf16[1024,1024]{1,0:T(8,128...) custom-call(bf16[4,256,256]{2,1,0:T(8,128)(2,1)} %copy-done.5, ...), custom_call_target="tpu_custom_call" | custom-call | flops 16106127360 | bytes 8388608 | tf_op jit(solution)/shard_map/feed/pallas_call | solution.py:308
  191.7 2.7 collective-permute-done.20.part_hbm
  194.4 1.5 collective-permute-start.22
  195.9 1.5 collective-permute-start.21
  197.4 6.4 %branch.1 = (bf16[256,1024]{1,0:T(8,128)(2,1)}, f32[256,1024]{1,0:T(8,128)}, bf16[4,256,256]{2,1,0:T(8,128)(2,1)}, bf16[512,1024]{1,0:T(8,128)(2,1)}, bf16[512,1024]{1,0:T(8,128)(2,1)}) custom-call(bf16[512,1024]{1,0:T(8,128)(2,1)} %copy-done.11, f32[256,1024]{1,0:T(8,128)} %get-tuple-element.97.outown_hbm, f32[256,1024]{1,0:T(8,128)} %get-tuple-element.98.gnown_hbm, ...), custom_call_target="tpu_custom_call" | custom-call | flops 1073741824 | bytes 8388608 | tf_op jit(solution)/shard_map/branch/pallas_call | solution.py:308
  203.8 4.3 %all-to-all-start.2 = ((bf16[4,256,256]{2,1,0:T(8,128)(2,1)}), bf16[4,256,256]{2,1,0:T(8,128)(2,1)}, u32[]{:S(2)}, u32[]{:S(2)}) async-start(bf16[4,256,256]{2,1,0:T(8,128)(2,1)} %get-tuple-element.104), calls=%async_computation.2 | async-start | bytes 1048576 | tf_op jit(solution)/shard_map/all_to_all | solution.py:852
  208.3 4.5 %collective-permute-done.22 = bf16[704,512]{1,0:T(8,128)(2,1)S(1)} collective-permute-done((bf16[704,512]{1,0:T(8,128)(2,1)}, bf16[704,512]{1,0:T(8,128)(2,1)S(1)}, u32[]{:S(2)}, u32[]{:S(2)}) %collective-permute-start.22) | collective-permute-done | bytes 720928 | tf_op jit(solution)/shard_map/ppermute | solution.py:733
  213.7 1.3 add_convert_fusion.6
  215.2 1.5 collective-permute-start.23
  217.5 1.5 collective-permute-start.36
  220.8 1.8 all-to-all-done.2
  222.6 22.4 %attend_back.1 = (bf16[1024,768]{1,0:T(8,128)(2,1)}, bf16[1024,1024]{1,0:T(8,128)(2,1)}) custom-call(bf16[1024,768]{1,0:T(8,128)(2,1)} %get-tuple-element.103.mixed_hbm, bf16[1024,256]{1,0:T(8,128)(2,1)} %bitcast.24.ga_hbm, f32[8,1024]{1,0:T(8,128)} %get-tuple-element.105.total_hbm, f32[1024,128]{1,0:T(8,128)} %get-tuple-element.239.refs_2_.cos_hbm, ...), custom_call_target="tpu_custom_call" | custom-call | flops 7516192768 | bytes 8388608 | tf_op jit(solution)/shard_map/attend_back/pallas_call | solution.py:308
  246.3 3.8 %collective-permute-done.23 = bf16[512,1408]{1,0:T(8,128)(2,1)} collective-permute-done((bf16[512,1408]{1,0:T(8,128)(2,1)}, bf16[512,1408]{1,0:T(8,128)(2,1)}, u32[]{:S(2)}, u32[]{:S(2)}) %collective-permute-start.23) | collective-permute-done | bytes 1441824 | tf_op jit(solution)/shard_map/ppermute | solution.py:733
  250.1 1.7 add_convert_fusion.1
  251.9 1.5 collective-permute-start.28
  253.4 6.5 %collective-permute-done.24 = bf16[512,1408]{1,0:T(8,128)(2,1)} collective-permute-done((bf16[512,1408]{1,0:T(8,128)(2,1)}, bf16[512,1408]{1,0:T(8,128)(2,1)}, u32[]{:S(2)}, u32[]{:S(2)}) %collective-permute-start.24) | collective-permute-done | bytes 1441824 | tf_op jit(solution)/shard_map/ppermute | solution.py:733
  259.9 1.7 add_convert_fusion
  262.9 1.6 add_convert_fusion.2
  264.5 10.4 %collective-permute-done.28 = bf16[256,1408]{1,0:T(8,128)(2,1)S(1)} collective-permute-done((bf16[256,1408]{1,0:T(8,128)(2,1)S(1)}, bf16[256,1408]{1,0:T(8,128)(2,1)S(1)}, u32[]{:S(2)}, u32[]{:S(2)}) %collective-permute-start.28) | collective-permute-done | bytes 720928 | tf_op jit(solution)/shard_map/ppermute | solution.py:733
  275.1 4.0 %collective-permute-done.29 = bf16[256,1408]{1,0:T(8,128)(2,1)S(1)} collective-permute-done((bf16[256,1408]{1,0:T(8,128)(2,1)S(1)}, bf16[256,1408]{1,0:T(8,128)(2,1)S(1)}, u32[]{:S(2)}, u32[]{:S(2)}) %collective-permute-start.29) | collective-permute-done | bytes 720928 | tf_op jit(solution)/shard_map/ppermute | solution.py:733
  280.2 1.5 collective-permute-start.34
  283.0 5.4 %collective-permute-done.32 = bf16[256,512]{1,0:T(8,128)(2,1)S(1)} collective-permute-done((bf16[256,512]{1,0:T(8,128)(2,1)S(1)}, bf16[256,512]{1,0:T(8,128)(2,1)S(1)}, u32[]{:S(2)}, u32[]{:S(2)}) %collective-permute-start.32) | collective-permute-done | bytes 262176 | tf_op jit(solution)/shard_map/ppermute | solution.py:733
  288.8 1.5 collective-permute-start.33
  290.4 1.5 collective-permute-start.35
  292.2 1.6 collective-permute-done.33
  293.9 1.5 collective-permute-done.35
  295.5 1.4 copy-done.3
  296.9 5.9 %project_weights.1 = (bf16[512,768]{1,0:T(8,128)(2,1)}, bf16[512,768]{1,0:T(8,128)(2,1)}) custom-call(bf16[1024,768]{1,0:T(8,128)(2,1)} %get-tuple-element.116.gm_hbm, bf16[1024,1024]{1,0:T(8,128)(2,1)} %get-tuple-element.117.normed_hbm), custom_call_target="tpu_custom_call" | custom-call | flops 1073741824 | bytes 8388608 | tf_op jit(solution)/shard_map/project_weights/pallas_call | solution.py:308
  302.9 2.5 collective-permute-done.25
  305.4 1.4 add_convert_fusion.3
  306.8 1.5 collective-permute-start.26
  310.5 3.6 all-to-all-start.4
  314.0 4.2 %collective-permute-done.26 = bf16[256,768]{1,0:T(8,128)(2,1)S(1)} collective-permute-done((bf16[256,768]{1,0:T(8,128)(2,1)S(1)}, bf16[256,768]{1,0:T(8,128)(2,1)S(1)}, u32[]{:S(2)}, u32[]{:S(2)}) %collective-permute-start.26) | collective-permute-done | bytes 393248 | tf_op jit(solution)/shard_map/ppermute | solution.py:733
  319.0 5.4 %all-to-all-done.4 = f32[32,8,128]{2,1,0:T(8,128)S(1)} async-done(((f32[32,8,128]{2,1,0:T(8,128)}), f32[32,8,128]{2,1,0:T(8,128)S(1)}, u32[]{:S(2)}, u32[]{:S(2)}) %all-to-all-start.4) | async-done | bytes 131104 | tf_op jit(solution)/shard_map/all_to_all | solution.py:901
  326.1 3.6 all-to-all-start.3
  330.1 12.6 %all-to-all-done.3 = bf16[4,32,768]{2,1,0:T(8,128)(2,1)S(1)} async-done(((bf16[4,32,768]{2,1,0:T(8,128)(2,1)}), bf16[4,32,768]{2,1,0:T(8,128)(2,1)S(1)}, u32[]{:S(2)}, u32[]{:S(2)}) %all-to-all-start.3) | async-done | bytes 196640 | tf_op jit(solution)/shard_map/all_to_all | solution.py:912
  344.4 1.5 fusion.3
  345.9 1.5 fusion.5
  347.4 1.4 add_bitcast_fusion
  348.8 3.5 reduce-scatter.5.cloned.1.call-done
  (244 shorter events, 42.3 us)
Async XLA Ops:
  7.2 49.3 %all-gather.5.cloned.1.call-start = ((), (), s32[]{:S(2)}) async-start(), calls=%async_computation.8 | async-start | bytes 2129920 | tf_op jit(solution)/shard_map/all_gather | solution.py:802
  9.8 1.6 collective-permute-start
  12.2 104.6 %all-gather.3.cloned.1.call-start = ((), (), s32[]{:S(2)}) async-start(), calls=%async_computation.7 | async-start | bytes 3604480 | tf_op jit(solution)/shard_map/all_gather | solution.py:804
  12.4 8.1 %copy-start.21 = (bf16[1,256,1024]{2,1,0:T(8,128)(2,1)S(1)}, bf16[1,256,1024]{2,1,0:T(8,128)(2,1)}, u32[]{:S(2)}) copy-start(bf16[1,256,1024]{2,1,0:T(8,128)(2,1)} %param.21) | copy-start | bytes 1572868
  14.3 17.7 %all-to-all-start = ((bf16[4,32,768]{2,1,0:T(8,128)(2,1)}), bf16[4,32,768]{2,1,0:T(8,128)(2,1)S(1)}, u32[]{:S(2)}, u32[]{:S(2)}) async-start(bf16[4,32,768]{2,1,0:T(8,128)(2,1)} %pad_maximum_fusion.9), calls=%async_computation | async-start | bytes 393216 | tf_op jit(solution)/shard_map/all_to_all | solution.py:811
  20.5 37.6 %collective-permute-start.1 = (bf16[256,1024]{1,0:T(8,128)(2,1)S(1)}, bf16[256,1024]{1,0:T(8,128)(2,1)S(1)}, u32[]{:S(2)}, u32[]{:S(2)}) collective-permute-start(bf16[256,1024]{1,0:T(8,128)(2,1)S(1)} %bitcast.77), channel_id=1, source_target_pairs={{0,4},{4,0},{8,12},{12,8},{16,20},{20,16},{24,28},{28,24},{1,5},{5... | collective-permute-start | bytes 1572872 | tf_op jit(solution)/shard_map/ppermute | solution.py:733
  20.5 37.6 %collective-permute-start.2 = (bf16[256,1024]{1,0:T(8,128)(2,1)S(1)}, bf16[256,1024]{1,0:T(8,128)(2,1)S(1)}, u32[]{:S(2)}, u32[]{:S(2)}) collective-permute-start(bf16[256,1024]{1,0:T(8,128)(2,1)S(1)} %bitcast.99), channel_id=1, source_target_pairs={{0,4},{4,0},{8,12},{12,8},{16,20},{20,16},{24,28},{28,24},{1,5},{5... | collective-permute-start | bytes 1572872 | tf_op jit(solution)/shard_map/ppermute | solution.py:733
  32.0 5.7 %collective-permute-start.9 = (bf16[128,768]{1,0:T(8,128)(2,1)S(1)}, bf16[128,768]{1,0:T(8,128)(2,1)S(1)}, u32[]{:S(2)}, u32[]{:S(2)}) collective-permute-start(bf16[128,768]{1,0:T(8,128)(2,1)S(1)} %bitcast.82), channel_id=1, source_target_pairs={{0,8},{4,12},{8,0},{12,4},{16,24},{20,28},{24,16},{28,20},{1,9},{5... | collective-permute-start | bytes 589832 | tf_op jit(solution)/shard_map/ppermute | solution.py:733
  38.4 24.5 %collective-permute-start.10 = (bf16[256,768]{1,0:T(8,128)(2,1)}, bf16[256,768]{1,0:T(8,128)(2,1)S(1)}, u32[]{:S(2)}, u32[]{:S(2)}) collective-permute-start(bf16[256,768]{1,0:T(8,128)(2,1)} %pad_maximum_fusion.8), channel_id=1, source_target_pairs={{0,16},{4,20},{8,24},{12,28},{16,0},{20,4},{24,8},{28,12},{1,17},{... | collective-permute-start | bytes 1179656 | tf_op jit(solution)/shard_map/ppermute | solution.py:733
  59.8 8.5 %copy-start.14 = (bf16[256,1664]{1,0:T(8,128)(2,1)}, bf16[256,1664]{1,0:T(8,128)(2,1)S(1)}, u32[]{:S(2)}) copy-start(bf16[256,1664]{1,0:T(8,128)(2,1)S(1)} %get-tuple-element.79.refs_5_.refs_6_) | copy-start | bytes 2555908
  59.8 9.0 %copy-start.13 = (bf16[256,1664]{1,0:T(8,128)(2,1)}, bf16[256,1664]{1,0:T(8,128)(2,1)S(1)}, u32[]{:S(2)}) copy-start(bf16[256,1664]{1,0:T(8,128)(2,1)S(1)} %get-tuple-element.83.refs_9_.refs_10_) | copy-start | bytes 2555908
  59.8 22.0 %collective-permute-start.3 = (bf16[256,1664]{1,0:T(8,128)(2,1)S(1)}, bf16[256,1664]{1,0:T(8,128)(2,1)}, u32[]{:S(2)}, u32[]{:S(2)}) collective-permute-start(bf16[256,1664]{1,0:T(8,128)(2,1)S(1)} %get-tuple-element.79.refs_5_.refs_6_), channel_id=1, source_target_pairs={{0,8},{4,12},{8,0},{12,4},{16,24},{20,28},{24,16},{28,20},{1,9},{5... | collective-permute-start | bytes 2555912 | tf_op jit(solution)/shard_map/ppermute | solution.py:733
  61.4 22.0 %collective-permute-start.6 = (bf16[256,1664]{1,0:T(8,128)(2,1)S(1)}, bf16[256,1664]{1,0:T(8,128)(2,1)}, u32[]{:S(2)}, u32[]{:S(2)}) collective-permute-start(bf16[256,1664]{1,0:T(8,128)(2,1)S(1)} %get-tuple-element.83.refs_9_.refs_10_), channel_id=1, source_target_pairs={{0,16},{4,20},{8,24},{12,28},{16,0},{20,4},{24,8},{28,12},{1,17},{... | collective-permute-start | bytes 2555912 | tf_op jit(solution)/shard_map/ppermute | solution.py:733
  63.7 21.8 %collective-permute-start.11 = (bf16[512,768]{1,0:T(8,128)(2,1)S(1)}, bf16[512,768]{1,0:T(8,128)(2,1)S(1)}, u32[]{:S(2)}, u32[]{:S(2)}) collective-permute-start(bf16[512,768]{1,0:T(8,128)(2,1)S(1)} %pad_maximum_fusion), channel_id=1, source_target_pairs={{0,4},{4,0},{8,12},{12,8},{16,20},{20,16},{24,28},{28,24},{1,5},{5... | collective-permute-start | bytes 2359304 | tf_op jit(solution)/shard_map/ppermute | solution.py:733
  68.3 51.5 %collective-permute-start.4 = (bf16[256,1664]{1,0:T(8,128)(2,1)S(1)}, bf16[256,1664]{1,0:T(8,128)(2,1)}, u32[]{:S(2)}, u32[]{:S(2)}) collective-permute-start(bf16[256,1664]{1,0:T(8,128)(2,1)S(1)} %get-tuple-element.79.refs_5_.refs_6_), channel_id=1, source_target_pairs={{0,16},{4,20},{8,24},{12,28},{16,0},{20,4},{24,8},{28,12},{1,17},{... | collective-permute-start | bytes 2555912 | tf_op jit(solution)/shard_map/ppermute | solution.py:733
  68.8 52.5 %collective-permute-start.7 = (bf16[256,1664]{1,0:T(8,128)(2,1)S(1)}, bf16[256,1664]{1,0:T(8,128)(2,1)}, u32[]{:S(2)}, u32[]{:S(2)}) collective-permute-start(bf16[256,1664]{1,0:T(8,128)(2,1)S(1)} %get-tuple-element.83.refs_9_.refs_10_), channel_id=1, source_target_pairs={{0,8},{4,12},{8,0},{12,4},{16,24},{20,28},{24,16},{28,20},{1,9},{5... | collective-permute-start | bytes 2555912 | tf_op jit(solution)/shard_map/ppermute | solution.py:733
  81.8 40.0 %collective-permute-start.5 = (bf16[256,1664]{1,0:T(8,128)(2,1)}, bf16[256,1664]{1,0:T(8,128)(2,1)}, u32[]{:S(2)}, u32[]{:S(2)}) collective-permute-start(bf16[256,1664]{1,0:T(8,128)(2,1)} %collective-permute-done.3.refs_6_.refs_7_), channel_id=1, source_target_pairs={{0,16},{4,20},{8,24},{12,28},{16,0},{20,4},{24,8},{28,12},{1,17},{... | collective-permute-start | bytes 2555912 | tf_op jit(solution)/shard_map/ppermute | solution.py:733
  83.3 39.0 %collective-permute-start.8 = (bf16[256,1664]{1,0:T(8,128)(2,1)}, bf16[256,1664]{1,0:T(8,128)(2,1)}, u32[]{:S(2)}, u32[]{:S(2)}) collective-permute-start(bf16[256,1664]{1,0:T(8,128)(2,1)} %collective-permute-done.6.refs_10_.refs_11_), channel_id=1, source_target_pairs={{0,8},{4,12},{8,0},{12,4},{16,24},{20,28},{24,16},{28,20},{1,9},{5... | collective-permute-start | bytes 2555912 | tf_op jit(solution)/shard_map/ppermute | solution.py:733
  118.2 22.9 %copy-start.25 = (bf16[352,512]{1,0:T(8,128)(2,1)}, bf16[352,512]{1,0:T(8,128)(2,1)S(1)}, u32[]{:S(2)}) copy-start(bf16[352,512]{1,0:T(8,128)(2,1)S(1)} %get-tuple-element.164.refs_18_) | copy-start | bytes 1081348
  118.2 22.9 %copy-start.26 = (bf16[352,512]{1,0:T(8,128)(2,1)}, bf16[352,512]{1,0:T(8,128)(2,1)S(1)}, u32[]{:S(2)}) copy-start(bf16[352,512]{1,0:T(8,128)(2,1)S(1)} %get-tuple-element.165.refs_14_) | copy-start | bytes 1081348
  118.2 22.9 %collective-permute-start.12 = (bf16[352,512]{1,0:T(8,128)(2,1)S(1)}, bf16[352,512]{1,0:T(8,128)(2,1)S(1)}, u32[]{:S(2)}, u32[]{:S(2)}) collective-permute-start(bf16[352,512]{1,0:T(8,128)(2,1)S(1)} %get-tuple-element.165.refs_14_), channel_id=1, source_target_pairs={{0,8},{4,12},{8,0},{12,4},{16,24},{20,28},{24,16},{28,20},{1,9},{5... | collective-permute-start | bytes 1081352 | tf_op jit(solution)/shard_map/ppermute | solution.py:733
  119.8 21.4 %collective-permute-start.13 = (bf16[352,512]{1,0:T(8,128)(2,1)S(1)}, bf16[352,512]{1,0:T(8,128)(2,1)S(1)}, u32[]{:S(2)}, u32[]{:S(2)}) collective-permute-start(bf16[352,512]{1,0:T(8,128)(2,1)S(1)} %get-tuple-element.165.refs_14_), channel_id=1, source_target_pairs={{0,16},{4,20},{8,24},{12,28},{16,0},{20,4},{24,8},{28,12},{1,17},{... | collective-permute-start | bytes 1081352 | tf_op jit(solution)/shard_map/ppermute | solution.py:733
  121.2 19.9 %collective-permute-start.14 = (bf16[352,512]{1,0:T(8,128)(2,1)S(1)}, bf16[352,512]{1,0:T(8,128)(2,1)S(1)}, u32[]{:S(2)}, u32[]{:S(2)}) collective-permute-start(bf16[352,512]{1,0:T(8,128)(2,1)S(1)} %get-tuple-element.164.refs_18_), channel_id=1, source_target_pairs={{0,16},{4,20},{8,24},{12,28},{16,0},{20,4},{24,8},{28,12},{1,17},{... | collective-permute-start | bytes 1081352 | tf_op jit(solution)/shard_map/ppermute | solution.py:733
  121.8 19.4 %collective-permute-start.15 = (bf16[352,512]{1,0:T(8,128)(2,1)S(1)}, bf16[352,512]{1,0:T(8,128)(2,1)S(1)}, u32[]{:S(2)}, u32[]{:S(2)}) collective-permute-start(bf16[352,512]{1,0:T(8,128)(2,1)S(1)} %get-tuple-element.164.refs_18_), channel_id=1, source_target_pairs={{0,8},{4,12},{8,0},{12,4},{16,24},{20,28},{24,16},{28,20},{1,9},{5... | collective-permute-start | bytes 1081352 | tf_op jit(solution)/shard_map/ppermute | solution.py:733
  141.1 19.8 %copy-start.45 = (bf16[352,512]{1,0:T(8,128)(2,1)}, bf16[352,512]{1,0:T(8,128)(2,1)S(1)}, u32[]{:S(2)}) copy-start(bf16[352,512]{1,0:T(8,128)(2,1)S(1)} %collective-permute-done.12.refs_15_) | copy-start | bytes 1081348
  141.1 4.5 %copy-start.47 = (bf16[352,512]{1,0:T(8,128)(2,1)}, bf16[352,512]{1,0:T(8,128)(2,1)S(1)}, u32[]{:S(2)}) copy-start(bf16[352,512]{1,0:T(8,128)(2,1)S(1)} %collective-permute-done.14.refs_19_) | copy-start | bytes 1081348
  142.0 17.1 %all-to-all-start.1 = ((bf16[4,256,256]{2,1,0:T(8,128)(2,1)}), bf16[4,256,256]{2,1,0:T(8,128)(2,1)S(1)}, u32[]{:S(2)}, u32[]{:S(2)}) async-start(bf16[4,256,256]{2,1,0:T(8,128)(2,1)} %bitcast.100), calls=%async_computation.1 | async-start | bytes 1048576 | tf_op jit(solution)/shard_map/all_to_all | solution.py:840
  145.7 13.4 %collective-permute-start.19 = (bf16[8,256,256]{2,1,0:T(8,128)(2,1)}, bf16[8,256,256]{2,1,0:T(8,128)(2,1)S(1)}, u32[]{:S(2)}, u32[]{:S(2)}) collective-permute-start(bf16[8,256,256]{2,1,0:T(8,128)(2,1)} %get-tuple-element.92), channel_id=1, source_target_pairs={{0,4},{4,0},{8,12},{12,8},{16,20},{20,16},{24,28},{28,24},{1,5},{5... | collective-permute-start | bytes 3145736 | tf_op jit(solution)/shard_map/ppermute | solution.py:733
  145.8 10.8 %collective-permute-start.16 = (bf16[352,512]{1,0:T(8,128)(2,1)S(1)}, bf16[352,512]{1,0:T(8,128)(2,1)S(1)}, u32[]{:S(2)}, u32[]{:S(2)}) collective-permute-start(bf16[352,512]{1,0:T(8,128)(2,1)S(1)} %collective-permute-done.12.refs_15_), channel_id=1, source_target_pairs={{0,16},{4,20},{8,24},{12,28},{16,0},{20,4},{24,8},{28,12},{1,17},{... | collective-permute-start | bytes 1081352 | tf_op jit(solution)/shard_map/ppermute | solution.py:733
  147.3 10.7 %collective-permute-start.17 = (bf16[352,512]{1,0:T(8,128)(2,1)}, bf16[352,512]{1,0:T(8,128)(2,1)S(1)}, u32[]{:S(2)}, u32[]{:S(2)}) collective-permute-start(bf16[352,512]{1,0:T(8,128)(2,1)} %copy-done.47), channel_id=1, source_target_pairs={{0,8},{4,12},{8,0},{12,4},{16,24},{20,28},{24,16},{28,20},{1,9},{5... | collective-permute-start | bytes 1081352 | tf_op jit(solution)/shard_map/ppermute | solution.py:733
  159.1 1.9 collective-permute-start.18
  191.5 2.9 collective-permute-start.20
  194.4 18.4 %collective-permute-start.22 = (bf16[704,512]{1,0:T(8,128)(2,1)}, bf16[704,512]{1,0:T(8,128)(2,1)S(1)}, u32[]{:S(2)}, u32[]{:S(2)}) collective-permute-start(bf16[704,512]{1,0:T(8,128)(2,1)} %get-tuple-element.113), channel_id=1, source_target_pairs={{0,16},{4,20},{8,24},{12,28},{16,0},{20,4},{24,8},{28,12},{1,17},{... | collective-permute-start | bytes 2162696 | tf_op jit(solution)/shard_map/ppermute | solution.py:733
  195.9 19.1 %collective-permute-start.21 = (bf16[704,512]{1,0:T(8,128)(2,1)}, bf16[704,512]{1,0:T(8,128)(2,1)S(1)}, u32[]{:S(2)}, u32[]{:S(2)}) collective-permute-start(bf16[704,512]{1,0:T(8,128)(2,1)} %get-tuple-element.111), channel_id=1, source_target_pairs={{0,8},{4,12},{8,0},{12,4},{16,24},{20,28},{24,16},{28,20},{1,9},{5... | collective-permute-start | bytes 2162696 | tf_op jit(solution)/shard_map/ppermute | solution.py:733
  197.4 16.3 %copy-start.19 = (bf16[704,512]{1,0:T(8,128)(2,1)S(1)}, bf16[704,512]{1,0:T(8,128)(2,1)}, u32[]{:S(2)}) copy-start(bf16[704,512]{1,0:T(8,128)(2,1)} %get-tuple-element.112) | copy-start | bytes 2162692
  203.8 11.2 %copy-start.18 = (bf16[704,512]{1,0:T(8,128)(2,1)S(1)}, bf16[704,512]{1,0:T(8,128)(2,1)}, u32[]{:S(2)}) copy-start(bf16[704,512]{1,0:T(8,128)(2,1)} %get-tuple-element.110) | copy-start | bytes 2162692
  203.8 18.9 %all-to-all-start.2 = ((bf16[4,256,256]{2,1,0:T(8,128)(2,1)}), bf16[4,256,256]{2,1,0:T(8,128)(2,1)}, u32[]{:S(2)}, u32[]{:S(2)}) async-start(bf16[4,256,256]{2,1,0:T(8,128)(2,1)} %get-tuple-element.104), calls=%async_computation.2 | async-start | bytes 1048576 | tf_op jit(solution)/shard_map/all_to_all | solution.py:852
  208.1 136.3 %reduce-scatter.3.cloned.1.call-start = ((), (), s32[]{:S(2)}) async-start(), calls=%async_computation.9 | async-start | bytes 2621440 | tf_op jit(solution)/shard_map/reduce_scatter | solution.py:905
  215.2 34.9 %collective-permute-start.23 = (bf16[512,1408]{1,0:T(8,128)(2,1)}, bf16[512,1408]{1,0:T(8,128)(2,1)}, u32[]{:S(2)}, u32[]{:S(2)}) collective-permute-start(bf16[512,1408]{1,0:T(8,128)(2,1)} %get-tuple-element.114), channel_id=1, source_target_pairs={{0,8},{4,12},{8,0},{12,4},{16,24},{20,28},{24,16},{28,20},{1,9},{5... | collective-permute-start | bytes 4325384 | tf_op jit(solution)/shard_map/ppermute | solution.py:733
  216.7 45.6 %collective-permute-start.31 = (bf16[512,1024]{1,0:T(8,128)(2,1)}, bf16[512,1024]{1,0:T(8,128)(2,1)}, u32[]{:S(2)}, u32[]{:S(2)}) collective-permute-start(bf16[512,1024]{1,0:T(8,128)(2,1)} %get-tuple-element.124), channel_id=1, source_target_pairs={{0,4},{4,0},{8,12},{12,8},{16,20},{20,16},{24,28},{28,24},{1,5},{5... | collective-permute-start | bytes 3145736 | tf_op jit(solution)/shard_map/ppermute | solution.py:733
  217.5 27.7 %collective-permute-start.36 = (bf16[352,512]{1,0:T(8,128)(2,1)}, bf16[352,512]{1,0:T(8,128)(2,1)}, u32[]{:S(2)}, u32[]{:S(2)}) collective-permute-start(bf16[352,512]{1,0:T(8,128)(2,1)} %slice.365), channel_id=1, source_target_pairs={{0,16},{4,20},{8,24},{12,28},{16,0},{20,4},{24,8},{28,12},{1,17},{... | collective-permute-start | bytes 1081352 | tf_op jit(solution)/shard_map/ppermute | solution.py:733
  219.7 62.0 %collective-permute-start.37 = (bf16[352,512]{1,0:T(8,128)(2,1)}, bf16[352,512]{1,0:T(8,128)(2,1)S(1)}, u32[]{:S(2)}, u32[]{:S(2)}) collective-permute-start(bf16[352,512]{1,0:T(8,128)(2,1)} %slice.367), channel_id=1, source_target_pairs={{0,8},{4,12},{8,0},{12,4},{16,24},{20,28},{24,16},{28,20},{1,9},{5... | collective-permute-start | bytes 1081352 | tf_op jit(solution)/shard_map/ppermute | solution.py:733
  220.3 39.6 %collective-permute-start.24 = (bf16[512,1408]{1,0:T(8,128)(2,1)}, bf16[512,1408]{1,0:T(8,128)(2,1)}, u32[]{:S(2)}, u32[]{:S(2)}) collective-permute-start(bf16[512,1408]{1,0:T(8,128)(2,1)} %get-tuple-element.115), channel_id=1, source_target_pairs={{0,16},{4,20},{8,24},{12,28},{16,0},{20,4},{24,8},{28,12},{1,17},{... | collective-permute-start | bytes 4325384 | tf_op jit(solution)/shard_map/ppermute | solution.py:733
  245.0 5.1 %copy-start.7 = (bf16[512,1408]{1,0:T(8,128)(2,1)S(1)}, bf16[512,1408]{1,0:T(8,128)(2,1)}, u32[]{:S(2)}) copy-start(bf16[512,1408]{1,0:T(8,128)(2,1)} %get-tuple-element.120) | copy-start | bytes 4325380
  245.1 107.1 %reduce-scatter.5.cloned.1.call-start = ((), (), s32[]{:S(2)}) async-start(), calls=%async_computation.10 | async-start | bytes 3112960 | tf_op jit(solution)/shard_map/reduce_scatter | solution.py:895
  251.8 8.1 %copy-start.6 = (bf16[512,1408]{1,0:T(8,128)(2,1)S(1)}, bf16[512,1408]{1,0:T(8,128)(2,1)}, u32[]{:S(2)}) copy-start(bf16[512,1408]{1,0:T(8,128)(2,1)} %get-tuple-element.121) | copy-start | bytes 4325380
  251.9 23.0 %collective-permute-start.28 = (bf16[256,1408]{1,0:T(8,128)(2,1)S(1)}, bf16[256,1408]{1,0:T(8,128)(2,1)S(1)}, u32[]{:S(2)}, u32[]{:S(2)}) collective-permute-start(bf16[256,1408]{1,0:T(8,128)(2,1)S(1)} %slice.413), channel_id=1, source_target_pairs={{0,16},{4,20},{8,24},{12,28},{16,0},{20,4},{24,8},{28,12},{1,17},{... | collective-permute-start | bytes 2162696 | tf_op jit(solution)/shard_map/ppermute | solution.py:733
  261.7 17.4 %collective-permute-start.29 = (bf16[256,1408]{1,0:T(8,128)(2,1)S(1)}, bf16[256,1408]{1,0:T(8,128)(2,1)S(1)}, u32[]{:S(2)}, u32[]{:S(2)}) collective-permute-start(bf16[256,1408]{1,0:T(8,128)(2,1)S(1)} %slice.415), channel_id=1, source_target_pairs={{0,8},{4,12},{8,0},{12,4},{16,24},{20,28},{24,16},{28,20},{1,9},{5... | collective-permute-start | bytes 2162696 | tf_op jit(solution)/shard_map/ppermute | solution.py:733
  279.5 12.4 %collective-permute-start.30 = (bf16[128,2816]{1,0:T(8,128)(2,1)S(1)}, bf16[128,2816]{1,0:T(8,128)(2,1)S(1)}, u32[]{:S(2)}, u32[]{:S(2)}) collective-permute-start(bf16[128,2816]{1,0:T(8,128)(2,1)S(1)} %pad_maximum_fusion.2), channel_id=1, source_target_pairs={{0,4},{4,0},{8,12},{12,8},{16,20},{20,16},{24,28},{28,24},{1,5},{5... | collective-permute-start | bytes 2162696 | tf_op jit(solution)/shard_map/ppermute | solution.py:733
  279.6 8.8 %collective-permute-start.32 = (bf16[256,512]{1,0:T(8,128)(2,1)S(1)}, bf16[256,512]{1,0:T(8,128)(2,1)S(1)}, u32[]{:S(2)}, u32[]{:S(2)}) collective-permute-start(bf16[256,512]{1,0:T(8,128)(2,1)S(1)} %get-tuple-element.159), channel_id=1, source_target_pairs={{0,8},{4,12},{8,0},{12,4},{16,24},{20,28},{24,16},{28,20},{1,9},{5... | collective-permute-start | bytes 786440 | tf_op jit(solution)/shard_map/ppermute | solution.py:733
  280.2 8.4 %collective-permute-start.34 = (bf16[256,512]{1,0:T(8,128)(2,1)S(1)}, bf16[256,512]{1,0:T(8,128)(2,1)S(1)}, u32[]{:S(2)}, u32[]{:S(2)}) collective-permute-start(bf16[256,512]{1,0:T(8,128)(2,1)S(1)} %get-tuple-element.158), channel_id=1, source_target_pairs={{0,16},{4,20},{8,24},{12,28},{16,0},{20,4},{24,8},{28,12},{1,17},{... | collective-permute-start | bytes 786440 | tf_op jit(solution)/shard_map/ppermute | solution.py:733
  288.8 5.0 %collective-permute-start.33 = (bf16[128,512]{1,0:T(8,128)(2,1)S(1)}, bf16[128,512]{1,0:T(8,128)(2,1)S(1)}, u32[]{:S(2)}, u32[]{:S(2)}) collective-permute-start(bf16[128,512]{1,0:T(8,128)(2,1)S(1)} %slice.419), channel_id=1, source_target_pairs={{0,16},{4,20},{8,24},{12,28},{16,0},{20,4},{24,8},{28,12},{1,17},{... | collective-permute-start | bytes 393224 | tf_op jit(solution)/shard_map/ppermute | solution.py:733
  290.4 5.0 %collective-permute-start.35 = (bf16[128,512]{1,0:T(8,128)(2,1)S(1)}, bf16[128,512]{1,0:T(8,128)(2,1)S(1)}, u32[]{:S(2)}, u32[]{:S(2)}) collective-permute-start(bf16[128,512]{1,0:T(8,128)(2,1)S(1)} %slice.423), channel_id=1, source_target_pairs={{0,8},{4,12},{8,0},{12,4},{16,24},{20,28},{24,16},{28,20},{1,9},{5... | collective-permute-start | bytes 393224 | tf_op jit(solution)/shard_map/ppermute | solution.py:733
  302.8 2.6 collective-permute-start.25
  306.8 11.4 %collective-permute-start.26 = (bf16[256,768]{1,0:T(8,128)(2,1)S(1)}, bf16[256,768]{1,0:T(8,128)(2,1)S(1)}, u32[]{:S(2)}, u32[]{:S(2)}) collective-permute-start(bf16[256,768]{1,0:T(8,128)(2,1)S(1)} %slice.397), channel_id=1, source_target_pairs={{0,8},{4,12},{8,0},{12,4},{16,24},{20,28},{24,16},{28,20},{1,9},{5... | collective-permute-start | bytes 1179656 | tf_op jit(solution)/shard_map/ppermute | solution.py:733
  310.5 13.9 %all-to-all-start.4 = ((f32[32,8,128]{2,1,0:T(8,128)}), f32[32,8,128]{2,1,0:T(8,128)S(1)}, u32[]{:S(2)}, u32[]{:S(2)}) async-start(f32[32,8,128]{2,1,0:T(8,128)} %broadcast_in_dim.39), calls=%async_computation.6 | async-start | bytes 262144 | tf_op jit(solution)/shard_map/all_to_all | solution.py:901
  318.3 24.4 %copy-start.35 = (f32[32,1024]{1,0:T(8,128)S(1)}, f32[32,1024]{1,0:T(8,128)}, u32[]{:S(2)}) copy-start(f32[32,1024]{1,0:T(8,128)} %param.31) | copy-start | bytes 393220
  318.4 7.0 %collective-permute-start.27 = (bf16[128,768]{1,0:T(8,128)(2,1)S(1)}, bf16[128,768]{1,0:T(8,128)(2,1)S(1)}, u32[]{:S(2)}, u32[]{:S(2)}) collective-permute-start(bf16[128,768]{1,0:T(8,128)(2,1)S(1)} %slice.399), channel_id=1, source_target_pairs={{0,16},{4,20},{8,24},{12,28},{16,0},{20,4},{24,8},{28,12},{1,17},{... | collective-permute-start | bytes 589832 | tf_op jit(solution)/shard_map/ppermute | solution.py:733
  324.4 19.1 %copy-start.30 = (bf16[32,1024]{1,0:T(8,128)(2,1)S(1)}, bf16[32,1024]{1,0:T(8,128)(2,1)}, u32[]{:S(2)}) copy-start(bf16[32,1024]{1,0:T(8,128)(2,1)} %param.22) | copy-start | bytes 196612
  324.4 19.1 %copy-start.33 = (f32[32,1024]{1,0:T(8,128)S(1)}, f32[32,1024]{1,0:T(8,128)}, u32[]{:S(2)}) copy-start(f32[32,1024]{1,0:T(8,128)} %param.30) | copy-start | bytes 393220
  324.4 19.1 %copy-start.34 = (f32[32,1024]{1,0:T(8,128)S(1)}, f32[32,1024]{1,0:T(8,128)}, u32[]{:S(2)}) copy-start(f32[32,1024]{1,0:T(8,128)} %param.29) | copy-start | bytes 393220
  326.1 16.6 %all-to-all-start.3 = ((bf16[4,32,768]{2,1,0:T(8,128)(2,1)}), bf16[4,32,768]{2,1,0:T(8,128)(2,1)S(1)}, u32[]{:S(2)}, u32[]{:S(2)}) async-start(bf16[4,32,768]{2,1,0:T(8,128)(2,1)} %bitcast.26), calls=%async_computation.4 | async-start | bytes 393216 | tf_op jit(solution)/shard_map/all_to_all | solution.py:912
  329.9 14.4 %copy-start.39 = (f32[16]{0:T(128)}, f32[16]{0:T(128)S(1)}, u32[]{:S(2)}) copy-start(f32[16]{0:T(128)S(1)} %reshape_squeeze.3) | copy-start | bytes 196
  329.9 14.4 %copy-start.40 = (f32[16]{0:T(128)}, f32[16]{0:T(128)S(1)}, u32[]{:S(2)}) copy-start(f32[16]{0:T(128)S(1)} %divide_sqrt_fusion) | copy-start | bytes 196
  (34 other events, 72.3 us)
Sparse Core Ops, SparseCore 0:
  12.4 44.0 all-gather.4
  58.6 58.1 all-gather.2
  245.2 41.9 reduce-scatter.2
  297.1 55.0 reduce-scatter.4

commit v5 on v4

--- a/solution.py
+++ b/solution.py
@@ -522,31 +522,38 @@
         [((n, 768), bf), ((n, 256), bf), ((8, n), f32), ((n, 128), f32), ((n, 128), f32),
          ((8, n), f32), ((1024, 768), bf), ((n, 768), bf), ((n, 1024), bf), ((n, 256), f32),
          ((n, 256), f32), ((256, n), bf), ((n, 128), f32)],
-        [19], 7, (mixed, ga, total, cosine, sine, ids, weight), 32,
-    )
-
-
-def weights_kernel(gm_hbm, normed_hbm, keep_hbm, send_hbm, gm_ref, normed_ref, gw, sems):
+        [19], 0, (mixed, ga, total, cosine, sine, ids, weight), 32,
+    )
+
+
+def weights_kernel(gm_hbm, normed_hbm, okeep_hbm, osend_hbm, keep_hbm, send_hbm,
+                   gm_ref, normed_ref, gw, okeep, osend, sems):
     go = Copies(sems)
-    wait_all([go.start(gm_hbm, gm_ref), go.start(normed_hbm, normed_ref)])
+    first = [go.start(gm_hbm, gm_ref), go.start(normed_hbm, normed_ref)]
+    second = [go.start(okeep_hbm, okeep), go.start(osend_hbm, osend)]
+    wait_all(first + second)
+    cols = pl.ds(768, 1024)
+    late = [go.start(okeep, keep_hbm.at[:, cols]), go.start(osend, send_hbm.at[:, cols])]
 
     @pl.loop(0, 4)
     def _(i):
         cols = aligned(i, 256)
         gw[cols, :] = dot(normed_ref[:, cols], gm_ref[...], TN).astype(bf)
 
-    wait_all([
+    late += [
         go.start(gw.at[aligned(place_of(p), 128)],
-                 (keep_hbm if p < 4 else send_hbm).at[pl.ds(128 * (p % 4), 128)])
+                 (keep_hbm if p < 4 else send_hbm).at[pl.ds(128 * (p % 4), 128), pl.ds(0, 768)])
         for p in range(8)
-    ])
-
-
-def project_weights(gm, normed):
+    ]
+    wait_all(late)
+
+
+def project_weights(gm, normed, okeep, osend):
     n = gm.shape[0]
     return call(
-        weights_kernel, "project_weights", [((512, 768), bf)] * 2,
-        [((n, 768), bf), ((n, 1024), bf), ((1024, 768), bf)], [10], 1, (gm, normed), 24,
+        weights_kernel, "project_weights", [((512, 1792), bf)] * 2,
+        [((n, 768), bf), ((n, 1024), bf), ((1024, 768), bf), ((512, 1024), bf), ((512, 1024), bf)],
+        [14], 1, (gm, normed, okeep, osend), 24,
     )
 
 
@@ -712,8 +719,7 @@
         j = yx ^ (fx + 2 * fy)
         for dst, c in ((keep_hbm, core), (send_hbm, 1 - core)):
             rows = aligned(j * 2 + c, 128)
-            done.append(go.start(gw.at[rows, pl.ds(0, 512)], dst.at[pl.ds(128 * (2 * fx + fy), 128), pl.ds(0, 512)]))
-            done.append(go.start(gw.at[rows, pl.ds(512, 512)], dst.at[pl.ds(128 * (2 * fy + fx), 128), pl.ds(512, 512)]))
+            done.append(go.start(gw.at[rows], dst.at[pl.ds(128 * (2 * fx + fy), 128)]))
     wait_all(done)
 
 
@@ -725,7 +731,7 @@
         [low, tall, ((4, 256, 256), bf), ((512, 1024), bf), ((512, 1024), bf)],
         [((512, 1024), bf), tall, tall, tall, low, low, ((1024, 1024), bf), low, tall, ((4, 256, 256), bf),
          ((1024, 1024), bf)],
-        [29], 1, (part, outown, gnown, res, cot, att, wo), 32,
+        [21], 1, (part, outown, gnown, res, cot, att, wo), 32,
     )
 
 
@@ -845,33 +851,33 @@
     )
     ga_keep, ga_send, gb_keep, gb_send, gda_keep, gda_send, gdb_keep, gdb_send = grads
     part = swap(part, 1)
-    gda_send, gdb_send, part = lax.optimization_barrier((gda_send, gdb_send, part))
+    ga_send, gb_send, gda_send, gdb_send, part = lax.optimization_barrier(
+        (ga_send, gb_send, gda_send, gdb_send, part)
+    )
+    gda_other = swap(gda_send, 2)
+    gdb_other = swap(gdb_send, 4)
+    ga_other = swap(ga_send, 2)
+    gb_other = swap(gb_send, 4)
     layer_out, grad_residual, grad_attended, go_keep, go_send = branch(
         part, out_own, back_own, residual, cot, attended, full_out
     )
     grad_attended = lax.all_to_all(grad_attended, "ctx", 0, 0, tiled=True).reshape(length, 256)
-    gda_other = swap(gda_send, 2)
-    gdb_other = swap(gdb_send, 4)
+    grad_mixed, grad_normed = attend_back(
+        mixed, grad_attended, totals, cosine, sine, ids, heads_rel
+    )
+    grad_mixed = tie(grad_mixed, ga_other, gb_other, gda_other, gdb_other)
+    grad_heads = project_weights(grad_mixed, normed, go_keep, go_send)
+    ga_keep, gb_keep, gda_keep, gdb_keep, grad_heads = lax.optimization_barrier(
+        (ga_keep, gb_keep, gda_keep, gdb_keep, grad_heads)
+    )
     grad_da = add_low(gda_keep, gda_other)
     grad_db = add_low(gdb_keep, gdb_other)
-    ga_send, gb_send, grad_da, grad_db = lax.optimization_barrier(
-        (ga_send, gb_send, grad_da, grad_db)
-    )
-    ga_other = swap(ga_send, 2)
-    gb_other = swap(gb_send, 4)
     grad_a = add_low(ga_keep, ga_other)
     grad_b = add_low(gb_keep, gb_other)
     grad_a = add_low(grad_a[:256], swap(grad_a[256:], 4))
     grad_b = add_low(grad_b[:256], swap(grad_b[256:], 2))
     grad_da = add_low(grad_da[:352], swap(grad_da[352:], 4))
     grad_db = add_low(grad_db[:352], swap(grad_db[352:], 2))
-    go_keep, ga_later = lax.optimization_barrier((go_keep, ga_other))
-    grad_out = add_low(go_keep, swap(go_send, 1))
-    grad_oa = add_low(grad_out[:256, :512], swap(grad_out[256:, :512], 2))
-    grad_ob = add_low(grad_out[:256, 512:], swap(grad_out[256:, 512:], 4))
-    grad_oa = add_low(grad_oa[:128], swap(grad_oa[128:], 4))
-    grad_ob = add_low(grad_ob[:128], swap(grad_ob[128:], 2))
-
     def core_rows(which):
         return jnp.concatenate(
             [lax.dynamic_slice_in_dim(g, which * 128, 128, 0) for g in (grad_a, grad_b)], axis=1
@@ -886,17 +892,11 @@
         [
             jnp.where(flip, other_half, own_half),
             jnp.where(flip, own_half, other_half),
-            grad_oa,
-            grad_ob,
             grad_d,
         ],
         axis=1,
     )
     grad_wide = lax.psum_scatter(grad_wide, "ctx", scatter_dimension=0, tiled=True).astype(f32)
-    grad_mixed, grad_normed = attend_back(
-        mixed, grad_attended, totals, cosine, sine, ids, heads_rel
-    )
-    grad_heads = project_weights(tie(grad_mixed, ga_other, gb_other), normed)
     peaks = tie(peaks, ga_other)
     peaks = lax.all_to_all(
         jnp.broadcast_to(peaks[None], (32, 8, 128)), ("dp", "ctx"), 0, 0, tiled=True
@@ -909,17 +909,19 @@
     grad_heads = add_low(grad_heads[0], swap(grad_heads[1], 1))
     grad_heads = add_low(grad_heads[:256], swap(grad_heads[256:], 2))
     grad_heads = add_low(grad_heads[:128], swap(grad_heads[128:], 4))
-    grad_heads = lax.all_to_all(grad_heads.reshape(4, 32, 768), "ctx", 0, 0, tiled=True)
+    grad_heads = lax.all_to_all(grad_heads.reshape(4, 32, 768 + width), "ctx", 0, 0, tiled=True)
     grad_heads = grad_heads.astype(f32)
+    parts = grad_heads[:, :, 768:]
+    grad_out = parts[0] + parts[1] + (parts[2] + parts[3])
     grad_qkv = [
         jnp.concatenate([grad_heads[i, :, 256 * k : 256 * k + 256] for i in range(4)], axis=1)
         for k in range(3)
     ]
-    grad_d_sum = grad_wide[:, 4 * FF2 + width :].reshape(32, 3, width).transpose(1, 0, 2)
+    grad_d_sum = grad_wide[:, 4 * FF2 :].reshape(32, 3, width).transpose(1, 0, 2)
     grad_d_sum = grad_d_sum.reshape(96, width)[:88]
     weight_grads = (
         *grad_qkv,
-        grad_wide[:, 4 * FF2 : 4 * FF2 + width],
+        grad_out,
         join_even(grad_wide[:, :FF2], grad_wide[:, 2 * FF2 : 3 * FF2]),
         join_even(grad_wide[:, FF2 : 2 * FF2], grad_wide[:, 3 * FF2 : 4 * FF2]),
         grad_d_sum,

time: 366 us -> 357 us (0.975)
  local copies, waits for them, and re-layouts: 23.4 us -> 16.3 us
  waiting for transfers between devices: 158 us -> 164 us
  starting transfers between devices: 57 us -> 51.2 us
    all_to_all x1, waiting for transfers between devices: 1.8 us -> 13 us  [fast_device(): lax.all_to_all(grad_attended, 'ctx', 0, 0, tiled=True).reshape(length, 256)]
    all_to_all x1, waiting for transfers between devices: 12.6 us -> 18.5 us  [fast_device(): lax.all_to_all(grad_heads.reshape(4, 32, 768 + width), 'ctx', 0, 0, tiled...]
    ppermute x38 -> x33, starting transfers between devices: 35.3 us -> 29.8 us  [swap(): return lax.ppermute(array, 'dp', [(i, i ^ bit) for i in range(8)])]
    all_to_all x1, waiting for transfers between devices: 5.41 us -> 0.01 us  [fast_device(): lax.all_to_all(jnp.broadcast_to(peaks[None], (32, 8, 128)), ('dp', 'ctx')...]
    unnamed x106 -> x100, local copies, waits for them, and re-layouts: 9.79 us -> 4.57 us
    ppermute x38 -> x33, waiting for transfers between devices: 76.3 us -> 71.5 us  [swap(): return lax.ppermute(array, 'dp', [(i, i ^ bit) for i in range(8)])]
    convert_element_type x13 -> x11, other arithmetic: 10.5 us -> 6.66 us  [add_low(): return (left.astype(f32) + right.astype(f32)).astype(bf)]
  transfers between devices with their start and end apart: 47 -> 42, of which waited for: 27 -> 20; matrix products, arithmetic and copies ran while one was open for 10% -> 8% of each run, Pallas kernels for 14% -> 15%
where the time goes in v5:
time: 357 us
  waiting for transfers between devices  164 us (46%)
  Pallas kernels  83.2 us (23%)
  starting transfers between devices  51.2 us (14%)
  other arithmetic  25.7 us (7%)
  local copies, waits for them, and re-layouts  16.3 us (5%)
  between operations  16.2 us (5%)
    pallas_call x5, Pallas kernels, call(): pl.pallas_call(kernel, out_shape=tuple((pltpu.HBM(*o) for o in outs)), in...  83.2 us
    ppermute x33, waiting for transfers between devices, swap(): return lax.ppermute(array, 'dp', [(i, i ^ bit) for i in range(8)])  71.5 us
    all_gather x1, waiting for transfers between devices, fast_device(): rows_all = lax.all_gather(padded, 'ctx', axis=0, tiled=True)  32.2 us
    ppermute x33, starting transfers between devices, swap(): return lax.ppermute(array, 'dp', [(i, i ^ bit) for i in range(8)])  29.8 us
    all_to_all x1, waiting for transfers between devices, fast_device(): lax.all_to_all(grad_heads.reshape(4, 32, 768 + width), 'ctx', 0, 0, tiled...  18.5 us
    all_gather x1, waiting for transfers between devices, fast_device(): lax.all_gather(wide, 'ctx', axis=2, tiled=True).reshape(2, 256, FF2 + 256)  16.5 us
    all_to_all x1, waiting for transfers between devices, fast_device(): lax.all_to_all(grad_attended, 'ctx', 0, 0, tiled=True).reshape(length, 256)  13 us
    all_to_all x1, waiting for transfers between devices, fast_device(): heads = lax.all_to_all(heads, 'ctx', 0, 0, tiled=True).reshape(128, 768)  11 us
  transfers between devices with their start and end apart: 42, of which 20 were waited for; matrix products, arithmetic and copies ran while one was open for 8% of the time, Pallas kernels for 15%

profile of v5, /device:TPU:0, one launch (start us, length us, event | category | flops | bytes accessed | tf_op | source)
XLA Modules:
  0.0 356.5 jit_solution(11081093979080176415)
XLA Ops:
  7.3 1.0 fusion.15
  8.3 1.0 fusion.16
  12.4 1.0 maximum_maximum_fusion
  14.3 6.2 %all-to-all-start = ((bf16[4,32,768]{2,1,0:T(8,128)(2,1)}), bf16[4,32,768]{2,1,0:T(8,128)(2,1)S(1)}, u32[]{:S(2)}, u32[]{:S(2)}) async-start(bf16[4,32,768]{2,1,0:T(8,128)(2,1)} %pad_maximum_fusion.10), calls=%async_computation | async-start | bytes 393216 | tf_op jit(solution)/shard_map/all_to_all | solution.py:817
  21.0 11.0 %all-to-all-done = bf16[4,32,768]{2,1,0:T(8,128)(2,1)S(1)} async-done(((bf16[4,32,768]{2,1,0:T(8,128)(2,1)}), bf16[4,32,768]{2,1,0:T(8,128)(2,1)S(1)}, u32[]{:S(2)}, u32[]{:S(2)}) %all-to-all-start) | async-done | bytes 196640 | tf_op jit(solution)/shard_map/all_to_all | solution.py:817
  32.0 1.5 collective-permute-start.9
  33.5 4.1 %collective-permute-done.9 = bf16[128,768]{1,0:T(8,128)(2,1)S(1)} collective-permute-done((bf16[128,768]{1,0:T(8,128)(2,1)S(1)}, bf16[128,768]{1,0:T(8,128)(2,1)S(1)}, u32[]{:S(2)}, u32[]{:S(2)}) %collective-permute-start.9) | collective-permute-done | bytes 196640 | tf_op jit(solution)/shard_map/ppermute | solution.py:739
  38.4 1.6 collective-permute-start.10
  40.0 16.5 %all-gather.5.cloned.1.call-done = bf16[2,2,128,1664]{3,2,0,1:T(8,128)(2,1)} async-done(((bf16[2,2,32,1664]{3,2,0,1:T(8,128)(2,1)}), bf16[2,2,128,1664]{3,2,0,1:T(8,128)(2,1)}) %all-gather.5.cloned.1.call-update) | async-done | bytes 1703952 | tf_op jit(solution)/shard_map/all_gather | solution.py:808
  56.5 1.6 copy.68
  58.1 1.4 slice_bitcast_fusion
  59.4 1.5 collective-permute-start.3
  61.0 1.5 collective-permute-start.6
  62.7 1.9 fusion.6
  64.6 1.9 pad_maximum_fusion.6
  67.6 14.0 %collective-permute-done.3.refs_6_.refs_7_ = bf16[256,1664]{1,0:T(8,128)(2,1)} collective-permute-done((bf16[256,1664]{1,0:T(8,128)(2,1)}, bf16[256,1664]{1,0:T(8,128)(2,1)}, u32[]{:S(2)}, u32[]{:S(2)}) %collective-permute-start.3) | collective-permute-done | bytes 852000 | tf_op jit(solution)/shard_map/ppermute | solution.py:739
  81.6 1.5 collective-permute-start.5
  83.1 1.5 collective-permute-start.8
  84.7 32.2 %all-gather.3.cloned.1.call-done.refs_0_ = bf16[1408,1024]{1,0:T(8,128)(2,1)} async-done(((bf16[352,1024]{1,0:T(8,128)(2,1)}), bf16[1408,1024]{1,0:T(8,128)(2,1)}) %all-gather.3.cloned.1.call-update) | async-done | bytes 2883600 | tf_op jit(solution)/shard_map/all_gather | solution.py:810
  116.8 1.2 fusion.11
  118.2 1.5 collective-permute-start.12
  119.8 1.5 collective-permute-start.13
  123.0 18.1 %attend.1 = (bf16[1024,1024]{1,0:T(8,128)(2,1)}, bf16[1024,768]{1,0:T(8,128)(2,1)}, bf16[1024,256]{1,0:T(8,128)(2,1)}, f32[8,1024]{1,0:T(8,128)}, f32[8,128]{1,0:T(8,128)}, /*index=5*/bf16[8,256,256]{2,1,0:T(8,128)(2,1)}) custom-call(bf16[1408,1024]{1,0:T(8,128)(2,1)} %all-gather.3.cloned.1.call-done.refs_0_, bf16[1024,768]{1,0:T(8,128)(2,1)} %copy-done.6, ...), custom_call_target="tpu_custom_call" | custom-call | flops 4294967296 | bytes 8388608 | tf_op jit(solution)/shard_map/attend/pallas_call | solution.py:308
  141.2 3.7 %all-to-all-start.1 = ((bf16[4,256,256]{2,1,0:T(8,128)(2,1)}), bf16[4,256,256]{2,1,0:T(8,128)(2,1)S(1)}, u32[]{:S(2)}, u32[]{:S(2)}) async-start(bf16[4,256,256]{2,1,0:T(8,128)(2,1)} %bitcast.104), calls=%async_computation.1 | async-start | bytes 1048576 | tf_op jit(solution)/shard_map/all_to_all | solution.py:846
  145.0 1.5 collective-permute-start.16
  146.5 1.5 collective-permute-start.17
  148.0 7.8 %collective-permute-done.16.refs_17_ = bf16[352,512]{1,0:T(8,128)(2,1)S(1)} collective-permute-done((bf16[352,512]{1,0:T(8,128)(2,1)S(1)}, bf16[352,512]{1,0:T(8,128)(2,1)S(1)}, u32[]{:S(2)}, u32[]{:S(2)}) %collective-permute-start.16) | collective-permute-done | bytes 360480 | tf_op jit(solution)/shard_map/ppermute | solution.py:739
  155.8 1.3 collective-permute-done.17.refs_21_
  157.1 1.2 all-to-all-done.1.refs_0_.att_hbm
  158.3 1.9 collective-permute-done.18.refs_1_
  161.0 29.7 %feed.1 = (bf16[512,1024]{1,0:T(8,128)(2,1)}, f32[256,1024]{1,0:T(8,128)}, f32[256,1024]{1,0:T(8,128)}, f32[256,1024]{1,0:T(8,128)}, bf16[1024,1024]{1,0:T(8,128...) custom-call(bf16[4,256,256]{2,1,0:T(8,128)(2,1)} %copy-done.4, ...), custom_call_target="tpu_custom_call" | custom-call | flops 16106127360 | bytes 8388608 | tf_op jit(solution)/shard_map/feed/pallas_call | solution.py:308
  190.9 2.7 collective-permute-done.20.part_hbm
  193.6 1.5 collective-permute-start.21
  195.1 1.5 collective-permute-start.22
  196.6 6.3 %branch.1 = (bf16[256,1024]{1,0:T(8,128)(2,1)}, f32[256,1024]{1,0:T(8,128)}, bf16[4,256,256]{2,1,0:T(8,128)(2,1)}, bf16[512,1024]{1,0:T(8,128)(2,1)}, bf16[512,1024]{1,0:T(8,128)(2,1)}) custom-call(bf16[512,1024]{1,0:T(8,128)(2,1)} %copy-done.12, f32[256,1024]{1,0:T(8,128)} %get-tuple-element.102.outown_hbm, f32[256,1024]{1,0:T(8,128)} %get-tuple-element.103.gnown_hbm, ...), custom_call_target="tpu_custom_call" | custom-call | flops 1073741824 | bytes 8388608 | tf_op jit(solution)/shard_map/branch/pallas_call | solution.py:308
  202.8 3.5 all-to-all-start.2
  207.8 13.0 %all-to-all-done.2 = bf16[4,256,256]{2,1,0:T(8,128)(2,1)S(1)} async-done(((bf16[4,256,256]{2,1,0:T(8,128)(2,1)}), bf16[4,256,256]{2,1,0:T(8,128)(2,1)S(1)}, u32[]{:S(2)}, u32[]{:S(2)}) %all-to-all-start.2) | async-done | bytes 524320 | tf_op jit(solution)/shard_map/all_to_all | solution.py:864
  221.6 22.5 %attend_back.1 = (bf16[1024,768]{1,0:T(8,128)(2,1)}, bf16[1024,1024]{1,0:T(8,128)(2,1)}) custom-call(bf16[1024,768]{1,0:T(8,128)(2,1)} %get-tuple-element.108.mixed_hbm, bf16[1024,256]{1,0:T(8,128)(2,1)} %bitcast.90, f32[8,1024]{1,0:T(8,128)} %get-tuple-element.110.total_hbm, f32[1024,128]{1,0:T(8,128)} %get-tuple-element.243.refs_2_.cos_hbm, ...), custom_call_target="tpu_custom_call" | custom-call | bytes 8388608 | tf_op jit(solution)/shard_map/attend_back/pallas_call | solution.py:308
  244.2 6.7 %project_weights.1 = (bf16[512,1792]{1,0:T(8,128)(2,1)}, bf16[512,1792]{1,0:T(8,128)(2,1)}) custom-call(bf16[1024,768]{1,0:T(8,128)(2,1)} %get-tuple-element.121.gm_hbm, bf16[1024,1024]{1,0:T(8,128)(2,1)} %get-tuple-element.122.normed_hbm, bf16[512,1024]{1,0:T(8,128)(2,1)} %get-tuple-element.123.okeep_hbm, bf16[512,1024]{1,0:T(8,128)(2,1)} %get-tuple-element.124.osend_hbm), custom_call_target="tpu_custom_call" | custom-call | flops 1073741824 | bytes 8388608 | tf_op jit(solution)/shard_map/project_weights/pallas_call | solution.py:308
  251.4 1.6 collective-permute-start.28
  254.4 1.3 add_convert_fusion.5
  255.7 1.3 collective-permute-start.31
  257.0 1.3 add_convert_fusion.4
  258.4 1.1 collective-permute-start.32
  259.5 11.0 %collective-permute-done.28 = bf16[256,1408]{1,0:T(8,128)(2,1)S(1)} collective-permute-done((bf16[256,1408]{1,0:T(8,128)(2,1)S(1)}, bf16[256,1408]{1,0:T(8,128)(2,1)S(1)}, u32[]{:S(2)}, u32[]{:S(2)}) %collective-permute-start.28) | collective-permute-done | bytes 720928 | tf_op jit(solution)/shard_map/ppermute | solution.py:739
  270.8 1.7 collective-permute-done.29
  272.9 3.3 collective-permute-done.31
  276.3 1.6 collective-permute-done.32
  279.5 1.3 copy-done.7
  282.0 1.5 pad_maximum_fusion
  285.7 3.7 %all-to-all-start.4 = ((f32[32,8,128]{2,1,0:T(8,128)}), f32[32,8,128]{2,1,0:T(8,128)S(1)}, u32[]{:S(2)}, u32[]{:S(2)}) async-start(f32[32,8,128]{2,1,0:T(8,128)} %broadcast_in_dim.39), calls=%async_computation.6 | async-start | bytes 262144 | tf_op jit(solution)/shard_map/all_to_all | solution.py:901
  289.4 13.6 %collective-permute-done.26 = bf16[256,1792]{1,0:T(8,128)(2,1)} collective-permute-done((bf16[256,1792]{1,0:T(8,128)(2,1)S(1)}, bf16[256,1792]{1,0:T(8,128)(2,1)}, u32[]{:S(2)}, u32[]{:S(2)}) %collective-permute-start.26) | collective-permute-done | bytes 917536 | tf_op jit(solution)/shard_map/ppermute | solution.py:739
  302.9 1.4 add_convert_fusion.3
  304.4 1.7 collective-permute-start.27
  306.5 7.4 %collective-permute-done.27 = bf16[128,1792]{1,0:T(8,128)(2,1)S(1)} collective-permute-done((bf16[128,1792]{1,0:T(8,128)(2,1)S(1)}, bf16[128,1792]{1,0:T(8,128)(2,1)S(1)}, u32[]{:S(2)}, u32[]{:S(2)}) %collective-permute-start.27) | collective-permute-done | bytes 458784 | tf_op jit(solution)/shard_map/ppermute | solution.py:739
  314.8 4.0 %all-to-all-start.3 = ((bf16[4,32,1792]{2,1,0:T(8,128)(2,1)}), bf16[4,32,1792]{2,1,0:T(8,128)(2,1)S(1)}, u32[]{:S(2)}, u32[]{:S(2)}) async-start(bf16[4,32,1792]{2,1,0:T(8,128)(2,1)} %bitcast.26), calls=%async_computation.4 | async-start | bytes 917504 | tf_op jit(solution)/shard_map/all_to_all | solution.py:912
  318.8 1.5 fusion.3
  320.4 1.5 fusion.5
  321.9 1.4 add_bitcast_fusion
  323.2 18.5 %all-to-all-done.3 = bf16[4,32,1792]{2,1,0:T(8,128)(2,1)S(1)} async-done(((bf16[4,32,1792]{2,1,0:T(8,128)(2,1)}), bf16[4,32,1792]{2,1,0:T(8,128)(2,1)S(1)}, u32[]{:S(2)}, u32[]{:S(2)}) %all-to-all-start.3) | async-done | bytes 458784 | tf_op jit(solution)/shard_map/all_to_all | solution.py:912
  344.3 1.0 slice.425
  345.9 1.0 subtract_convert_fusion
  348.0 0.9 subtract_convert_fusion.1
  349.1 0.9 subtract_convert_fusion.2
  (220 shorter events, 23.5 us)
Async XLA Ops:
  7.2 3.2 copy-start.30
  7.2 49.3 %all-gather.5.cloned.1.call-start = ((), (), s32[]{:S(2)}) async-start(), calls=%async_computation.8 | async-start | bytes 2129920 | tf_op jit(solution)/shard_map/all_gather | solution.py:808
  9.8 1.6 collective-permute-start
  12.2 104.6 %all-gather.3.cloned.1.call-start = ((), (), s32[]{:S(2)}) async-start(), calls=%async_computation.7 | async-start | bytes 3604480 | tf_op jit(solution)/shard_map/all_gather | solution.py:810
  12.4 8.1 %copy-start.20 = (bf16[1,256,1024]{2,1,0:T(8,128)(2,1)S(1)}, bf16[1,256,1024]{2,1,0:T(8,128)(2,1)}, u32[]{:S(2)}) copy-start(bf16[1,256,1024]{2,1,0:T(8,128)(2,1)} %param.21) | copy-start | bytes 1572868
  14.3 17.7 %all-to-all-start = ((bf16[4,32,768]{2,1,0:T(8,128)(2,1)}), bf16[4,32,768]{2,1,0:T(8,128)(2,1)S(1)}, u32[]{:S(2)}, u32[]{:S(2)}) async-start(bf16[4,32,768]{2,1,0:T(8,128)(2,1)} %pad_maximum_fusion.10), calls=%async_computation | async-start | bytes 393216 | tf_op jit(solution)/shard_map/all_to_all | solution.py:817
  20.5 37.6 %collective-permute-start.1 = (bf16[256,1024]{1,0:T(8,128)(2,1)S(1)}, bf16[256,1024]{1,0:T(8,128)(2,1)}, u32[]{:S(2)}, u32[]{:S(2)}) collective-permute-start(bf16[256,1024]{1,0:T(8,128)(2,1)S(1)} %bitcast.80), channel_id=1, source_target_pairs={{0,4},{4,0},{8,12},{12,8},{16,20},{20,16},{24,28},{28,24},{1,5},{5... | collective-permute-start | bytes 1572872 | tf_op jit(solution)/shard_map/ppermute | solution.py:739
  20.5 37.6 %collective-permute-start.2 = (bf16[256,1024]{1,0:T(8,128)(2,1)S(1)}, bf16[256,1024]{1,0:T(8,128)(2,1)}, u32[]{:S(2)}, u32[]{:S(2)}) collective-permute-start(bf16[256,1024]{1,0:T(8,128)(2,1)S(1)} %bitcast.103), channel_id=1, source_target_pairs={{0,4},{4,0},{8,12},{12,8},{16,20},{20,16},{24,28},{28,24},{1,5},{5... | collective-permute-start | bytes 1572872 | tf_op jit(solution)/shard_map/ppermute | solution.py:739
  32.0 5.7 %collective-permute-start.9 = (bf16[128,768]{1,0:T(8,128)(2,1)S(1)}, bf16[128,768]{1,0:T(8,128)(2,1)S(1)}, u32[]{:S(2)}, u32[]{:S(2)}) collective-permute-start(bf16[128,768]{1,0:T(8,128)(2,1)S(1)} %bitcast.84), channel_id=1, source_target_pairs={{0,8},{4,12},{8,0},{12,4},{16,24},{20,28},{24,16},{28,20},{1,9},{5... | collective-permute-start | bytes 589832 | tf_op jit(solution)/shard_map/ppermute | solution.py:739
  38.4 24.0 %collective-permute-start.10 = (bf16[256,768]{1,0:T(8,128)(2,1)}, bf16[256,768]{1,0:T(8,128)(2,1)S(1)}, u32[]{:S(2)}, u32[]{:S(2)}) collective-permute-start(bf16[256,768]{1,0:T(8,128)(2,1)} %pad_maximum_fusion.9), channel_id=1, source_target_pairs={{0,16},{4,20},{8,24},{12,28},{16,0},{20,4},{24,8},{28,12},{1,17},{... | collective-permute-start | bytes 1179656 | tf_op jit(solution)/shard_map/ppermute | solution.py:739
  59.4 3.2 copy-start.37
  59.4 22.1 %collective-permute-start.3 = (bf16[256,1664]{1,0:T(8,128)(2,1)}, bf16[256,1664]{1,0:T(8,128)(2,1)}, u32[]{:S(2)}, u32[]{:S(2)}) collective-permute-start(bf16[256,1664]{1,0:T(8,128)(2,1)} %get-tuple-element.82.refs_5_.refs_6_), channel_id=1, source_target_pairs={{0,8},{4,12},{8,0},{12,4},{16,24},{20,28},{24,16},{28,20},{1,9},{5... | collective-permute-start | bytes 2555912 | tf_op jit(solution)/shard_map/ppermute | solution.py:739
  61.0 22.2 %collective-permute-start.6 = (bf16[256,1664]{1,0:T(8,128)(2,1)}, bf16[256,1664]{1,0:T(8,128)(2,1)}, u32[]{:S(2)}, u32[]{:S(2)}) collective-permute-start(bf16[256,1664]{1,0:T(8,128)(2,1)} %get-tuple-element.86.refs_9_.refs_10_), channel_id=1, source_target_pairs={{0,16},{4,20},{8,24},{12,28},{16,0},{20,4},{24,8},{28,12},{1,17},{... | collective-permute-start | bytes 2555912 | tf_op jit(solution)/shard_map/ppermute | solution.py:739
  62.6 22.0 %collective-permute-start.11 = (bf16[512,768]{1,0:T(8,128)(2,1)S(1)}, bf16[512,768]{1,0:T(8,128)(2,1)S(1)}, u32[]{:S(2)}, u32[]{:S(2)}) collective-permute-start(bf16[512,768]{1,0:T(8,128)(2,1)S(1)} %pad_maximum_fusion.1), channel_id=1, source_target_pairs={{0,4},{4,0},{8,12},{12,8},{16,20},{20,16},{24,28},{28,24},{1,5},{5... | collective-permute-start | bytes 2359304 | tf_op jit(solution)/shard_map/ppermute | solution.py:739
  66.5 53.3 %collective-permute-start.4 = (bf16[256,1664]{1,0:T(8,128)(2,1)}, bf16[256,1664]{1,0:T(8,128)(2,1)}, u32[]{:S(2)}, u32[]{:S(2)}) collective-permute-start(bf16[256,1664]{1,0:T(8,128)(2,1)} %get-tuple-element.82.refs_5_.refs_6_), channel_id=1, source_target_pairs={{0,16},{4,20},{8,24},{12,28},{16,0},{20,4},{24,8},{28,12},{1,17},{... | collective-permute-start | bytes 2555912 | tf_op jit(solution)/shard_map/ppermute | solution.py:739
  67.1 54.2 %collective-permute-start.7 = (bf16[256,1664]{1,0:T(8,128)(2,1)}, bf16[256,1664]{1,0:T(8,128)(2,1)}, u32[]{:S(2)}, u32[]{:S(2)}) collective-permute-start(bf16[256,1664]{1,0:T(8,128)(2,1)} %get-tuple-element.86.refs_9_.refs_10_), channel_id=1, source_target_pairs={{0,8},{4,12},{8,0},{12,4},{16,24},{20,28},{24,16},{28,20},{1,9},{5... | collective-permute-start | bytes 2555912 | tf_op jit(solution)/shard_map/ppermute | solution.py:739
  81.6 40.2 %collective-permute-start.5 = (bf16[256,1664]{1,0:T(8,128)(2,1)}, bf16[256,1664]{1,0:T(8,128)(2,1)}, u32[]{:S(2)}, u32[]{:S(2)}) collective-permute-start(bf16[256,1664]{1,0:T(8,128)(2,1)} %collective-permute-done.3.refs_6_.refs_7_), channel_id=1, source_target_pairs={{0,16},{4,20},{8,24},{12,28},{16,0},{20,4},{24,8},{28,12},{1,17},{... | collective-permute-start | bytes 2555912 | tf_op jit(solution)/shard_map/ppermute | solution.py:739
  83.1 39.2 %collective-permute-start.8 = (bf16[256,1664]{1,0:T(8,128)(2,1)}, bf16[256,1664]{1,0:T(8,128)(2,1)}, u32[]{:S(2)}, u32[]{:S(2)}) collective-permute-start(bf16[256,1664]{1,0:T(8,128)(2,1)} %collective-permute-done.6.refs_10_.refs_11_), channel_id=1, source_target_pairs={{0,8},{4,12},{8,0},{12,4},{16,24},{20,28},{24,16},{28,20},{1,9},{5... | collective-permute-start | bytes 2555912 | tf_op jit(solution)/shard_map/ppermute | solution.py:739
  84.7 33.5 %copy-start.6 = (bf16[1024,768]{1,0:T(8,128)(2,1)}, bf16[1024,768]{1,0:T(8,128)(2,1)S(1)}, u32[]{:S(2)}) copy-start(bf16[1024,768]{1,0:T(8,128)(2,1)S(1)} %constant_dynamic-update-slice_fusion.refs_1_.weight_hbm) | copy-start | bytes 4718596
  118.2 22.9 %copy-start.24 = (bf16[352,512]{1,0:T(8,128)(2,1)}, bf16[352,512]{1,0:T(8,128)(2,1)S(1)}, u32[]{:S(2)}) copy-start(bf16[352,512]{1,0:T(8,128)(2,1)S(1)} %get-tuple-element.180.refs_18_) | copy-start | bytes 1081348
  118.2 22.9 %copy-start.25 = (bf16[352,512]{1,0:T(8,128)(2,1)}, bf16[352,512]{1,0:T(8,128)(2,1)S(1)}, u32[]{:S(2)}) copy-start(bf16[352,512]{1,0:T(8,128)(2,1)S(1)} %get-tuple-element.181.refs_14_) | copy-start | bytes 1081348
  118.2 22.9 %collective-permute-start.12 = (bf16[352,512]{1,0:T(8,128)(2,1)S(1)}, bf16[352,512]{1,0:T(8,128)(2,1)S(1)}, u32[]{:S(2)}, u32[]{:S(2)}) collective-permute-start(bf16[352,512]{1,0:T(8,128)(2,1)S(1)} %get-tuple-element.181.refs_14_), channel_id=1, source_target_pairs={{0,8},{4,12},{8,0},{12,4},{16,24},{20,28},{24,16},{28,20},{1,9},{5... | collective-permute-start | bytes 1081352 | tf_op jit(solution)/shard_map/ppermute | solution.py:739
  119.8 21.4 %collective-permute-start.13 = (bf16[352,512]{1,0:T(8,128)(2,1)S(1)}, bf16[352,512]{1,0:T(8,128)(2,1)S(1)}, u32[]{:S(2)}, u32[]{:S(2)}) collective-permute-start(bf16[352,512]{1,0:T(8,128)(2,1)S(1)} %get-tuple-element.181.refs_14_), channel_id=1, source_target_pairs={{0,16},{4,20},{8,24},{12,28},{16,0},{20,4},{24,8},{28,12},{1,17},{... | collective-permute-start | bytes 1081352 | tf_op jit(solution)/shard_map/ppermute | solution.py:739
  121.3 19.9 %collective-permute-start.14 = (bf16[352,512]{1,0:T(8,128)(2,1)S(1)}, bf16[352,512]{1,0:T(8,128)(2,1)S(1)}, u32[]{:S(2)}, u32[]{:S(2)}) collective-permute-start(bf16[352,512]{1,0:T(8,128)(2,1)S(1)} %get-tuple-element.180.refs_18_), channel_id=1, source_target_pairs={{0,16},{4,20},{8,24},{12,28},{16,0},{20,4},{24,8},{28,12},{1,17},{... | collective-permute-start | bytes 1081352 | tf_op jit(solution)/shard_map/ppermute | solution.py:739
  121.8 19.4 %collective-permute-start.15 = (bf16[352,512]{1,0:T(8,128)(2,1)S(1)}, bf16[352,512]{1,0:T(8,128)(2,1)S(1)}, u32[]{:S(2)}, u32[]{:S(2)}) collective-permute-start(bf16[352,512]{1,0:T(8,128)(2,1)S(1)} %get-tuple-element.180.refs_18_), channel_id=1, source_target_pairs={{0,8},{4,12},{8,0},{12,4},{16,24},{20,28},{24,16},{28,20},{1,9},{5... | collective-permute-start | bytes 1081352 | tf_op jit(solution)/shard_map/ppermute | solution.py:739
  141.1 19.1 %copy-start.43 = (bf16[352,512]{1,0:T(8,128)(2,1)}, bf16[352,512]{1,0:T(8,128)(2,1)S(1)}, u32[]{:S(2)}) copy-start(bf16[352,512]{1,0:T(8,128)(2,1)S(1)} %collective-permute-done.12.refs_15_) | copy-start | bytes 1081348
  141.1 15.9 %copy-start.45 = (bf16[352,512]{1,0:T(8,128)(2,1)}, bf16[352,512]{1,0:T(8,128)(2,1)S(1)}, u32[]{:S(2)}) copy-start(bf16[352,512]{1,0:T(8,128)(2,1)S(1)} %collective-permute-done.14.refs_19_) | copy-start | bytes 1081348
  141.2 19.0 %copy-start.44 = (bf16[352,512]{1,0:T(8,128)(2,1)}, bf16[352,512]{1,0:T(8,128)(2,1)S(1)}, u32[]{:S(2)}) copy-start(bf16[352,512]{1,0:T(8,128)(2,1)S(1)} %collective-permute-done.13.refs_16_) | copy-start | bytes 1081348
  141.2 3.7 %copy-start.46 = (bf16[352,512]{1,0:T(8,128)(2,1)}, bf16[352,512]{1,0:T(8,128)(2,1)S(1)}, u32[]{:S(2)}) copy-start(bf16[352,512]{1,0:T(8,128)(2,1)S(1)} %collective-permute-done.15.refs_20_) | copy-start | bytes 1081348
  141.2 17.1 %all-to-all-start.1 = ((bf16[4,256,256]{2,1,0:T(8,128)(2,1)}), bf16[4,256,256]{2,1,0:T(8,128)(2,1)S(1)}, u32[]{:S(2)}, u32[]{:S(2)}) async-start(bf16[4,256,256]{2,1,0:T(8,128)(2,1)} %bitcast.104), calls=%async_computation.1 | async-start | bytes 1048576 | tf_op jit(solution)/shard_map/all_to_all | solution.py:846
  144.9 13.4 %collective-permute-start.19 = (bf16[8,256,256]{2,1,0:T(8,128)(2,1)}, bf16[8,256,256]{2,1,0:T(8,128)(2,1)S(1)}, u32[]{:S(2)}, u32[]{:S(2)}) collective-permute-start(bf16[8,256,256]{2,1,0:T(8,128)(2,1)} %get-tuple-element.95), channel_id=1, source_target_pairs={{0,4},{4,0},{8,12},{12,8},{16,20},{20,16},{24,28},{28,24},{1,5},{5... | collective-permute-start | bytes 3145736 | tf_op jit(solution)/shard_map/ppermute | solution.py:739
  145.0 10.8 %collective-permute-start.16 = (bf16[352,512]{1,0:T(8,128)(2,1)S(1)}, bf16[352,512]{1,0:T(8,128)(2,1)S(1)}, u32[]{:S(2)}, u32[]{:S(2)}) collective-permute-start(bf16[352,512]{1,0:T(8,128)(2,1)S(1)} %collective-permute-done.12.refs_15_), channel_id=1, source_target_pairs={{0,16},{4,20},{8,24},{12,28},{16,0},{20,4},{24,8},{28,12},{1,17},{... | collective-permute-start | bytes 1081352 | tf_op jit(solution)/shard_map/ppermute | solution.py:739
  146.5 10.6 %collective-permute-start.17 = (bf16[352,512]{1,0:T(8,128)(2,1)S(1)}, bf16[352,512]{1,0:T(8,128)(2,1)}, u32[]{:S(2)}, u32[]{:S(2)}) collective-permute-start(bf16[352,512]{1,0:T(8,128)(2,1)S(1)} %collective-permute-done.14.refs_19_), channel_id=1, source_target_pairs={{0,8},{4,12},{8,0},{12,4},{16,24},{20,28},{24,16},{28,20},{1,9},{5... | collective-permute-start | bytes 1081352 | tf_op jit(solution)/shard_map/ppermute | solution.py:739
  155.8 4.4 %copy-start.47 = (bf16[352,512]{1,0:T(8,128)(2,1)}, bf16[352,512]{1,0:T(8,128)(2,1)S(1)}, u32[]{:S(2)}) copy-start(bf16[352,512]{1,0:T(8,128)(2,1)S(1)} %collective-permute-done.16.refs_17_) | copy-start | bytes 1081348
  158.3 1.9 collective-permute-start.18
  190.7 2.9 collective-permute-start.20
  193.6 3.0 copy-start.12
  193.6 50.6 %collective-permute-start.21 = (bf16[512,1408]{1,0:T(8,128)(2,1)}, bf16[512,1408]{1,0:T(8,128)(2,1)S(1)}, u32[]{:S(2)}, u32[]{:S(2)}) collective-permute-start(bf16[512,1408]{1,0:T(8,128)(2,1)} %get-tuple-element.117), channel_id=1, source_target_pairs={{0,8},{4,12},{8,0},{12,4},{16,24},{20,28},{24,16},{28,20},{1,9},{5... | collective-permute-start | bytes 4325384 | tf_op jit(solution)/shard_map/ppermute | solution.py:739
  195.1 49.1 %collective-permute-start.22 = (bf16[512,1408]{1,0:T(8,128)(2,1)}, bf16[512,1408]{1,0:T(8,128)(2,1)S(1)}, u32[]{:S(2)}, u32[]{:S(2)}) collective-permute-start(bf16[512,1408]{1,0:T(8,128)(2,1)} %get-tuple-element.118), channel_id=1, source_target_pairs={{0,16},{4,20},{8,24},{12,28},{16,0},{20,4},{24,8},{28,12},{1,17},{... | collective-permute-start | bytes 4325384 | tf_op jit(solution)/shard_map/ppermute | solution.py:739
  202.8 18.0 %all-to-all-start.2 = ((bf16[4,256,256]{2,1,0:T(8,128)(2,1)}), bf16[4,256,256]{2,1,0:T(8,128)(2,1)S(1)}, u32[]{:S(2)}, u32[]{:S(2)}) async-start(bf16[4,256,256]{2,1,0:T(8,128)(2,1)} %get-tuple-element.109), calls=%async_computation.2 | async-start | bytes 1048576 | tf_op jit(solution)/shard_map/all_to_all | solution.py:864
  206.3 112.5 %reduce-scatter.3.cloned.1.call-start = ((), (), s32[]{:S(2)}) async-start(), calls=%async_computation.9 | async-start | bytes 2621440 | tf_op jit(solution)/shard_map/reduce_scatter | solution.py:905
  206.6 37.6 %collective-permute-start.23 = (bf16[704,512]{1,0:T(8,128)(2,1)}, bf16[704,512]{1,0:T(8,128)(2,1)}, u32[]{:S(2)}, u32[]{:S(2)}) collective-permute-start(bf16[704,512]{1,0:T(8,128)(2,1)} %get-tuple-element.119), channel_id=1, source_target_pairs={{0,8},{4,12},{8,0},{12,4},{16,24},{20,28},{24,16},{28,20},{1,9},{5... | collective-permute-start | bytes 2162696 | tf_op jit(solution)/shard_map/ppermute | solution.py:739
  207.2 37.0 %collective-permute-start.24 = (bf16[704,512]{1,0:T(8,128)(2,1)}, bf16[704,512]{1,0:T(8,128)(2,1)}, u32[]{:S(2)}, u32[]{:S(2)}) collective-permute-start(bf16[704,512]{1,0:T(8,128)(2,1)} %get-tuple-element.120), channel_id=1, source_target_pairs={{0,16},{4,20},{8,24},{12,28},{16,0},{20,4},{24,8},{28,12},{1,17},{... | collective-permute-start | bytes 2162696 | tf_op jit(solution)/shard_map/ppermute | solution.py:739
  244.1 100.2 %reduce-scatter.5.cloned.1.call-start = ((), (), s32[]{:S(2)}) async-start(), calls=%async_computation.10 | async-start | bytes 2785280 | tf_op jit(solution)/shard_map/reduce_scatter | solution.py:899
  244.2 6.7 %copy-start.9 = (bf16[512,1408]{1,0:T(8,128)(2,1)S(1)}, bf16[512,1408]{1,0:T(8,128)(2,1)}, u32[]{:S(2)}) copy-start(bf16[512,1408]{1,0:T(8,128)(2,1)} %get-tuple-element.129) | copy-start | bytes 4325380
  251.4 19.1 %collective-permute-start.28 = (bf16[256,1408]{1,0:T(8,128)(2,1)S(1)}, bf16[256,1408]{1,0:T(8,128)(2,1)S(1)}, u32[]{:S(2)}, u32[]{:S(2)}) collective-permute-start(bf16[256,1408]{1,0:T(8,128)(2,1)S(1)} %slice.402), channel_id=1, source_target_pairs={{0,16},{4,20},{8,24},{12,28},{16,0},{20,4},{24,8},{28,12},{1,17},{... | collective-permute-start | bytes 2162696 | tf_op jit(solution)/shard_map/ppermute | solution.py:739
  253.3 3.7 %copy-start.18 = (bf16[704,512]{1,0:T(8,128)(2,1)S(1)}, bf16[704,512]{1,0:T(8,128)(2,1)}, u32[]{:S(2)}) copy-start(bf16[704,512]{1,0:T(8,128)(2,1)} %get-tuple-element.132) | copy-start | bytes 2162692
  253.4 19.1 %collective-permute-start.29 = (bf16[256,1408]{1,0:T(8,128)(2,1)S(1)}, bf16[256,1408]{1,0:T(8,128)(2,1)S(1)}, u32[]{:S(2)}, u32[]{:S(2)}) collective-permute-start(bf16[256,1408]{1,0:T(8,128)(2,1)S(1)} %slice.404), channel_id=1, source_target_pairs={{0,8},{4,12},{8,0},{12,4},{16,24},{20,28},{24,16},{28,20},{1,9},{5... | collective-permute-start | bytes 2162696 | tf_op jit(solution)/shard_map/ppermute | solution.py:739
  255.7 3.8 %copy-start.40 = (bf16[512,1792]{1,0:T(8,128)(2,1)S(1)}, bf16[512,1792]{1,0:T(8,128)(2,1)}, u32[]{:S(2)}) copy-start(bf16[512,1792]{1,0:T(8,128)(2,1)} %get-tuple-element.128) | copy-start | bytes 5505028
  255.7 20.5 %collective-permute-start.31 = (bf16[352,512]{1,0:T(8,128)(2,1)S(1)}, bf16[352,512]{1,0:T(8,128)(2,1)S(1)}, u32[]{:S(2)}, u32[]{:S(2)}) collective-permute-start(bf16[352,512]{1,0:T(8,128)(2,1)S(1)} %slice.406), channel_id=1, source_target_pairs={{0,16},{4,20},{8,24},{12,28},{16,0},{20,4},{24,8},{28,12},{1,17},{... | collective-permute-start | bytes 1081352 | tf_op jit(solution)/shard_map/ppermute | solution.py:739
  258.4 19.6 %collective-permute-start.32 = (bf16[352,512]{1,0:T(8,128)(2,1)S(1)}, bf16[352,512]{1,0:T(8,128)(2,1)S(1)}, u32[]{:S(2)}, u32[]{:S(2)}) collective-permute-start(bf16[352,512]{1,0:T(8,128)(2,1)S(1)} %slice.408), channel_id=1, source_target_pairs={{0,8},{4,12},{8,0},{12,4},{16,24},{20,28},{24,16},{28,20},{1,9},{5... | collective-permute-start | bytes 1081352 | tf_op jit(solution)/shard_map/ppermute | solution.py:739
  259.5 20.0 %collective-permute-start.25 = (bf16[512,1792]{1,0:T(8,128)(2,1)S(1)}, bf16[512,1792]{1,0:T(8,128)(2,1)S(1)}, u32[]{:S(2)}, u32[]{:S(2)}) collective-permute-start(bf16[512,1792]{1,0:T(8,128)(2,1)S(1)} %copy-done.40), channel_id=1, source_target_pairs={{0,4},{4,0},{8,12},{12,8},{16,20},{20,16},{24,28},{28,24},{1,5},{5... | collective-permute-start | bytes 5505032 | tf_op jit(solution)/shard_map/ppermute | solution.py:739
  272.8 6.4 %collective-permute-start.30 = (bf16[128,2816]{1,0:T(8,128)(2,1)S(1)}, bf16[128,2816]{1,0:T(8,128)(2,1)S(1)}, u32[]{:S(2)}, u32[]{:S(2)}) collective-permute-start(bf16[128,2816]{1,0:T(8,128)(2,1)S(1)} %pad_maximum_fusion.3), channel_id=1, source_target_pairs={{0,4},{4,0},{8,12},{12,8},{16,20},{20,16},{24,28},{28,24},{1,5},{5... | collective-permute-start | bytes 2162696 | tf_op jit(solution)/shard_map/ppermute | solution.py:739
  281.4 21.6 %collective-permute-start.26 = (bf16[256,1792]{1,0:T(8,128)(2,1)S(1)}, bf16[256,1792]{1,0:T(8,128)(2,1)}, u32[]{:S(2)}, u32[]{:S(2)}) collective-permute-start(bf16[256,1792]{1,0:T(8,128)(2,1)S(1)} %slice.382), channel_id=1, source_target_pairs={{0,8},{4,12},{8,0},{12,4},{16,24},{20,28},{24,16},{28,20},{1,9},{5... | collective-permute-start | bytes 2752520 | tf_op jit(solution)/shard_map/ppermute | solution.py:739
  285.7 20.4 %all-to-all-start.4 = ((f32[32,8,128]{2,1,0:T(8,128)}), f32[32,8,128]{2,1,0:T(8,128)S(1)}, u32[]{:S(2)}, u32[]{:S(2)}) async-start(f32[32,8,128]{2,1,0:T(8,128)} %broadcast_in_dim.39), calls=%async_computation.6 | async-start | bytes 262144 | tf_op jit(solution)/shard_map/all_to_all | solution.py:901
  304.4 9.5 %collective-permute-start.27 = (bf16[128,1792]{1,0:T(8,128)(2,1)S(1)}, bf16[128,1792]{1,0:T(8,128)(2,1)S(1)}, u32[]{:S(2)}, u32[]{:S(2)}) collective-permute-start(bf16[128,1792]{1,0:T(8,128)(2,1)S(1)} %slice.384), channel_id=1, source_target_pairs={{0,16},{4,20},{8,24},{12,28},{16,0},{20,4},{24,8},{28,12},{1,17},{... | collective-permute-start | bytes 1376264 | tf_op jit(solution)/shard_map/ppermute | solution.py:739
  306.3 14.0 %copy-start.38 = (f32[16]{0:T(128)}, f32[16]{0:T(128)S(1)}, u32[]{:S(2)}) copy-start(f32[16]{0:T(128)S(1)} %reshape_squeeze.3) | copy-start | bytes 196
  306.3 14.0 %copy-start.39 = (f32[16]{0:T(128)}, f32[16]{0:T(128)S(1)}, u32[]{:S(2)}) copy-start(f32[16]{0:T(128)S(1)} %divide_sqrt_fusion) | copy-start | bytes 196
  314.8 7.0 %copy-start.13 = (f32[256,1024]{1,0:T(8,128)S(1)}, f32[256,1024]{1,0:T(8,128)}, u32[]{:S(2)}) copy-start(f32[256,1024]{1,0:T(8,128)} %get-tuple-element.107) | copy-start | bytes 3145732
  314.8 27.0 %all-to-all-start.3 = ((bf16[4,32,1792]{2,1,0:T(8,128)(2,1)}), bf16[4,32,1792]{2,1,0:T(8,128)(2,1)S(1)}, u32[]{:S(2)}, u32[]{:S(2)}) async-start(bf16[4,32,1792]{2,1,0:T(8,128)(2,1)} %bitcast.26), calls=%async_computation.4 | async-start | bytes 917504 | tf_op jit(solution)/shard_map/all_to_all | solution.py:912
  318.8 3.0 copy-start.2
  323.2 18.7 %copy-start.34 = (f32[32,1024]{1,0:T(8,128)S(1)}, f32[32,1024]{1,0:T(8,128)}, u32[]{:S(2)}) copy-start(f32[32,1024]{1,0:T(8,128)} %param.31) | copy-start | bytes 393220
  323.2 19.4 %copy-start.31 = (bf16[32,1024]{1,0:T(8,128)(2,1)S(1)}, bf16[32,1024]{1,0:T(8,128)(2,1)}, u32[]{:S(2)}) copy-start(bf16[32,1024]{1,0:T(8,128)(2,1)} %param.25) | copy-start | bytes 196612
  323.2 19.4 %copy-start.35 = (f32[32,1024]{1,0:T(8,128)S(1)}, f32[32,1024]{1,0:T(8,128)}, u32[]{:S(2)}) copy-start(f32[32,1024]{1,0:T(8,128)} %param.32) | copy-start | bytes 393220
  (26 other events, 41.6 us)
Sparse Core Ops, SparseCore 0:
  12.4 44.0 all-gather.4
  58.6 58.1 all-gather.2
  244.2 41.4 reduce-scatter.2
  288.0 52.5 reduce-scatter.4

commit v6 on v5

--- a/solution.py
+++ b/solution.py
@@ -382,36 +382,40 @@
     peak_ref[...] = jnp.zeros_like(peak_ref)
     total_ref[...] = jnp.zeros_like(total_ref)
 
-    @pl.loop(0, 4)
-    def _(h):
-        lanes = pl.multiple_of(h // 2 * 128, 128)
+    @pl.loop(0, 2)
+    def _(pair):
+        lanes = pl.multiple_of(pair * 128, 128)
         lane = lax.broadcasted_iota(jnp.int32, (256, 128), 1)
-        mine = lane // 64 == h % 2
-        best = None
+        best = [None, None]
         for i in range(4):
             width = min(256 * (i + 2), 1024)
             low = 256 * i
-            q = mixed_ref[low : low + 256, pl.ds(lanes, 128)]
-            q = jnp.where(mine, q, jnp.zeros_like(q))
-            s = dot(mixed_ref[0:width, pl.ds(pl.multiple_of(256 + lanes, 128), 128)], q, NT)
+            both = mixed_ref[low : low + 256, pl.ds(lanes, 128)]
+            keys = mixed_ref[0:width, pl.ds(pl.multiple_of(256 + lanes, 128), 128)]
+            values = value_t[pl.ds(lanes, 128), 0:width]
             ok = id_col[low:width, 0:1] <= ids[0:1, low : low + 256]
-            tail = jnp.where(ok, s[low:width], MASK_FILL)
-            top = jnp.max(tail, axis=0, keepdims=True)
-            if i:
-                top = jnp.maximum(top, jnp.max(s[0:low], axis=0, keepdims=True))
-                s = jnp.concatenate([s[0:low], tail], axis=0)
-            else:
-                s = tail
-            e = jnp.exp(s - top)
-            total = jnp.sum(e, axis=0, keepdims=True)
-            o = dot(value_t[pl.ds(lanes, 128), 0:width], e.astype(bf), NN)
-            o = (o * (1.0 / total)).T.astype(bf)
-            old = attended[low : low + 256, pl.ds(lanes, 128)]
-            attended[low : low + 256, pl.ds(lanes, 128)] = jnp.where(mine, o, old)
-            total_ref[pl.ds(h, 1), low : low + 256] = top + jnp.log(total)
-            m = jnp.max(top, axis=1, keepdims=True)
-            best = m if best is None else jnp.maximum(best, m)
-        peak_ref[pl.ds(h, 1), :] = jnp.broadcast_to(best, (1, 128))
+            outs = []
+            for half in range(2):
+                q = jnp.where(lane // 64 == half, both, jnp.zeros_like(both))
+                s = dot(keys, q, NT)
+                tail = jnp.where(ok, s[low:width], MASK_FILL)
+                top = jnp.max(tail, axis=0, keepdims=True)
+                if i:
+                    top = jnp.maximum(top, jnp.max(s[0:low], axis=0, keepdims=True))
+                    s = jnp.concatenate([s[0:low], tail], axis=0)
+                else:
+                    s = tail
+                e = jnp.exp(s - top)
+                total = jnp.sum(e, axis=0, keepdims=True)
+                o = dot(values, e.astype(bf), NN)
+                outs.append(o[64 * half : 64 * half + 64] * (1.0 / total))
+                total_ref[pl.ds(pair * 2 + half, 1), low : low + 256] = top + jnp.log(total)
+                m = jnp.max(top, axis=1, keepdims=True)
+                best[half] = m if best[half] is None else jnp.maximum(best[half], m)
+            o = jnp.concatenate(outs, axis=0).T.astype(bf)
+            attended[low : low + 256, pl.ds(lanes, 128)] = o
+        for half in range(2):
+            peak_ref[pl.ds(pair * 2 + half, 1), :] = jnp.broadcast_to(best[half], (1, 128))
 
     late.append(go.start(attended, attended_hbm))
     late.append(go.start(total_ref, total_hbm))
@@ -487,7 +491,7 @@
                 gk_acc[0:width, pl.ds(lanes, 128)] += dot(ds, q, NN)
                 return jnp.where(sub // 64 == half, dot(kt, ds, NN), gq)
 
-            gq = lax.fori_loop(0, 2, one, jnp.zeros((128, 256), f32))
+            gq = one(1, one(0, jnp.zeros((128, 256), f32)))
             gq = gq.T * 0.125
             cosine = cos_ref[low : low + 256, :]
             sine = sin_ref[low : low + 256, :]
@@ -735,6 +739,52 @@
     )
 
 
+def update_kernel(coeff_ref, wide_ref, mg, mu, md, wg, wu, wd, *refs):
+    outs, (gg, gu, gd, ng, nu, nd, og, ou, od), sems = refs[:9], refs[9:18], refs[18]
+    coeff = coeff_ref[0]
+    go = Copies(sems)
+    done = []
+    part = FF2 // 4
+
+    def finish(i, grad, moment, weight, new_moment, new_weight):
+        done.append(go.start(grad, outs[i]))
+        moved = coeff * moment[...] + grad[...]
+        new_moment[...] = moved
+        done.append(go.start(new_moment, outs[3 + i]))
+        new_weight[...] = (weight[...].astype(f32) - LEARN_RATE * moved).astype(bf)
+        done.append(go.start(new_weight, outs[6 + i]))
+
+    for i, (grad, moment, weight, nm, nw) in enumerate(((gg, mg, wg, ng, og), (gu, mu, wu, nu, ou))):
+        for side in range(2):
+            columns = wide_ref[:, FF2 * (2 * side + i) : FF2 * (2 * side + i + 1)].astype(f32)
+            for j in range(4):
+                low = part * (2 * j + side)
+                grad[:, low : low + part] = columns[:, part * j : part * j + part]
+        finish(i, grad, moment, weight, nm, nw)
+    for j in range(3):
+        rows = min(32, 88 - 32 * j)
+        low = 4 * FF2 + 1024 * j
+        gd[32 * j : 32 * j + rows, :] = wide_ref[:, low : low + 1024].astype(f32)[0:rows]
+    finish(2, gd, md, wd, nd, od)
+    wait_all(done)
+
+
+def update(coeff, wide, moments, weights):
+    shapes = [(32, 2 * FF2), (32, 2 * FF2), (88, 1024)]
+    outs = [(s, f32) for s in shapes] * 2 + [(s, bf) for s in shapes]
+    vmem = pl.BlockSpec(memory_space=pltpu.VMEM)
+    return pl.pallas_call(
+        update_kernel,
+        out_shape=tuple(pltpu.HBM(*o) for o in outs),
+        in_specs=[pl.BlockSpec(memory_space=pltpu.SMEM)] + [vmem] * 7,
+        out_specs=(MAIN,) * 9,
+        scratch_shapes=[pltpu.VMEM(*o) for o in outs] + [pltpu.SemaphoreType.DMA((9,))],
+        compiler_params=pltpu.CompilerParams(vmem_limit_bytes=16 << 20),
+        cost_estimate=pl.CostEstimate(flops=1 << 20, bytes_accessed=6 << 20, transcendentals=0),
+        name="update",
+    )(coeff, wide, *moments, *weights)
+
+
 def swap(array, bit):
     return lax.ppermute(array, "dp", [(i, i ^ bit) for i in range(8)])
 
@@ -751,14 +801,6 @@
     n = matrix.shape[1] // 8
     parts = [matrix[:, n * i : n * i + n] for i in range(8)]
     return jnp.concatenate(parts[0::2], axis=1), jnp.concatenate(parts[1::2], axis=1)
-
-
-def join_even(even, odd):
-    n = even.shape[1] // 4
-    parts = []
-    for i in range(4):
-        parts += [even[:, n * i : n * i + n], odd[:, n * i : n * i + n]]
-    return jnp.concatenate(parts, axis=1)
 
 
 def tie(value, *anchors):
@@ -865,15 +907,19 @@
     grad_mixed, grad_normed = attend_back(
         mixed, grad_attended, totals, cosine, sine, ids, heads_rel
     )
-    grad_mixed = tie(grad_mixed, ga_other, gb_other, gda_other, gdb_other)
-    grad_heads = project_weights(grad_mixed, normed, go_keep, go_send)
-    ga_keep, gb_keep, gda_keep, gdb_keep, grad_heads = lax.optimization_barrier(
-        (ga_keep, gb_keep, gda_keep, gdb_keep, grad_heads)
-    )
+    (ga_keep, gb_keep, gda_keep, gdb_keep, ga_other, gb_other, gda_other, gdb_other, grad_mixed) = (
+        lax.optimization_barrier(
+            (ga_keep, gb_keep, gda_keep, gdb_keep, ga_other, gb_other, gda_other, gdb_other,
+             grad_mixed)
+        )
+    )
+    grad_a = add_low(ga_keep, ga_other)
+    grad_b = add_low(gb_keep, gb_other)
     grad_da = add_low(gda_keep, gda_other)
     grad_db = add_low(gdb_keep, gdb_other)
-    grad_a = add_low(ga_keep, ga_other)
-    grad_b = add_low(gb_keep, gb_other)
+    grad_heads = project_weights(
+        tie(grad_mixed, grad_a, grad_b, grad_da, grad_db), normed, go_keep, go_send
+    )
     grad_a = add_low(grad_a[:256], swap(grad_a[256:], 4))
     grad_b = add_low(grad_b[:256], swap(grad_b[256:], 2))
     grad_da = add_low(grad_da[:352], swap(grad_da[352:], 4))
@@ -896,7 +942,7 @@
         ],
         axis=1,
     )
-    grad_wide = lax.psum_scatter(grad_wide, "ctx", scatter_dimension=0, tiled=True).astype(f32)
+    grad_wide = lax.psum_scatter(grad_wide, "ctx", scatter_dimension=0, tiled=True)
     peaks = tie(peaks, ga_other)
     peaks = lax.all_to_all(
         jnp.broadcast_to(peaks[None], (32, 8, 128)), ("dp", "ctx"), 0, 0, tiled=True
@@ -917,23 +963,18 @@
         jnp.concatenate([grad_heads[i, :, 256 * k : 256 * k + 256] for i in range(4)], axis=1)
         for k in range(3)
     ]
-    grad_d_sum = grad_wide[:, 4 * FF2 :].reshape(32, 3, width).transpose(1, 0, 2)
-    grad_d_sum = grad_d_sum.reshape(96, width)[:88]
-    weight_grads = (
-        *grad_qkv,
-        grad_out,
-        join_even(grad_wide[:, :FF2], grad_wide[:, 2 * FF2 : 3 * FF2]),
-        join_even(grad_wide[:, FF2 : 2 * FF2], grad_wide[:, 3 * FF2 : 4 * FF2]),
-        grad_d_sum,
-    )
-    moments = (m_query, m_key, m_value, m_out, m_gate, m_up, m_down)
+    big = update(
+        momentum_coeff.reshape(1), grad_wide, (m_gate, m_up, m_down), (w_gate, w_up, w_down)
+    )
+    weight_grads = (*grad_qkv, grad_out)
+    moments = (m_query, m_key, m_value, m_out)
     new_moments = tuple(
         (momentum_coeff * moment + gradient for moment, gradient in zip(moments, weight_grads))
     )
     head_scale = jnp.sqrt(clip_threshold / jnp.maximum(head_peaks, clip_threshold))
     column_scale = jnp.repeat(head_scale, HEAD_DIM)
-    rates = (LEARN_RATE, LEARN_RATE, LEARN_RATE, OUT_RATE, LEARN_RATE, LEARN_RATE, LEARN_RATE)
-    shard_list = (w_query, w_key, w_value, w_out, w_gate, w_up, w_down)
+    rates = (LEARN_RATE, LEARN_RATE, LEARN_RATE, OUT_RATE)
+    shard_list = (w_query, w_key, w_value, w_out)
     updated = [
         matrix.astype(jnp.float32) - rate * moment
         for matrix, moment, rate in zip(shard_list, new_moments, rates)
@@ -945,8 +986,11 @@
         layer_out[None],
         input_grad[None],
         *weight_grads,
+        *big[:3],
         *new_moments,
+        *big[3:6],
         *updated,
+        *big[6:],
         head_peaks,
         head_scale,
     )

time: 357 us -> 351 us (0.983)
    pallas_call x5, Pallas kernels: 83.2 us -> 78.4 us  [call(): pl.pallas_call(kernel, out_shape=tuple((pltpu.HBM(*o) for o in outs)), in...]
  transfers between devices with their start and end apart: 42 -> 42, of which waited for: 20 -> 21; matrix products, arithmetic and copies ran while one was open for 8% -> 9% of each run, Pallas kernels for 15% -> 14%
where the time goes in v6:
time: 351 us; the launch traced here: 350 us
  waiting for transfers between devices  162 us (46%)
  Pallas kernels  80.2 us (23%)
  starting transfers between devices  51.4 us (15%)
  other arithmetic  24.4 us (7%)
  between operations  16.2 us (5%)
  local copies, waits for them, and re-layouts  15.9 us (5%)
    pallas_call x5, Pallas kernels, call(): pl.pallas_call(kernel, out_shape=tuple((pltpu.HBM(*o) for o in outs)), in...  78.4 us
    ppermute x33, waiting for transfers between devices, swap(): return lax.ppermute(array, 'dp', [(i, i ^ bit) for i in range(8)])  68.6 us
    all_gather x1, waiting for transfers between devices, fast_device(): rows_all = lax.all_gather(padded, 'ctx', axis=0, tiled=True)  32.2 us
    ppermute x33, starting transfers between devices, swap(): return lax.ppermute(array, 'dp', [(i, i ^ bit) for i in range(8)])  30.1 us
    all_to_all x1, waiting for transfers between devices, fast_device(): lax.all_to_all(grad_heads.reshape(4, 32, 768 + width), 'ctx', 0, 0, tiled...  19.1 us
    all_gather x1, waiting for transfers between devices, fast_device(): lax.all_gather(wide, 'ctx', axis=2, tiled=True).reshape(2, 256, FF2 + 256)  17.2 us
    all_to_all x1, waiting for transfers between devices, fast_device(): lax.all_to_all(grad_attended, 'ctx', 0, 0, tiled=True).reshape(length, 256)  13 us
    all_to_all x1, waiting for transfers between devices, fast_device(): heads = lax.all_to_all(heads, 'ctx', 0, 0, tiled=True).reshape(128, 768)  11 us
  transfers between devices with their start and end apart: 42, of which 21 were waited for; matrix products, arithmetic and copies ran while one was open for 9% of the time, Pallas kernels for 14%

profile of v6, /device:TPU:0, one launch (start us, length us, event | category | flops | bytes accessed | tf_op | source)
XLA Modules:
  0.0 350.5 jit_solution(12261828671408863345)
XLA Ops:
  7.3 1.0 fusion.14
  12.4 1.0 maximum_maximum_fusion
  14.3 6.2 %all-to-all-start = ((bf16[4,32,768]{2,1,0:T(8,128)(2,1)}), bf16[4,32,768]{2,1,0:T(8,128)(2,1)S(1)}, u32[]{:S(2)}, u32[]{:S(2)}) async-start(bf16[4,32,768]{2,1,0:T(8,128)(2,1)} %pad_maximum_fusion.10), calls=%async_computation | async-start | bytes 393216 | tf_op jit(solution)/shard_map/all_to_all | solution.py:859
  21.0 11.0 %all-to-all-done = bf16[4,32,768]{2,1,0:T(8,128)(2,1)S(1)} async-done(((bf16[4,32,768]{2,1,0:T(8,128)(2,1)}), bf16[4,32,768]{2,1,0:T(8,128)(2,1)S(1)}, u32[]{:S(2)}, u32[]{:S(2)}) %all-to-all-start) | async-done | bytes 196640 | tf_op jit(solution)/shard_map/all_to_all | solution.py:859
  32.0 1.5 collective-permute-start.9
  33.5 4.1 %collective-permute-done.9 = bf16[128,768]{1,0:T(8,128)(2,1)S(1)} collective-permute-done((bf16[128,768]{1,0:T(8,128)(2,1)S(1)}, bf16[128,768]{1,0:T(8,128)(2,1)S(1)}, u32[]{:S(2)}, u32[]{:S(2)}) %collective-permute-start.9) | collective-permute-done | bytes 196640 | tf_op jit(solution)/shard_map/ppermute | solution.py:789
  37.7 1.6 collective-permute-start.10
  39.3 17.2 %all-gather.5.cloned.1.call-done = bf16[2,2,128,1664]{3,2,0,1:T(8,128)(2,1)} async-done(((bf16[2,2,32,1664]{3,2,0,1:T(8,128)(2,1)}), bf16[2,2,128,1664]{3,2,0,1:T(8,128)(2,1)}) %all-gather.5.cloned.1.call-update) | async-done | bytes 1703952 | tf_op jit(solution)/shard_map/all_gather | solution.py:850
  56.5 1.6 copy.60
  58.1 1.4 slice_bitcast_fusion
  59.4 1.5 collective-permute-start.3
  60.9 1.5 collective-permute-start.6
  62.7 1.9 fusion.6
  64.6 1.9 pad_maximum_fusion.6
  67.6 13.9 %collective-permute-done.3.refs_6_.refs_7_ = bf16[256,1664]{1,0:T(8,128)(2,1)} collective-permute-done((bf16[256,1664]{1,0:T(8,128)(2,1)}, bf16[256,1664]{1,0:T(8,128)(2,1)}, u32[]{:S(2)}, u32[]{:S(2)}) %collective-permute-start.3) | collective-permute-done | bytes 852000 | tf_op jit(solution)/shard_map/ppermute | solution.py:789
  81.6 1.5 collective-permute-start.5
  83.1 1.5 collective-permute-start.8
  84.7 32.2 %all-gather.3.cloned.1.call-done.refs_0_ = bf16[1408,1024]{1,0:T(8,128)(2,1)} async-done(((bf16[352,1024]{1,0:T(8,128)(2,1)}), bf16[1408,1024]{1,0:T(8,128)(2,1)}) %all-gather.3.cloned.1.call-update) | async-done | bytes 2883600 | tf_op jit(solution)/shard_map/all_gather | solution.py:852
  116.8 1.2 fusion.11
  118.2 1.5 collective-permute-start.12
  119.8 1.5 collective-permute-start.13
  123.0 17.7 %attend.1 = (bf16[1024,1024]{1,0:T(8,128)(2,1)}, bf16[1024,768]{1,0:T(8,128)(2,1)}, bf16[1024,256]{1,0:T(8,128)(2,1)}, f32[8,1024]{1,0:T(8,128)}, f32[8,128]{1,0:T(8,128)}, /*index=5*/bf16[8,256,256]{2,1,0:T(8,128)(2,1)}) custom-call(bf16[1408,1024]{1,0:T(8,128)(2,1)} %all-gather.3.cloned.1.call-done.refs_0_, bf16[1024,768]{1,0:T(8,128)(2,1)} %copy-done.12, ...), custom_call_target="tpu_custom_call" | custom-call | flops 4294967296 | bytes 8388608 | tf_op jit(solution)/shard_map/attend/pallas_call | solution.py:308
  142.4 3.7 %all-to-all-start.1 = ((bf16[4,256,256]{2,1,0:T(8,128)(2,1)}), bf16[4,256,256]{2,1,0:T(8,128)(2,1)S(1)}, u32[]{:S(2)}, u32[]{:S(2)}) async-start(bf16[4,256,256]{2,1,0:T(8,128)(2,1)} %bitcast.99), calls=%async_computation.1 | async-start | bytes 1048576 | tf_op jit(solution)/shard_map/all_to_all | solution.py:888
  146.1 1.5 collective-permute-start.16
  147.6 1.5 collective-permute-start.17
  149.1 7.8 %collective-permute-done.16.refs_17_ = bf16[352,512]{1,0:T(8,128)(2,1)S(1)} collective-permute-done((bf16[352,512]{1,0:T(8,128)(2,1)S(1)}, bf16[352,512]{1,0:T(8,128)(2,1)S(1)}, u32[]{:S(2)}, u32[]{:S(2)}) %collective-permute-start.16) | collective-permute-done | bytes 360480 | tf_op jit(solution)/shard_map/ppermute | solution.py:789
  156.9 1.2 collective-permute-done.17.refs_21_
  158.1 1.3 all-to-all-done.1.refs_0_.att_hbm
  159.4 1.9 collective-permute-done.18.refs_1_
  162.2 29.7 %feed.1 = (bf16[512,1024]{1,0:T(8,128)(2,1)}, f32[256,1024]{1,0:T(8,128)}, f32[256,1024]{1,0:T(8,128)}, f32[256,1024]{1,0:T(8,128)}, bf16[1024,1024]{1,0:T(8,128...) custom-call(bf16[4,256,256]{2,1,0:T(8,128)(2,1)} %copy-done.10, ...), custom_call_target="tpu_custom_call" | custom-call | flops 16106127360 | bytes 8388608 | tf_op jit(solution)/shard_map/feed/pallas_call | solution.py:308
  192.0 2.7 collective-permute-done.20.part_hbm
  194.8 1.5 collective-permute-start.21
  196.2 1.5 collective-permute-start.22
  197.7 6.3 %branch.1 = (bf16[256,1024]{1,0:T(8,128)(2,1)}, f32[256,1024]{1,0:T(8,128)}, bf16[4,256,256]{2,1,0:T(8,128)(2,1)}, bf16[512,1024]{1,0:T(8,128)(2,1)}, bf16[512,1024]{1,0:T(8,128)(2,1)}) custom-call(bf16[512,1024]{1,0:T(8,128)(2,1)} %copy-done.16, f32[256,1024]{1,0:T(8,128)} %get-tuple-element.114.outown_hbm, f32[256,1024]{1,0:T(8,128)} %get-tuple-element.115.gnown_hbm, ...), custom_call_target="tpu_custom_call" | custom-call | flops 1073741824 | bytes 8388608 | tf_op jit(solution)/shard_map/branch/pallas_call | solution.py:308
  204.0 3.5 all-to-all-start.2
  208.9 13.0 %all-to-all-done.2 = bf16[4,256,256]{2,1,0:T(8,128)(2,1)S(1)} async-done(((bf16[4,256,256]{2,1,0:T(8,128)(2,1)}), bf16[4,256,256]{2,1,0:T(8,128)(2,1)S(1)}, u32[]{:S(2)}, u32[]{:S(2)}) %all-to-all-start.2) | async-done | bytes 524320 | tf_op jit(solution)/shard_map/all_to_all | solution.py:906
  222.7 18.0 %attend_back.1 = (bf16[1024,768]{1,0:T(8,128)(2,1)}, bf16[1024,1024]{1,0:T(8,128)(2,1)}) custom-call(bf16[1024,768]{1,0:T(8,128)(2,1)} %get-tuple-element.120.mixed_hbm, bf16[1024,256]{1,0:T(8,128)(2,1)} %bitcast.90, f32[8,1024]{1,0:T(8,128)} %get-tuple-element.122.total_hbm, f32[1024,128]{1,0:T(8,128)} %get-tuple-element.244.refs_2_.cos_hbm, ...), custom_call_target="tpu_custom_call" | custom-call | bytes 8388608 | tf_op jit(solution)/shard_map/attend_back/pallas_call | solution.py:308
  240.8 3.3 collective-permute-done.23
  244.2 1.2 collective-permute-done.24
  245.4 1.7 add_convert_fusion.2
  247.1 1.6 collective-permute-start.28
  250.2 1.3 add_convert_fusion.7
  251.5 1.3 collective-permute-start.31
  252.8 1.3 add_convert_fusion.6
  254.2 1.1 collective-permute-start.32
  255.3 6.7 %project_weights.1 = (bf16[512,1792]{1,0:T(8,128)(2,1)}, bf16[512,1792]{1,0:T(8,128)(2,1)}) custom-call(bf16[1024,768]{1,0:T(8,128)(2,1)} %get-tuple-element.142.gm_hbm, bf16[1024,1024]{1,0:T(8,128)(2,1)} %get-tuple-element.143.normed_hbm, bf16[512,1024]{1,0:T(8,128)(2,1)} %get-tuple-element.144.okeep_hbm, bf16[512,1024]{1,0:T(8,128)(2,1)} %get-tuple-element.145.osend_hbm), custom_call_target="tpu_custom_call" | custom-call | flops 1073741824 | bytes 8388608 | tf_op jit(solution)/shard_map/project_weights/pallas_call | solution.py:308
  262.1 4.2 %collective-permute-done.28 = bf16[256,1408]{1,0:T(8,128)(2,1)S(1)} collective-permute-done((bf16[256,1408]{1,0:T(8,128)(2,1)S(1)}, bf16[256,1408]{1,0:T(8,128)(2,1)S(1)}, u32[]{:S(2)}, u32[]{:S(2)}) %collective-permute-start.28) | collective-permute-done | bytes 720928 | tf_op jit(solution)/shard_map/ppermute | solution.py:789
  266.5 1.8 collective-permute-done.29
  268.7 3.4 collective-permute-done.31
  272.2 1.7 collective-permute-done.32
  275.5 1.2 copy-done.13
  277.8 1.5 pad_maximum_fusion
  281.5 4.0 %all-to-all-start.4 = ((f32[32,8,128]{2,1,0:T(8,128)}), f32[32,8,128]{2,1,0:T(8,128)}, u32[]{:S(2)}, u32[]{:S(2)}) async-start(f32[32,8,128]{2,1,0:T(8,128)} %broadcast_in_dim.39), calls=%async_computation.6 | async-start | bytes 262144 | tf_op jit(solution)/shard_map/all_to_all | solution.py:947
  285.5 13.6 %collective-permute-done.26 = bf16[256,1792]{1,0:T(8,128)(2,1)} collective-permute-done((bf16[256,1792]{1,0:T(8,128)(2,1)S(1)}, bf16[256,1792]{1,0:T(8,128)(2,1)}, u32[]{:S(2)}, u32[]{:S(2)}) %collective-permute-start.26) | collective-permute-done | bytes 917536 | tf_op jit(solution)/shard_map/ppermute | solution.py:789
  299.1 1.4 add_convert_fusion.3
  300.6 1.8 collective-permute-start.27
  303.7 6.7 %collective-permute-done.27 = bf16[128,1792]{1,0:T(8,128)(2,1)S(1)} collective-permute-done((bf16[128,1792]{1,0:T(8,128)(2,1)S(1)}, bf16[128,1792]{1,0:T(8,128)(2,1)S(1)}, u32[]{:S(2)}, u32[]{:S(2)}) %collective-permute-start.27) | collective-permute-done | bytes 458784 | tf_op jit(solution)/shard_map/ppermute | solution.py:789
  311.3 3.6 %all-to-all-start.3 = ((bf16[4,32,1792]{2,1,0:T(8,128)(2,1)}), bf16[4,32,1792]{2,1,0:T(8,128)(2,1)S(1)}, u32[]{:S(2)}, u32[]{:S(2)}) async-start(bf16[4,32,1792]{2,1,0:T(8,128)(2,1)} %bitcast.26), calls=%async_computation.4 | async-start | bytes 917504 | tf_op jit(solution)/shard_map/all_to_all | solution.py:958
  314.9 1.5 fusion.3
  316.5 1.5 fusion.5
  318.0 1.4 add_bitcast_fusion
  319.3 19.1 %all-to-all-done.3 = bf16[4,32,1792]{2,1,0:T(8,128)(2,1)S(1)} async-done(((bf16[4,32,1792]{2,1,0:T(8,128)(2,1)}), bf16[4,32,1792]{2,1,0:T(8,128)(2,1)S(1)}, u32[]{:S(2)}, u32[]{:S(2)}) %all-to-all-start.3) | async-done | bytes 458784 | tf_op jit(solution)/shard_map/all_to_all | solution.py:958
  341.1 1.0 copy-done.3
  342.1 1.8 update.1
  (206 shorter events, 24.0 us)
Async XLA Ops:
  7.2 3.2 copy-start.27
  7.2 49.3 %all-gather.5.cloned.1.call-start = ((), (), s32[]{:S(2)}) async-start(), calls=%async_computation.8 | async-start | bytes 2129920 | tf_op jit(solution)/shard_map/all_gather | solution.py:850
  9.7 2.7 copy-start.2
  9.7 2.7 copy-start.7
  9.8 1.6 collective-permute-start
  12.2 104.6 %all-gather.3.cloned.1.call-start = ((), (), s32[]{:S(2)}) async-start(), calls=%async_computation.7 | async-start | bytes 3604480 | tf_op jit(solution)/shard_map/all_gather | solution.py:852
  14.3 17.7 %all-to-all-start = ((bf16[4,32,768]{2,1,0:T(8,128)(2,1)}), bf16[4,32,768]{2,1,0:T(8,128)(2,1)S(1)}, u32[]{:S(2)}, u32[]{:S(2)}) async-start(bf16[4,32,768]{2,1,0:T(8,128)(2,1)} %pad_maximum_fusion.10), calls=%async_computation | async-start | bytes 393216 | tf_op jit(solution)/shard_map/all_to_all | solution.py:859
  20.5 37.6 %collective-permute-start.1 = (bf16[256,1024]{1,0:T(8,128)(2,1)S(1)}, bf16[256,1024]{1,0:T(8,128)(2,1)}, u32[]{:S(2)}, u32[]{:S(2)}) collective-permute-start(bf16[256,1024]{1,0:T(8,128)(2,1)S(1)} %bitcast.80), channel_id=1, source_target_pairs={{0,4},{4,0},{8,12},{12,8},{16,20},{20,16},{24,28},{28,24},{1,5},{5... | collective-permute-start | bytes 1572872 | tf_op jit(solution)/shard_map/ppermute | solution.py:789
  20.5 37.6 %collective-permute-start.2 = (bf16[256,1024]{1,0:T(8,128)(2,1)}, bf16[256,1024]{1,0:T(8,128)(2,1)}, u32[]{:S(2)}, u32[]{:S(2)}) collective-permute-start(bf16[256,1024]{1,0:T(8,128)(2,1)} %bitcast.13.refs_4_.cot_hbm), channel_id=1, source_target_pairs={{0,4},{4,0},{8,12},{12,8},{16,20},{20,16},{24,28},{28,24},{1,5},{5... | collective-permute-start | bytes 1572872 | tf_op jit(solution)/shard_map/ppermute | solution.py:789
  32.0 5.7 %collective-permute-start.9 = (bf16[128,768]{1,0:T(8,128)(2,1)S(1)}, bf16[128,768]{1,0:T(8,128)(2,1)S(1)}, u32[]{:S(2)}, u32[]{:S(2)}) collective-permute-start(bf16[128,768]{1,0:T(8,128)(2,1)S(1)} %bitcast.84), channel_id=1, source_target_pairs={{0,8},{4,12},{8,0},{12,4},{16,24},{20,28},{24,16},{28,20},{1,9},{5... | collective-permute-start | bytes 589832 | tf_op jit(solution)/shard_map/ppermute | solution.py:789
  37.7 24.8 %collective-permute-start.10 = (bf16[256,768]{1,0:T(8,128)(2,1)S(1)}, bf16[256,768]{1,0:T(8,128)(2,1)S(1)}, u32[]{:S(2)}, u32[]{:S(2)}) collective-permute-start(bf16[256,768]{1,0:T(8,128)(2,1)S(1)} %pad_maximum_fusion.9), channel_id=1, source_target_pairs={{0,16},{4,20},{8,24},{12,28},{16,0},{20,4},{24,8},{28,12},{1,17},{... | collective-permute-start | bytes 1179656 | tf_op jit(solution)/shard_map/ppermute | solution.py:789
  59.4 3.2 copy-start.34
  59.4 22.1 %collective-permute-start.3 = (bf16[256,1664]{1,0:T(8,128)(2,1)}, bf16[256,1664]{1,0:T(8,128)(2,1)}, u32[]{:S(2)}, u32[]{:S(2)}) collective-permute-start(bf16[256,1664]{1,0:T(8,128)(2,1)} %get-tuple-element.94.refs_5_.refs_6_), channel_id=1, source_target_pairs={{0,8},{4,12},{8,0},{12,4},{16,24},{20,28},{24,16},{28,20},{1,9},{5... | collective-permute-start | bytes 2555912 | tf_op jit(solution)/shard_map/ppermute | solution.py:789
  60.9 22.2 %collective-permute-start.6 = (bf16[256,1664]{1,0:T(8,128)(2,1)}, bf16[256,1664]{1,0:T(8,128)(2,1)}, u32[]{:S(2)}, u32[]{:S(2)}) collective-permute-start(bf16[256,1664]{1,0:T(8,128)(2,1)} %get-tuple-element.98.refs_9_.refs_10_), channel_id=1, source_target_pairs={{0,16},{4,20},{8,24},{12,28},{16,0},{20,4},{24,8},{28,12},{1,17},{... | collective-permute-start | bytes 2555912 | tf_op jit(solution)/shard_map/ppermute | solution.py:789
  62.5 22.0 %collective-permute-start.11 = (bf16[512,768]{1,0:T(8,128)(2,1)S(1)}, bf16[512,768]{1,0:T(8,128)(2,1)S(1)}, u32[]{:S(2)}, u32[]{:S(2)}) collective-permute-start(bf16[512,768]{1,0:T(8,128)(2,1)S(1)} %pad_maximum_fusion.1), channel_id=1, source_target_pairs={{0,4},{4,0},{8,12},{12,8},{16,20},{20,16},{24,28},{28,24},{1,5},{5... | collective-permute-start | bytes 2359304 | tf_op jit(solution)/shard_map/ppermute | solution.py:789
  66.5 53.3 %collective-permute-start.4 = (bf16[256,1664]{1,0:T(8,128)(2,1)}, bf16[256,1664]{1,0:T(8,128)(2,1)}, u32[]{:S(2)}, u32[]{:S(2)}) collective-permute-start(bf16[256,1664]{1,0:T(8,128)(2,1)} %get-tuple-element.94.refs_5_.refs_6_), channel_id=1, source_target_pairs={{0,16},{4,20},{8,24},{12,28},{16,0},{20,4},{24,8},{28,12},{1,17},{... | collective-permute-start | bytes 2555912 | tf_op jit(solution)/shard_map/ppermute | solution.py:789
  67.1 54.2 %collective-permute-start.7 = (bf16[256,1664]{1,0:T(8,128)(2,1)}, bf16[256,1664]{1,0:T(8,128)(2,1)}, u32[]{:S(2)}, u32[]{:S(2)}) collective-permute-start(bf16[256,1664]{1,0:T(8,128)(2,1)} %get-tuple-element.98.refs_9_.refs_10_), channel_id=1, source_target_pairs={{0,8},{4,12},{8,0},{12,4},{16,24},{20,28},{24,16},{28,20},{1,9},{5... | collective-permute-start | bytes 2555912 | tf_op jit(solution)/shard_map/ppermute | solution.py:789
  81.6 40.3 %collective-permute-start.5 = (bf16[256,1664]{1,0:T(8,128)(2,1)}, bf16[256,1664]{1,0:T(8,128)(2,1)}, u32[]{:S(2)}, u32[]{:S(2)}) collective-permute-start(bf16[256,1664]{1,0:T(8,128)(2,1)} %collective-permute-done.3.refs_6_.refs_7_), channel_id=1, source_target_pairs={{0,16},{4,20},{8,24},{12,28},{16,0},{20,4},{24,8},{28,12},{1,17},{... | collective-permute-start | bytes 2555912 | tf_op jit(solution)/shard_map/ppermute | solution.py:789
  83.1 39.3 %collective-permute-start.8 = (bf16[256,1664]{1,0:T(8,128)(2,1)}, bf16[256,1664]{1,0:T(8,128)(2,1)}, u32[]{:S(2)}, u32[]{:S(2)}) collective-permute-start(bf16[256,1664]{1,0:T(8,128)(2,1)} %collective-permute-done.6.refs_10_.refs_11_), channel_id=1, source_target_pairs={{0,8},{4,12},{8,0},{12,4},{16,24},{20,28},{24,16},{28,20},{1,9},{5... | collective-permute-start | bytes 2555912 | tf_op jit(solution)/shard_map/ppermute | solution.py:789
  84.7 33.5 %copy-start.12 = (bf16[1024,768]{1,0:T(8,128)(2,1)}, bf16[1024,768]{1,0:T(8,128)(2,1)S(1)}, u32[]{:S(2)}) copy-start(bf16[1024,768]{1,0:T(8,128)(2,1)S(1)} %constant_dynamic-update-slice_fusion.refs_1_.weight_hbm) | copy-start | bytes 4718596
  118.2 22.5 %copy-start.20 = (bf16[352,512]{1,0:T(8,128)(2,1)}, bf16[352,512]{1,0:T(8,128)(2,1)S(1)}, u32[]{:S(2)}) copy-start(bf16[352,512]{1,0:T(8,128)(2,1)S(1)} %get-tuple-element.197.refs_18_) | copy-start | bytes 1081348
  118.2 22.5 %copy-start.21 = (bf16[352,512]{1,0:T(8,128)(2,1)}, bf16[352,512]{1,0:T(8,128)(2,1)S(1)}, u32[]{:S(2)}) copy-start(bf16[352,512]{1,0:T(8,128)(2,1)S(1)} %get-tuple-element.198.refs_14_) | copy-start | bytes 1081348
  118.2 22.5 %collective-permute-start.12 = (bf16[352,512]{1,0:T(8,128)(2,1)S(1)}, bf16[352,512]{1,0:T(8,128)(2,1)S(1)}, u32[]{:S(2)}, u32[]{:S(2)}) collective-permute-start(bf16[352,512]{1,0:T(8,128)(2,1)S(1)} %get-tuple-element.198.refs_14_), channel_id=1, source_target_pairs={{0,8},{4,12},{8,0},{12,4},{16,24},{20,28},{24,16},{28,20},{1,9},{5... | collective-permute-start | bytes 1081352 | tf_op jit(solution)/shard_map/ppermute | solution.py:789
  119.8 21.0 %collective-permute-start.13 = (bf16[352,512]{1,0:T(8,128)(2,1)S(1)}, bf16[352,512]{1,0:T(8,128)(2,1)S(1)}, u32[]{:S(2)}, u32[]{:S(2)}) collective-permute-start(bf16[352,512]{1,0:T(8,128)(2,1)S(1)} %get-tuple-element.198.refs_14_), channel_id=1, source_target_pairs={{0,16},{4,20},{8,24},{12,28},{16,0},{20,4},{24,8},{28,12},{1,17},{... | collective-permute-start | bytes 1081352 | tf_op jit(solution)/shard_map/ppermute | solution.py:789
  121.3 19.5 %collective-permute-start.14 = (bf16[352,512]{1,0:T(8,128)(2,1)S(1)}, bf16[352,512]{1,0:T(8,128)(2,1)S(1)}, u32[]{:S(2)}, u32[]{:S(2)}) collective-permute-start(bf16[352,512]{1,0:T(8,128)(2,1)S(1)} %get-tuple-element.197.refs_18_), channel_id=1, source_target_pairs={{0,16},{4,20},{8,24},{12,28},{16,0},{20,4},{24,8},{28,12},{1,17},{... | collective-permute-start | bytes 1081352 | tf_op jit(solution)/shard_map/ppermute | solution.py:789
  121.8 19.0 %collective-permute-start.15 = (bf16[352,512]{1,0:T(8,128)(2,1)S(1)}, bf16[352,512]{1,0:T(8,128)(2,1)S(1)}, u32[]{:S(2)}, u32[]{:S(2)}) collective-permute-start(bf16[352,512]{1,0:T(8,128)(2,1)S(1)} %get-tuple-element.197.refs_18_), channel_id=1, source_target_pairs={{0,8},{4,12},{8,0},{12,4},{16,24},{20,28},{24,16},{28,20},{1,9},{5... | collective-permute-start | bytes 1081352 | tf_op jit(solution)/shard_map/ppermute | solution.py:789
  140.8 20.6 %copy-start.39 = (bf16[352,512]{1,0:T(8,128)(2,1)}, bf16[352,512]{1,0:T(8,128)(2,1)S(1)}, u32[]{:S(2)}) copy-start(bf16[352,512]{1,0:T(8,128)(2,1)S(1)} %collective-permute-done.12.refs_15_) | copy-start | bytes 1081348
  140.8 17.3 %copy-start.41 = (bf16[352,512]{1,0:T(8,128)(2,1)}, bf16[352,512]{1,0:T(8,128)(2,1)S(1)}, u32[]{:S(2)}) copy-start(bf16[352,512]{1,0:T(8,128)(2,1)S(1)} %collective-permute-done.14.refs_19_) | copy-start | bytes 1081348
  142.4 17.1 %all-to-all-start.1 = ((bf16[4,256,256]{2,1,0:T(8,128)(2,1)}), bf16[4,256,256]{2,1,0:T(8,128)(2,1)S(1)}, u32[]{:S(2)}, u32[]{:S(2)}) async-start(bf16[4,256,256]{2,1,0:T(8,128)(2,1)} %bitcast.99), calls=%async_computation.1 | async-start | bytes 1048576 | tf_op jit(solution)/shard_map/all_to_all | solution.py:888
  146.0 13.4 %collective-permute-start.19 = (bf16[8,256,256]{2,1,0:T(8,128)(2,1)}, bf16[8,256,256]{2,1,0:T(8,128)(2,1)S(1)}, u32[]{:S(2)}, u32[]{:S(2)}) collective-permute-start(bf16[8,256,256]{2,1,0:T(8,128)(2,1)} %get-tuple-element.107), channel_id=1, source_target_pairs={{0,4},{4,0},{8,12},{12,8},{16,20},{20,16},{24,28},{28,24},{1,5},{5... | collective-permute-start | bytes 3145736 | tf_op jit(solution)/shard_map/ppermute | solution.py:789
  146.1 10.8 %collective-permute-start.16 = (bf16[352,512]{1,0:T(8,128)(2,1)S(1)}, bf16[352,512]{1,0:T(8,128)(2,1)S(1)}, u32[]{:S(2)}, u32[]{:S(2)}) collective-permute-start(bf16[352,512]{1,0:T(8,128)(2,1)S(1)} %collective-permute-done.12.refs_15_), channel_id=1, source_target_pairs={{0,16},{4,20},{8,24},{12,28},{16,0},{20,4},{24,8},{28,12},{1,17},{... | collective-permute-start | bytes 1081352 | tf_op jit(solution)/shard_map/ppermute | solution.py:789
  147.6 10.5 %collective-permute-start.17 = (bf16[352,512]{1,0:T(8,128)(2,1)S(1)}, bf16[352,512]{1,0:T(8,128)(2,1)S(1)}, u32[]{:S(2)}, u32[]{:S(2)}) collective-permute-start(bf16[352,512]{1,0:T(8,128)(2,1)S(1)} %collective-permute-done.14.refs_19_), channel_id=1, source_target_pairs={{0,8},{4,12},{8,0},{12,4},{16,24},{20,28},{24,16},{28,20},{1,9},{5... | collective-permute-start | bytes 1081352 | tf_op jit(solution)/shard_map/ppermute | solution.py:789
  156.9 4.4 %copy-start.43 = (bf16[352,512]{1,0:T(8,128)(2,1)}, bf16[352,512]{1,0:T(8,128)(2,1)S(1)}, u32[]{:S(2)}) copy-start(bf16[352,512]{1,0:T(8,128)(2,1)S(1)} %collective-permute-done.16.refs_17_) | copy-start | bytes 1081348
  158.1 3.2 copy-start.44
  159.4 1.9 collective-permute-start.18
  191.8 2.9 collective-permute-start.20
  194.8 2.9 copy-start.16
  194.8 50.6 %collective-permute-start.21 = (bf16[512,1408]{1,0:T(8,128)(2,1)}, bf16[512,1408]{1,0:T(8,128)(2,1)}, u32[]{:S(2)}, u32[]{:S(2)}) collective-permute-start(bf16[512,1408]{1,0:T(8,128)(2,1)} %get-tuple-element.128), channel_id=1, source_target_pairs={{0,8},{4,12},{8,0},{12,4},{16,24},{20,28},{24,16},{28,20},{1,9},{5... | collective-permute-start | bytes 4325384 | tf_op jit(solution)/shard_map/ppermute | solution.py:789
  196.2 49.1 %collective-permute-start.22 = (bf16[512,1408]{1,0:T(8,128)(2,1)}, bf16[512,1408]{1,0:T(8,128)(2,1)S(1)}, u32[]{:S(2)}, u32[]{:S(2)}) collective-permute-start(bf16[512,1408]{1,0:T(8,128)(2,1)} %get-tuple-element.129), channel_id=1, source_target_pairs={{0,16},{4,20},{8,24},{12,28},{16,0},{20,4},{24,8},{28,12},{1,17},{... | collective-permute-start | bytes 4325384 | tf_op jit(solution)/shard_map/ppermute | solution.py:789
  204.0 18.0 %all-to-all-start.2 = ((bf16[4,256,256]{2,1,0:T(8,128)(2,1)}), bf16[4,256,256]{2,1,0:T(8,128)(2,1)S(1)}, u32[]{:S(2)}, u32[]{:S(2)}) async-start(bf16[4,256,256]{2,1,0:T(8,128)(2,1)} %get-tuple-element.121), calls=%async_computation.2 | async-start | bytes 1048576 | tf_op jit(solution)/shard_map/all_to_all | solution.py:906
  207.5 107.5 %reduce-scatter.3.cloned.1.call-start = ((), (), s32[]{:S(2)}) async-start(), calls=%async_computation.9 | async-start | bytes 2621440 | tf_op jit(solution)/shard_map/reduce_scatter | solution.py:951
  207.7 36.4 %collective-permute-start.23 = (bf16[704,512]{1,0:T(8,128)(2,1)}, bf16[704,512]{1,0:T(8,128)(2,1)}, u32[]{:S(2)}, u32[]{:S(2)}) collective-permute-start(bf16[704,512]{1,0:T(8,128)(2,1)} %get-tuple-element.130), channel_id=1, source_target_pairs={{0,8},{4,12},{8,0},{12,4},{16,24},{20,28},{24,16},{28,20},{1,9},{5... | collective-permute-start | bytes 2162696 | tf_op jit(solution)/shard_map/ppermute | solution.py:789
  208.4 37.0 %collective-permute-start.24 = (bf16[704,512]{1,0:T(8,128)(2,1)}, bf16[704,512]{1,0:T(8,128)(2,1)}, u32[]{:S(2)}, u32[]{:S(2)}) collective-permute-start(bf16[704,512]{1,0:T(8,128)(2,1)} %get-tuple-element.131), channel_id=1, source_target_pairs={{0,16},{4,20},{8,24},{12,28},{16,0},{20,4},{24,8},{28,12},{1,17},{... | collective-permute-start | bytes 2162696 | tf_op jit(solution)/shard_map/ppermute | solution.py:789
  240.7 4.6 %copy-start.15 = (bf16[512,1408]{1,0:T(8,128)(2,1)S(1)}, bf16[512,1408]{1,0:T(8,128)(2,1)}, u32[]{:S(2)}) copy-start(bf16[512,1408]{1,0:T(8,128)(2,1)} %get-tuple-element.134) | copy-start | bytes 4325380
  240.8 100.3 %reduce-scatter.5.cloned.1.call-start = ((), (), s32[]{:S(2)}) async-start(), calls=%async_computation.10 | async-start | bytes 2785280 | tf_op jit(solution)/shard_map/reduce_scatter | solution.py:945
  247.1 19.1 %collective-permute-start.28 = (bf16[256,1408]{1,0:T(8,128)(2,1)S(1)}, bf16[256,1408]{1,0:T(8,128)(2,1)S(1)}, u32[]{:S(2)}, u32[]{:S(2)}) collective-permute-start(bf16[256,1408]{1,0:T(8,128)(2,1)S(1)} %slice.310), channel_id=1, source_target_pairs={{0,16},{4,20},{8,24},{12,28},{16,0},{20,4},{24,8},{28,12},{1,17},{... | collective-permute-start | bytes 2162696 | tf_op jit(solution)/shard_map/ppermute | solution.py:789
  249.2 3.7 %copy-start.18 = (bf16[704,512]{1,0:T(8,128)(2,1)S(1)}, bf16[704,512]{1,0:T(8,128)(2,1)}, u32[]{:S(2)}) copy-start(bf16[704,512]{1,0:T(8,128)(2,1)} %get-tuple-element.140) | copy-start | bytes 2162692
  249.2 19.1 %collective-permute-start.29 = (bf16[256,1408]{1,0:T(8,128)(2,1)S(1)}, bf16[256,1408]{1,0:T(8,128)(2,1)S(1)}, u32[]{:S(2)}, u32[]{:S(2)}) collective-permute-start(bf16[256,1408]{1,0:T(8,128)(2,1)S(1)} %slice.312), channel_id=1, source_target_pairs={{0,8},{4,12},{8,0},{12,4},{16,24},{20,28},{24,16},{28,20},{1,9},{5... | collective-permute-start | bytes 2162696 | tf_op jit(solution)/shard_map/ppermute | solution.py:789
  251.5 20.6 %collective-permute-start.31 = (bf16[352,512]{1,0:T(8,128)(2,1)S(1)}, bf16[352,512]{1,0:T(8,128)(2,1)S(1)}, u32[]{:S(2)}, u32[]{:S(2)}) collective-permute-start(bf16[352,512]{1,0:T(8,128)(2,1)S(1)} %slice.314), channel_id=1, source_target_pairs={{0,16},{4,20},{8,24},{12,28},{16,0},{20,4},{24,8},{28,12},{1,17},{... | collective-permute-start | bytes 1081352 | tf_op jit(solution)/shard_map/ppermute | solution.py:789
  254.2 19.8 %collective-permute-start.32 = (bf16[352,512]{1,0:T(8,128)(2,1)S(1)}, bf16[352,512]{1,0:T(8,128)(2,1)S(1)}, u32[]{:S(2)}, u32[]{:S(2)}) collective-permute-start(bf16[352,512]{1,0:T(8,128)(2,1)S(1)} %slice.316), channel_id=1, source_target_pairs={{0,8},{4,12},{8,0},{12,4},{16,24},{20,28},{24,16},{28,20},{1,9},{5... | collective-permute-start | bytes 1081352 | tf_op jit(solution)/shard_map/ppermute | solution.py:789
  262.0 13.5 %collective-permute-start.25 = (bf16[512,1792]{1,0:T(8,128)(2,1)}, bf16[512,1792]{1,0:T(8,128)(2,1)S(1)}, u32[]{:S(2)}, u32[]{:S(2)}) collective-permute-start(bf16[512,1792]{1,0:T(8,128)(2,1)} %get-tuple-element.147), channel_id=1, source_target_pairs={{0,4},{4,0},{8,12},{12,8},{16,20},{20,16},{24,28},{28,24},{1,5},{5... | collective-permute-start | bytes 5505032 | tf_op jit(solution)/shard_map/ppermute | solution.py:789
  268.6 6.7 %collective-permute-start.30 = (bf16[128,2816]{1,0:T(8,128)(2,1)S(1)}, bf16[128,2816]{1,0:T(8,128)(2,1)S(1)}, u32[]{:S(2)}, u32[]{:S(2)}) collective-permute-start(bf16[128,2816]{1,0:T(8,128)(2,1)S(1)} %pad_maximum_fusion.3), channel_id=1, source_target_pairs={{0,4},{4,0},{8,12},{12,8},{16,20},{20,16},{24,28},{28,24},{1,5},{5... | collective-permute-start | bytes 2162696 | tf_op jit(solution)/shard_map/ppermute | solution.py:789
  277.3 21.8 %collective-permute-start.26 = (bf16[256,1792]{1,0:T(8,128)(2,1)S(1)}, bf16[256,1792]{1,0:T(8,128)(2,1)}, u32[]{:S(2)}, u32[]{:S(2)}) collective-permute-start(bf16[256,1792]{1,0:T(8,128)(2,1)S(1)} %slice.290), channel_id=1, source_target_pairs={{0,8},{4,12},{8,0},{12,4},{16,24},{20,28},{24,16},{28,20},{1,9},{5... | collective-permute-start | bytes 2752520 | tf_op jit(solution)/shard_map/ppermute | solution.py:789
  281.5 20.9 %all-to-all-start.4 = ((f32[32,8,128]{2,1,0:T(8,128)}), f32[32,8,128]{2,1,0:T(8,128)}, u32[]{:S(2)}, u32[]{:S(2)}) async-start(f32[32,8,128]{2,1,0:T(8,128)} %broadcast_in_dim.39), calls=%async_computation.6 | async-start | bytes 262144 | tf_op jit(solution)/shard_map/all_to_all | solution.py:947
  300.6 9.8 %collective-permute-start.27 = (bf16[128,1792]{1,0:T(8,128)(2,1)S(1)}, bf16[128,1792]{1,0:T(8,128)(2,1)S(1)}, u32[]{:S(2)}, u32[]{:S(2)}) collective-permute-start(bf16[128,1792]{1,0:T(8,128)(2,1)S(1)} %slice.292), channel_id=1, source_target_pairs={{0,16},{4,20},{8,24},{12,28},{16,0},{20,4},{24,8},{28,12},{1,17},{... | collective-permute-start | bytes 1376264 | tf_op jit(solution)/shard_map/ppermute | solution.py:789
  303.5 12.9 %copy-start.35 = (f32[16]{0:T(128)}, f32[16]{0:T(128)S(1)}, u32[]{:S(2)}) copy-start(f32[16]{0:T(128)S(1)} %reshape_squeeze.3) | copy-start | bytes 196
  303.6 12.9 %copy-start.36 = (f32[16]{0:T(128)}, f32[16]{0:T(128)S(1)}, u32[]{:S(2)}) copy-start(f32[16]{0:T(128)S(1)} %divide_sqrt_fusion) | copy-start | bytes 196
  311.3 6.7 %copy-start.17 = (f32[256,1024]{1,0:T(8,128)S(1)}, f32[256,1024]{1,0:T(8,128)}, u32[]{:S(2)}) copy-start(f32[256,1024]{1,0:T(8,128)} %get-tuple-element.119) | copy-start | bytes 3145732
  311.3 27.1 %all-to-all-start.3 = ((bf16[4,32,1792]{2,1,0:T(8,128)(2,1)}), bf16[4,32,1792]{2,1,0:T(8,128)(2,1)S(1)}, u32[]{:S(2)}, u32[]{:S(2)}) async-start(bf16[4,32,1792]{2,1,0:T(8,128)(2,1)} %bitcast.26), calls=%async_computation.4 | async-start | bytes 917504 | tf_op jit(solution)/shard_map/all_to_all | solution.py:958
  314.9 3.0 copy-start.9
  319.3 19.3 %copy-start.31 = (f32[32,1024]{1,0:T(8,128)S(1)}, f32[32,1024]{1,0:T(8,128)}, u32[]{:S(2)}) copy-start(f32[32,1024]{1,0:T(8,128)} %param.31) | copy-start | bytes 393220
  319.3 20.0 %copy-start.28 = (bf16[32,1024]{1,0:T(8,128)(2,1)S(1)}, bf16[32,1024]{1,0:T(8,128)(2,1)}, u32[]{:S(2)}) copy-start(bf16[32,1024]{1,0:T(8,128)(2,1)} %param.25) | copy-start | bytes 196612
  319.3 20.0 %copy-start.32 = (f32[32,1024]{1,0:T(8,128)S(1)}, f32[32,1024]{1,0:T(8,128)}, u32[]{:S(2)}) copy-start(f32[32,1024]{1,0:T(8,128)} %param.32) | copy-start | bytes 393220
  338.6 2.5 copy-start
  (23 other events, 36.9 us)
Sparse Core Ops, SparseCore 0:
  12.4 44.0 all-gather.4
  58.6 58.1 all-gather.2
  240.9 41.4 reduce-scatter.2
  284.7 52.5 reduce-scatter.4

commit v7 on v6

--- a/solution.py
+++ b/solution.py
@@ -564,10 +564,10 @@
 def feed_kernel(*refs):
     att_hbm, attp_hbm, act_hbm, actp_hbm, cot_hbm, cotp_hbm = refs[:6]
     a_in, b_in, da_in, db_in, outs = refs[6:10], refs[10:14], refs[14:18], refs[18:22], refs[22]
-    part_hbm, outown_hbm, gnown_hbm, res_hbm, wo_hbm = refs[23:28]
-    (ga_keep, ga_send, gb_keep, gb_send, gda_keep, gda_send, gdb_keep, gdb_send) = refs[28:36]
-    (wg, wu, wd, wo, att, act, n2, n2t, cot, res_ref, out_acc, gn_acc, part, dg, du, dd,
-     sems, osem, tsem) = refs[36:]
+    part_hbm, gnown_hbm, res_hbm, wo_hbm, h_hbm = refs[23:28]
+    ga_keep, ga_send, gb_keep, gb_send = refs[28:32]
+    (wg, wu, wd, wo, att, act, n2, n2t, cot, res_ref, gn_acc, part, dg, du, hidden,
+     sems, osem, tsem) = refs[32:]
     me = lax.axis_index("dp")
     core = me % 2
     yx = me // 2
@@ -601,7 +601,6 @@
     wg[:, FF2:FFP] = jnp.zeros((1024, FFP - FF2), bf)
     wu[:, FF2:FFP] = jnp.zeros((1024, FFP - FF2), bf)
     wd[FF2:FFP, :] = jnp.zeros((FFP - FF2, 1024), bf)
-    out_acc[...] = jnp.zeros_like(out_acc)
     gn_acc[...] = jnp.zeros_like(gn_acc)
     wait_all(small)
     ogo = Copies(osem)
@@ -628,6 +627,7 @@
             for k, src, dst, slot in ((0, dg, ga_send if fx else ga_keep, fy), (1, du, gb_send if fy else gb_keep, fx)):
                 copies.append(pltpu.make_async_copy(
                     src.at[rows, cols], dst.at[pl.ds(256 * slot, 256), cols], tsem.at[t, 2 * q + k]))
+        copies.append(pltpu.make_async_copy(hidden.at[:, cols], h_hbm.at[:, cols], tsem.at[t, 8]))
         return copies
 
     last = FFP // 256 - 1
@@ -640,7 +640,7 @@
         gh = dot(cot[...], wd[cols, :], NT)
         sig = 1.0 / (1.0 + jnp.exp(-g))
         silu = g * sig
-        h = (silu * u).astype(bf)
+        hidden[:, cols] = (silu * u).astype(bf)
         gu = (gh * silu).astype(bf)
         gg = (gh * u * (sig + silu * (1.0 - sig))).astype(bf)
         dg[:, cols] = dot(n2t[...], gg, NN).astype(bf)
@@ -651,23 +651,14 @@
             for copy in tile_copies(t, 256):
                 copy.start()
 
-        dd[cols, :] = dot(h, cot[...], TN).astype(bf)
         gn_acc[...] += dot(gg, wg[:, cols], NT) + dot(gu, wu[:, cols], NT)
-        out_acc[...] += dot(h, wd[cols, :], NN)
 
     ends = tile_copies(last, FF2 - 256 * last)
     for copy in ends:
         copy.start()
-    part[0:256, :] = out_acc[256:512, :].astype(bf)
-    part[256:512, :] = gn_acc[256:512, :].astype(bf)
+    part[...] = gn_acc[256:512, :].astype(bf)
     done.append(ogo.start(part, part_hbm))
     done.append(ogo.start(gn_acc.at[pl.ds(0, 256)], gnown_hbm))
-    done.append(ogo.start(out_acc.at[pl.ds(0, 256)], outown_hbm))
-    for q in range(4):
-        fx, fy = FLIPS_A[q]
-        rows = aligned(yx ^ (fx + 2 * fy), 352)
-        done.append(ogo.start(dd.at[rows, pl.ds(0, 512)], (gda_send if fx else gda_keep).at[pl.ds(352 * fy, 352)]))
-        done.append(ogo.start(dd.at[rows, pl.ds(512, 512)], (gdb_send if fy else gdb_keep).at[pl.ds(352 * fx, 352)]))
     for t in range(last):
         wait_all(tile_copies(t, 256))
     wait_all(ends)
@@ -678,30 +669,90 @@
     big = [((1024, FFP), bf), ((1024, FFP), bf), ((FFP, 1024), bf)]
     return call(
         feed_kernel, "feed",
-        [((512, 1024), bf), ((256, 1024), f32), ((256, 1024), f32), ((256, 1024), f32), ((1024, 1024), bf)]
-        + [((512, FF2), bf)] * 4 + [((704, 512), bf)] * 4,
+        [((256, 1024), bf), ((256, 1024), f32), ((256, 1024), f32), ((1024, 1024), bf), ((512, FF2), bf)]
+        + [((512, FF2), bf)] * 4,
         big + [((1024, 1024), bf), ((512, 1024), bf), ((512, 1024), bf), ((512, 1024), bf), ((1024, 512), bf),
-               ((512, 1024), bf), ((512, 1024), f32), ((512, 1024), f32), ((512, 1024), f32), ((512, 1024), bf)] + big,
-        [68, 13, (6, 8)], 15, (att, attp, act, actp, cot, cotp, *a, *b, *da, *db, outs), 50,
-    )
-
-
-def branch_kernel(part_hbm, outown_hbm, gnown_hbm, res_hbm, cot_hbm, att_hbm, wo_hbm,
-                  layer_hbm, gres_hbm, gatt_hbm, keep_hbm, send_hbm,
-                  part, outown, gnown, res_ref, cot, att, wo, layer, gres_ref, gatt, gw, sems):
+               ((512, 1024), bf), ((512, 1024), f32), ((512, 1024), f32), ((256, 1024), bf)]
+        + big[:2] + [((512, FFP), bf)],
+        [68, 4, (6, 9)], 12, (att, attp, act, actp, cot, cotp, *a, *b, *da, *db, outs), 50,
+    )
+
+
+def finish_kernel(*refs):
+    h_hbm, cot_hbm, cotp_hbm, att_hbm, gres_hbm = refs[:5]
+    da_in, db_in = refs[5:9], refs[9:13]
+    part_hbm, own_hbm, gda_keep, gda_send, gdb_keep, gdb_send, keep_hbm, send_hbm = refs[13:21]
+    hidden, cot, att, gres, wd, out, part, dd, gw, sems = refs[21:]
     me = lax.axis_index("dp")
     core = me % 2
     yx = me // 2
     go = Copies(sems)
+    first = [go.start(h_hbm, hidden), go.start(cot_hbm, cot.at[pl.ds(0, 256)]),
+             go.start(cotp_hbm, cot.at[pl.ds(256, 256)])]
+    second = []
+    for p in range(4):
+        (ax, ay), (bx, by) = FLIPS_A[p], FLIPS_B[p]
+        second.append(go.start(da_in[p], wd.at[aligned(yx ^ (ax + 2 * ay), 352), pl.ds(0, 512)]))
+        second.append(go.start(db_in[p], wd.at[aligned(yx ^ (bx + 2 * by), 352), pl.ds(512, 512)]))
+    third = [go.start(gres_hbm, gres)]
+    third += [go.start(att_hbm.at[i], att.at[:, pl.ds(256 * i, 256)]) for i in range(4)]
+    wait_all(first)
+    done = []
+
+    @pl.loop(0, FF2 // 128)
+    def _(t):
+        cols = aligned(t, 128)
+        dd[cols, :] = dot(hidden[:, cols], cot[...], TN).astype(bf)
+
+    for q in range(4):
+        fx, fy = FLIPS_A[q]
+        rows = aligned(yx ^ (fx + 2 * fy), 352)
+        done.append(go.start(dd.at[rows, pl.ds(0, 512)], (gda_send if fx else gda_keep).at[pl.ds(352 * fy, 352)]))
+        done.append(go.start(dd.at[rows, pl.ds(512, 512)], (gdb_send if fy else gdb_keep).at[pl.ds(352 * fx, 352)]))
+    wait_all(second)
+    part[...] = dot(hidden[256:512, :], wd[...], NN).astype(bf)
+    done.append(go.start(part, part_hbm))
+    out[...] = dot(hidden[0:256, :], wd[...], NN)
+    done.append(go.start(out, own_hbm))
+    wait_all(third)
+    low = gres[...].astype(bf)
+
+    @pl.loop(0, 4)
+    def _(i):
+        cols = aligned(i, 256)
+        gw[cols, :] = dot(att[:, cols], low, TN).astype(bf)
+
+    for q in range(4):
+        fx, fy = FLIPS_A[q]
+        j = yx ^ (fx + 2 * fy)
+        for dst, c in ((keep_hbm, core), (send_hbm, 1 - core)):
+            done.append(go.start(gw.at[aligned(j * 2 + c, 128)], dst.at[pl.ds(128 * (2 * fx + fy), 128)]))
+    wait_all(done)
+
+
+def finish(hidden, cot, cotp, att, gres, da, db):
+    tall = ((256, 1024), f32)
+    low = ((256, 1024), bf)
+    half = ((512, 1024), bf)
+    return call(
+        finish_kernel, "finish",
+        [low, tall] + [((704, 512), bf)] * 4 + [half] * 2,
+        [((512, FF2), bf), half, low, tall, ((FF2, 1024), bf), tall, low, ((FF2, 1024), bf), ((1024, 1024), bf)],
+        [34], 60, (hidden, cot, cotp, att, gres, *da, *db), 32,
+    )
+
+
+def branch_kernel(part_hbm, gnown_hbm, res_hbm, cot_hbm, wo_hbm, gres_hbm, gatt_hbm,
+                  part, gnown, res_ref, cot, wo, gres_ref, gatt, sems):
+    go = Copies(sems)
     first = [
         go.start(a, b)
-        for a, b in ((part_hbm, part), (gnown_hbm, gnown), (res_hbm, res_ref), (cot_hbm, cot))
+        for a, b in ((res_hbm, res_ref), (gnown_hbm, gnown), (part_hbm, part), (cot_hbm, cot))
     ]
-    late = [go.start(wo_hbm, wo), go.start(outown_hbm, outown)]
-    late += [go.start(att_hbm.at[i], att.at[:, pl.ds(256 * i, 256)]) for i in range(4)]
+    late = go.start(wo_hbm, wo)
     wait_all(first)
     res = res_ref[...]
-    g = gnown[...] + part[256:512, :].astype(f32)
+    g = gnown[...] + part[...].astype(f32)
     c = res - jnp.mean(res, axis=-1, keepdims=True)
     r = lax.rsqrt(jnp.mean(c * c, axis=-1, keepdims=True) + NORM_EPS)
     xh = c * r
@@ -709,33 +760,22 @@
     gres = cot[...].astype(f32) + d
     gres_ref[...] = gres
     low = gres.astype(bf)
-    wait_all(late)
     done = [go.start(gres_ref, gres_hbm)]
+    late.wait()
     ga = dot(low, wo[...], NT).astype(bf)
     for z in range(4):
         gatt[z] = ga[:, 256 * z : 256 * z + 256]
     done.append(go.start(gatt, gatt_hbm))
-    layer[...] = (res + (outown[...] + part[0:256, :].astype(f32))).astype(bf)
-    done.append(go.start(layer, layer_hbm))
-    gw[...] = dot(att[...], low, TN).astype(bf)
-    for q in range(4):
-        fx, fy = FLIPS_A[q]
-        j = yx ^ (fx + 2 * fy)
-        for dst, c in ((keep_hbm, core), (send_hbm, 1 - core)):
-            rows = aligned(j * 2 + c, 128)
-            done.append(go.start(gw.at[rows], dst.at[pl.ds(128 * (2 * fx + fy), 128)]))
     wait_all(done)
 
 
-def branch(part, outown, gnown, res, cot, att, wo):
+def branch(part, gnown, res, cot, wo):
     tall = ((256, 1024), f32)
     low = ((256, 1024), bf)
     return call(
-        branch_kernel, "branch",
-        [low, tall, ((4, 256, 256), bf), ((512, 1024), bf), ((512, 1024), bf)],
-        [((512, 1024), bf), tall, tall, tall, low, low, ((1024, 1024), bf), low, tall, ((4, 256, 256), bf),
-         ((1024, 1024), bf)],
-        [21], 1, (part, outown, gnown, res, cot, att, wo), 32,
+        branch_kernel, "branch", [tall, ((4, 256, 256), bf)],
+        [low, tall, tall, low, ((1024, 1024), bf), tall, ((4, 256, 256), bf)],
+        [7], 1, (part, gnown, res, cot, wo), 32,
     )
 
 
@@ -887,39 +927,35 @@
     attended = tie(attended, *piece_da[1:3], *piece_db[1:3])
     attended = lax.all_to_all(attended.reshape(4, span, 256), "ctx", 0, 0, tiled=True)
     attended_other = swap(tie(attended, piece_da[3], piece_db[3]), 1)
-    (part, out_own, back_own, residual, full_out, *grads) = feed(
+    part, back_own, residual, full_out, hidden, ga_keep, ga_send, gb_keep, gb_send = feed(
         attended, attended_other, act, act_other, cot, cot_other,
         piece_a, piece_b, piece_da, piece_db, outs,
     )
-    ga_keep, ga_send, gb_keep, gb_send, gda_keep, gda_send, gdb_keep, gdb_send = grads
     part = swap(part, 1)
-    ga_send, gb_send, gda_send, gdb_send, part = lax.optimization_barrier(
-        (ga_send, gb_send, gda_send, gdb_send, part)
+    ga_send, gb_send, part = lax.optimization_barrier((ga_send, gb_send, part))
+    ga_other = swap(ga_send, 2)
+    gb_other = swap(gb_send, 4)
+    grad_residual, grad_attended = branch(part, back_own, residual, cot, full_out)
+    grad_attended = lax.all_to_all(grad_attended, "ctx", 0, 0, tiled=True).reshape(length, 256)
+    (out_part, out_own, gda_keep, gda_send, gdb_keep, gdb_send, go_keep, go_send) = finish(
+        hidden, cot, cot_other, attended, grad_residual, piece_da, piece_db
     )
     gda_other = swap(gda_send, 2)
     gdb_other = swap(gdb_send, 4)
-    ga_other = swap(ga_send, 2)
-    gb_other = swap(gb_send, 4)
-    layer_out, grad_residual, grad_attended, go_keep, go_send = branch(
-        part, out_own, back_own, residual, cot, attended, full_out
-    )
-    grad_attended = lax.all_to_all(grad_attended, "ctx", 0, 0, tiled=True).reshape(length, 256)
+    grad_attended, out_part = lax.optimization_barrier((grad_attended, out_part))
+    layer_out = (residual + (out_own + swap(out_part, 1).astype(f32))).astype(bf)
     grad_mixed, grad_normed = attend_back(
         mixed, grad_attended, totals, cosine, sine, ids, heads_rel
     )
-    (ga_keep, gb_keep, gda_keep, gdb_keep, ga_other, gb_other, gda_other, gdb_other, grad_mixed) = (
-        lax.optimization_barrier(
-            (ga_keep, gb_keep, gda_keep, gdb_keep, ga_other, gb_other, gda_other, gdb_other,
-             grad_mixed)
-        )
+    grad_mixed = tie(grad_mixed, ga_other, gb_other)
+    grad_heads = project_weights(grad_mixed, normed, go_keep, go_send)
+    ga_keep, gb_keep, gda_keep, gdb_keep, grad_heads = lax.optimization_barrier(
+        (ga_keep, gb_keep, gda_keep, gdb_keep, grad_heads)
     )
     grad_a = add_low(ga_keep, ga_other)
     grad_b = add_low(gb_keep, gb_other)
     grad_da = add_low(gda_keep, gda_other)
     grad_db = add_low(gdb_keep, gdb_other)
-    grad_heads = project_weights(
-        tie(grad_mixed, grad_a, grad_b, grad_da, grad_db), normed, go_keep, go_send
-    )
     grad_a = add_low(grad_a[:256], swap(grad_a[256:], 4))
     grad_b = add_low(grad_b[:256], swap(grad_b[256:], 2))
     grad_da = add_low(grad_da[:352], swap(grad_da[352:], 4))

time: 351 us -> 349 us (level)
  waiting for transfers between devices: 162 us -> 152 us
    all_to_all x1, waiting for transfers between devices: 13 us -> 0.41 us  [fast_device(): lax.all_to_all(grad_attended, 'ctx', 0, 0, tiled=True).reshape(length, 256)]
    ppermute x33 -> x34, waiting for transfers between devices: 68.6 us -> 73.3 us  [swap(): return lax.ppermute(array, 'dp', [(i, i ^ bit) for i in range(8)])]
    pallas_call x5 -> x6, Pallas kernels: 78.4 us -> 81.9 us  [call(): pl.pallas_call(kernel, out_shape=tuple((pltpu.HBM(*o) for o in outs)), in...]
    ppermute x33 -> x34, starting transfers between devices: 30.1 us -> 30.1 us  [swap(): return lax.ppermute(array, 'dp', [(i, i ^ bit) for i in range(8)])]
  transfers between devices with their start and end apart: 42 -> 43, of which waited for: 21 -> 20; matrix products, arithmetic and copies ran while one was open for 9% -> 9% of each run, Pallas kernels for 14% -> 15%
where the time goes in v7:
time: 349 us; the launch traced here: 348 us
  waiting for transfers between devices  152 us (44%)
  Pallas kernels  83.7 us (24%)
  starting transfers between devices  54.2 us (16%)
  other arithmetic  25.4 us (7%)
  local copies, waits for them, and re-layouts  16.5 us (5%)
  between operations  16.2 us (5%)
    pallas_call x6, Pallas kernels, call(): pl.pallas_call(kernel, out_shape=tuple((pltpu.HBM(*o) for o in outs)), in...  81.9 us
    ppermute x34, waiting for transfers between devices, swap(): return lax.ppermute(array, 'dp', [(i, i ^ bit) for i in range(8)])  73.3 us
    all_gather x1, waiting for transfers between devices, fast_device(): rows_all = lax.all_gather(padded, 'ctx', axis=0, tiled=True)  32.2 us
    ppermute x34, starting transfers between devices, swap(): return lax.ppermute(array, 'dp', [(i, i ^ bit) for i in range(8)])  30.1 us
    all_gather x1, waiting for transfers between devices, fast_device(): lax.all_gather(wide, 'ctx', axis=2, tiled=True).reshape(2, 256, FF2 + 256)  17.2 us
    all_to_all x1, waiting for transfers between devices, fast_device(): lax.all_to_all(grad_heads.reshape(4, 32, 768 + width), 'ctx', 0, 0, tiled...  16.8 us
    all_to_all x1, waiting for transfers between devices, fast_device(): heads = lax.all_to_all(heads, 'ctx', 0, 0, tiled=True).reshape(128, 768)  11 us
  transfers between devices with their start and end apart: 43, of which 20 were waited for; matrix products, arithmetic and copies ran while one was open for 9% of the time, Pallas kernels for 15%

profile of v7, /device:TPU:0, one launch (start us, length us, event | category | flops | bytes accessed | tf_op | source)
XLA Modules:
  0.0 348.0 jit_solution(8216697260770008647)
XLA Ops:
  7.3 1.0 fusion.15
  8.3 1.0 fusion.16
  12.4 1.0 maximum_maximum_fusion
  14.3 6.2 %all-to-all-start = ((bf16[4,32,768]{2,1,0:T(8,128)(2,1)}), bf16[4,32,768]{2,1,0:T(8,128)(2,1)S(1)}, u32[]{:S(2)}, u32[]{:S(2)}) async-start(bf16[4,32,768]{2,1,0:T(8,128)(2,1)} %pad_maximum_fusion.10), calls=%async_computation | async-start | bytes 393216 | tf_op jit(solution)/shard_map/all_to_all | solution.py:899
  21.0 11.0 %all-to-all-done = bf16[4,32,768]{2,1,0:T(8,128)(2,1)S(1)} async-done(((bf16[4,32,768]{2,1,0:T(8,128)(2,1)}), bf16[4,32,768]{2,1,0:T(8,128)(2,1)S(1)}, u32[]{:S(2)}, u32[]{:S(2)}) %all-to-all-start) | async-done | bytes 196640 | tf_op jit(solution)/shard_map/all_to_all | solution.py:899
  32.0 1.5 collective-permute-start.9
  33.5 4.1 %collective-permute-done.9 = bf16[128,768]{1,0:T(8,128)(2,1)S(1)} collective-permute-done((bf16[128,768]{1,0:T(8,128)(2,1)S(1)}, bf16[128,768]{1,0:T(8,128)(2,1)S(1)}, u32[]{:S(2)}, u32[]{:S(2)}) %collective-permute-start.9) | collective-permute-done | bytes 196640 | tf_op jit(solution)/shard_map/ppermute | solution.py:829
  37.7 1.6 collective-permute-start.10
  39.3 17.2 %all-gather.5.cloned.1.call-done = bf16[2,2,128,1664]{3,2,0,1:T(8,128)(2,1)} async-done(((bf16[2,2,32,1664]{3,2,0,1:T(8,128)(2,1)}), bf16[2,2,128,1664]{3,2,0,1:T(8,128)(2,1)}) %all-gather.5.cloned.1.call-update) | async-done | bytes 1703952 | tf_op jit(solution)/shard_map/all_gather | solution.py:890
  56.5 1.6 copy.60
  58.1 1.3 slice_bitcast_fusion
  59.4 1.5 collective-permute-start.3
  60.9 1.5 collective-permute-start.6
  62.7 1.9 fusion.7
  64.6 1.9 pad_maximum_fusion.6
  67.5 14.0 %collective-permute-done.3.refs_6_.refs_7_ = bf16[256,1664]{1,0:T(8,128)(2,1)} collective-permute-done((bf16[256,1664]{1,0:T(8,128)(2,1)}, bf16[256,1664]{1,0:T(8,128)(2,1)}, u32[]{:S(2)}, u32[]{:S(2)}) %collective-permute-start.3) | collective-permute-done | bytes 852000 | tf_op jit(solution)/shard_map/ppermute | solution.py:829
  81.5 1.5 collective-permute-start.5
  83.1 1.5 collective-permute-start.8
  84.7 32.2 %all-gather.3.cloned.1.call-done.refs_0_ = bf16[1408,1024]{1,0:T(8,128)(2,1)} async-done(((bf16[352,1024]{1,0:T(8,128)(2,1)}), bf16[1408,1024]{1,0:T(8,128)(2,1)}) %all-gather.3.cloned.1.call-update) | async-done | bytes 2883600 | tf_op jit(solution)/shard_map/all_gather | solution.py:892
  116.9 1.2 fusion.12
  118.3 1.5 collective-permute-start.12
  119.8 1.5 collective-permute-start.13
  123.0 17.8 %attend.1 = (bf16[1024,1024]{1,0:T(8,128)(2,1)}, bf16[1024,768]{1,0:T(8,128)(2,1)}, bf16[1024,256]{1,0:T(8,128)(2,1)}, f32[8,1024]{1,0:T(8,128)}, f32[8,128]{1,0:T(8,128)}, /*index=5*/bf16[8,256,256]{2,1,0:T(8,128)(2,1)}) custom-call(bf16[1408,1024]{1,0:T(8,128)(2,1)} %all-gather.3.cloned.1.call-done.refs_0_, bf16[1024,768]{1,0:T(8,128)(2,1)} %copy-done.12, ...), custom_call_target="tpu_custom_call" | custom-call | flops 4294967296 | bytes 8388608 | tf_op jit(solution)/shard_map/attend/pallas_call | solution.py:308
  142.4 3.6 %all-to-all-start.1 = ((bf16[4,256,256]{2,1,0:T(8,128)(2,1)}), bf16[4,256,256]{2,1,0:T(8,128)(2,1)S(1)}, u32[]{:S(2)}, u32[]{:S(2)}) async-start(bf16[4,256,256]{2,1,0:T(8,128)(2,1)} %bitcast.100), calls=%async_computation.1 | async-start | bytes 1048576 | tf_op jit(solution)/shard_map/all_to_all | solution.py:928
  146.1 1.5 collective-permute-start.16
  147.7 1.5 collective-permute-start.17
  149.1 7.8 %collective-permute-done.16.refs_17_.refs_8_ = bf16[352,512]{1,0:T(8,128)(2,1)S(1)} collective-permute-done((bf16[352,512]{1,0:T(8,128)(2,1)S(1)}, bf16[352,512]{1,0:T(8,128)(2,1)S(1)}, u32[]{:S(2)}, u32[]{:S(2)}) %collective-permute-start.16) | collective-permute-done | bytes 360480 | tf_op jit(solution)/shard_map/ppermute | solution.py:829
  157.0 1.4 collective-permute-done.17.refs_21_.refs_12_
  158.4 1.1 all-to-all-done.1.refs_0_.refs_3_
  159.5 1.9 collective-permute-done.18.refs_1_
  162.2 25.2 %feed.1 = (bf16[256,1024]{1,0:T(8,128)(2,1)}, f32[256,1024]{1,0:T(8,128)}, f32[256,1024]{1,0:T(8,128)}, bf16[1024,1024]{1,0:T(8,128)(2,1)}, bf16[512,1408]{1,0:T...) custom-call(bf16[4,256,256]{2,1,0:T(8,128)(2,1)} %copy-done.21, ...), custom_call_target="tpu_custom_call" | custom-call | flops 12884901888 | bytes 8388608 | tf_op jit(solution)/shard_map/feed/pallas_call | solution.py:308
  187.6 2.0 collective-permute-done.20.part_hbm
  190.3 4.1 %branch.1 = (f32[256,1024]{1,0:T(8,128)}, bf16[4,256,256]{2,1,0:T(8,128)(2,1)}) custom-call(bf16[256,1024]{1,0:T(8,128)(2,1)} %copy-done.20, f32[256,1024]{1,0:T(8,128)} %get-tuple-element.112.gnown_hbm, f32[256,1024]{1,0:T(8,128)} %get-tuple-element.106.res_hbm, bf16[256,1024]{1,0:T(8,128)(2,1)} %bitcast.13.refs_4_.cot_hbm.refs_1_, ...), custom_call_target="tpu_custom_call" | custom-call | flops 1073741824 | bytes 8388608 | tf_op jit(solution)/shard_map/branch/pallas_call | solution.py:308
  194.5 3.8 %all-to-all-start.2 = ((bf16[4,256,256]{2,1,0:T(8,128)(2,1)}), bf16[4,256,256]{2,1,0:T(8,128)(2,1)S(1)}, u32[]{:S(2)}, u32[]{:S(2)}) async-start(bf16[4,256,256]{2,1,0:T(8,128)(2,1)} %get-tuple-element.116), calls=%async_computation.2 | async-start | bytes 1048576 | tf_op jit(solution)/shard_map/all_to_all | solution.py:939
  198.3 1.5 collective-permute-start.22
  199.8 1.3 collective-permute-start.23
  201.0 10.2 %finish.1 = (bf16[256,1024]{1,0:T(8,128)(2,1)}, f32[256,1024]{1,0:T(8,128)}, bf16[704,512]{1,0:T(8,128)(2,1)}, bf16[704,512]{1,0:T(8,128)(2,1)}, bf16[704,512]{1...) custom-call(bf16[512,1408]{1,0:T(8,128)(2,1)} %get-tuple-element.107.refs_0_, ...), custom_call_target="tpu_custom_call" | custom-call | flops 64424509440 | bytes 8388608 | tf_op jit(solution)/shard_map/finish/pallas_call | solution.py:308
  213.9 17.9 %attend_back.1 = (bf16[1024,768]{1,0:T(8,128)(2,1)}, bf16[1024,1024]{1,0:T(8,128)(2,1)}) custom-call(bf16[1024,768]{1,0:T(8,128)(2,1)} %get-tuple-element.119.mixed_hbm, bf16[1024,256]{1,0:T(8,128)(2,1)} %bitcast.91, f32[8,1024]{1,0:T(8,128)} %get-tuple-element.121.total_hbm, f32[1024,128]{1,0:T(8,128)} %get-tuple-element.240.refs_2_.cos_hbm, ...), custom_call_target="tpu_custom_call" | custom-call | bytes 8388608 | tf_op jit(solution)/shard_map/attend_back/pallas_call | solution.py:308
  232.2 0.9 collective-permute-done.22
  233.1 1.4 collective-permute-done.23
  234.5 6.7 %project_weights.1 = (bf16[512,1792]{1,0:T(8,128)(2,1)}, bf16[512,1792]{1,0:T(8,128)(2,1)}) custom-call(bf16[1024,768]{1,0:T(8,128)(2,1)} %get-tuple-element.130.gm_hbm, bf16[1024,1024]{1,0:T(8,128)(2,1)} %get-tuple-element.131.normed_hbm, bf16[512,1024]{1,0:T(8,128)(2,1)} %get-tuple-element.132.okeep_hbm, bf16[512,1024]{1,0:T(8,128)(2,1)} %get-tuple-element.133.osend_hbm), custom_call_target="tpu_custom_call" | custom-call | flops 1073741824 | bytes 8388608 | tf_op jit(solution)/shard_map/project_weights/pallas_call | solution.py:308
  241.2 1.7 add_convert_fusion.2
  242.9 1.3 collective-permute-start.27
  245.3 3.2 collective-permute-done.30
  248.5 1.3 add_convert_fusion.5
  249.9 1.3 collective-permute-start.31
  251.4 1.5 collective-permute-start.33
  253.0 12.4 %collective-permute-done.27 = bf16[256,1408]{1,0:T(8,128)(2,1)S(1)} collective-permute-done((bf16[256,1408]{1,0:T(8,128)(2,1)S(1)}, bf16[256,1408]{1,0:T(8,128)(2,1)S(1)}, u32[]{:S(2)}, u32[]{:S(2)}) %collective-permute-start.27) | collective-permute-done | bytes 720928 | tf_op jit(solution)/shard_map/ppermute | solution.py:829
  266.1 5.7 %collective-permute-done.31 = bf16[352,512]{1,0:T(8,128)(2,1)S(1)} collective-permute-done((bf16[352,512]{1,0:T(8,128)(2,1)S(1)}, bf16[352,512]{1,0:T(8,128)(2,1)S(1)}, u32[]{:S(2)}, u32[]{:S(2)}) %collective-permute-start.31) | collective-permute-done | bytes 360480 | tf_op jit(solution)/shard_map/ppermute | solution.py:829
  273.4 1.3 copy-done.13
  275.9 1.5 pad_maximum_fusion
  279.7 5.8 %all-to-all-start.4 = ((f32[32,8,128]{2,1,0:T(8,128)}), f32[32,8,128]{2,1,0:T(8,128)}, u32[]{:S(2)}, u32[]{:S(2)}) async-start(f32[32,8,128]{2,1,0:T(8,128)} %broadcast_in_dim.39), calls=%async_computation.6 | async-start | bytes 262144 | tf_op jit(solution)/shard_map/all_to_all | solution.py:983
  285.5 12.2 %collective-permute-done.25 = bf16[256,1792]{1,0:T(8,128)(2,1)} collective-permute-done((bf16[256,1792]{1,0:T(8,128)(2,1)S(1)}, bf16[256,1792]{1,0:T(8,128)(2,1)}, u32[]{:S(2)}, u32[]{:S(2)}) %collective-permute-start.25) | collective-permute-done | bytes 917536 | tf_op jit(solution)/shard_map/ppermute | solution.py:829
  297.7 1.4 add_convert_fusion.3
  299.2 1.8 collective-permute-start.26
  301.0 2.1 fusion.6
  304.4 5.2 %collective-permute-done.26 = bf16[128,1792]{1,0:T(8,128)(2,1)S(1)} collective-permute-done((bf16[128,1792]{1,0:T(8,128)(2,1)S(1)}, bf16[128,1792]{1,0:T(8,128)(2,1)S(1)}, u32[]{:S(2)}, u32[]{:S(2)}) %collective-permute-start.26) | collective-permute-done | bytes 458784 | tf_op jit(solution)/shard_map/ppermute | solution.py:829
  310.5 4.2 %all-to-all-start.3 = ((bf16[4,32,1792]{2,1,0:T(8,128)(2,1)}), bf16[4,32,1792]{2,1,0:T(8,128)(2,1)S(1)}, u32[]{:S(2)}, u32[]{:S(2)}) async-start(bf16[4,32,1792]{2,1,0:T(8,128)(2,1)} %bitcast.26), calls=%async_computation.4 | async-start | bytes 917504 | tf_op jit(solution)/shard_map/all_to_all | solution.py:994
  314.7 1.5 fusion.3
  316.2 1.5 fusion.5
  317.7 1.4 add_bitcast_fusion
  319.1 16.8 %all-to-all-done.3 = bf16[4,32,1792]{2,1,0:T(8,128)(2,1)S(1)} async-done(((bf16[4,32,1792]{2,1,0:T(8,128)(2,1)}), bf16[4,32,1792]{2,1,0:T(8,128)(2,1)S(1)}, u32[]{:S(2)}, u32[]{:S(2)}) %all-to-all-start.3) | async-done | bytes 458784 | tf_op jit(solution)/shard_map/all_to_all | solution.py:994
  338.6 1.0 copy-done.3
  339.6 1.8 update.1
  (216 shorter events, 24.3 us)
Async XLA Ops:
  7.2 3.2 copy-start.29
  7.2 49.3 %all-gather.5.cloned.1.call-start = ((), (), s32[]{:S(2)}) async-start(), calls=%async_computation.8 | async-start | bytes 2129920 | tf_op jit(solution)/shard_map/all_gather | solution.py:890
  9.9 1.6 collective-permute-start
  12.3 104.6 %all-gather.3.cloned.1.call-start = ((), (), s32[]{:S(2)}) async-start(), calls=%async_computation.7 | async-start | bytes 3604480 | tf_op jit(solution)/shard_map/all_gather | solution.py:892
  14.3 17.7 %all-to-all-start = ((bf16[4,32,768]{2,1,0:T(8,128)(2,1)}), bf16[4,32,768]{2,1,0:T(8,128)(2,1)S(1)}, u32[]{:S(2)}, u32[]{:S(2)}) async-start(bf16[4,32,768]{2,1,0:T(8,128)(2,1)} %pad_maximum_fusion.10), calls=%async_computation | async-start | bytes 393216 | tf_op jit(solution)/shard_map/all_to_all | solution.py:899
  20.5 37.6 %collective-permute-start.2 = (bf16[256,1024]{1,0:T(8,128)(2,1)}, bf16[256,1024]{1,0:T(8,128)(2,1)}, u32[]{:S(2)}, u32[]{:S(2)}) collective-permute-start(bf16[256,1024]{1,0:T(8,128)(2,1)} %bitcast.13.refs_4_.cot_hbm.refs_1_), channel_id=1, source_target_pairs={{0,4},{4,0},{8,12},{12,8},{16,20},{20,16},{24,28},{28,24},{1,5},{5... | collective-permute-start | bytes 1572872 | tf_op jit(solution)/shard_map/ppermute | solution.py:829
  20.5 37.6 %collective-permute-start.1 = (bf16[256,1024]{1,0:T(8,128)(2,1)S(1)}, bf16[256,1024]{1,0:T(8,128)(2,1)}, u32[]{:S(2)}, u32[]{:S(2)}) collective-permute-start(bf16[256,1024]{1,0:T(8,128)(2,1)S(1)} %bitcast.81), channel_id=1, source_target_pairs={{0,4},{4,0},{8,12},{12,8},{16,20},{20,16},{24,28},{28,24},{1,5},{5... | collective-permute-start | bytes 1572872 | tf_op jit(solution)/shard_map/ppermute | solution.py:829
  32.0 5.7 %collective-permute-start.9 = (bf16[128,768]{1,0:T(8,128)(2,1)S(1)}, bf16[128,768]{1,0:T(8,128)(2,1)S(1)}, u32[]{:S(2)}, u32[]{:S(2)}) collective-permute-start(bf16[128,768]{1,0:T(8,128)(2,1)S(1)} %bitcast.85), channel_id=1, source_target_pairs={{0,8},{4,12},{8,0},{12,4},{16,24},{20,28},{24,16},{28,20},{1,9},{5... | collective-permute-start | bytes 589832 | tf_op jit(solution)/shard_map/ppermute | solution.py:829
  37.7 24.7 %collective-permute-start.10 = (bf16[256,768]{1,0:T(8,128)(2,1)S(1)}, bf16[256,768]{1,0:T(8,128)(2,1)S(1)}, u32[]{:S(2)}, u32[]{:S(2)}) collective-permute-start(bf16[256,768]{1,0:T(8,128)(2,1)S(1)} %pad_maximum_fusion.9), channel_id=1, source_target_pairs={{0,16},{4,20},{8,24},{12,28},{16,0},{20,4},{24,8},{28,12},{1,17},{... | collective-permute-start | bytes 1179656 | tf_op jit(solution)/shard_map/ppermute | solution.py:829
  59.4 3.2 copy-start.36
  59.4 22.1 %collective-permute-start.3 = (bf16[256,1664]{1,0:T(8,128)(2,1)}, bf16[256,1664]{1,0:T(8,128)(2,1)}, u32[]{:S(2)}, u32[]{:S(2)}) collective-permute-start(bf16[256,1664]{1,0:T(8,128)(2,1)} %get-tuple-element.92.refs_5_.refs_6_), channel_id=1, source_target_pairs={{0,8},{4,12},{8,0},{12,4},{16,24},{20,28},{24,16},{28,20},{1,9},{5... | collective-permute-start | bytes 2555912 | tf_op jit(solution)/shard_map/ppermute | solution.py:829
  60.9 22.2 %collective-permute-start.6 = (bf16[256,1664]{1,0:T(8,128)(2,1)}, bf16[256,1664]{1,0:T(8,128)(2,1)}, u32[]{:S(2)}, u32[]{:S(2)}) collective-permute-start(bf16[256,1664]{1,0:T(8,128)(2,1)} %get-tuple-element.96.refs_9_.refs_10_), channel_id=1, source_target_pairs={{0,16},{4,20},{8,24},{12,28},{16,0},{20,4},{24,8},{28,12},{1,17},{... | collective-permute-start | bytes 2555912 | tf_op jit(solution)/shard_map/ppermute | solution.py:829
  62.5 22.0 %collective-permute-start.11 = (bf16[512,768]{1,0:T(8,128)(2,1)S(1)}, bf16[512,768]{1,0:T(8,128)(2,1)S(1)}, u32[]{:S(2)}, u32[]{:S(2)}) collective-permute-start(bf16[512,768]{1,0:T(8,128)(2,1)S(1)} %pad_maximum_fusion.1), channel_id=1, source_target_pairs={{0,4},{4,0},{8,12},{12,8},{16,20},{20,16},{24,28},{28,24},{1,5},{5... | collective-permute-start | bytes 2359304 | tf_op jit(solution)/shard_map/ppermute | solution.py:829
  66.4 53.4 %collective-permute-start.4 = (bf16[256,1664]{1,0:T(8,128)(2,1)}, bf16[256,1664]{1,0:T(8,128)(2,1)}, u32[]{:S(2)}, u32[]{:S(2)}) collective-permute-start(bf16[256,1664]{1,0:T(8,128)(2,1)} %get-tuple-element.92.refs_5_.refs_6_), channel_id=1, source_target_pairs={{0,16},{4,20},{8,24},{12,28},{16,0},{20,4},{24,8},{28,12},{1,17},{... | collective-permute-start | bytes 2555912 | tf_op jit(solution)/shard_map/ppermute | solution.py:829
  67.0 54.3 %collective-permute-start.7 = (bf16[256,1664]{1,0:T(8,128)(2,1)}, bf16[256,1664]{1,0:T(8,128)(2,1)}, u32[]{:S(2)}, u32[]{:S(2)}) collective-permute-start(bf16[256,1664]{1,0:T(8,128)(2,1)} %get-tuple-element.96.refs_9_.refs_10_), channel_id=1, source_target_pairs={{0,8},{4,12},{8,0},{12,4},{16,24},{20,28},{24,16},{28,20},{1,9},{5... | collective-permute-start | bytes 2555912 | tf_op jit(solution)/shard_map/ppermute | solution.py:829
  81.5 40.3 %collective-permute-start.5 = (bf16[256,1664]{1,0:T(8,128)(2,1)}, bf16[256,1664]{1,0:T(8,128)(2,1)}, u32[]{:S(2)}, u32[]{:S(2)}) collective-permute-start(bf16[256,1664]{1,0:T(8,128)(2,1)} %collective-permute-done.3.refs_6_.refs_7_), channel_id=1, source_target_pairs={{0,16},{4,20},{8,24},{12,28},{16,0},{20,4},{24,8},{28,12},{1,17},{... | collective-permute-start | bytes 2555912 | tf_op jit(solution)/shard_map/ppermute | solution.py:829
  83.1 39.3 %collective-permute-start.8 = (bf16[256,1664]{1,0:T(8,128)(2,1)}, bf16[256,1664]{1,0:T(8,128)(2,1)}, u32[]{:S(2)}, u32[]{:S(2)}) collective-permute-start(bf16[256,1664]{1,0:T(8,128)(2,1)} %collective-permute-done.6.refs_10_.refs_11_), channel_id=1, source_target_pairs={{0,8},{4,12},{8,0},{12,4},{16,24},{20,28},{24,16},{28,20},{1,9},{5... | collective-permute-start | bytes 2555912 | tf_op jit(solution)/shard_map/ppermute | solution.py:829
  84.6 33.6 %copy-start.12 = (bf16[1024,768]{1,0:T(8,128)(2,1)}, bf16[1024,768]{1,0:T(8,128)(2,1)S(1)}, u32[]{:S(2)}) copy-start(bf16[1024,768]{1,0:T(8,128)(2,1)S(1)} %constant_dynamic-update-slice_fusion.refs_1_.weight_hbm) | copy-start | bytes 4718596
  118.2 22.5 %copy-start.22 = (bf16[352,512]{1,0:T(8,128)(2,1)}, bf16[352,512]{1,0:T(8,128)(2,1)S(1)}, u32[]{:S(2)}) copy-start(bf16[352,512]{1,0:T(8,128)(2,1)S(1)} %get-tuple-element.193.refs_18_.refs_9_) | copy-start | bytes 1081348
  118.2 22.5 %copy-start.23 = (bf16[352,512]{1,0:T(8,128)(2,1)}, bf16[352,512]{1,0:T(8,128)(2,1)S(1)}, u32[]{:S(2)}) copy-start(bf16[352,512]{1,0:T(8,128)(2,1)S(1)} %get-tuple-element.194.refs_14_.refs_5_) | copy-start | bytes 1081348
  118.3 22.5 %collective-permute-start.12 = (bf16[352,512]{1,0:T(8,128)(2,1)S(1)}, bf16[352,512]{1,0:T(8,128)(2,1)S(1)}, u32[]{:S(2)}, u32[]{:S(2)}) collective-permute-start(bf16[352,512]{1,0:T(8,128)(2,1)S(1)} %get-tuple-element.194.refs_14_.refs_5_), channel_id=1, source_target_pairs={{0,8},{4,12},{8,0},{12,4},{16,24},{20,28},{24,16},{28,20},{1,9},{5... | collective-permute-start | bytes 1081352 | tf_op jit(solution)/shard_map/ppermute | solution.py:829
  119.8 21.0 %collective-permute-start.13 = (bf16[352,512]{1,0:T(8,128)(2,1)S(1)}, bf16[352,512]{1,0:T(8,128)(2,1)S(1)}, u32[]{:S(2)}, u32[]{:S(2)}) collective-permute-start(bf16[352,512]{1,0:T(8,128)(2,1)S(1)} %get-tuple-element.194.refs_14_.refs_5_), channel_id=1, source_target_pairs={{0,16},{4,20},{8,24},{12,28},{16,0},{20,4},{24,8},{28,12},{1,17},{... | collective-permute-start | bytes 1081352 | tf_op jit(solution)/shard_map/ppermute | solution.py:829
  121.3 19.5 %collective-permute-start.14 = (bf16[352,512]{1,0:T(8,128)(2,1)S(1)}, bf16[352,512]{1,0:T(8,128)(2,1)S(1)}, u32[]{:S(2)}, u32[]{:S(2)}) collective-permute-start(bf16[352,512]{1,0:T(8,128)(2,1)S(1)} %get-tuple-element.193.refs_18_.refs_9_), channel_id=1, source_target_pairs={{0,16},{4,20},{8,24},{12,28},{16,0},{20,4},{24,8},{28,12},{1,17},{... | collective-permute-start | bytes 1081352 | tf_op jit(solution)/shard_map/ppermute | solution.py:829
  121.8 19.0 %collective-permute-start.15 = (bf16[352,512]{1,0:T(8,128)(2,1)S(1)}, bf16[352,512]{1,0:T(8,128)(2,1)S(1)}, u32[]{:S(2)}, u32[]{:S(2)}) collective-permute-start(bf16[352,512]{1,0:T(8,128)(2,1)S(1)} %get-tuple-element.193.refs_18_.refs_9_), channel_id=1, source_target_pairs={{0,8},{4,12},{8,0},{12,4},{16,24},{20,28},{24,16},{28,20},{1,9},{5... | collective-permute-start | bytes 1081352 | tf_op jit(solution)/shard_map/ppermute | solution.py:829
  140.8 17.6 %copy-start.42 = (bf16[352,512]{1,0:T(8,128)(2,1)}, bf16[352,512]{1,0:T(8,128)(2,1)S(1)}, u32[]{:S(2)}) copy-start(bf16[352,512]{1,0:T(8,128)(2,1)S(1)} %collective-permute-done.12.refs_15_.refs_6_) | copy-start | bytes 1081348
  142.4 17.1 %all-to-all-start.1 = ((bf16[4,256,256]{2,1,0:T(8,128)(2,1)}), bf16[4,256,256]{2,1,0:T(8,128)(2,1)S(1)}, u32[]{:S(2)}, u32[]{:S(2)}) async-start(bf16[4,256,256]{2,1,0:T(8,128)(2,1)} %bitcast.100), calls=%async_computation.1 | async-start | bytes 1048576 | tf_op jit(solution)/shard_map/all_to_all | solution.py:928
  146.0 13.4 %collective-permute-start.19 = (bf16[8,256,256]{2,1,0:T(8,128)(2,1)}, bf16[8,256,256]{2,1,0:T(8,128)(2,1)S(1)}, u32[]{:S(2)}, u32[]{:S(2)}) collective-permute-start(bf16[8,256,256]{2,1,0:T(8,128)(2,1)} %get-tuple-element.105), channel_id=1, source_target_pairs={{0,4},{4,0},{8,12},{12,8},{16,20},{20,16},{24,28},{28,24},{1,5},{5... | collective-permute-start | bytes 3145736 | tf_op jit(solution)/shard_map/ppermute | solution.py:829
  146.1 10.8 %collective-permute-start.16 = (bf16[352,512]{1,0:T(8,128)(2,1)S(1)}, bf16[352,512]{1,0:T(8,128)(2,1)S(1)}, u32[]{:S(2)}, u32[]{:S(2)}) collective-permute-start(bf16[352,512]{1,0:T(8,128)(2,1)S(1)} %collective-permute-done.12.refs_15_.refs_6_), channel_id=1, source_target_pairs={{0,16},{4,20},{8,24},{12,28},{16,0},{20,4},{24,8},{28,12},{1,17},{... | collective-permute-start | bytes 1081352 | tf_op jit(solution)/shard_map/ppermute | solution.py:829
  147.7 10.7 %collective-permute-start.17 = (bf16[352,512]{1,0:T(8,128)(2,1)}, bf16[352,512]{1,0:T(8,128)(2,1)S(1)}, u32[]{:S(2)}, u32[]{:S(2)}) collective-permute-start(bf16[352,512]{1,0:T(8,128)(2,1)} %copy-done.44), channel_id=1, source_target_pairs={{0,8},{4,12},{8,0},{12,4},{16,24},{20,28},{24,16},{28,20},{1,9},{5... | collective-permute-start | bytes 1081352 | tf_op jit(solution)/shard_map/ppermute | solution.py:829
  157.0 4.4 %copy-start.46 = (bf16[352,512]{1,0:T(8,128)(2,1)}, bf16[352,512]{1,0:T(8,128)(2,1)S(1)}, u32[]{:S(2)}) copy-start(bf16[352,512]{1,0:T(8,128)(2,1)S(1)} %collective-permute-done.16.refs_17_.refs_8_) | copy-start | bytes 1081348
  158.4 3.0 copy-start.47
  159.4 1.9 collective-permute-start.18
  187.4 2.2 collective-permute-start.20
  194.5 18.6 %all-to-all-start.2 = ((bf16[4,256,256]{2,1,0:T(8,128)(2,1)}), bf16[4,256,256]{2,1,0:T(8,128)(2,1)S(1)}, u32[]{:S(2)}, u32[]{:S(2)}) async-start(bf16[4,256,256]{2,1,0:T(8,128)(2,1)} %get-tuple-element.116), calls=%async_computation.2 | async-start | bytes 1048576 | tf_op jit(solution)/shard_map/all_to_all | solution.py:939
  198.3 116.4 %reduce-scatter.3.cloned.1.call-start = ((), (), s32[]{:S(2)}) async-start(), calls=%async_computation.9 | async-start | bytes 2621440 | tf_op jit(solution)/shard_map/reduce_scatter | solution.py:987
  198.3 34.8 %collective-permute-start.22 = (bf16[512,1408]{1,0:T(8,128)(2,1)}, bf16[512,1408]{1,0:T(8,128)(2,1)}, u32[]{:S(2)}, u32[]{:S(2)}) collective-permute-start(bf16[512,1408]{1,0:T(8,128)(2,1)} %get-tuple-element.128), channel_id=1, source_target_pairs={{0,8},{4,12},{8,0},{12,4},{16,24},{20,28},{24,16},{28,20},{1,9},{5... | collective-permute-start | bytes 4325384 | tf_op jit(solution)/shard_map/ppermute | solution.py:829
  199.8 34.7 %collective-permute-start.23 = (bf16[512,1408]{1,0:T(8,128)(2,1)}, bf16[512,1408]{1,0:T(8,128)(2,1)S(1)}, u32[]{:S(2)}, u32[]{:S(2)}) collective-permute-start(bf16[512,1408]{1,0:T(8,128)(2,1)} %get-tuple-element.129), channel_id=1, source_target_pairs={{0,16},{4,20},{8,24},{12,28},{16,0},{20,4},{24,8},{28,12},{1,17},{... | collective-permute-start | bytes 4325384 | tf_op jit(solution)/shard_map/ppermute | solution.py:829
  211.3 37.2 %collective-permute-start.30 = (bf16[704,512]{1,0:T(8,128)(2,1)}, bf16[704,512]{1,0:T(8,128)(2,1)}, u32[]{:S(2)}, u32[]{:S(2)}) collective-permute-start(bf16[704,512]{1,0:T(8,128)(2,1)} %get-tuple-element.141), channel_id=1, source_target_pairs={{0,8},{4,12},{8,0},{12,4},{16,24},{20,28},{24,16},{28,20},{1,9},{5... | collective-permute-start | bytes 2162696 | tf_op jit(solution)/shard_map/ppermute | solution.py:829
  211.9 39.3 %collective-permute-start.32 = (bf16[704,512]{1,0:T(8,128)(2,1)}, bf16[704,512]{1,0:T(8,128)(2,1)S(1)}, u32[]{:S(2)}, u32[]{:S(2)}) collective-permute-start(bf16[704,512]{1,0:T(8,128)(2,1)} %get-tuple-element.143), channel_id=1, source_target_pairs={{0,16},{4,20},{8,24},{12,28},{16,0},{20,4},{24,8},{28,12},{1,17},{... | collective-permute-start | bytes 2162696 | tf_op jit(solution)/shard_map/ppermute | solution.py:829
  231.9 106.6 %reduce-scatter.5.cloned.1.call-start = ((), (), s32[]{:S(2)}) async-start(), calls=%async_computation.10 | async-start | bytes 2785280 | tf_op jit(solution)/shard_map/reduce_scatter | solution.py:981
  234.5 6.7 %copy-start.15 = (bf16[512,1408]{1,0:T(8,128)(2,1)S(1)}, bf16[512,1408]{1,0:T(8,128)(2,1)}, u32[]{:S(2)}) copy-start(bf16[512,1408]{1,0:T(8,128)(2,1)} %get-tuple-element.138) | copy-start | bytes 4325380
  242.9 22.4 %collective-permute-start.27 = (bf16[256,1408]{1,0:T(8,128)(2,1)S(1)}, bf16[256,1408]{1,0:T(8,128)(2,1)S(1)}, u32[]{:S(2)}, u32[]{:S(2)}) collective-permute-start(bf16[256,1408]{1,0:T(8,128)(2,1)S(1)} %slice.310), channel_id=1, source_target_pairs={{0,16},{4,20},{8,24},{12,28},{16,0},{20,4},{24,8},{28,12},{1,17},{... | collective-permute-start | bytes 2162696 | tf_op jit(solution)/shard_map/ppermute | solution.py:829
  244.6 3.9 %copy-start.19 = (bf16[704,512]{1,0:T(8,128)(2,1)S(1)}, bf16[704,512]{1,0:T(8,128)(2,1)}, u32[]{:S(2)}) copy-start(bf16[704,512]{1,0:T(8,128)(2,1)} %get-tuple-element.140) | copy-start | bytes 2162692
  244.7 6.5 %copy-start.18 = (bf16[704,512]{1,0:T(8,128)(2,1)S(1)}, bf16[704,512]{1,0:T(8,128)(2,1)}, u32[]{:S(2)}) copy-start(bf16[704,512]{1,0:T(8,128)(2,1)} %get-tuple-element.142) | copy-start | bytes 2162692
  244.7 21.0 %collective-permute-start.28 = (bf16[256,1408]{1,0:T(8,128)(2,1)S(1)}, bf16[256,1408]{1,0:T(8,128)(2,1)S(1)}, u32[]{:S(2)}, u32[]{:S(2)}) collective-permute-start(bf16[256,1408]{1,0:T(8,128)(2,1)S(1)} %slice.312), channel_id=1, source_target_pairs={{0,8},{4,12},{8,0},{12,4},{16,24},{20,28},{24,16},{28,20},{1,9},{5... | collective-permute-start | bytes 2162696 | tf_op jit(solution)/shard_map/ppermute | solution.py:829
  249.9 3.1 copy-start.39
  249.9 21.9 %collective-permute-start.31 = (bf16[352,512]{1,0:T(8,128)(2,1)S(1)}, bf16[352,512]{1,0:T(8,128)(2,1)S(1)}, u32[]{:S(2)}, u32[]{:S(2)}) collective-permute-start(bf16[352,512]{1,0:T(8,128)(2,1)S(1)} %slice.314), channel_id=1, source_target_pairs={{0,16},{4,20},{8,24},{12,28},{16,0},{20,4},{24,8},{28,12},{1,17},{... | collective-permute-start | bytes 1081352 | tf_op jit(solution)/shard_map/ppermute | solution.py:829
  251.4 20.4 %collective-permute-start.33 = (bf16[352,512]{1,0:T(8,128)(2,1)S(1)}, bf16[352,512]{1,0:T(8,128)(2,1)S(1)}, u32[]{:S(2)}, u32[]{:S(2)}) collective-permute-start(bf16[352,512]{1,0:T(8,128)(2,1)S(1)} %slice.316), channel_id=1, source_target_pairs={{0,8},{4,12},{8,0},{12,4},{16,24},{20,28},{24,16},{28,20},{1,9},{5... | collective-permute-start | bytes 1081352 | tf_op jit(solution)/shard_map/ppermute | solution.py:829
  252.9 20.5 %collective-permute-start.24 = (bf16[512,1792]{1,0:T(8,128)(2,1)S(1)}, bf16[512,1792]{1,0:T(8,128)(2,1)S(1)}, u32[]{:S(2)}, u32[]{:S(2)}) collective-permute-start(bf16[512,1792]{1,0:T(8,128)(2,1)S(1)} %copy-done.39), channel_id=1, source_target_pairs={{0,4},{4,0},{8,12},{12,8},{16,20},{20,16},{24,28},{28,24},{1,5},{5... | collective-permute-start | bytes 5505032 | tf_op jit(solution)/shard_map/ppermute | solution.py:829
  266.0 7.2 %collective-permute-start.29 = (bf16[128,2816]{1,0:T(8,128)(2,1)S(1)}, bf16[128,2816]{1,0:T(8,128)(2,1)S(1)}, u32[]{:S(2)}, u32[]{:S(2)}) collective-permute-start(bf16[128,2816]{1,0:T(8,128)(2,1)S(1)} %pad_maximum_fusion.3), channel_id=1, source_target_pairs={{0,4},{4,0},{8,12},{12,8},{16,20},{20,16},{24,28},{28,24},{1,5},{5... | collective-permute-start | bytes 2162696 | tf_op jit(solution)/shard_map/ppermute | solution.py:829
  275.3 22.5 %collective-permute-start.25 = (bf16[256,1792]{1,0:T(8,128)(2,1)S(1)}, bf16[256,1792]{1,0:T(8,128)(2,1)}, u32[]{:S(2)}, u32[]{:S(2)}) collective-permute-start(bf16[256,1792]{1,0:T(8,128)(2,1)S(1)} %slice.290), channel_id=1, source_target_pairs={{0,8},{4,12},{8,0},{12,4},{16,24},{20,28},{24,16},{28,20},{1,9},{5... | collective-permute-start | bytes 2752520 | tf_op jit(solution)/shard_map/ppermute | solution.py:829
  278.9 22.0 %collective-permute-start.21 = (bf16[256,1024]{1,0:T(8,128)(2,1)}, bf16[256,1024]{1,0:T(8,128)(2,1)}, u32[]{:S(2)}, u32[]{:S(2)}) collective-permute-start(bf16[256,1024]{1,0:T(8,128)(2,1)} %get-tuple-element.118), channel_id=1, source_target_pairs={{0,4},{4,0},{8,12},{12,8},{16,20},{20,16},{24,28},{28,24},{1,5},{5... | collective-permute-start | bytes 1572872 | tf_op jit(solution)/shard_map/ppermute | solution.py:829
  279.7 23.4 %all-to-all-start.4 = ((f32[32,8,128]{2,1,0:T(8,128)}), f32[32,8,128]{2,1,0:T(8,128)}, u32[]{:S(2)}, u32[]{:S(2)}) async-start(f32[32,8,128]{2,1,0:T(8,128)} %broadcast_in_dim.39), calls=%async_computation.6 | async-start | bytes 262144 | tf_op jit(solution)/shard_map/all_to_all | solution.py:983
  285.5 15.5 %copy-start.10 = (f32[256,1024]{1,0:T(8,128)S(1)}, f32[256,1024]{1,0:T(8,128)}, u32[]{:S(2)}) copy-start(f32[256,1024]{1,0:T(8,128)} %get-tuple-element.106.res_hbm) | copy-start | bytes 3145732
  285.5 15.5 %copy-start.16 = (f32[256,1024]{1,0:T(8,128)S(1)}, f32[256,1024]{1,0:T(8,128)}, u32[]{:S(2)}) copy-start(f32[256,1024]{1,0:T(8,128)} %get-tuple-element.115) | copy-start | bytes 3145732
  299.2 10.4 %collective-permute-start.26 = (bf16[128,1792]{1,0:T(8,128)(2,1)S(1)}, bf16[128,1792]{1,0:T(8,128)(2,1)S(1)}, u32[]{:S(2)}, u32[]{:S(2)}) collective-permute-start(bf16[128,1792]{1,0:T(8,128)(2,1)S(1)} %slice.292), channel_id=1, source_target_pairs={{0,16},{4,20},{8,24},{12,28},{16,0},{20,4},{24,8},{28,12},{1,17},{... | collective-permute-start | bytes 1376264 | tf_op jit(solution)/shard_map/ppermute | solution.py:829
  304.2 12.0 %copy-start.37 = (f32[16]{0:T(128)}, f32[16]{0:T(128)S(1)}, u32[]{:S(2)}) copy-start(f32[16]{0:T(128)S(1)} %reshape_squeeze.3) | copy-start | bytes 196
  304.2 12.0 %copy-start.38 = (f32[16]{0:T(128)}, f32[16]{0:T(128)S(1)}, u32[]{:S(2)}) copy-start(f32[16]{0:T(128)S(1)} %divide_sqrt_fusion) | copy-start | bytes 196
  310.5 7.2 %copy-start.17 = (f32[256,1024]{1,0:T(8,128)S(1)}, f32[256,1024]{1,0:T(8,128)}, u32[]{:S(2)}) copy-start(f32[256,1024]{1,0:T(8,128)} %get-tuple-element.114.refs_4_) | copy-start | bytes 3145732
  310.5 25.4 %all-to-all-start.3 = ((bf16[4,32,1792]{2,1,0:T(8,128)(2,1)}), bf16[4,32,1792]{2,1,0:T(8,128)(2,1)S(1)}, u32[]{:S(2)}, u32[]{:S(2)}) async-start(bf16[4,32,1792]{2,1,0:T(8,128)(2,1)} %bitcast.26), calls=%async_computation.4 | async-start | bytes 917504 | tf_op jit(solution)/shard_map/all_to_all | solution.py:994
  314.7 3.0 copy-start.9
  319.1 17.1 %copy-start.33 = (f32[32,1024]{1,0:T(8,128)S(1)}, f32[32,1024]{1,0:T(8,128)}, u32[]{:S(2)}) copy-start(f32[32,1024]{1,0:T(8,128)} %param.31) | copy-start | bytes 393220
  319.1 17.8 %copy-start.30 = (bf16[32,1024]{1,0:T(8,128)(2,1)S(1)}, bf16[32,1024]{1,0:T(8,128)(2,1)}, u32[]{:S(2)}) copy-start(bf16[32,1024]{1,0:T(8,128)(2,1)} %param.25) | copy-start | bytes 196612
  319.1 17.8 %copy-start.34 = (f32[32,1024]{1,0:T(8,128)S(1)}, f32[32,1024]{1,0:T(8,128)}, u32[]{:S(2)}) copy-start(f32[32,1024]{1,0:T(8,128)} %param.32) | copy-start | bytes 393220
  (27 other events, 45.2 us)
Sparse Core Ops, SparseCore 0:
  12.4 44.0 all-gather.4
  58.6 58.1 all-gather.2
  232.0 44.4 reduce-scatter.2
  278.8 54.5 reduce-scatter.4

commit v8 on v7

--- a/solution.py
+++ b/solution.py
@@ -345,7 +345,7 @@
      peak_ref, outs, sems) = refs[19:]
     n = normed.shape[0]
     go = Copies(sems)
-    early = [go.start(rows_hbm.at[pl.ds(352 * i, 256)], act.at[pl.ds(256 * i, 256)]) for i in range(4)]
+    early = [go.start(rows_hbm.at[pl.ds(344 * i, 256)], act.at[pl.ds(256 * i, 256)]) for i in range(4)]
     middle = [
         go.start(weight_hbm.at[pl.ds(128 * p, 128)], weight.at[aligned(place_of(p), 128)])
         for p in range(8)
@@ -354,19 +354,11 @@
     packs = [go.start(piece.at[:, pl.ds(FF2, 256)], outs.at[i]) for i, piece in enumerate(pieces)]
     wait_all(early)
 
-    @pl.loop(0, n // 128)
-    def _(i):
-        rows = aligned(i, 128)
+    def norm(i):
+        rows = aligned(i, 256)
         normed[rows, :] = layer_norm(act[rows, :].astype(f32)).astype(bf)
 
-    late = [go.start(normed, normed_hbm)]
-    wait_all(middle)
-    wait_all(packs)
-    late.append(go.start(outs, outs_hbm))
-    id_col[...] = jnp.broadcast_to(ids[0:1, :], (128, n)).T
-
-    @pl.loop(0, n // 256)
-    def _(i):
+    def mix(i):
         rows = aligned(i, 256)
         mixed = dot(normed[rows, :], weight[...], NN)
         cosine = cos_ref[rows, :]
@@ -378,6 +370,18 @@
         mixed_ref[rows, 512:768] = value.astype(bf)
         value_t[:, rows] = value.T.astype(bf)
 
+    norm(0)
+    wait_all(middle)
+    wait_all(packs)
+    id_col[...] = jnp.broadcast_to(ids[0:1, :], (128, n)).T
+
+    @pl.loop(0, n // 256 - 1)
+    def _(i):
+        mix(i)
+        norm(i + 1)
+
+    mix(n // 256 - 1)
+    late = [go.start(normed, normed_hbm), go.start(outs, outs_hbm)]
     late.append(go.start(mixed_ref, mixed_hbm))
     peak_ref[...] = jnp.zeros_like(peak_ref)
     total_ref[...] = jnp.zeros_like(total_ref)
@@ -888,7 +892,7 @@
     wide = jnp.stack([mine, other], axis=1)
     wide = jnp.concatenate([wide, out_rows.transpose(0, 2, 1, 3)], axis=3)
     wide = lax.all_gather(wide, "ctx", axis=2, tiled=True).reshape(2, 256, FF2 + 256)
-    padded = jnp.concatenate([act, w_down, jnp.zeros((8, width), bf)], axis=0)
+    padded = jnp.concatenate([act, w_down], axis=0)
     rows_all = lax.all_gather(padded, "ctx", axis=0, tiled=True)
     heads = jnp.stack(
         [
@@ -910,7 +914,7 @@
     piece_a = spread(wide[0], 2, 4)
     piece_b = spread(wide[1], 4, 2)
     down = jnp.concatenate(
-        [rows_all[352 * i + 256 : 352 * i + 344] for i in range(4)], axis=0
+        [rows_all[344 * i + 256 : 344 * i + 344] for i in range(4)], axis=0
     )
     piece_da = spread(down[:, :512], 2, 4)
     piece_db = spread(down[:, 512:], 4, 2)
@@ -992,6 +996,10 @@
     grad_heads = add_low(grad_heads[:256], swap(grad_heads[256:], 2))
     grad_heads = add_low(grad_heads[:128], swap(grad_heads[128:], 4))
     grad_heads = lax.all_to_all(grad_heads.reshape(4, 32, 768 + width), "ctx", 0, 0, tiled=True)
+    big = update(
+        momentum_coeff.reshape(1), grad_wide, (m_gate, m_up, m_down), (w_gate, w_up, w_down)
+    )
+    grad_heads, *big = lax.optimization_barrier((grad_heads, *big))
     grad_heads = grad_heads.astype(f32)
     parts = grad_heads[:, :, 768:]
     grad_out = parts[0] + parts[1] + (parts[2] + parts[3])
@@ -999,9 +1007,6 @@
         jnp.concatenate([grad_heads[i, :, 256 * k : 256 * k + 256] for i in range(4)], axis=1)
         for k in range(3)
     ]
-    big = update(
-        momentum_coeff.reshape(1), grad_wide, (m_gate, m_up, m_down), (w_gate, w_up, w_down)
-    )
     weight_grads = (*grad_qkv, grad_out)
     moments = (m_query, m_key, m_value, m_out)
     new_moments = tuple(

time: 349 us -> 345 us (0.989)
  waiting for transfers between devices: 152 us -> 145 us
    all_to_all x1, waiting for transfers between devices: 16.8 us -> 1.13 us  [fast_device(): lax.all_to_all(grad_heads.reshape(4, 32, 768 + width), 'ctx', 0, 0, tiled...]
    reduce_scatter x1, waiting for transfers between devices: 0.01 us -> 8.63 us  [fast_device(): lax.psum_scatter(grad_wide, 'ctx', scatter_dimension=0, tiled=True)]
    unnamed x100 -> x96, local copies, waits for them, and re-layouts: 6.83 us -> 7.4 us
  transfers between devices with their start and end apart: 43 -> 43, of which waited for: 20 -> 21; matrix products, arithmetic and copies ran while one was open for 9% -> 10% of each run, Pallas kernels for 15% -> 16%
where the time goes in v8:
time: 345 us; the launch traced here: 342 us
  waiting for transfers between devices  145 us (42%)
  Pallas kernels  83.2 us (24%)
  starting transfers between devices  52.8 us (15%)
  other arithmetic  28.6 us (8%)
  local copies, waits for them, and re-layouts  17 us (5%)
  between operations  16.2 us (5%)
    pallas_call x6, Pallas kernels, call(): pl.pallas_call(kernel, out_shape=tuple((pltpu.HBM(*o) for o in outs)), in...  81.4 us
    ppermute x34, waiting for transfers between devices, swap(): return lax.ppermute(array, 'dp', [(i, i ^ bit) for i in range(8)])  74.8 us
    all_gather x1, waiting for transfers between devices, fast_device(): rows_all = lax.all_gather(padded, 'ctx', axis=0, tiled=True)  31.1 us
    ppermute x34, starting transfers between devices, swap(): return lax.ppermute(array, 'dp', [(i, i ^ bit) for i in range(8)])  28.4 us
    all_gather x1, waiting for transfers between devices, fast_device(): lax.all_gather(wide, 'ctx', axis=2, tiled=True).reshape(2, 256, FF2 + 256)  17.3 us
    all_to_all x1, waiting for transfers between devices, fast_device(): heads = lax.all_to_all(heads, 'ctx', 0, 0, tiled=True).reshape(128, 768)  10.9 us
    convert_element_type x11, other arithmetic, add_low(): return (left.astype(f32) + right.astype(f32)).astype(bf)  8.88 us
    reduce_scatter x1, waiting for transfers between devices, fast_device(): lax.psum_scatter(grad_wide, 'ctx', scatter_dimension=0, tiled=True)  8.63 us
  transfers between devices with their start and end apart: 43, of which 21 were waited for; matrix products, arithmetic and copies ran while one was open for 10% of the time, Pallas kernels for 16%

profile of v8, /device:TPU:0, one launch (start us, length us, event | category | flops | bytes accessed | tf_op | source)
XLA Modules:
  0.0 342.5 jit_solution(1101044558046797517)
XLA Ops:
  7.3 1.0 fusion.15
  8.3 1.0 fusion.16
  12.3 0.9 pad_maximum_fusion.6
  14.0 6.2 %all-to-all-start = ((bf16[4,32,768]{2,1,0:T(8,128)(2,1)}), bf16[4,32,768]{2,1,0:T(8,128)(2,1)S(1)}, u32[]{:S(2)}, u32[]{:S(2)}) async-start(bf16[4,32,768]{2,1,0:T(8,128)(2,1)} %pad_maximum_fusion.11), calls=%async_computation | async-start | bytes 393216 | tf_op jit(solution)/shard_map/all_to_all | solution.py:903
  20.8 10.9 %all-to-all-done = bf16[4,32,768]{2,1,0:T(8,128)(2,1)S(1)} async-done(((bf16[4,32,768]{2,1,0:T(8,128)(2,1)}), bf16[4,32,768]{2,1,0:T(8,128)(2,1)S(1)}, u32[]{:S(2)}, u32[]{:S(2)}) %all-to-all-start) | async-done | bytes 196640 | tf_op jit(solution)/shard_map/all_to_all | solution.py:903
  31.7 1.5 collective-permute-start.9
  33.2 4.2 %collective-permute-done.9 = bf16[128,768]{1,0:T(8,128)(2,1)S(1)} collective-permute-done((bf16[128,768]{1,0:T(8,128)(2,1)S(1)}, bf16[128,768]{1,0:T(8,128)(2,1)S(1)}, u32[]{:S(2)}, u32[]{:S(2)}) %collective-permute-start.9) | collective-permute-done | bytes 196640 | tf_op jit(solution)/shard_map/ppermute | solution.py:833
  37.4 1.6 collective-permute-start.10
  39.0 17.3 %all-gather.5.cloned.1.call-done = bf16[2,2,128,1664]{3,2,0,1:T(8,128)(2,1)} async-done(((bf16[2,2,32,1664]{3,2,0,1:T(8,128)(2,1)}), bf16[2,2,128,1664]{3,2,0,1:T(8,128)(2,1)}) %all-gather.5.cloned.1.call-update) | async-done | bytes 1703952 | tf_op jit(solution)/shard_map/all_gather | solution.py:894
  56.3 1.6 copy.60
  57.9 1.3 slice_bitcast_fusion
  59.2 1.5 collective-permute-start.3
  60.7 1.5 collective-permute-start.6
  62.4 1.9 fusion.7
  64.3 1.9 pad_maximum_fusion.7
  67.3 14.0 %collective-permute-done.3.refs_6_.refs_7_ = bf16[256,1664]{1,0:T(8,128)(2,1)} collective-permute-done((bf16[256,1664]{1,0:T(8,128)(2,1)}, bf16[256,1664]{1,0:T(8,128)(2,1)}, u32[]{:S(2)}, u32[]{:S(2)}) %collective-permute-start.3) | collective-permute-done | bytes 852000 | tf_op jit(solution)/shard_map/ppermute | solution.py:833
  81.3 1.5 collective-permute-start.5
  82.8 1.5 collective-permute-start.8
  84.4 31.1 %all-gather.3.cloned.1.call-done.refs_0_ = bf16[1376,1024]{1,0:T(8,128)(2,1)} async-done(((bf16[344,1024]{1,0:T(8,128)(2,1)}), bf16[1376,1024]{1,0:T(8,128)(2,1)}) %all-gather.3.cloned.1.call-update) | async-done | bytes 2818064 | tf_op jit(solution)/shard_map/all_gather | solution.py:896
  115.6 1.2 fusion.12
  116.9 1.5 collective-permute-start.12
  118.5 1.5 collective-permute-start.13
  121.7 17.2 %attend.1 = (bf16[1024,1024]{1,0:T(8,128)(2,1)}, bf16[1024,768]{1,0:T(8,128)(2,1)}, bf16[1024,256]{1,0:T(8,128)(2,1)}, f32[8,1024]{1,0:T(8,128)}, f32[8,128]{1,0:T(8,128)}, /*index=5*/bf16[8,256,256]{2,1,0:T(8,128)(2,1)}) custom-call(bf16[1376,1024]{1,0:T(8,128)(2,1)} %all-gather.3.cloned.1.call-done.refs_0_, bf16[1024,768]{1,0:T(8,128)(2,1)} %copy-done.12, ...), custom_call_target="tpu_custom_call" | custom-call | flops 4294967296 | bytes 8388608 | tf_op jit(solution)/shard_map/attend/pallas_call | solution.py:308
  139.9 3.6 %all-to-all-start.1 = ((bf16[4,256,256]{2,1,0:T(8,128)(2,1)}), bf16[4,256,256]{2,1,0:T(8,128)(2,1)S(1)}, u32[]{:S(2)}, u32[]{:S(2)}) async-start(bf16[4,256,256]{2,1,0:T(8,128)(2,1)} %bitcast.100), calls=%async_computation.1 | async-start | bytes 1048576 | tf_op jit(solution)/shard_map/all_to_all | solution.py:932
  143.7 1.5 collective-permute-start.16
  145.2 1.5 collective-permute-start.17
  146.7 7.8 %collective-permute-done.16.refs_17_.refs_8_ = bf16[352,512]{1,0:T(8,128)(2,1)S(1)} collective-permute-done((bf16[352,512]{1,0:T(8,128)(2,1)S(1)}, bf16[352,512]{1,0:T(8,128)(2,1)S(1)}, u32[]{:S(2)}, u32[]{:S(2)}) %collective-permute-start.16) | collective-permute-done | bytes 360480 | tf_op jit(solution)/shard_map/ppermute | solution.py:833
  154.5 1.4 collective-permute-done.17.refs_21_.refs_12_
  157.0 1.9 collective-permute-done.18.refs_1_
  159.7 25.2 %feed.1 = (bf16[256,1024]{1,0:T(8,128)(2,1)}, f32[256,1024]{1,0:T(8,128)}, f32[256,1024]{1,0:T(8,128)}, bf16[1024,1024]{1,0:T(8,128)(2,1)}, bf16[512,1408]{1,0:T...) custom-call(bf16[4,256,256]{2,1,0:T(8,128)(2,1)} %copy-done.19, ...), custom_call_target="tpu_custom_call" | custom-call | flops 12884901888 | bytes 8388608 | tf_op jit(solution)/shard_map/feed/pallas_call | solution.py:308
  185.1 2.0 collective-permute-done.20.part_hbm
  187.8 4.1 %branch.1 = (f32[256,1024]{1,0:T(8,128)}, bf16[4,256,256]{2,1,0:T(8,128)(2,1)}) custom-call(bf16[256,1024]{1,0:T(8,128)(2,1)} %copy-done.18, f32[256,1024]{1,0:T(8,128)} %get-tuple-element.122.gnown_hbm, f32[256,1024]{1,0:T(8,128)} %get-tuple-element.116.res_hbm, bf16[256,1024]{1,0:T(8,128)(2,1)} %bitcast.13.refs_4_.cot_hbm.refs_1_, ...), custom_call_target="tpu_custom_call" | custom-call | flops 1073741824 | bytes 8388608 | tf_op jit(solution)/shard_map/branch/pallas_call | solution.py:308
  192.0 4.5 %all-to-all-start.2 = ((bf16[4,256,256]{2,1,0:T(8,128)(2,1)}), bf16[4,256,256]{2,1,0:T(8,128)(2,1)S(1)}, u32[]{:S(2)}, u32[]{:S(2)}) async-start(bf16[4,256,256]{2,1,0:T(8,128)(2,1)} %get-tuple-element.126), calls=%async_computation.2 | async-start | bytes 1048576 | tf_op jit(solution)/shard_map/all_to_all | solution.py:943
  196.4 1.5 collective-permute-start.22
  198.7 10.2 %finish.1 = (bf16[256,1024]{1,0:T(8,128)(2,1)}, f32[256,1024]{1,0:T(8,128)}, bf16[704,512]{1,0:T(8,128)(2,1)}, bf16[704,512]{1,0:T(8,128)(2,1)}, bf16[704,512]{1...) custom-call(bf16[512,1408]{1,0:T(8,128)(2,1)} %get-tuple-element.117.refs_0_, ...), custom_call_target="tpu_custom_call" | custom-call | flops 64424509440 | bytes 8388608 | tf_op jit(solution)/shard_map/finish/pallas_call | solution.py:308
  209.6 1.2 collective-permute-start.32
  212.1 17.9 %attend_back.1 = (bf16[1024,768]{1,0:T(8,128)(2,1)}, bf16[1024,1024]{1,0:T(8,128)(2,1)}) custom-call(bf16[1024,768]{1,0:T(8,128)(2,1)} %get-tuple-element.129.mixed_hbm, bf16[1024,256]{1,0:T(8,128)(2,1)} %bitcast.91, f32[8,1024]{1,0:T(8,128)} %get-tuple-element.131.total_hbm, f32[1024,128]{1,0:T(8,128)} %get-tuple-element.260.refs_2_.cos_hbm, ...), custom_call_target="tpu_custom_call" | custom-call | bytes 8388608 | tf_op jit(solution)/shard_map/attend_back/pallas_call | solution.py:308
  230.3 0.9 collective-permute-done.22
  231.2 1.4 collective-permute-done.23
  232.6 6.7 %project_weights.1 = (bf16[512,1792]{1,0:T(8,128)(2,1)}, bf16[512,1792]{1,0:T(8,128)(2,1)}) custom-call(bf16[1024,768]{1,0:T(8,128)(2,1)} %get-tuple-element.140.gm_hbm, bf16[1024,1024]{1,0:T(8,128)(2,1)} %get-tuple-element.141.normed_hbm, bf16[512,1024]{1,0:T(8,128)(2,1)} %get-tuple-element.142.okeep_hbm, bf16[512,1024]{1,0:T(8,128)(2,1)} %get-tuple-element.143.osend_hbm), custom_call_target="tpu_custom_call" | custom-call | flops 1073741824 | bytes 8388608 | tf_op jit(solution)/shard_map/project_weights/pallas_call | solution.py:308
  239.4 1.7 add_convert_fusion.2
  243.5 3.2 collective-permute-done.30
  246.7 1.3 add_convert_fusion.5
  249.1 1.5 collective-permute-start.33
  250.7 12.9 %collective-permute-done.27 = bf16[256,1408]{1,0:T(8,128)(2,1)S(1)} collective-permute-done((bf16[256,1408]{1,0:T(8,128)(2,1)S(1)}, bf16[256,1408]{1,0:T(8,128)(2,1)S(1)}, u32[]{:S(2)}, u32[]{:S(2)}) %collective-permute-start.27) | collective-permute-done | bytes 720928 | tf_op jit(solution)/shard_map/ppermute | solution.py:833
  264.2 1.3 copy-done.37
  265.5 4.3 %collective-permute-done.31 = bf16[352,512]{1,0:T(8,128)(2,1)S(1)} collective-permute-done((bf16[352,512]{1,0:T(8,128)(2,1)S(1)}, bf16[352,512]{1,0:T(8,128)(2,1)S(1)}, u32[]{:S(2)}, u32[]{:S(2)}) %collective-permute-start.31) | collective-permute-done | bytes 360480 | tf_op jit(solution)/shard_map/ppermute | solution.py:833
  271.5 1.5 pad_maximum_fusion
  273.1 2.5 add_convert_fusion
  278.5 5.3 %all-to-all-start.4 = ((f32[32,8,128]{2,1,0:T(8,128)}), f32[32,8,128]{2,1,0:T(8,128)}, u32[]{:S(2)}, u32[]{:S(2)}) async-start(f32[32,8,128]{2,1,0:T(8,128)} %broadcast_in_dim.35), calls=%async_computation.6 | async-start | bytes 262144 | tf_op jit(solution)/shard_map/all_to_all | solution.py:987
  283.8 14.3 %collective-permute-done.25 = bf16[256,1792]{1,0:T(8,128)(2,1)} collective-permute-done((bf16[256,1792]{1,0:T(8,128)(2,1)S(1)}, bf16[256,1792]{1,0:T(8,128)(2,1)}, u32[]{:S(2)}, u32[]{:S(2)}) %collective-permute-start.25) | collective-permute-done | bytes 917536 | tf_op jit(solution)/shard_map/ppermute | solution.py:833
  298.1 1.4 add_convert_fusion.3
  299.5 1.1 collective-permute-start.26
  300.6 2.1 fusion.6
  302.7 0.9 reduce_max.9
  304.0 5.7 %collective-permute-done.26 = bf16[128,1792]{1,0:T(8,128)(2,1)S(1)} collective-permute-done((bf16[128,1792]{1,0:T(8,128)(2,1)S(1)}, bf16[128,1792]{1,0:T(8,128)(2,1)S(1)}, u32[]{:S(2)}, u32[]{:S(2)}) %collective-permute-start.26) | collective-permute-done | bytes 458784 | tf_op jit(solution)/shard_map/ppermute | solution.py:833
  310.5 4.4 %all-to-all-start.3 = ((bf16[4,32,1792]{2,1,0:T(8,128)(2,1)}), bf16[4,32,1792]{2,1,0:T(8,128)(2,1)S(1)}, u32[]{:S(2)}, u32[]{:S(2)}) async-start(bf16[4,32,1792]{2,1,0:T(8,128)(2,1)} %bitcast.26), calls=%async_computation.4 | async-start | bytes 917504 | tf_op jit(solution)/shard_map/all_to_all | solution.py:998
  314.9 1.5 fusion.3
  316.4 1.5 fusion.5
  318.0 2.7 add_bitcast_fusion
  320.7 8.6 %reduce-scatter.5.cloned.1.call-done.wide_ref = bf16[32,8704]{1,0:T(8,128)(2,1)} async-done(((bf16[128,8704]{1,0:T(8,128)(2,1)}), bf16[32,8704]{1,0:T(8,128)(2,1)}) %reduce-scatter.5.cloned.1.call-update) | async-done | bytes 557072 | tf_op jit(solution)/shard_map/reduce_scatter | solution.py:985
  329.3 1.0 copy-done.3
  330.4 1.8 update.1
  332.2 1.1 all-to-all-done.3
  (210 shorter events, 25.5 us)
Async XLA Ops:
  7.2 3.2 copy-start.27
  7.2 49.0 %all-gather.5.cloned.1.call-start = ((), (), s32[]{:S(2)}) async-start(), calls=%async_computation.8 | async-start | bytes 2129920 | tf_op jit(solution)/shard_map/all_gather | solution.py:894
  9.6 2.6 copy-start.2
  9.8 1.6 collective-permute-start
  12.2 103.3 %all-gather.3.cloned.1.call-start = ((), (), s32[]{:S(2)}) async-start(), calls=%async_computation.7 | async-start | bytes 3522560 | tf_op jit(solution)/shard_map/all_gather | solution.py:896
  14.0 17.7 %all-to-all-start = ((bf16[4,32,768]{2,1,0:T(8,128)(2,1)}), bf16[4,32,768]{2,1,0:T(8,128)(2,1)S(1)}, u32[]{:S(2)}, u32[]{:S(2)}) async-start(bf16[4,32,768]{2,1,0:T(8,128)(2,1)} %pad_maximum_fusion.11), calls=%async_computation | async-start | bytes 393216 | tf_op jit(solution)/shard_map/all_to_all | solution.py:903
  20.3 37.6 %collective-permute-start.2 = (bf16[256,1024]{1,0:T(8,128)(2,1)}, bf16[256,1024]{1,0:T(8,128)(2,1)}, u32[]{:S(2)}, u32[]{:S(2)}) collective-permute-start(bf16[256,1024]{1,0:T(8,128)(2,1)} %bitcast.13.refs_4_.cot_hbm.refs_1_), channel_id=1, source_target_pairs={{0,4},{4,0},{8,12},{12,8},{16,20},{20,16},{24,28},{28,24},{1,5},{5... | collective-permute-start | bytes 1572872 | tf_op jit(solution)/shard_map/ppermute | solution.py:833
  20.3 37.6 %collective-permute-start.1 = (bf16[256,1024]{1,0:T(8,128)(2,1)S(1)}, bf16[256,1024]{1,0:T(8,128)(2,1)}, u32[]{:S(2)}, u32[]{:S(2)}) collective-permute-start(bf16[256,1024]{1,0:T(8,128)(2,1)S(1)} %bitcast.81), channel_id=1, source_target_pairs={{0,4},{4,0},{8,12},{12,8},{16,20},{20,16},{24,28},{28,24},{1,5},{5... | collective-permute-start | bytes 1572872 | tf_op jit(solution)/shard_map/ppermute | solution.py:833
  31.7 5.7 %collective-permute-start.9 = (bf16[128,768]{1,0:T(8,128)(2,1)S(1)}, bf16[128,768]{1,0:T(8,128)(2,1)S(1)}, u32[]{:S(2)}, u32[]{:S(2)}) collective-permute-start(bf16[128,768]{1,0:T(8,128)(2,1)S(1)} %bitcast.85), channel_id=1, source_target_pairs={{0,8},{4,12},{8,0},{12,4},{16,24},{20,28},{24,16},{28,20},{1,9},{5... | collective-permute-start | bytes 589832 | tf_op jit(solution)/shard_map/ppermute | solution.py:833
  37.4 24.8 %collective-permute-start.10 = (bf16[256,768]{1,0:T(8,128)(2,1)S(1)}, bf16[256,768]{1,0:T(8,128)(2,1)S(1)}, u32[]{:S(2)}, u32[]{:S(2)}) collective-permute-start(bf16[256,768]{1,0:T(8,128)(2,1)S(1)} %pad_maximum_fusion.10), channel_id=1, source_target_pairs={{0,16},{4,20},{8,24},{12,28},{16,0},{20,4},{24,8},{28,12},{1,17},{... | collective-permute-start | bytes 1179656 | tf_op jit(solution)/shard_map/ppermute | solution.py:833
  59.2 3.2 copy-start.34
  59.2 22.1 %collective-permute-start.3 = (bf16[256,1664]{1,0:T(8,128)(2,1)}, bf16[256,1664]{1,0:T(8,128)(2,1)}, u32[]{:S(2)}, u32[]{:S(2)}) collective-permute-start(bf16[256,1664]{1,0:T(8,128)(2,1)} %get-tuple-element.102.refs_5_.refs_6_), channel_id=1, source_target_pairs={{0,8},{4,12},{8,0},{12,4},{16,24},{20,28},{24,16},{28,20},{1,9},{5... | collective-permute-start | bytes 2555912 | tf_op jit(solution)/shard_map/ppermute | solution.py:833
  60.7 22.2 %collective-permute-start.6 = (bf16[256,1664]{1,0:T(8,128)(2,1)}, bf16[256,1664]{1,0:T(8,128)(2,1)}, u32[]{:S(2)}, u32[]{:S(2)}) collective-permute-start(bf16[256,1664]{1,0:T(8,128)(2,1)} %get-tuple-element.106.refs_9_.refs_10_), channel_id=1, source_target_pairs={{0,16},{4,20},{8,24},{12,28},{16,0},{20,4},{24,8},{28,12},{1,17},{... | collective-permute-start | bytes 2555912 | tf_op jit(solution)/shard_map/ppermute | solution.py:833
  62.3 22.0 %collective-permute-start.11 = (bf16[512,768]{1,0:T(8,128)(2,1)S(1)}, bf16[512,768]{1,0:T(8,128)(2,1)S(1)}, u32[]{:S(2)}, u32[]{:S(2)}) collective-permute-start(bf16[512,768]{1,0:T(8,128)(2,1)S(1)} %pad_maximum_fusion.1), channel_id=1, source_target_pairs={{0,4},{4,0},{8,12},{12,8},{16,20},{20,16},{24,28},{28,24},{1,5},{5... | collective-permute-start | bytes 2359304 | tf_op jit(solution)/shard_map/ppermute | solution.py:833
  66.2 52.3 %collective-permute-start.4 = (bf16[256,1664]{1,0:T(8,128)(2,1)}, bf16[256,1664]{1,0:T(8,128)(2,1)}, u32[]{:S(2)}, u32[]{:S(2)}) collective-permute-start(bf16[256,1664]{1,0:T(8,128)(2,1)} %get-tuple-element.102.refs_5_.refs_6_), channel_id=1, source_target_pairs={{0,16},{4,20},{8,24},{12,28},{16,0},{20,4},{24,8},{28,12},{1,17},{... | collective-permute-start | bytes 2555912 | tf_op jit(solution)/shard_map/ppermute | solution.py:833
  66.8 53.2 %collective-permute-start.7 = (bf16[256,1664]{1,0:T(8,128)(2,1)}, bf16[256,1664]{1,0:T(8,128)(2,1)}, u32[]{:S(2)}, u32[]{:S(2)}) collective-permute-start(bf16[256,1664]{1,0:T(8,128)(2,1)} %get-tuple-element.106.refs_9_.refs_10_), channel_id=1, source_target_pairs={{0,8},{4,12},{8,0},{12,4},{16,24},{20,28},{24,16},{28,20},{1,9},{5... | collective-permute-start | bytes 2555912 | tf_op jit(solution)/shard_map/ppermute | solution.py:833
  81.3 39.2 %collective-permute-start.5 = (bf16[256,1664]{1,0:T(8,128)(2,1)}, bf16[256,1664]{1,0:T(8,128)(2,1)}, u32[]{:S(2)}, u32[]{:S(2)}) collective-permute-start(bf16[256,1664]{1,0:T(8,128)(2,1)} %collective-permute-done.3.refs_6_.refs_7_), channel_id=1, source_target_pairs={{0,16},{4,20},{8,24},{12,28},{16,0},{20,4},{24,8},{28,12},{1,17},{... | collective-permute-start | bytes 2555912 | tf_op jit(solution)/shard_map/ppermute | solution.py:833
  82.8 38.2 %collective-permute-start.8 = (bf16[256,1664]{1,0:T(8,128)(2,1)}, bf16[256,1664]{1,0:T(8,128)(2,1)}, u32[]{:S(2)}, u32[]{:S(2)}) collective-permute-start(bf16[256,1664]{1,0:T(8,128)(2,1)} %collective-permute-done.6.refs_10_.refs_11_), channel_id=1, source_target_pairs={{0,8},{4,12},{8,0},{12,4},{16,24},{20,28},{24,16},{28,20},{1,9},{5... | collective-permute-start | bytes 2555912 | tf_op jit(solution)/shard_map/ppermute | solution.py:833
  84.4 32.5 %copy-start.12 = (bf16[1024,768]{1,0:T(8,128)(2,1)}, bf16[1024,768]{1,0:T(8,128)(2,1)S(1)}, u32[]{:S(2)}) copy-start(bf16[1024,768]{1,0:T(8,128)(2,1)S(1)} %constant_dynamic-update-slice_fusion.refs_1_.weight_hbm) | copy-start | bytes 4718596
  116.9 22.0 %copy-start.20 = (bf16[352,512]{1,0:T(8,128)(2,1)}, bf16[352,512]{1,0:T(8,128)(2,1)S(1)}, u32[]{:S(2)}) copy-start(bf16[352,512]{1,0:T(8,128)(2,1)S(1)} %get-tuple-element.213.refs_18_.refs_9_) | copy-start | bytes 1081348
  116.9 22.0 %copy-start.21 = (bf16[352,512]{1,0:T(8,128)(2,1)}, bf16[352,512]{1,0:T(8,128)(2,1)S(1)}, u32[]{:S(2)}) copy-start(bf16[352,512]{1,0:T(8,128)(2,1)S(1)} %get-tuple-element.214.refs_14_.refs_5_) | copy-start | bytes 1081348
  116.9 22.0 %collective-permute-start.12 = (bf16[352,512]{1,0:T(8,128)(2,1)S(1)}, bf16[352,512]{1,0:T(8,128)(2,1)S(1)}, u32[]{:S(2)}, u32[]{:S(2)}) collective-permute-start(bf16[352,512]{1,0:T(8,128)(2,1)S(1)} %get-tuple-element.214.refs_14_.refs_5_), channel_id=1, source_target_pairs={{0,8},{4,12},{8,0},{12,4},{16,24},{20,28},{24,16},{28,20},{1,9},{5... | collective-permute-start | bytes 1081352 | tf_op jit(solution)/shard_map/ppermute | solution.py:833
  118.5 20.5 %collective-permute-start.13 = (bf16[352,512]{1,0:T(8,128)(2,1)S(1)}, bf16[352,512]{1,0:T(8,128)(2,1)S(1)}, u32[]{:S(2)}, u32[]{:S(2)}) collective-permute-start(bf16[352,512]{1,0:T(8,128)(2,1)S(1)} %get-tuple-element.214.refs_14_.refs_5_), channel_id=1, source_target_pairs={{0,16},{4,20},{8,24},{12,28},{16,0},{20,4},{24,8},{28,12},{1,17},{... | collective-permute-start | bytes 1081352 | tf_op jit(solution)/shard_map/ppermute | solution.py:833
  120.0 19.0 %collective-permute-start.14 = (bf16[352,512]{1,0:T(8,128)(2,1)S(1)}, bf16[352,512]{1,0:T(8,128)(2,1)S(1)}, u32[]{:S(2)}, u32[]{:S(2)}) collective-permute-start(bf16[352,512]{1,0:T(8,128)(2,1)S(1)} %get-tuple-element.213.refs_18_.refs_9_), channel_id=1, source_target_pairs={{0,16},{4,20},{8,24},{12,28},{16,0},{20,4},{24,8},{28,12},{1,17},{... | collective-permute-start | bytes 1081352 | tf_op jit(solution)/shard_map/ppermute | solution.py:833
  120.5 18.5 %collective-permute-start.15 = (bf16[352,512]{1,0:T(8,128)(2,1)S(1)}, bf16[352,512]{1,0:T(8,128)(2,1)S(1)}, u32[]{:S(2)}, u32[]{:S(2)}) collective-permute-start(bf16[352,512]{1,0:T(8,128)(2,1)S(1)} %get-tuple-element.213.refs_18_.refs_9_), channel_id=1, source_target_pairs={{0,8},{4,12},{8,0},{12,4},{16,24},{20,28},{24,16},{28,20},{1,9},{5... | collective-permute-start | bytes 1081352 | tf_op jit(solution)/shard_map/ppermute | solution.py:833
  138.9 19.9 %copy-start.40 = (bf16[352,512]{1,0:T(8,128)(2,1)}, bf16[352,512]{1,0:T(8,128)(2,1)S(1)}, u32[]{:S(2)}) copy-start(bf16[352,512]{1,0:T(8,128)(2,1)S(1)} %collective-permute-done.12.refs_15_.refs_6_) | copy-start | bytes 1081348
  139.0 19.9 %copy-start.41 = (bf16[352,512]{1,0:T(8,128)(2,1)}, bf16[352,512]{1,0:T(8,128)(2,1)S(1)}, u32[]{:S(2)}) copy-start(bf16[352,512]{1,0:T(8,128)(2,1)S(1)} %collective-permute-done.13.refs_16_.refs_7_) | copy-start | bytes 1081348
  139.9 17.1 %all-to-all-start.1 = ((bf16[4,256,256]{2,1,0:T(8,128)(2,1)}), bf16[4,256,256]{2,1,0:T(8,128)(2,1)S(1)}, u32[]{:S(2)}, u32[]{:S(2)}) async-start(bf16[4,256,256]{2,1,0:T(8,128)(2,1)} %bitcast.100), calls=%async_computation.1 | async-start | bytes 1048576 | tf_op jit(solution)/shard_map/all_to_all | solution.py:932
  143.6 13.4 %collective-permute-start.19 = (bf16[8,256,256]{2,1,0:T(8,128)(2,1)}, bf16[8,256,256]{2,1,0:T(8,128)(2,1)S(1)}, u32[]{:S(2)}, u32[]{:S(2)}) collective-permute-start(bf16[8,256,256]{2,1,0:T(8,128)(2,1)} %get-tuple-element.115), channel_id=1, source_target_pairs={{0,4},{4,0},{8,12},{12,8},{16,20},{20,16},{24,28},{28,24},{1,5},{5... | collective-permute-start | bytes 3145736 | tf_op jit(solution)/shard_map/ppermute | solution.py:833
  143.7 10.8 %collective-permute-start.16 = (bf16[352,512]{1,0:T(8,128)(2,1)S(1)}, bf16[352,512]{1,0:T(8,128)(2,1)S(1)}, u32[]{:S(2)}, u32[]{:S(2)}) collective-permute-start(bf16[352,512]{1,0:T(8,128)(2,1)S(1)} %collective-permute-done.12.refs_15_.refs_6_), channel_id=1, source_target_pairs={{0,16},{4,20},{8,24},{12,28},{16,0},{20,4},{24,8},{28,12},{1,17},{... | collective-permute-start | bytes 1081352 | tf_op jit(solution)/shard_map/ppermute | solution.py:833
  145.2 10.7 %collective-permute-start.17 = (bf16[352,512]{1,0:T(8,128)(2,1)}, bf16[352,512]{1,0:T(8,128)(2,1)S(1)}, u32[]{:S(2)}, u32[]{:S(2)}) collective-permute-start(bf16[352,512]{1,0:T(8,128)(2,1)} %copy-done.42), channel_id=1, source_target_pairs={{0,8},{4,12},{8,0},{12,4},{16,24},{20,28},{24,16},{28,20},{1,9},{5... | collective-permute-start | bytes 1081352 | tf_op jit(solution)/shard_map/ppermute | solution.py:833
  157.0 1.9 collective-permute-start.18
  184.9 2.2 collective-permute-start.20
  192.0 19.2 %all-to-all-start.2 = ((bf16[4,256,256]{2,1,0:T(8,128)(2,1)}), bf16[4,256,256]{2,1,0:T(8,128)(2,1)S(1)}, u32[]{:S(2)}, u32[]{:S(2)}) async-start(bf16[4,256,256]{2,1,0:T(8,128)(2,1)} %get-tuple-element.126), calls=%async_computation.2 | async-start | bytes 1048576 | tf_op jit(solution)/shard_map/all_to_all | solution.py:943
  196.4 118.4 %reduce-scatter.3.cloned.1.call-start = ((), (), s32[]{:S(2)}) async-start(), calls=%async_computation.9 | async-start | bytes 2621440 | tf_op jit(solution)/shard_map/reduce_scatter | solution.py:991
  196.4 34.8 %collective-permute-start.22 = (bf16[512,1408]{1,0:T(8,128)(2,1)}, bf16[512,1408]{1,0:T(8,128)(2,1)}, u32[]{:S(2)}, u32[]{:S(2)}) collective-permute-start(bf16[512,1408]{1,0:T(8,128)(2,1)} %get-tuple-element.138), channel_id=1, source_target_pairs={{0,8},{4,12},{8,0},{12,4},{16,24},{20,28},{24,16},{28,20},{1,9},{5... | collective-permute-start | bytes 4325384 | tf_op jit(solution)/shard_map/ppermute | solution.py:833
  197.9 34.7 %collective-permute-start.23 = (bf16[512,1408]{1,0:T(8,128)(2,1)}, bf16[512,1408]{1,0:T(8,128)(2,1)S(1)}, u32[]{:S(2)}, u32[]{:S(2)}) collective-permute-start(bf16[512,1408]{1,0:T(8,128)(2,1)} %get-tuple-element.139), channel_id=1, source_target_pairs={{0,16},{4,20},{8,24},{12,28},{16,0},{20,4},{24,8},{28,12},{1,17},{... | collective-permute-start | bytes 4325384 | tf_op jit(solution)/shard_map/ppermute | solution.py:833
  209.0 37.7 %collective-permute-start.30 = (bf16[704,512]{1,0:T(8,128)(2,1)}, bf16[704,512]{1,0:T(8,128)(2,1)}, u32[]{:S(2)}, u32[]{:S(2)}) collective-permute-start(bf16[704,512]{1,0:T(8,128)(2,1)} %get-tuple-element.151), channel_id=1, source_target_pairs={{0,8},{4,12},{8,0},{12,4},{16,24},{20,28},{24,16},{28,20},{1,9},{5... | collective-permute-start | bytes 2162696 | tf_op jit(solution)/shard_map/ppermute | solution.py:833
  209.6 39.3 %collective-permute-start.32 = (bf16[704,512]{1,0:T(8,128)(2,1)}, bf16[704,512]{1,0:T(8,128)(2,1)S(1)}, u32[]{:S(2)}, u32[]{:S(2)}) collective-permute-start(bf16[704,512]{1,0:T(8,128)(2,1)} %get-tuple-element.153), channel_id=1, source_target_pairs={{0,16},{4,20},{8,24},{12,28},{16,0},{20,4},{24,8},{28,12},{1,17},{... | collective-permute-start | bytes 2162696 | tf_op jit(solution)/shard_map/ppermute | solution.py:833
  230.0 99.3 %reduce-scatter.5.cloned.1.call-start = ((), (), s32[]{:S(2)}) async-start(), calls=%async_computation.10 | async-start | bytes 2785280 | tf_op jit(solution)/shard_map/reduce_scatter | solution.py:985
  232.6 6.7 %copy-start.14 = (bf16[512,1408]{1,0:T(8,128)(2,1)S(1)}, bf16[512,1408]{1,0:T(8,128)(2,1)}, u32[]{:S(2)}) copy-start(bf16[512,1408]{1,0:T(8,128)(2,1)} %get-tuple-element.148) | copy-start | bytes 4325380
  241.1 22.4 %collective-permute-start.27 = (bf16[256,1408]{1,0:T(8,128)(2,1)S(1)}, bf16[256,1408]{1,0:T(8,128)(2,1)S(1)}, u32[]{:S(2)}, u32[]{:S(2)}) collective-permute-start(bf16[256,1408]{1,0:T(8,128)(2,1)S(1)} %slice.294), channel_id=1, source_target_pairs={{0,16},{4,20},{8,24},{12,28},{16,0},{20,4},{24,8},{28,12},{1,17},{... | collective-permute-start | bytes 2162696 | tf_op jit(solution)/shard_map/ppermute | solution.py:833
  242.8 3.9 %copy-start.17 = (bf16[704,512]{1,0:T(8,128)(2,1)S(1)}, bf16[704,512]{1,0:T(8,128)(2,1)}, u32[]{:S(2)}) copy-start(bf16[704,512]{1,0:T(8,128)(2,1)} %get-tuple-element.150) | copy-start | bytes 2162692
  242.8 6.0 %copy-start.16 = (bf16[704,512]{1,0:T(8,128)(2,1)S(1)}, bf16[704,512]{1,0:T(8,128)(2,1)}, u32[]{:S(2)}) copy-start(bf16[704,512]{1,0:T(8,128)(2,1)} %get-tuple-element.152) | copy-start | bytes 2162692
  242.9 20.9 %collective-permute-start.28 = (bf16[256,1408]{1,0:T(8,128)(2,1)S(1)}, bf16[256,1408]{1,0:T(8,128)(2,1)S(1)}, u32[]{:S(2)}, u32[]{:S(2)}) collective-permute-start(bf16[256,1408]{1,0:T(8,128)(2,1)S(1)} %slice.296), channel_id=1, source_target_pairs={{0,8},{4,12},{8,0},{12,4},{16,24},{20,28},{24,16},{28,20},{1,9},{5... | collective-permute-start | bytes 2162696 | tf_op jit(solution)/shard_map/ppermute | solution.py:833
  248.0 21.8 %collective-permute-start.31 = (bf16[352,512]{1,0:T(8,128)(2,1)S(1)}, bf16[352,512]{1,0:T(8,128)(2,1)S(1)}, u32[]{:S(2)}, u32[]{:S(2)}) collective-permute-start(bf16[352,512]{1,0:T(8,128)(2,1)S(1)} %slice.298), channel_id=1, source_target_pairs={{0,16},{4,20},{8,24},{12,28},{16,0},{20,4},{24,8},{28,12},{1,17},{... | collective-permute-start | bytes 1081352 | tf_op jit(solution)/shard_map/ppermute | solution.py:833
  249.1 20.8 %collective-permute-start.33 = (bf16[352,512]{1,0:T(8,128)(2,1)S(1)}, bf16[352,512]{1,0:T(8,128)(2,1)S(1)}, u32[]{:S(2)}, u32[]{:S(2)}) collective-permute-start(bf16[352,512]{1,0:T(8,128)(2,1)S(1)} %slice.300), channel_id=1, source_target_pairs={{0,8},{4,12},{8,0},{12,4},{16,24},{20,28},{24,16},{28,20},{1,9},{5... | collective-permute-start | bytes 1081352 | tf_op jit(solution)/shard_map/ppermute | solution.py:833
  264.1 7.1 %collective-permute-start.29 = (bf16[128,2816]{1,0:T(8,128)(2,1)S(1)}, bf16[128,2816]{1,0:T(8,128)(2,1)S(1)}, u32[]{:S(2)}, u32[]{:S(2)}) collective-permute-start(bf16[128,2816]{1,0:T(8,128)(2,1)S(1)} %pad_maximum_fusion.3), channel_id=1, source_target_pairs={{0,4},{4,0},{8,12},{12,8},{16,20},{20,16},{24,28},{28,24},{1,5},{5... | collective-permute-start | bytes 2162696 | tf_op jit(solution)/shard_map/ppermute | solution.py:833
  265.5 7.6 %collective-permute-start.24 = (bf16[512,1792]{1,0:T(8,128)(2,1)S(1)}, bf16[512,1792]{1,0:T(8,128)(2,1)}, u32[]{:S(2)}, u32[]{:S(2)}) collective-permute-start(bf16[512,1792]{1,0:T(8,128)(2,1)S(1)} %copy-done.37), channel_id=1, source_target_pairs={{0,4},{4,0},{8,12},{12,8},{16,20},{20,16},{24,28},{28,24},{1,5},{5... | collective-permute-start | bytes 5505032 | tf_op jit(solution)/shard_map/ppermute | solution.py:833
  275.7 22.4 %collective-permute-start.25 = (bf16[256,1792]{1,0:T(8,128)(2,1)S(1)}, bf16[256,1792]{1,0:T(8,128)(2,1)}, u32[]{:S(2)}, u32[]{:S(2)}) collective-permute-start(bf16[256,1792]{1,0:T(8,128)(2,1)S(1)} %slice.290), channel_id=1, source_target_pairs={{0,8},{4,12},{8,0},{12,4},{16,24},{20,28},{24,16},{28,20},{1,9},{5... | collective-permute-start | bytes 2752520 | tf_op jit(solution)/shard_map/ppermute | solution.py:833
  277.7 22.8 %collective-permute-start.21 = (bf16[256,1024]{1,0:T(8,128)(2,1)}, bf16[256,1024]{1,0:T(8,128)(2,1)}, u32[]{:S(2)}, u32[]{:S(2)}) collective-permute-start(bf16[256,1024]{1,0:T(8,128)(2,1)} %get-tuple-element.128), channel_id=1, source_target_pairs={{0,4},{4,0},{8,12},{12,8},{16,20},{20,16},{24,28},{28,24},{1,5},{5... | collective-permute-start | bytes 1572872 | tf_op jit(solution)/shard_map/ppermute | solution.py:833
  278.5 24.2 %all-to-all-start.4 = ((f32[32,8,128]{2,1,0:T(8,128)}), f32[32,8,128]{2,1,0:T(8,128)}, u32[]{:S(2)}, u32[]{:S(2)}) async-start(f32[32,8,128]{2,1,0:T(8,128)} %broadcast_in_dim.35), calls=%async_computation.6 | async-start | bytes 262144 | tf_op jit(solution)/shard_map/all_to_all | solution.py:987
  283.8 16.8 %copy-start.10 = (f32[256,1024]{1,0:T(8,128)S(1)}, f32[256,1024]{1,0:T(8,128)}, u32[]{:S(2)}) copy-start(f32[256,1024]{1,0:T(8,128)} %get-tuple-element.116.res_hbm) | copy-start | bytes 3145732
  283.8 16.8 %copy-start.15 = (f32[256,1024]{1,0:T(8,128)S(1)}, f32[256,1024]{1,0:T(8,128)}, u32[]{:S(2)}) copy-start(f32[256,1024]{1,0:T(8,128)} %get-tuple-element.125) | copy-start | bytes 3145732
  299.5 10.1 %collective-permute-start.26 = (bf16[128,1792]{1,0:T(8,128)(2,1)S(1)}, bf16[128,1792]{1,0:T(8,128)(2,1)S(1)}, u32[]{:S(2)}, u32[]{:S(2)}) collective-permute-start(bf16[128,1792]{1,0:T(8,128)(2,1)S(1)} %slice.292), channel_id=1, source_target_pairs={{0,16},{4,20},{8,24},{12,28},{16,0},{20,4},{24,8},{28,12},{1,17},{... | collective-permute-start | bytes 1376264 | tf_op jit(solution)/shard_map/ppermute | solution.py:833
  303.8 12.6 %copy-start.35 = (f32[16]{0:T(128)}, f32[16]{0:T(128)S(1)}, u32[]{:S(2)}) copy-start(f32[16]{0:T(128)S(1)} %reshape_squeeze.3) | copy-start | bytes 196
  303.8 12.6 %copy-start.36 = (f32[16]{0:T(128)}, f32[16]{0:T(128)S(1)}, u32[]{:S(2)}) copy-start(f32[16]{0:T(128)S(1)} %divide_sqrt_fusion) | copy-start | bytes 196
  310.5 22.9 %all-to-all-start.3 = ((bf16[4,32,1792]{2,1,0:T(8,128)(2,1)}), bf16[4,32,1792]{2,1,0:T(8,128)(2,1)S(1)}, u32[]{:S(2)}, u32[]{:S(2)}) async-start(bf16[4,32,1792]{2,1,0:T(8,128)(2,1)} %bitcast.26), calls=%async_computation.4 | async-start | bytes 917504 | tf_op jit(solution)/shard_map/all_to_all | solution.py:998
  314.9 3.0 copy-start.9
  317.9 11.4 %copy-start = (bf16[32,2816]{1,0:T(8,128)(2,1)S(1)}, bf16[32,2816]{1,0:T(8,128)(2,1)}, u32[]{:S(2)}) copy-start(bf16[32,2816]{1,0:T(8,128)(2,1)} %wu.1) | copy-start | bytes 540676
  317.9 11.4 %copy-start.1 = (bf16[32,2816]{1,0:T(8,128)(2,1)S(1)}, bf16[32,2816]{1,0:T(8,128)(2,1)}, u32[]{:S(2)}) copy-start(bf16[32,2816]{1,0:T(8,128)(2,1)} %wg.1) | copy-start | bytes 540676
  317.9 11.4 %copy-start.4 = (f32[32,2816]{1,0:T(8,128)S(1)}, f32[32,2816]{1,0:T(8,128)}, u32[]{:S(2)}) copy-start(f32[32,2816]{1,0:T(8,128)} %mg.1) | copy-start | bytes 1081348
  317.9 11.4 %copy-start.5 = (f32[32,2816]{1,0:T(8,128)S(1)}, f32[32,2816]{1,0:T(8,128)}, u32[]{:S(2)}) copy-start(f32[32,2816]{1,0:T(8,128)} %mu.1) | copy-start | bytes 1081348
  317.9 11.4 %copy-start.6 = (f32[88,1024]{1,0:T(8,128)S(1)}, f32[88,1024]{1,0:T(8,128)}, u32[]{:S(2)}) copy-start(f32[88,1024]{1,0:T(8,128)} %md.1) | copy-start | bytes 1081348
  (25 other events, 35.5 us)
Sparse Core Ops, SparseCore 0:
  12.4 43.8 all-gather.4
  58.4 57.1 all-gather.2
  230.2 44.1 reduce-scatter.2
  276.6 52.6 reduce-scatter.4

commit v9 on v8

--- a/solution.py
+++ b/solution.py
@@ -338,11 +338,22 @@
     return c * lax.rsqrt(v + NORM_EPS)
 
 
+def wide_pieces(own, by_x, by_y, a_far, b_far):
+    return ([own.at[0], by_x.at[0], by_y.at[0], a_far], [own.at[1], by_y.at[1], by_x.at[1], b_far])
+
+
+def down_pieces(own, by_x, by_y, a_far, b_far):
+    low, high = pl.ds(0, 512), pl.ds(512, 512)
+    return ([own.at[:, low], by_x.at[:, low], by_y.at[:, low], a_far],
+            [own.at[:, high], by_y.at[:, high], by_x.at[:, high], b_far])
+
+
 def attend_kernel(*refs):
-    (rows_hbm, weight_hbm, cos_hbm, sin_hbm, id_hbm, *pieces) = refs[:13]
-    normed_hbm, mixed_hbm, attended_hbm, total_hbm, peak_hbm, outs_hbm = refs[13:19]
+    rows_hbm, weight_hbm, cos_hbm, sin_hbm, id_hbm = refs[:5]
+    pieces = sum(wide_pieces(*refs[5:10]), [])
+    normed_hbm, mixed_hbm, attended_hbm, total_hbm, peak_hbm, outs_hbm = refs[10:16]
     (act, weight, cos_ref, sin_ref, ids, id_col, normed, mixed_ref, attended, value_t, total_ref,
-     peak_ref, outs, sems) = refs[19:]
+     peak_ref, outs, sems) = refs[16:]
     n = normed.shape[0]
     go = Copies(sems)
     early = [go.start(rows_hbm.at[pl.ds(344 * i, 256)], act.at[pl.ds(256 * i, 256)]) for i in range(4)]
@@ -567,11 +578,13 @@
 
 def feed_kernel(*refs):
     att_hbm, attp_hbm, act_hbm, actp_hbm, cot_hbm, cotp_hbm = refs[:6]
-    a_in, b_in, da_in, db_in, outs = refs[6:10], refs[10:14], refs[14:18], refs[18:22], refs[22]
-    part_hbm, gnown_hbm, res_hbm, wo_hbm, h_hbm = refs[23:28]
-    ga_keep, ga_send, gb_keep, gb_send = refs[28:32]
+    a_in, b_in = wide_pieces(*refs[6:11])
+    da_in, db_in = down_pieces(*refs[11:16])
+    outs = refs[16]
+    part_hbm, gnown_hbm, res_hbm, wo_hbm, h_hbm = refs[17:22]
+    ga_keep, ga_send, gb_keep, gb_send = refs[22:26]
     (wg, wu, wd, wo, att, act, n2, n2t, cot, res_ref, gn_acc, part, dg, du, hidden,
-     sems, osem, tsem) = refs[32:]
+     sems, osem, tsem) = refs[26:]
     me = lax.axis_index("dp")
     core = me % 2
     yx = me // 2
@@ -669,7 +682,7 @@
     wait_all(done)
 
 
-def feed(att, attp, act, actp, cot, cotp, a, b, da, db, outs):
+def feed(att, attp, act, actp, cot, cotp, wide, down, outs):
     big = [((1024, FFP), bf), ((1024, FFP), bf), ((FFP, 1024), bf)]
     return call(
         feed_kernel, "feed",
@@ -678,15 +691,15 @@
         big + [((1024, 1024), bf), ((512, 1024), bf), ((512, 1024), bf), ((512, 1024), bf), ((1024, 512), bf),
                ((512, 1024), bf), ((512, 1024), f32), ((512, 1024), f32), ((256, 1024), bf)]
         + big[:2] + [((512, FFP), bf)],
-        [68, 4, (6, 9)], 12, (att, attp, act, actp, cot, cotp, *a, *b, *da, *db, outs), 50,
+        [68, 4, (6, 9)], 12, (att, attp, act, actp, cot, cotp, *wide, *down, outs), 50,
     )
 
 
 def finish_kernel(*refs):
     h_hbm, cot_hbm, cotp_hbm, att_hbm, gres_hbm = refs[:5]
-    da_in, db_in = refs[5:9], refs[9:13]
-    part_hbm, own_hbm, gda_keep, gda_send, gdb_keep, gdb_send, keep_hbm, send_hbm = refs[13:21]
-    hidden, cot, att, gres, wd, out, part, dd, gw, sems = refs[21:]
+    da_in, db_in = down_pieces(*refs[5:10])
+    part_hbm, own_hbm, gda_keep, gda_send, gdb_keep, gdb_send, keep_hbm, send_hbm = refs[10:18]
+    hidden, cot, att, gres, wd, out, part, dd, gw, sems = refs[18:]
     me = lax.axis_index("dp")
     core = me % 2
     yx = me // 2
@@ -734,7 +747,7 @@
     wait_all(done)
 
 
-def finish(hidden, cot, cotp, att, gres, da, db):
+def finish(hidden, cot, cotp, att, gres, down):
     tall = ((256, 1024), f32)
     low = ((256, 1024), bf)
     half = ((512, 1024), bf)
@@ -742,7 +755,7 @@
         finish_kernel, "finish",
         [low, tall] + [((704, 512), bf)] * 4 + [half] * 2,
         [((512, FF2), bf), half, low, tall, ((FF2, 1024), bf), tall, low, ((FF2, 1024), bf), ((1024, 1024), bf)],
-        [34], 60, (hidden, cot, cotp, att, gres, *da, *db), 32,
+        [34], 60, (hidden, cot, cotp, att, gres, *down), 32,
     )
 
 
@@ -905,35 +918,30 @@
     hy = swap(jnp.concatenate([heads, hx], axis=0), 4)
     four = jnp.concatenate([heads, hy[:128], hx, hy[128:]], axis=0)
     heads_rel = jnp.concatenate([four, swap(four, 1)], axis=0)
-    wide, act_other, cot_other = lax.optimization_barrier((wide, act_other, cot_other))
-
-    def spread(own, first, second):
-        near = swap(own, first)
-        return [own, near, swap(own, second), swap(near, second)]
-
-    piece_a = spread(wide[0], 2, 4)
-    piece_b = spread(wide[1], 4, 2)
-    down = jnp.concatenate(
-        [rows_all[344 * i + 256 : 344 * i + 344] for i in range(4)], axis=0
-    )
-    piece_da = spread(down[:, :512], 2, 4)
-    piece_db = spread(down[:, 512:], 4, 2)
     cosine, sine = rotary_tables(jnp.arange(length, dtype=jnp.int32), HEAD_DIM)
     cosine = jnp.concatenate([cosine] * 4, axis=1)
     sine = jnp.concatenate([-sine, sine, -sine, sine], axis=1)
     ids = jnp.broadcast_to(block_ids, (8, length)).astype(f32)
-    pieces = lax.optimization_barrier((rows_all, *piece_a, *piece_b))
+    wide, act_other, cot_other, heads_rel, cosine, sine, ids = lax.optimization_barrier(
+        (wide, act_other, cot_other, heads_rel, cosine, sine, ids)
+    )
+
+    wide_x, wide_y = swap(wide, 2), swap(wide, 4)
+    wide_all = [wide, wide_x, wide_y, swap(wide_x[0], 4), swap(wide_y[1], 2)]
+    down = jnp.concatenate([rows_all[344 * i + 256 : 344 * i + 344] for i in range(4)], axis=0)
+    down_x, down_y = swap(down, 2), swap(down, 4)
+    rows_all, *wide_all = lax.optimization_barrier((rows_all, *wide_all))
     normed, mixed, attended, totals, peaks, outs = attend(
-        pieces[0], heads_rel, cosine, sine, ids, pieces[1:]
-    )
-    piece_a, piece_b = pieces[1:5], pieces[5:]
+        rows_all, heads_rel, cosine, sine, ids, wide_all
+    )
     outs = swap(outs, 1)
-    attended = tie(attended, *piece_da[1:3], *piece_db[1:3])
+    attended, down_x, down_y = lax.optimization_barrier((attended, down_x, down_y))
+    down_all = [down, down_x, down_y, swap(down_x[:, :512], 4), swap(down_y[:, 512:], 2)]
     attended = lax.all_to_all(attended.reshape(4, span, 256), "ctx", 0, 0, tiled=True)
-    attended_other = swap(tie(attended, piece_da[3], piece_db[3]), 1)
+    attended_other = swap(tie(attended, *down_all[3:]), 1)
     part, back_own, residual, full_out, hidden, ga_keep, ga_send, gb_keep, gb_send = feed(
         attended, attended_other, act, act_other, cot, cot_other,
-        piece_a, piece_b, piece_da, piece_db, outs,
+        wide_all, down_all, outs,
     )
     part = swap(part, 1)
     ga_send, gb_send, part = lax.optimization_barrier((ga_send, gb_send, part))
@@ -942,7 +950,7 @@
     grad_residual, grad_attended = branch(part, back_own, residual, cot, full_out)
     grad_attended = lax.all_to_all(grad_attended, "ctx", 0, 0, tiled=True).reshape(length, 256)
     (out_part, out_own, gda_keep, gda_send, gdb_keep, gdb_send, go_keep, go_send) = finish(
-        hidden, cot, cot_other, attended, grad_residual, piece_da, piece_db
+        hidden, cot, cot_other, attended, grad_residual, down_all
     )
     gda_other = swap(gda_send, 2)
     gdb_other = swap(gdb_send, 4)

time: 345 us -> 344 us (level)
  blocking collectives: 0 us -> 13.8 us
  waiting for transfers between devices: 145 us -> 135 us
  starting transfers between devices: 52.8 us -> 46.9 us
    ppermute x34 -> x30, waiting for transfers between devices: 74.8 us -> 101 us  [swap(): return lax.ppermute(array, 'dp', [(i, i ^ bit) for i in range(8)])]
    all_gather x1, waiting for transfers between devices: 31.1 us -> 13.4 us  [fast_device(): rows_all = lax.all_gather(padded, 'ctx', axis=0, tiled=True)]
    all_to_all x0 -> x1, blocking collectives: none -> 13.8 us  [fast_device(): heads = lax.all_to_all(heads, 'ctx', 0, 0, tiled=True).reshape(128, 768)]
    all_to_all x1 -> x0, waiting for transfers between devices: 10.9 us -> none  [fast_device(): heads = lax.all_to_all(heads, 'ctx', 0, 0, tiled=True).reshape(128, 768)]
    all_gather x1, waiting for transfers between devices: 17.3 us -> 9.72 us  [fast_device(): lax.all_gather(wide, 'ctx', axis=2, tiled=True).reshape(2, 256, FF2 + 256)]
    all_to_all x1 -> x0, starting transfers between devices: 6.23 us -> none  [fast_device(): heads = lax.all_to_all(heads, 'ctx', 0, 0, tiled=True).reshape(128, 768)]
    unnamed x96 -> x98, local copies, waits for them, and re-layouts: 7.4 us -> 8.65 us
    ppermute x34 -> x30, starting transfers between devices: 28.4 us -> 27.4 us  [swap(): return lax.ppermute(array, 'dp', [(i, i ^ bit) for i in range(8)])]
  transfers between devices with their start and end apart: 43 -> 38, of which waited for: 21 -> 22; matrix products, arithmetic and copies ran while one was open for 10% -> 9% of each run, Pallas kernels for 16% -> 16%
where the time goes in v9:
time: 344 us; the launch traced here: 341 us
  waiting for transfers between devices  135 us (39%)
  Pallas kernels  83.2 us (24%)
  starting transfers between devices  46.9 us (14%)
  other arithmetic  27.8 us (8%)
  local copies, waits for them, and re-layouts  18.1 us (5%)
  between operations  16.1 us (5%)
  blocking collectives  13.8 us (4%)
    ppermute x30, waiting for transfers between devices, swap(): return lax.ppermute(array, 'dp', [(i, i ^ bit) for i in range(8)])  101 us
    pallas_call x6, Pallas kernels, call(): pl.pallas_call(kernel, out_shape=tuple((pltpu.HBM(*o) for o in outs)), in...  81.4 us
    ppermute x30, starting transfers between devices, swap(): return lax.ppermute(array, 'dp', [(i, i ^ bit) for i in range(8)])  27.4 us
    all_to_all x1, blocking collectives, fast_device(): heads = lax.all_to_all(heads, 'ctx', 0, 0, tiled=True).reshape(128, 768)  13.8 us
    all_gather x1, waiting for transfers between devices, fast_device(): rows_all = lax.all_gather(padded, 'ctx', axis=0, tiled=True)  13.4 us
    reduce_scatter x1, waiting for transfers between devices, fast_device(): lax.psum_scatter(grad_wide, 'ctx', scatter_dimension=0, tiled=True)  10.3 us
    all_gather x1, waiting for transfers between devices, fast_device(): lax.all_gather(wide, 'ctx', axis=2, tiled=True).reshape(2, 256, FF2 + 256)  9.72 us
    convert_element_type x11, other arithmetic, add_low(): return (left.astype(f32) + right.astype(f32)).astype(bf)  8.84 us
  transfers between devices with their start and end apart: 38, of which 22 were waited for; matrix products, arithmetic and copies ran while one was open for 9% of the time, Pallas kernels for 16%

profile of v9, /device:TPU:0, one launch (start us, length us, event | category | flops | bytes accessed | tf_op | source)
XLA Modules:
  0.0 341.3 jit_solution(3484073886245974898)
XLA Ops:
  7.3 1.0 fusion.14
  8.3 1.0 fusion.15
  12.5 13.8 %all_to_all.25 = bf16[4,32,768]{2,1,0:T(8,128)(2,1)S(1)} all-to-all(bf16[4,32,768]{2,1,0:T(8,128)(2,1)S(1)} %pad_maximum_fusion.11), channel_id=1, replica_groups=mesh['dp'=8,'ctx'=4] {'ctx'}, dimensions={0} | all-to-all | bytes 393216 | tf_op jit(solution)/shard_map/all_to_all | solution.py:916
  26.3 1.5 collective-permute-start.3
  27.8 4.2 %collective-permute-done.3 = bf16[128,768]{1,0:T(8,128)(2,1)S(1)} collective-permute-done((bf16[128,768]{1,0:T(8,128)(2,1)S(1)}, bf16[128,768]{1,0:T(8,128)(2,1)S(1)}, u32[]{:S(2)}, u32[]{:S(2)}) %collective-permute-start.3) | collective-permute-done | bytes 196640 | tf_op jit(solution)/shard_map/ppermute | solution.py:846
  32.0 1.6 collective-permute-start.4
  35.0 5.4 %collective-permute-done.4 = bf16[256,768]{1,0:T(8,128)(2,1)S(1)} collective-permute-done((bf16[256,768]{1,0:T(8,128)(2,1)S(1)}, bf16[256,768]{1,0:T(8,128)(2,1)S(1)}, u32[]{:S(2)}, u32[]{:S(2)}) %collective-permute-start.4) | collective-permute-done | bytes 393248 | tf_op jit(solution)/shard_map/ppermute | solution.py:846
  40.6 1.9 fusion.7
  42.6 1.9 pad_maximum_fusion.7
  44.5 9.7 %all-gather.5.cloned.1.call-done = bf16[2,2,128,1664]{3,2,0,1:T(8,128)(2,1)} async-done(((bf16[2,2,32,1664]{3,2,0,1:T(8,128)(2,1)}), bf16[2,2,128,1664]{3,2,0,1:T(8,128)(2,1)}) %all-gather.5.cloned.1.call-update) | async-done | bytes 1703952 | tf_op jit(solution)/shard_map/all_gather | solution.py:907
  54.3 1.6 copy.60
  56.6 1.5 collective-permute-start.6
  58.0 1.5 collective-permute-start.7
  59.5 36.0 %collective-permute-done.6.refs_6_.refs_7_ = bf16[2,256,1664]{2,1,0:T(8,128)(2,1)S(1)} collective-permute-done((bf16[2,256,1664]{2,1,0:T(8,128)(2,1)S(1)}, bf16[2,256,1664]{2,1,0:T(8,128)(2,1)S(1)}, u32[]{:S(2)}, u32[]{:S(2)}) %collective-permute-start.6) | collective-permute-done | bytes 1703968 | tf_op jit(solution)/shard_map/ppermute | solution.py:846
  95.6 1.5 collective-permute-start.8
  97.1 1.3 copy-done.23
  98.4 1.5 collective-permute-start.9
  100.0 13.4 %all-gather.3.cloned.1.call-done.refs_0_ = bf16[1376,1024]{1,0:T(8,128)(2,1)} async-done(((bf16[344,1024]{1,0:T(8,128)(2,1)}), bf16[1376,1024]{1,0:T(8,128)(2,1)}) %all-gather.3.cloned.1.call-update) | async-done | bytes 2818064 | tf_op jit(solution)/shard_map/all_gather | solution.py:909
  113.4 1.2 fusion.12
  114.7 1.5 collective-permute-start.10
  116.3 1.5 collective-permute-start.11
  117.7 1.3 collective-permute-done.9.refs_9_.refs_10_
  119.0 17.2 %attend.1 = (bf16[1024,1024]{1,0:T(8,128)(2,1)}, bf16[1024,768]{1,0:T(8,128)(2,1)}, bf16[1024,256]{1,0:T(8,128)(2,1)}, f32[8,1024]{1,0:T(8,128)}, f32[8,128]{1,0:T(8,128)}, /*index=5*/bf16[8,256,256]{2,1,0:T(8,128)(2,1)}) custom-call(bf16[1376,1024]{1,0:T(8,128)(2,1)} %all-gather.3.cloned.1.call-done.refs_0_, bf16[1024,768]{1,0:T(8,128)(2,1)} %copy-done.12, ...), custom_call_target="tpu_custom_call" | custom-call | flops 4294967296 | bytes 8388608 | tf_op jit(solution)/shard_map/attend/pallas_call | solution.py:308
  138.0 4.1 %all-to-all-start.1 = ((bf16[4,256,256]{2,1,0:T(8,128)(2,1)}), bf16[4,256,256]{2,1,0:T(8,128)(2,1)S(1)}, u32[]{:S(2)}, u32[]{:S(2)}) async-start(bf16[4,256,256]{2,1,0:T(8,128)(2,1)} %bitcast.103), calls=%async_computation.1 | async-start | bytes 1048576 | tf_op jit(solution)/shard_map/all_to_all | solution.py:940
  142.1 1.0 slice.250
  143.5 1.0 collective-permute-start.13
  144.6 9.4 %collective-permute-done.12.refs_14_.refs_8_ = bf16[352,512]{1,0:T(8,128)(2,1)S(1)} collective-permute-done((bf16[352,512]{1,0:T(8,128)(2,1)S(1)}, bf16[352,512]{1,0:T(8,128)(2,1)S(1)}, u32[]{:S(2)}, u32[]{:S(2)}) %collective-permute-start.12) | collective-permute-done | bytes 360480 | tf_op jit(solution)/shard_map/ppermute | solution.py:846
  154.5 1.9 collective-permute-done.14.refs_1_
  157.2 25.2 %feed.1 = (bf16[256,1024]{1,0:T(8,128)(2,1)}, f32[256,1024]{1,0:T(8,128)}, f32[256,1024]{1,0:T(8,128)}, bf16[1024,1024]{1,0:T(8,128)(2,1)}, bf16[512,1408]{1,0:T...) custom-call(bf16[4,256,256]{2,1,0:T(8,128)(2,1)} %copy-done.21, ...), custom_call_target="tpu_custom_call" | custom-call | flops 12884901888 | bytes 8388608 | tf_op jit(solution)/shard_map/feed/pallas_call | solution.py:308
  182.7 2.0 collective-permute-done.16.part_hbm
  185.4 4.1 %branch.1 = (f32[256,1024]{1,0:T(8,128)}, bf16[4,256,256]{2,1,0:T(8,128)(2,1)}) custom-call(bf16[256,1024]{1,0:T(8,128)(2,1)} %copy-done.20, f32[256,1024]{1,0:T(8,128)} %get-tuple-element.128.gnown_hbm, f32[256,1024]{1,0:T(8,128)} %get-tuple-element.122.res_hbm, bf16[256,1024]{1,0:T(8,128)(2,1)} %bitcast.13.refs_4_.cot_hbm.refs_1_, ...), custom_call_target="tpu_custom_call" | custom-call | flops 1073741824 | bytes 8388608 | tf_op jit(solution)/shard_map/branch/pallas_call | solution.py:308
  189.6 4.8 %all-to-all-start.2 = ((bf16[4,256,256]{2,1,0:T(8,128)(2,1)}), bf16[4,256,256]{2,1,0:T(8,128)(2,1)S(1)}, u32[]{:S(2)}, u32[]{:S(2)}) async-start(bf16[4,256,256]{2,1,0:T(8,128)(2,1)} %get-tuple-element.132), calls=%async_computation.2 | async-start | bytes 1048576 | tf_op jit(solution)/shard_map/all_to_all | solution.py:951
  194.4 1.2 collective-permute-start.18
  195.6 1.7 collective-permute-start.19
  197.3 10.3 %finish.1 = (bf16[256,1024]{1,0:T(8,128)(2,1)}, f32[256,1024]{1,0:T(8,128)}, bf16[704,512]{1,0:T(8,128)(2,1)}, bf16[704,512]{1,0:T(8,128)(2,1)}, bf16[704,512]{1...) custom-call(bf16[512,1408]{1,0:T(8,128)(2,1)} %get-tuple-element.123.refs_0_, ...), custom_call_target="tpu_custom_call" | custom-call | flops 64424509440 | bytes 8388608 | tf_op jit(solution)/shard_map/finish/pallas_call | solution.py:308
  210.0 17.9 %attend_back.1 = (bf16[1024,768]{1,0:T(8,128)(2,1)}, bf16[1024,1024]{1,0:T(8,128)(2,1)}) custom-call(bf16[1024,768]{1,0:T(8,128)(2,1)} %get-tuple-element.135.mixed_hbm, bf16[1024,256]{1,0:T(8,128)(2,1)} %bitcast.90, f32[8,1024]{1,0:T(8,128)} %get-tuple-element.137.total_hbm, f32[1024,128]{1,0:T(8,128)} %get-tuple-element.106.refs_2_.cos_hbm, ...), custom_call_target="tpu_custom_call" | custom-call | bytes 8388608 | tf_op jit(solution)/shard_map/attend_back/pallas_call | solution.py:308
  228.2 1.0 collective-permute-done.18
  229.2 1.2 collective-permute-done.19
  230.3 6.7 %project_weights.1 = (bf16[512,1792]{1,0:T(8,128)(2,1)}, bf16[512,1792]{1,0:T(8,128)(2,1)}) custom-call(bf16[1024,768]{1,0:T(8,128)(2,1)} %get-tuple-element.146.gm_hbm, bf16[1024,1024]{1,0:T(8,128)(2,1)} %get-tuple-element.147.normed_hbm, bf16[512,1024]{1,0:T(8,128)(2,1)} %get-tuple-element.148.okeep_hbm, bf16[512,1024]{1,0:T(8,128)(2,1)} %get-tuple-element.149.osend_hbm), custom_call_target="tpu_custom_call" | custom-call | flops 1073741824 | bytes 8388608 | tf_op jit(solution)/shard_map/project_weights/pallas_call | solution.py:308
  237.1 1.7 add_convert_fusion.2
  238.8 1.8 collective-permute-start.23
  241.9 2.7 collective-permute-done.26
  244.6 1.3 add_convert_fusion.5
  246.0 1.7 collective-permute-start.27
  247.9 1.3 collective-permute-start.29
  249.3 12.0 %collective-permute-done.23 = bf16[256,1408]{1,0:T(8,128)(2,1)S(1)} collective-permute-done((bf16[256,1408]{1,0:T(8,128)(2,1)S(1)}, bf16[256,1408]{1,0:T(8,128)(2,1)S(1)}, u32[]{:S(2)}, u32[]{:S(2)}) %collective-permute-start.23) | collective-permute-done | bytes 720928 | tf_op jit(solution)/shard_map/ppermute | solution.py:846
  261.9 1.3 copy-done.42
  263.2 4.3 %collective-permute-done.27 = bf16[352,512]{1,0:T(8,128)(2,1)S(1)} collective-permute-done((bf16[352,512]{1,0:T(8,128)(2,1)S(1)}, bf16[352,512]{1,0:T(8,128)(2,1)S(1)}, u32[]{:S(2)}, u32[]{:S(2)}) %collective-permute-start.27) | collective-permute-done | bytes 360480 | tf_op jit(solution)/shard_map/ppermute | solution.py:846
  269.2 1.5 pad_maximum_fusion
  270.7 2.5 add_convert_fusion
  276.4 5.9 %all-to-all-start.4 = ((f32[32,8,128]{2,1,0:T(8,128)}), f32[32,8,128]{2,1,0:T(8,128)}, u32[]{:S(2)}, u32[]{:S(2)}) async-start(f32[32,8,128]{2,1,0:T(8,128)} %broadcast_in_dim.35), calls=%async_computation.6 | async-start | bytes 262144 | tf_op jit(solution)/shard_map/all_to_all | solution.py:995
  282.3 13.4 %collective-permute-done.21 = bf16[256,1792]{1,0:T(8,128)(2,1)} collective-permute-done((bf16[256,1792]{1,0:T(8,128)(2,1)S(1)}, bf16[256,1792]{1,0:T(8,128)(2,1)}, u32[]{:S(2)}, u32[]{:S(2)}) %collective-permute-start.21) | collective-permute-done | bytes 917536 | tf_op jit(solution)/shard_map/ppermute | solution.py:846
  295.7 1.4 add_convert_fusion.3
  297.1 1.8 collective-permute-start.22
  298.9 2.1 fusion.6
  301.0 0.9 reduce_max.9
  302.3 5.0 %collective-permute-done.22 = bf16[128,1792]{1,0:T(8,128)(2,1)S(1)} collective-permute-done((bf16[128,1792]{1,0:T(8,128)(2,1)S(1)}, bf16[128,1792]{1,0:T(8,128)(2,1)S(1)}, u32[]{:S(2)}, u32[]{:S(2)}) %collective-permute-start.22) | collective-permute-done | bytes 458784 | tf_op jit(solution)/shard_map/ppermute | solution.py:846
  308.2 4.3 %all-to-all-start.3 = ((bf16[4,32,1792]{2,1,0:T(8,128)(2,1)}), bf16[4,32,1792]{2,1,0:T(8,128)(2,1)S(1)}, u32[]{:S(2)}, u32[]{:S(2)}) async-start(bf16[4,32,1792]{2,1,0:T(8,128)(2,1)} %bitcast.26), calls=%async_computation.4 | async-start | bytes 917504 | tf_op jit(solution)/shard_map/all_to_all | solution.py:1006
  312.5 1.5 fusion.3
  314.0 1.5 fusion.5
  315.6 2.7 add_bitcast_fusion
  318.3 10.3 %reduce-scatter.5.cloned.1.call-done.wide_ref = bf16[32,8704]{1,0:T(8,128)(2,1)} async-done(((bf16[128,8704]{1,0:T(8,128)(2,1)}), bf16[32,8704]{1,0:T(8,128)(2,1)}) %reduce-scatter.5.cloned.1.call-update) | async-done | bytes 557072 | tf_op jit(solution)/shard_map/reduce_scatter | solution.py:993
  328.6 1.0 copy-done.3
  329.7 1.8 update.1
  (205 shorter events, 23.0 us)
Async XLA Ops:
  7.2 3.2 copy-start.29
  7.2 47.1 %all-gather.5.cloned.1.call-start = ((), (), s32[]{:S(2)}) async-start(), calls=%async_computation.8 | async-start | bytes 2129920 | tf_op jit(solution)/shard_map/all_gather | solution.py:907
  9.7 2.7 copy-start.27
  9.7 2.7 copy-start.25
  9.8 2.6 copy-start.24
  9.9 1.6 collective-permute-start
  12.2 21.3 %copy-start.7 = (bf16[1,256,1024]{2,1,0:T(8,128)(2,1)S(1)}, bf16[1,256,1024]{2,1,0:T(8,128)(2,1)}, u32[]{:S(2)}) copy-start(bf16[1,256,1024]{2,1,0:T(8,128)(2,1)} %param.19) | copy-start | bytes 1572868
  12.2 21.9 %copy-start.2 = (bf16[88,1024]{1,0:T(8,128)(2,1)S(1)}, bf16[88,1024]{1,0:T(8,128)(2,1)}, u32[]{:S(2)}) copy-start(bf16[88,1024]{1,0:T(8,128)(2,1)} %wd.1) | copy-start | bytes 540676
  12.3 101.2 %all-gather.3.cloned.1.call-start = ((), (), s32[]{:S(2)}) async-start(), calls=%async_computation.7 | async-start | bytes 3522560 | tf_op jit(solution)/shard_map/all_gather | solution.py:909
  26.3 5.7 %collective-permute-start.3 = (bf16[128,768]{1,0:T(8,128)(2,1)S(1)}, bf16[128,768]{1,0:T(8,128)(2,1)S(1)}, u32[]{:S(2)}, u32[]{:S(2)}) collective-permute-start(bf16[128,768]{1,0:T(8,128)(2,1)S(1)} %bitcast.84), channel_id=1, source_target_pairs={{0,8},{4,12},{8,0},{12,4},{16,24},{20,28},{24,16},{28,20},{1,9},{5... | collective-permute-start | bytes 589832 | tf_op jit(solution)/shard_map/ppermute | solution.py:846
  32.0 8.5 %collective-permute-start.4 = (bf16[256,768]{1,0:T(8,128)(2,1)S(1)}, bf16[256,768]{1,0:T(8,128)(2,1)S(1)}, u32[]{:S(2)}, u32[]{:S(2)}) collective-permute-start(bf16[256,768]{1,0:T(8,128)(2,1)S(1)} %pad_maximum_fusion.10), channel_id=1, source_target_pairs={{0,16},{4,20},{8,24},{12,28},{16,0},{20,4},{24,8},{28,12},{1,17},{... | collective-permute-start | bytes 1179656 | tf_op jit(solution)/shard_map/ppermute | solution.py:846
  33.6 22.3 %collective-permute-start.2 = (bf16[256,1024]{1,0:T(8,128)(2,1)}, bf16[256,1024]{1,0:T(8,128)(2,1)}, u32[]{:S(2)}, u32[]{:S(2)}) collective-permute-start(bf16[256,1024]{1,0:T(8,128)(2,1)} %bitcast.13.refs_4_.cot_hbm.refs_1_), channel_id=1, source_target_pairs={{0,4},{4,0},{8,12},{12,8},{16,20},{20,16},{24,28},{28,24},{1,5},{5... | collective-permute-start | bytes 1572872 | tf_op jit(solution)/shard_map/ppermute | solution.py:846
  33.6 22.3 %collective-permute-start.1 = (bf16[256,1024]{1,0:T(8,128)(2,1)S(1)}, bf16[256,1024]{1,0:T(8,128)(2,1)}, u32[]{:S(2)}, u32[]{:S(2)}) collective-permute-start(bf16[256,1024]{1,0:T(8,128)(2,1)S(1)} %bitcast.80), channel_id=1, source_target_pairs={{0,4},{4,0},{8,12},{12,8},{16,20},{20,16},{24,28},{28,24},{1,5},{5... | collective-permute-start | bytes 1572872 | tf_op jit(solution)/shard_map/ppermute | solution.py:846
  40.5 3.9 %collective-permute-start.5 = (bf16[512,768]{1,0:T(8,128)(2,1)S(1)}, bf16[512,768]{1,0:T(8,128)(2,1)S(1)}, u32[]{:S(2)}, u32[]{:S(2)}) collective-permute-start(bf16[512,768]{1,0:T(8,128)(2,1)S(1)} %pad_maximum_fusion.1), channel_id=1, source_target_pairs={{0,4},{4,0},{8,12},{12,8},{16,20},{20,16},{24,28},{28,24},{1,5},{5... | collective-permute-start | bytes 2359304 | tf_op jit(solution)/shard_map/ppermute | solution.py:846
  44.5 11.3 %copy-start.12 = (bf16[1024,768]{1,0:T(8,128)(2,1)}, bf16[1024,768]{1,0:T(8,128)(2,1)S(1)}, u32[]{:S(2)}) copy-start(bf16[1024,768]{1,0:T(8,128)(2,1)S(1)} %constant_dynamic-update-slice_fusion.refs_1_.weight_hbm) | copy-start | bytes 4718596
  55.9 42.6 %copy-start.13 = (bf16[2,2,128,1664]{3,2,1,0:T(8,128)(2,1)}, bf16[2,2,128,1664]{3,2,1,0:T(8,128)(2,1)S(1)}, u32[]{:S(2)}) copy-start(bf16[2,2,128,1664]{3,2,1,0:T(8,128)(2,1)S(1)} %copy.60) | copy-start | bytes 5111812
  56.6 38.9 %collective-permute-start.6 = (bf16[2,256,1664]{2,1,0:T(8,128)(2,1)S(1)}, bf16[2,256,1664]{2,1,0:T(8,128)(2,1)S(1)}, u32[]{:S(2)}, u32[]{:S(2)}) collective-permute-start(bf16[2,256,1664]{2,1,0:T(8,128)(2,1)S(1)} %bitcast.91), channel_id=1, source_target_pairs={{0,8},{4,12},{8,0},{12,4},{16,24},{20,28},{24,16},{28,20},{1,9},{5... | collective-permute-start | bytes 5111816 | tf_op jit(solution)/shard_map/ppermute | solution.py:846
  58.0 39.0 %collective-permute-start.7 = (bf16[2,256,1664]{2,1,0:T(8,128)(2,1)S(1)}, bf16[2,256,1664]{2,1,0:T(8,128)(2,1)S(1)}, u32[]{:S(2)}, u32[]{:S(2)}) collective-permute-start(bf16[2,256,1664]{2,1,0:T(8,128)(2,1)S(1)} %bitcast.92), channel_id=1, source_target_pairs={{0,16},{4,20},{8,24},{12,28},{16,0},{20,4},{24,8},{28,12},{1,17},{... | collective-permute-start | bytes 5111816 | tf_op jit(solution)/shard_map/ppermute | solution.py:846
  95.5 2.9 copy-start.22
  95.6 22.2 %collective-permute-start.8 = (bf16[256,1664]{1,0:T(8,128)(2,1)S(1)}, bf16[256,1664]{1,0:T(8,128)(2,1)}, u32[]{:S(2)}, u32[]{:S(2)}) collective-permute-start(bf16[256,1664]{1,0:T(8,128)(2,1)S(1)} %slice_bitcast_fusion.1), channel_id=1, source_target_pairs={{0,16},{4,20},{8,24},{12,28},{16,0},{20,4},{24,8},{28,12},{1,17},{... | collective-permute-start | bytes 2555912 | tf_op jit(solution)/shard_map/ppermute | solution.py:846
  98.4 20.6 %collective-permute-start.9 = (bf16[256,1664]{1,0:T(8,128)(2,1)S(1)}, bf16[256,1664]{1,0:T(8,128)(2,1)}, u32[]{:S(2)}, u32[]{:S(2)}) collective-permute-start(bf16[256,1664]{1,0:T(8,128)(2,1)S(1)} %slice_bitcast_fusion), channel_id=1, source_target_pairs={{0,8},{4,12},{8,0},{12,4},{16,24},{20,28},{24,16},{28,20},{1,9},{5... | collective-permute-start | bytes 2555912 | tf_op jit(solution)/shard_map/ppermute | solution.py:846
  114.7 21.5 %copy-start.17 = (bf16[352,1024]{1,0:T(8,128)(2,1)}, bf16[352,1024]{1,0:T(8,128)(2,1)S(1)}, u32[]{:S(2)}) copy-start(bf16[352,1024]{1,0:T(8,128)(2,1)S(1)} %pad_maximum_fusion.2.refs_11_.refs_5_) | copy-start | bytes 2162692
  114.7 21.5 %collective-permute-start.10 = (bf16[352,1024]{1,0:T(8,128)(2,1)S(1)}, bf16[352,1024]{1,0:T(8,128)(2,1)S(1)}, u32[]{:S(2)}, u32[]{:S(2)}) collective-permute-start(bf16[352,1024]{1,0:T(8,128)(2,1)S(1)} %pad_maximum_fusion.2.refs_11_.refs_5_), channel_id=1, source_target_pairs={{0,8},{4,12},{8,0},{12,4},{16,24},{20,28},{24,16},{28,20},{1,9},{5... | collective-permute-start | bytes 2162696 | tf_op jit(solution)/shard_map/ppermute | solution.py:846
  116.3 20.0 %collective-permute-start.11 = (bf16[352,1024]{1,0:T(8,128)(2,1)S(1)}, bf16[352,1024]{1,0:T(8,128)(2,1)S(1)}, u32[]{:S(2)}, u32[]{:S(2)}) collective-permute-start(bf16[352,1024]{1,0:T(8,128)(2,1)S(1)} %pad_maximum_fusion.2.refs_11_.refs_5_), channel_id=1, source_target_pairs={{0,16},{4,20},{8,24},{12,28},{16,0},{20,4},{24,8},{28,12},{1,17},{... | collective-permute-start | bytes 2162696 | tf_op jit(solution)/shard_map/ppermute | solution.py:846
  138.0 5.5 %copy-start.33 = (bf16[352,1024]{1,0:T(8,128)(2,1)S(1)}, bf16[352,1024]{1,0:T(8,128)(2,1)}, u32[]{:S(2)}) copy-start(bf16[352,1024]{1,0:T(8,128)(2,1)} %copy-done.32) | copy-start | bytes 2162692
  138.0 16.5 %all-to-all-start.1 = ((bf16[4,256,256]{2,1,0:T(8,128)(2,1)}), bf16[4,256,256]{2,1,0:T(8,128)(2,1)S(1)}, u32[]{:S(2)}, u32[]{:S(2)}) async-start(bf16[4,256,256]{2,1,0:T(8,128)(2,1)} %bitcast.103), calls=%async_computation.1 | async-start | bytes 1048576 | tf_op jit(solution)/shard_map/all_to_all | solution.py:940
  142.1 12.4 %collective-permute-start.15 = (bf16[8,256,256]{2,1,0:T(8,128)(2,1)}, bf16[8,256,256]{2,1,0:T(8,128)(2,1)S(1)}, u32[]{:S(2)}, u32[]{:S(2)}) collective-permute-start(bf16[8,256,256]{2,1,0:T(8,128)(2,1)} %get-tuple-element.121), channel_id=1, source_target_pairs={{0,4},{4,0},{8,12},{12,8},{16,20},{20,16},{24,28},{28,24},{1,5},{5... | collective-permute-start | bytes 3145736 | tf_op jit(solution)/shard_map/ppermute | solution.py:846
  143.1 10.9 %collective-permute-start.12 = (bf16[352,512]{1,0:T(8,128)(2,1)S(1)}, bf16[352,512]{1,0:T(8,128)(2,1)S(1)}, u32[]{:S(2)}, u32[]{:S(2)}) collective-permute-start(bf16[352,512]{1,0:T(8,128)(2,1)S(1)} %slice.250), channel_id=1, source_target_pairs={{0,16},{4,20},{8,24},{12,28},{16,0},{20,4},{24,8},{28,12},{1,17},{... | collective-permute-start | bytes 1081352 | tf_op jit(solution)/shard_map/ppermute | solution.py:846
  143.5 10.6 %collective-permute-start.13 = (bf16[352,512]{1,0:T(8,128)(2,1)S(1)}, bf16[352,512]{1,0:T(8,128)(2,1)S(1)}, u32[]{:S(2)}, u32[]{:S(2)}) collective-permute-start(bf16[352,512]{1,0:T(8,128)(2,1)S(1)} %slice.251), channel_id=1, source_target_pairs={{0,8},{4,12},{8,0},{12,4},{16,24},{20,28},{24,16},{28,20},{1,9},{5... | collective-permute-start | bytes 1081352 | tf_op jit(solution)/shard_map/ppermute | solution.py:846
  154.0 2.4 copy-start.45
  154.5 1.9 collective-permute-start.14
  182.5 2.2 collective-permute-start.16
  189.6 19.6 %all-to-all-start.2 = ((bf16[4,256,256]{2,1,0:T(8,128)(2,1)}), bf16[4,256,256]{2,1,0:T(8,128)(2,1)S(1)}, u32[]{:S(2)}, u32[]{:S(2)}) async-start(bf16[4,256,256]{2,1,0:T(8,128)(2,1)} %get-tuple-element.132), calls=%async_computation.2 | async-start | bytes 1048576 | tf_op jit(solution)/shard_map/all_to_all | solution.py:951
  194.4 118.1 %reduce-scatter.3.cloned.1.call-start = ((), (), s32[]{:S(2)}) async-start(), calls=%async_computation.9 | async-start | bytes 2621440 | tf_op jit(solution)/shard_map/reduce_scatter | solution.py:999
  194.4 34.8 %collective-permute-start.18 = (bf16[512,1408]{1,0:T(8,128)(2,1)}, bf16[512,1408]{1,0:T(8,128)(2,1)}, u32[]{:S(2)}, u32[]{:S(2)}) collective-permute-start(bf16[512,1408]{1,0:T(8,128)(2,1)} %get-tuple-element.144), channel_id=1, source_target_pairs={{0,8},{4,12},{8,0},{12,4},{16,24},{20,28},{24,16},{28,20},{1,9},{5... | collective-permute-start | bytes 4325384 | tf_op jit(solution)/shard_map/ppermute | solution.py:846
  195.6 34.7 %collective-permute-start.19 = (bf16[512,1408]{1,0:T(8,128)(2,1)}, bf16[512,1408]{1,0:T(8,128)(2,1)S(1)}, u32[]{:S(2)}, u32[]{:S(2)}) collective-permute-start(bf16[512,1408]{1,0:T(8,128)(2,1)} %get-tuple-element.145), channel_id=1, source_target_pairs={{0,16},{4,20},{8,24},{12,28},{16,0},{20,4},{24,8},{28,12},{1,17},{... | collective-permute-start | bytes 4325384 | tf_op jit(solution)/shard_map/ppermute | solution.py:846
  207.6 37.0 %collective-permute-start.26 = (bf16[704,512]{1,0:T(8,128)(2,1)}, bf16[704,512]{1,0:T(8,128)(2,1)}, u32[]{:S(2)}, u32[]{:S(2)}) collective-permute-start(bf16[704,512]{1,0:T(8,128)(2,1)} %get-tuple-element.157), channel_id=1, source_target_pairs={{0,8},{4,12},{8,0},{12,4},{16,24},{20,28},{24,16},{28,20},{1,9},{5... | collective-permute-start | bytes 2162696 | tf_op jit(solution)/shard_map/ppermute | solution.py:846
  208.4 39.3 %collective-permute-start.28 = (bf16[704,512]{1,0:T(8,128)(2,1)}, bf16[704,512]{1,0:T(8,128)(2,1)S(1)}, u32[]{:S(2)}, u32[]{:S(2)}) collective-permute-start(bf16[704,512]{1,0:T(8,128)(2,1)} %get-tuple-element.159), channel_id=1, source_target_pairs={{0,16},{4,20},{8,24},{12,28},{16,0},{20,4},{24,8},{28,12},{1,17},{... | collective-permute-start | bytes 2162696 | tf_op jit(solution)/shard_map/ppermute | solution.py:846
  227.9 100.7 %reduce-scatter.5.cloned.1.call-start = ((), (), s32[]{:S(2)}) async-start(), calls=%async_computation.10 | async-start | bytes 2785280 | tf_op jit(solution)/shard_map/reduce_scatter | solution.py:993
  230.3 6.7 %copy-start.15 = (bf16[512,1408]{1,0:T(8,128)(2,1)S(1)}, bf16[512,1408]{1,0:T(8,128)(2,1)}, u32[]{:S(2)}) copy-start(bf16[512,1408]{1,0:T(8,128)(2,1)} %get-tuple-element.154) | copy-start | bytes 4325380
  238.8 22.4 %collective-permute-start.23 = (bf16[256,1408]{1,0:T(8,128)(2,1)S(1)}, bf16[256,1408]{1,0:T(8,128)(2,1)S(1)}, u32[]{:S(2)}, u32[]{:S(2)}) collective-permute-start(bf16[256,1408]{1,0:T(8,128)(2,1)S(1)} %slice.294), channel_id=1, source_target_pairs={{0,16},{4,20},{8,24},{12,28},{16,0},{20,4},{24,8},{28,12},{1,17},{... | collective-permute-start | bytes 2162696 | tf_op jit(solution)/shard_map/ppermute | solution.py:846
  241.0 3.7 %copy-start.19 = (bf16[704,512]{1,0:T(8,128)(2,1)S(1)}, bf16[704,512]{1,0:T(8,128)(2,1)}, u32[]{:S(2)}) copy-start(bf16[704,512]{1,0:T(8,128)(2,1)} %get-tuple-element.156) | copy-start | bytes 2162692
  241.0 6.7 %copy-start.18 = (bf16[704,512]{1,0:T(8,128)(2,1)S(1)}, bf16[704,512]{1,0:T(8,128)(2,1)}, u32[]{:S(2)}) copy-start(bf16[704,512]{1,0:T(8,128)(2,1)} %get-tuple-element.158) | copy-start | bytes 2162692
  241.0 20.4 %collective-permute-start.24 = (bf16[256,1408]{1,0:T(8,128)(2,1)S(1)}, bf16[256,1408]{1,0:T(8,128)(2,1)S(1)}, u32[]{:S(2)}, u32[]{:S(2)}) collective-permute-start(bf16[256,1408]{1,0:T(8,128)(2,1)S(1)} %slice.296), channel_id=1, source_target_pairs={{0,8},{4,12},{8,0},{12,4},{16,24},{20,28},{24,16},{28,20},{1,9},{5... | collective-permute-start | bytes 2162696 | tf_op jit(solution)/shard_map/ppermute | solution.py:846
  246.0 21.5 %collective-permute-start.27 = (bf16[352,512]{1,0:T(8,128)(2,1)S(1)}, bf16[352,512]{1,0:T(8,128)(2,1)S(1)}, u32[]{:S(2)}, u32[]{:S(2)}) collective-permute-start(bf16[352,512]{1,0:T(8,128)(2,1)S(1)} %slice.298), channel_id=1, source_target_pairs={{0,16},{4,20},{8,24},{12,28},{16,0},{20,4},{24,8},{28,12},{1,17},{... | collective-permute-start | bytes 1081352 | tf_op jit(solution)/shard_map/ppermute | solution.py:846
  247.9 19.7 %collective-permute-start.29 = (bf16[352,512]{1,0:T(8,128)(2,1)S(1)}, bf16[352,512]{1,0:T(8,128)(2,1)S(1)}, u32[]{:S(2)}, u32[]{:S(2)}) collective-permute-start(bf16[352,512]{1,0:T(8,128)(2,1)S(1)} %slice.300), channel_id=1, source_target_pairs={{0,8},{4,12},{8,0},{12,4},{16,24},{20,28},{24,16},{28,20},{1,9},{5... | collective-permute-start | bytes 1081352 | tf_op jit(solution)/shard_map/ppermute | solution.py:846
  261.8 7.1 %collective-permute-start.25 = (bf16[128,2816]{1,0:T(8,128)(2,1)S(1)}, bf16[128,2816]{1,0:T(8,128)(2,1)S(1)}, u32[]{:S(2)}, u32[]{:S(2)}) collective-permute-start(bf16[128,2816]{1,0:T(8,128)(2,1)S(1)} %pad_maximum_fusion.3), channel_id=1, source_target_pairs={{0,4},{4,0},{8,12},{12,8},{16,20},{20,16},{24,28},{28,24},{1,5},{5... | collective-permute-start | bytes 2162696 | tf_op jit(solution)/shard_map/ppermute | solution.py:846
  263.2 7.5 %collective-permute-start.20 = (bf16[512,1792]{1,0:T(8,128)(2,1)S(1)}, bf16[512,1792]{1,0:T(8,128)(2,1)}, u32[]{:S(2)}, u32[]{:S(2)}) collective-permute-start(bf16[512,1792]{1,0:T(8,128)(2,1)S(1)} %copy-done.42), channel_id=1, source_target_pairs={{0,4},{4,0},{8,12},{12,8},{16,20},{20,16},{24,28},{28,24},{1,5},{5... | collective-permute-start | bytes 5505032 | tf_op jit(solution)/shard_map/ppermute | solution.py:846
  273.2 2.5 copy-start.38
  273.3 22.4 %collective-permute-start.21 = (bf16[256,1792]{1,0:T(8,128)(2,1)S(1)}, bf16[256,1792]{1,0:T(8,128)(2,1)}, u32[]{:S(2)}, u32[]{:S(2)}) collective-permute-start(bf16[256,1792]{1,0:T(8,128)(2,1)S(1)} %slice.290), channel_id=1, source_target_pairs={{0,8},{4,12},{8,0},{12,4},{16,24},{20,28},{24,16},{28,20},{1,9},{5... | collective-permute-start | bytes 2752520 | tf_op jit(solution)/shard_map/ppermute | solution.py:846
  275.6 23.3 %collective-permute-start.17 = (bf16[256,1024]{1,0:T(8,128)(2,1)}, bf16[256,1024]{1,0:T(8,128)(2,1)}, u32[]{:S(2)}, u32[]{:S(2)}) collective-permute-start(bf16[256,1024]{1,0:T(8,128)(2,1)} %get-tuple-element.134), channel_id=1, source_target_pairs={{0,4},{4,0},{8,12},{12,8},{16,20},{20,16},{24,28},{28,24},{1,5},{5... | collective-permute-start | bytes 1572872 | tf_op jit(solution)/shard_map/ppermute | solution.py:846
  276.4 24.7 %all-to-all-start.4 = ((f32[32,8,128]{2,1,0:T(8,128)}), f32[32,8,128]{2,1,0:T(8,128)}, u32[]{:S(2)}, u32[]{:S(2)}) async-start(f32[32,8,128]{2,1,0:T(8,128)} %broadcast_in_dim.35), calls=%async_computation.6 | async-start | bytes 262144 | tf_op jit(solution)/shard_map/all_to_all | solution.py:995
  282.3 16.6 %copy-start.10 = (f32[256,1024]{1,0:T(8,128)S(1)}, f32[256,1024]{1,0:T(8,128)}, u32[]{:S(2)}) copy-start(f32[256,1024]{1,0:T(8,128)} %get-tuple-element.122.res_hbm) | copy-start | bytes 3145732
  282.3 16.6 %copy-start.16 = (f32[256,1024]{1,0:T(8,128)S(1)}, f32[256,1024]{1,0:T(8,128)}, u32[]{:S(2)}) copy-start(f32[256,1024]{1,0:T(8,128)} %get-tuple-element.131) | copy-start | bytes 3145732
  297.1 10.2 %collective-permute-start.22 = (bf16[128,1792]{1,0:T(8,128)(2,1)S(1)}, bf16[128,1792]{1,0:T(8,128)(2,1)S(1)}, u32[]{:S(2)}, u32[]{:S(2)}) collective-permute-start(bf16[128,1792]{1,0:T(8,128)(2,1)S(1)} %slice.292), channel_id=1, source_target_pairs={{0,16},{4,20},{8,24},{12,28},{16,0},{20,4},{24,8},{28,12},{1,17},{... | collective-permute-start | bytes 1376264 | tf_op jit(solution)/shard_map/ppermute | solution.py:846
  302.1 11.8 %copy-start.40 = (f32[16]{0:T(128)}, f32[16]{0:T(128)S(1)}, u32[]{:S(2)}) copy-start(f32[16]{0:T(128)S(1)} %reshape_squeeze.3) | copy-start | bytes 196
  302.2 11.8 %copy-start.41 = (f32[16]{0:T(128)}, f32[16]{0:T(128)S(1)}, u32[]{:S(2)}) copy-start(f32[16]{0:T(128)S(1)} %divide_sqrt_fusion) | copy-start | bytes 196
  308.2 23.8 %all-to-all-start.3 = ((bf16[4,32,1792]{2,1,0:T(8,128)(2,1)}), bf16[4,32,1792]{2,1,0:T(8,128)(2,1)S(1)}, u32[]{:S(2)}, u32[]{:S(2)}) async-start(bf16[4,32,1792]{2,1,0:T(8,128)(2,1)} %bitcast.26), calls=%async_computation.4 | async-start | bytes 917504 | tf_op jit(solution)/shard_map/all_to_all | solution.py:1006
  312.5 3.0 copy-start.9
  315.5 13.1 %copy-start = (bf16[32,2816]{1,0:T(8,128)(2,1)S(1)}, bf16[32,2816]{1,0:T(8,128)(2,1)}, u32[]{:S(2)}) copy-start(bf16[32,2816]{1,0:T(8,128)(2,1)} %wu.1) | copy-start | bytes 540676
  315.5 13.1 %copy-start.1 = (bf16[32,2816]{1,0:T(8,128)(2,1)S(1)}, bf16[32,2816]{1,0:T(8,128)(2,1)}, u32[]{:S(2)}) copy-start(bf16[32,2816]{1,0:T(8,128)(2,1)} %wg.1) | copy-start | bytes 540676
  315.5 13.1 %copy-start.4 = (f32[32,2816]{1,0:T(8,128)S(1)}, f32[32,2816]{1,0:T(8,128)}, u32[]{:S(2)}) copy-start(f32[32,2816]{1,0:T(8,128)} %mg.1) | copy-start | bytes 1081348
  315.5 13.1 %copy-start.5 = (f32[32,2816]{1,0:T(8,128)S(1)}, f32[32,2816]{1,0:T(8,128)}, u32[]{:S(2)}) copy-start(f32[32,2816]{1,0:T(8,128)} %mu.1) | copy-start | bytes 1081348
  315.5 13.0 %copy-start.6 = (f32[88,1024]{1,0:T(8,128)S(1)}, f32[88,1024]{1,0:T(8,128)}, u32[]{:S(2)}) copy-start(f32[88,1024]{1,0:T(8,128)} %md.1) | copy-start | bytes 1081348
  (21 other events, 30.7 us)
Sparse Core Ops, SparseCore 0:
  12.4 41.8 all-gather.4
  56.4 56.9 all-gather.2
  228.0 44.8 reduce-scatter.2
  275.2 53.3 reduce-scatter.4

commit v10 on v9

--- a/solution.py
+++ b/solution.py
@@ -304,17 +304,17 @@
         copy.wait()
 
 
-def call(kernel, name, outs, scratch, sems, flops, args, limit):
+def call(kernel, name, outs, scratch, sems, flops, args, limit, free=0):
     return pl.pallas_call(
         kernel,
         out_shape=tuple(pltpu.HBM(*o) for o in outs),
-        in_specs=[MAIN] * len(args),
+        in_specs=[pl.BlockSpec(memory_space=pl.ANY)] * free + [MAIN] * (len(args) - free),
         out_specs=(MAIN,) * len(outs),
         scratch_shapes=[pltpu.VMEM(*s) for s in scratch] + [pltpu.SemaphoreType.DMA(n if isinstance(n, tuple) else (n,)) for n in sems],
         compiler_params=pltpu.CompilerParams(vmem_limit_bytes=limit << 20),
         cost_estimate=pl.CostEstimate(flops=flops << 30, bytes_accessed=8 << 20, transcendentals=0),
         name=name,
-    )(*(pltpu.with_memory_space_constraint(arg, pltpu.HBM) for arg in args))
+    )(*args[:free], *(pltpu.with_memory_space_constraint(arg, pltpu.HBM) for arg in args[free:]))
 
 
 def place_of(p):
@@ -451,7 +451,7 @@
     )
 
 
-def attend_back_kernel(mixed_hbm, ga_hbm, total_hbm, cos_hbm, sin_hbm, id_hbm, weight_hbm,
+def attend_back_kernel(ga_hbm, mixed_hbm, total_hbm, cos_hbm, sin_hbm, id_hbm, weight_hbm,
                        gm_hbm, gn_hbm,
                        mixed_ref, ga_ref, total_ref, cos_ref, sin_ref, ids, weight,
                        gm_ref, gn_ref, gk_acc, gv_acc, key_t, id_col, sems):
@@ -541,7 +541,7 @@
         [((n, 768), bf), ((n, 256), bf), ((8, n), f32), ((n, 128), f32), ((n, 128), f32),
          ((8, n), f32), ((1024, 768), bf), ((n, 768), bf), ((n, 1024), bf), ((n, 256), f32),
          ((n, 256), f32), ((256, n), bf), ((n, 128), f32)],
-        [19], 0, (mixed, ga, total, cosine, sine, ids, weight), 32,
+        [19], 0, (ga, mixed, total, cosine, sine, ids, weight), 32, 1,
     )
 
 
@@ -691,7 +691,7 @@
         big + [((1024, 1024), bf), ((512, 1024), bf), ((512, 1024), bf), ((512, 1024), bf), ((1024, 512), bf),
                ((512, 1024), bf), ((512, 1024), f32), ((512, 1024), f32), ((256, 1024), bf)]
         + big[:2] + [((512, FFP), bf)],
-        [68, 4, (6, 9)], 12, (att, attp, act, actp, cot, cotp, *wide, *down, outs), 50,
+        [68, 4, (6, 9)], 12, (att, attp, act, actp, cot, cotp, *wide, *down, outs), 50, 2,
     )
 
 
@@ -792,7 +792,7 @@
     return call(
         branch_kernel, "branch", [tall, ((4, 256, 256), bf)],
         [low, tall, tall, low, ((1024, 1024), bf), tall, ((4, 256, 256), bf)],
-        [7], 1, (part, gnown, res, cot, wo), 32,
+        [7], 1, (part, gnown, res, cot, wo), 32, 1,
     )
 
 

time: 344 us -> 341 us (level)
    unnamed x98 -> x92, local copies, waits for them, and re-layouts: 8.65 us -> 5.9 us
where the time goes in v10:
time: 341 us; the launch traced here: 338 us
  waiting for transfers between devices  135 us (40%)
  Pallas kernels  82.7 us (24%)
  starting transfers between devices  46.9 us (14%)
  other arithmetic  27.9 us (8%)
  between operations  16.1 us (5%)
  local copies, waits for them, and re-layouts  15.3 us (4%)
  blocking collectives  13.8 us (4%)
    ppermute x30, waiting for transfers between devices, swap(): return lax.ppermute(array, 'dp', [(i, i ^ bit) for i in range(8)])  102 us
    pallas_call x6, Pallas kernels, call(): pl.pallas_call(kernel, out_shape=tuple((pltpu.HBM(*o) for o in outs)), in...  80.9 us
    ppermute x30, starting transfers between devices, swap(): return lax.ppermute(array, 'dp', [(i, i ^ bit) for i in range(8)])  27.3 us
    all_to_all x1, blocking collectives, fast_device(): heads = lax.all_to_all(heads, 'ctx', 0, 0, tiled=True).reshape(128, 768)  13.8 us
    all_gather x1, waiting for transfers between devices, fast_device(): rows_all = lax.all_gather(padded, 'ctx', axis=0, tiled=True)  13.4 us
    all_gather x1, waiting for transfers between devices, fast_device(): lax.all_gather(wide, 'ctx', axis=2, tiled=True).reshape(2, 256, FF2 + 256)  9.74 us
    convert_element_type x11, other arithmetic, add_low(): return (left.astype(f32) + right.astype(f32)).astype(bf)  8.9 us
    reduce_scatter x1, waiting for transfers between devices, fast_device(): lax.psum_scatter(grad_wide, 'ctx', scatter_dimension=0, tiled=True)  8.6 us
  transfers between devices with their start and end apart: 38, of which 22 were waited for; matrix products, arithmetic and copies ran while one was open for 9% of the time, Pallas kernels for 16%

profile of v10, /device:TPU:0, one launch (start us, length us, event | category | flops | bytes accessed | tf_op | source)
XLA Modules:
  0.0 338.1 jit_solution(16655740255569338239)
XLA Ops:
  7.3 1.0 fusion.14
  8.3 1.0 fusion.15
  12.5 13.8 %all_to_all.25 = bf16[4,32,768]{2,1,0:T(8,128)(2,1)S(1)} all-to-all(bf16[4,32,768]{2,1,0:T(8,128)(2,1)S(1)} %pad_maximum_fusion.11), channel_id=1, replica_groups=mesh['dp'=8,'ctx'=4] {'ctx'}, dimensions={0} | all-to-all | bytes 393216 | tf_op jit(solution)/shard_map/all_to_all | solution.py:916
  26.3 1.5 collective-permute-start.3
  27.8 4.2 %collective-permute-done.3 = bf16[128,768]{1,0:T(8,128)(2,1)S(1)} collective-permute-done((bf16[128,768]{1,0:T(8,128)(2,1)S(1)}, bf16[128,768]{1,0:T(8,128)(2,1)S(1)}, u32[]{:S(2)}, u32[]{:S(2)}) %collective-permute-start.3) | collective-permute-done | bytes 196640 | tf_op jit(solution)/shard_map/ppermute | solution.py:846
  32.0 1.6 collective-permute-start.4
  35.0 5.4 %collective-permute-done.4 = bf16[256,768]{1,0:T(8,128)(2,1)S(1)} collective-permute-done((bf16[256,768]{1,0:T(8,128)(2,1)S(1)}, bf16[256,768]{1,0:T(8,128)(2,1)S(1)}, u32[]{:S(2)}, u32[]{:S(2)}) %collective-permute-start.4) | collective-permute-done | bytes 393248 | tf_op jit(solution)/shard_map/ppermute | solution.py:846
  40.6 1.9 fusion.7
  42.5 1.8 pad_maximum_fusion.7
  44.5 9.7 %all-gather.5.cloned.1.call-done = bf16[2,2,128,1664]{3,2,0,1:T(8,128)(2,1)} async-done(((bf16[2,2,32,1664]{3,2,0,1:T(8,128)(2,1)}), bf16[2,2,128,1664]{3,2,0,1:T(8,128)(2,1)}) %all-gather.5.cloned.1.call-update) | async-done | bytes 1703952 | tf_op jit(solution)/shard_map/all_gather | solution.py:907
  54.3 1.6 copy.60
  56.6 1.5 collective-permute-start.6
  58.0 1.5 collective-permute-start.7
  59.5 36.0 %collective-permute-done.6.refs_6_.refs_7_ = bf16[2,256,1664]{2,1,0:T(8,128)(2,1)S(1)} collective-permute-done((bf16[2,256,1664]{2,1,0:T(8,128)(2,1)S(1)}, bf16[2,256,1664]{2,1,0:T(8,128)(2,1)S(1)}, u32[]{:S(2)}, u32[]{:S(2)}) %collective-permute-start.6) | collective-permute-done | bytes 1703968 | tf_op jit(solution)/shard_map/ppermute | solution.py:846
  95.6 1.5 collective-permute-start.8
  97.1 1.3 copy-done.21
  98.4 1.5 collective-permute-start.9
  100.0 13.4 %all-gather.3.cloned.1.call-done.refs_0_ = bf16[1376,1024]{1,0:T(8,128)(2,1)} async-done(((bf16[344,1024]{1,0:T(8,128)(2,1)}), bf16[1376,1024]{1,0:T(8,128)(2,1)}) %all-gather.3.cloned.1.call-update) | async-done | bytes 2818064 | tf_op jit(solution)/shard_map/all_gather | solution.py:909
  113.4 1.2 fusion.12
  114.7 1.5 collective-permute-start.10
  116.3 1.5 collective-permute-start.11
  117.7 1.3 collective-permute-done.9.refs_9_.refs_10_
  119.0 17.2 %attend.1 = (bf16[1024,1024]{1,0:T(8,128)(2,1)}, bf16[1024,768]{1,0:T(8,128)(2,1)}, bf16[1024,256]{1,0:T(8,128)(2,1)}, f32[8,1024]{1,0:T(8,128)}, f32[8,128]{1,0:T(8,128)}, /*index=5*/bf16[8,256,256]{2,1,0:T(8,128)(2,1)}) custom-call(bf16[1376,1024]{1,0:T(8,128)(2,1)} %all-gather.3.cloned.1.call-done.refs_0_, bf16[1024,768]{1,0:T(8,128)(2,1)} %copy-done.12, ...), custom_call_target="tpu_custom_call" | custom-call | flops 4294967296 | bytes 8388608 | tf_op jit(solution)/shard_map/attend/pallas_call | solution.py:308
  138.0 4.0 %all-to-all-start.1 = ((bf16[4,256,256]{2,1,0:T(8,128)(2,1)}), bf16[4,256,256]{2,1,0:T(8,128)(2,1)S(1)}, u32[]{:S(2)}, u32[]{:S(2)}) async-start(bf16[4,256,256]{2,1,0:T(8,128)(2,1)} %bitcast.103), calls=%async_computation.1 | async-start | bytes 1048576 | tf_op jit(solution)/shard_map/all_to_all | solution.py:940
  142.0 1.0 slice.250
  143.5 1.0 collective-permute-start.13
  144.5 9.4 %collective-permute-done.12.refs_14_.refs_8_ = bf16[352,512]{1,0:T(8,128)(2,1)S(1)} collective-permute-done((bf16[352,512]{1,0:T(8,128)(2,1)S(1)}, bf16[352,512]{1,0:T(8,128)(2,1)S(1)}, u32[]{:S(2)}, u32[]{:S(2)}) %collective-permute-start.12) | collective-permute-done | bytes 360480 | tf_op jit(solution)/shard_map/ppermute | solution.py:846
  154.5 1.9 collective-permute-done.14.refs_1_
  156.4 24.9 %feed.1 = (bf16[256,1024]{1,0:T(8,128)(2,1)}, f32[256,1024]{1,0:T(8,128)}, f32[256,1024]{1,0:T(8,128)}, bf16[1024,1024]{1,0:T(8,128)(2,1)}, bf16[512,1408]{1,0:T...) custom-call(bf16[4,256,256]{2,1,0:T(8,128)(2,1)S(1)} %all-to-all-don, ...), custom_call_target="tpu_custom_call" | custom-call | flops 12884901888 | bytes 8388608 | tf_op jit(solution)/shard_map/feed/pallas_call | solution.py:308
  181.5 2.0 collective-permute-done.16.part_hbm
  183.5 4.0 %branch.1 = (f32[256,1024]{1,0:T(8,128)}, bf16[4,256,256]{2,1,0:T(8,128)(2,1)}) custom-call(bf16[256,1024]{1,0:T(8,128)(2,1)S(1)} %collective-permute-done.16.part_hbm, f32[256,1024]{1,0:T(8,128)} %get-tuple-element.128.gnown_hbm, f32[256,1024]{1,0:T(8,128)} %get-tuple-element.122.res_hbm, bf16[256,1024]{1,0:T(8,128)(2,1)} %bitcast.13.refs_4_.cot_hbm.refs_1_, ...), custom_call_target="tpu_custom_call" | custom-call | flops 1073741824 | bytes 8388608 | tf_op jit(solution)/shard_map/branch/pallas_call | solution.py:308
  187.5 4.8 %all-to-all-start.2 = ((bf16[4,256,256]{2,1,0:T(8,128)(2,1)}), bf16[4,256,256]{2,1,0:T(8,128)(2,1)S(1)}, u32[]{:S(2)}, u32[]{:S(2)}) async-start(bf16[4,256,256]{2,1,0:T(8,128)(2,1)} %get-tuple-element.132), calls=%async_computation.2 | async-start | bytes 1048576 | tf_op jit(solution)/shard_map/all_to_all | solution.py:951
  192.4 1.2 collective-permute-start.18
  193.6 1.7 collective-permute-start.19
  195.3 10.3 %finish.1 = (bf16[256,1024]{1,0:T(8,128)(2,1)}, f32[256,1024]{1,0:T(8,128)}, bf16[704,512]{1,0:T(8,128)(2,1)}, bf16[704,512]{1,0:T(8,128)(2,1)}, bf16[704,512]{1...) custom-call(bf16[512,1408]{1,0:T(8,128)(2,1)} %get-tuple-element.123.refs_0_, ...), custom_call_target="tpu_custom_call" | custom-call | flops 64424509440 | bytes 8388608 | tf_op jit(solution)/shard_map/finish/pallas_call | solution.py:308
  207.2 17.7 %attend_back.1 = (bf16[1024,768]{1,0:T(8,128)(2,1)}, bf16[1024,1024]{1,0:T(8,128)(2,1)}) custom-call(bf16[1024,256]{1,0:T(8,128)(2,1)S(1)} %bitcast.79, bf16[1024,768]{1,0:T(8,128)(2,1)} %get-tuple-element.136.mixed_hbm, f32[8,1024]{1,0:T(8,128)} %get-tuple-element.137.total_hbm, f32[1024,128]{1,0:T(8,128)} %get-tuple-element.106.refs_2_.cos_hbm, ...), custom_call_target="tpu_custom_call" | custom-call | bytes 8388608 | tf_op jit(solution)/shard_map/attend_back/pallas_call | solution.py:308
  225.2 1.9 collective-permute-done.18
  227.2 1.2 collective-permute-done.19
  228.3 6.7 %project_weights.1 = (bf16[512,1792]{1,0:T(8,128)(2,1)}, bf16[512,1792]{1,0:T(8,128)(2,1)}) custom-call(bf16[1024,768]{1,0:T(8,128)(2,1)} %get-tuple-element.146.gm_hbm, bf16[1024,1024]{1,0:T(8,128)(2,1)} %get-tuple-element.147.normed_hbm, bf16[512,1024]{1,0:T(8,128)(2,1)} %get-tuple-element.148.okeep_hbm, bf16[512,1024]{1,0:T(8,128)(2,1)} %get-tuple-element.149.osend_hbm), custom_call_target="tpu_custom_call" | custom-call | flops 1073741824 | bytes 8388608 | tf_op jit(solution)/shard_map/project_weights/pallas_call | solution.py:308
  235.0 1.7 add_convert_fusion.2
  236.8 1.8 collective-permute-start.23
  239.8 2.8 collective-permute-done.26
  242.6 1.3 add_convert_fusion.5
  243.9 1.7 collective-permute-start.27
  245.9 1.3 collective-permute-start.29
  247.2 12.0 %collective-permute-done.23 = bf16[256,1408]{1,0:T(8,128)(2,1)S(1)} collective-permute-done((bf16[256,1408]{1,0:T(8,128)(2,1)S(1)}, bf16[256,1408]{1,0:T(8,128)(2,1)S(1)}, u32[]{:S(2)}, u32[]{:S(2)}) %collective-permute-start.23) | collective-permute-done | bytes 720928 | tf_op jit(solution)/shard_map/ppermute | solution.py:846
  259.9 1.3 copy-done.40
  261.2 4.3 %collective-permute-done.27 = bf16[352,512]{1,0:T(8,128)(2,1)S(1)} collective-permute-done((bf16[352,512]{1,0:T(8,128)(2,1)S(1)}, bf16[352,512]{1,0:T(8,128)(2,1)S(1)}, u32[]{:S(2)}, u32[]{:S(2)}) %collective-permute-start.27) | collective-permute-done | bytes 360480 | tf_op jit(solution)/shard_map/ppermute | solution.py:846
  267.2 1.5 pad_maximum_fusion
  268.7 2.5 add_convert_fusion
  274.4 5.9 %all-to-all-start.4 = ((f32[32,8,128]{2,1,0:T(8,128)}), f32[32,8,128]{2,1,0:T(8,128)}, u32[]{:S(2)}, u32[]{:S(2)}) async-start(f32[32,8,128]{2,1,0:T(8,128)} %broadcast_in_dim.35), calls=%async_computation.6 | async-start | bytes 262144 | tf_op jit(solution)/shard_map/all_to_all | solution.py:995
  280.3 13.4 %collective-permute-done.21 = bf16[256,1792]{1,0:T(8,128)(2,1)} collective-permute-done((bf16[256,1792]{1,0:T(8,128)(2,1)S(1)}, bf16[256,1792]{1,0:T(8,128)(2,1)}, u32[]{:S(2)}, u32[]{:S(2)}) %collective-permute-start.21) | collective-permute-done | bytes 917536 | tf_op jit(solution)/shard_map/ppermute | solution.py:846
  293.7 1.4 add_convert_fusion.3
  295.1 1.8 collective-permute-start.22
  296.9 2.1 fusion.6
  300.3 4.9 %collective-permute-done.22 = bf16[128,1792]{1,0:T(8,128)(2,1)S(1)} collective-permute-done((bf16[128,1792]{1,0:T(8,128)(2,1)S(1)}, bf16[128,1792]{1,0:T(8,128)(2,1)S(1)}, u32[]{:S(2)}, u32[]{:S(2)}) %collective-permute-start.22) | collective-permute-done | bytes 458784 | tf_op jit(solution)/shard_map/ppermute | solution.py:846
  306.1 4.4 %all-to-all-start.3 = ((bf16[4,32,1792]{2,1,0:T(8,128)(2,1)}), bf16[4,32,1792]{2,1,0:T(8,128)(2,1)S(1)}, u32[]{:S(2)}, u32[]{:S(2)}) async-start(bf16[4,32,1792]{2,1,0:T(8,128)(2,1)} %bitcast.26), calls=%async_computation.4 | async-start | bytes 917504 | tf_op jit(solution)/shard_map/all_to_all | solution.py:1006
  310.5 1.5 fusion.3
  312.1 1.5 fusion.5
  313.6 2.7 add_bitcast_fusion
  316.3 8.6 %reduce-scatter.5.cloned.1.call-done.wide_ref = bf16[32,8704]{1,0:T(8,128)(2,1)} async-done(((bf16[128,8704]{1,0:T(8,128)(2,1)}), bf16[32,8704]{1,0:T(8,128)(2,1)}) %reduce-scatter.5.cloned.1.call-update) | async-done | bytes 557072 | tf_op jit(solution)/shard_map/reduce_scatter | solution.py:993
  324.9 1.0 copy-done.3
  326.0 1.8 update.1
  327.9 1.2 all-to-all-done.3
  (199 shorter events, 20.7 us)
Async XLA Ops:
  7.2 3.2 copy-start.27
  7.2 47.1 %all-gather.5.cloned.1.call-start = ((), (), s32[]{:S(2)}) async-start(), calls=%async_computation.8 | async-start | bytes 2129920 | tf_op jit(solution)/shard_map/all_gather | solution.py:907
  9.7 2.7 copy-start.25
  9.7 2.7 copy-start.23
  9.8 2.6 copy-start.22
  9.9 1.6 collective-permute-start
  12.2 21.3 %copy-start.8 = (bf16[1,256,1024]{2,1,0:T(8,128)(2,1)S(1)}, bf16[1,256,1024]{2,1,0:T(8,128)(2,1)}, u32[]{:S(2)}) copy-start(bf16[1,256,1024]{2,1,0:T(8,128)(2,1)} %param.19) | copy-start | bytes 1572868
  12.2 21.9 %copy-start.2 = (bf16[88,1024]{1,0:T(8,128)(2,1)S(1)}, bf16[88,1024]{1,0:T(8,128)(2,1)}, u32[]{:S(2)}) copy-start(bf16[88,1024]{1,0:T(8,128)(2,1)} %wd.1) | copy-start | bytes 540676
  12.3 101.2 %all-gather.3.cloned.1.call-start = ((), (), s32[]{:S(2)}) async-start(), calls=%async_computation.7 | async-start | bytes 3522560 | tf_op jit(solution)/shard_map/all_gather | solution.py:909
  26.3 5.7 %collective-permute-start.3 = (bf16[128,768]{1,0:T(8,128)(2,1)S(1)}, bf16[128,768]{1,0:T(8,128)(2,1)S(1)}, u32[]{:S(2)}, u32[]{:S(2)}) collective-permute-start(bf16[128,768]{1,0:T(8,128)(2,1)S(1)} %bitcast.85), channel_id=1, source_target_pairs={{0,8},{4,12},{8,0},{12,4},{16,24},{20,28},{24,16},{28,20},{1,9},{5... | collective-permute-start | bytes 589832 | tf_op jit(solution)/shard_map/ppermute | solution.py:846
  32.0 8.5 %collective-permute-start.4 = (bf16[256,768]{1,0:T(8,128)(2,1)S(1)}, bf16[256,768]{1,0:T(8,128)(2,1)S(1)}, u32[]{:S(2)}, u32[]{:S(2)}) collective-permute-start(bf16[256,768]{1,0:T(8,128)(2,1)S(1)} %pad_maximum_fusion.10), channel_id=1, source_target_pairs={{0,16},{4,20},{8,24},{12,28},{16,0},{20,4},{24,8},{28,12},{1,17},{... | collective-permute-start | bytes 1179656 | tf_op jit(solution)/shard_map/ppermute | solution.py:846
  33.6 22.3 %collective-permute-start.2 = (bf16[256,1024]{1,0:T(8,128)(2,1)}, bf16[256,1024]{1,0:T(8,128)(2,1)}, u32[]{:S(2)}, u32[]{:S(2)}) collective-permute-start(bf16[256,1024]{1,0:T(8,128)(2,1)} %bitcast.13.refs_4_.cot_hbm.refs_1_), channel_id=1, source_target_pairs={{0,4},{4,0},{8,12},{12,8},{16,20},{20,16},{24,28},{28,24},{1,5},{5... | collective-permute-start | bytes 1572872 | tf_op jit(solution)/shard_map/ppermute | solution.py:846
  33.6 22.3 %collective-permute-start.1 = (bf16[256,1024]{1,0:T(8,128)(2,1)S(1)}, bf16[256,1024]{1,0:T(8,128)(2,1)}, u32[]{:S(2)}, u32[]{:S(2)}) collective-permute-start(bf16[256,1024]{1,0:T(8,128)(2,1)S(1)} %bitcast.81), channel_id=1, source_target_pairs={{0,4},{4,0},{8,12},{12,8},{16,20},{20,16},{24,28},{28,24},{1,5},{5... | collective-permute-start | bytes 1572872 | tf_op jit(solution)/shard_map/ppermute | solution.py:846
  40.5 3.9 %collective-permute-start.5 = (bf16[512,768]{1,0:T(8,128)(2,1)S(1)}, bf16[512,768]{1,0:T(8,128)(2,1)S(1)}, u32[]{:S(2)}, u32[]{:S(2)}) collective-permute-start(bf16[512,768]{1,0:T(8,128)(2,1)S(1)} %pad_maximum_fusion.1), channel_id=1, source_target_pairs={{0,4},{4,0},{8,12},{12,8},{16,20},{20,16},{24,28},{28,24},{1,5},{5... | collective-permute-start | bytes 2359304 | tf_op jit(solution)/shard_map/ppermute | solution.py:846
  44.5 11.3 %copy-start.12 = (bf16[1024,768]{1,0:T(8,128)(2,1)}, bf16[1024,768]{1,0:T(8,128)(2,1)S(1)}, u32[]{:S(2)}) copy-start(bf16[1024,768]{1,0:T(8,128)(2,1)S(1)} %constant_dynamic-update-slice_fusion.refs_1_.weight_hbm) | copy-start | bytes 4718596
  55.9 42.6 %copy-start.13 = (bf16[2,2,128,1664]{3,2,1,0:T(8,128)(2,1)}, bf16[2,2,128,1664]{3,2,1,0:T(8,128)(2,1)S(1)}, u32[]{:S(2)}) copy-start(bf16[2,2,128,1664]{3,2,1,0:T(8,128)(2,1)S(1)} %copy.60) | copy-start | bytes 5111812
  56.6 38.9 %collective-permute-start.6 = (bf16[2,256,1664]{2,1,0:T(8,128)(2,1)S(1)}, bf16[2,256,1664]{2,1,0:T(8,128)(2,1)S(1)}, u32[]{:S(2)}, u32[]{:S(2)}) collective-permute-start(bf16[2,256,1664]{2,1,0:T(8,128)(2,1)S(1)} %bitcast.91), channel_id=1, source_target_pairs={{0,8},{4,12},{8,0},{12,4},{16,24},{20,28},{24,16},{28,20},{1,9},{5... | collective-permute-start | bytes 5111816 | tf_op jit(solution)/shard_map/ppermute | solution.py:846
  58.0 39.0 %collective-permute-start.7 = (bf16[2,256,1664]{2,1,0:T(8,128)(2,1)S(1)}, bf16[2,256,1664]{2,1,0:T(8,128)(2,1)S(1)}, u32[]{:S(2)}, u32[]{:S(2)}) collective-permute-start(bf16[2,256,1664]{2,1,0:T(8,128)(2,1)S(1)} %bitcast.92), channel_id=1, source_target_pairs={{0,16},{4,20},{8,24},{12,28},{16,0},{20,4},{24,8},{28,12},{1,17},{... | collective-permute-start | bytes 5111816 | tf_op jit(solution)/shard_map/ppermute | solution.py:846
  95.5 2.9 copy-start.20
  95.6 22.2 %collective-permute-start.8 = (bf16[256,1664]{1,0:T(8,128)(2,1)S(1)}, bf16[256,1664]{1,0:T(8,128)(2,1)}, u32[]{:S(2)}, u32[]{:S(2)}) collective-permute-start(bf16[256,1664]{1,0:T(8,128)(2,1)S(1)} %slice_bitcast_fusion.1), channel_id=1, source_target_pairs={{0,16},{4,20},{8,24},{12,28},{16,0},{20,4},{24,8},{28,12},{1,17},{... | collective-permute-start | bytes 2555912 | tf_op jit(solution)/shard_map/ppermute | solution.py:846
  98.4 20.6 %collective-permute-start.9 = (bf16[256,1664]{1,0:T(8,128)(2,1)S(1)}, bf16[256,1664]{1,0:T(8,128)(2,1)}, u32[]{:S(2)}, u32[]{:S(2)}) collective-permute-start(bf16[256,1664]{1,0:T(8,128)(2,1)S(1)} %slice_bitcast_fusion), channel_id=1, source_target_pairs={{0,8},{4,12},{8,0},{12,4},{16,24},{20,28},{24,16},{28,20},{1,9},{5... | collective-permute-start | bytes 2555912 | tf_op jit(solution)/shard_map/ppermute | solution.py:846
  114.7 21.5 %copy-start.17 = (bf16[352,1024]{1,0:T(8,128)(2,1)}, bf16[352,1024]{1,0:T(8,128)(2,1)S(1)}, u32[]{:S(2)}) copy-start(bf16[352,1024]{1,0:T(8,128)(2,1)S(1)} %pad_maximum_fusion.2.refs_11_.refs_5_) | copy-start | bytes 2162692
  114.7 21.5 %collective-permute-start.10 = (bf16[352,1024]{1,0:T(8,128)(2,1)S(1)}, bf16[352,1024]{1,0:T(8,128)(2,1)S(1)}, u32[]{:S(2)}, u32[]{:S(2)}) collective-permute-start(bf16[352,1024]{1,0:T(8,128)(2,1)S(1)} %pad_maximum_fusion.2.refs_11_.refs_5_), channel_id=1, source_target_pairs={{0,8},{4,12},{8,0},{12,4},{16,24},{20,28},{24,16},{28,20},{1,9},{5... | collective-permute-start | bytes 2162696 | tf_op jit(solution)/shard_map/ppermute | solution.py:846
  116.3 20.0 %collective-permute-start.11 = (bf16[352,1024]{1,0:T(8,128)(2,1)S(1)}, bf16[352,1024]{1,0:T(8,128)(2,1)S(1)}, u32[]{:S(2)}, u32[]{:S(2)}) collective-permute-start(bf16[352,1024]{1,0:T(8,128)(2,1)S(1)} %pad_maximum_fusion.2.refs_11_.refs_5_), channel_id=1, source_target_pairs={{0,16},{4,20},{8,24},{12,28},{16,0},{20,4},{24,8},{28,12},{1,17},{... | collective-permute-start | bytes 2162696 | tf_op jit(solution)/shard_map/ppermute | solution.py:846
  138.0 5.5 %copy-start.31 = (bf16[352,1024]{1,0:T(8,128)(2,1)S(1)}, bf16[352,1024]{1,0:T(8,128)(2,1)}, u32[]{:S(2)}) copy-start(bf16[352,1024]{1,0:T(8,128)(2,1)} %copy-done.30) | copy-start | bytes 2162692
  138.0 16.5 %all-to-all-start.1 = ((bf16[4,256,256]{2,1,0:T(8,128)(2,1)}), bf16[4,256,256]{2,1,0:T(8,128)(2,1)S(1)}, u32[]{:S(2)}, u32[]{:S(2)}) async-start(bf16[4,256,256]{2,1,0:T(8,128)(2,1)} %bitcast.103), calls=%async_computation.1 | async-start | bytes 1048576 | tf_op jit(solution)/shard_map/all_to_all | solution.py:940
  142.0 12.4 %collective-permute-start.15 = (bf16[8,256,256]{2,1,0:T(8,128)(2,1)}, bf16[8,256,256]{2,1,0:T(8,128)(2,1)S(1)}, u32[]{:S(2)}, u32[]{:S(2)}) collective-permute-start(bf16[8,256,256]{2,1,0:T(8,128)(2,1)} %get-tuple-element.121), channel_id=1, source_target_pairs={{0,4},{4,0},{8,12},{12,8},{16,20},{20,16},{24,28},{28,24},{1,5},{5... | collective-permute-start | bytes 3145736 | tf_op jit(solution)/shard_map/ppermute | solution.py:846
  143.0 10.9 %collective-permute-start.12 = (bf16[352,512]{1,0:T(8,128)(2,1)S(1)}, bf16[352,512]{1,0:T(8,128)(2,1)S(1)}, u32[]{:S(2)}, u32[]{:S(2)}) collective-permute-start(bf16[352,512]{1,0:T(8,128)(2,1)S(1)} %slice.250), channel_id=1, source_target_pairs={{0,16},{4,20},{8,24},{12,28},{16,0},{20,4},{24,8},{28,12},{1,17},{... | collective-permute-start | bytes 1081352 | tf_op jit(solution)/shard_map/ppermute | solution.py:846
  143.5 10.6 %collective-permute-start.13 = (bf16[352,512]{1,0:T(8,128)(2,1)S(1)}, bf16[352,512]{1,0:T(8,128)(2,1)S(1)}, u32[]{:S(2)}, u32[]{:S(2)}) collective-permute-start(bf16[352,512]{1,0:T(8,128)(2,1)S(1)} %slice.251), channel_id=1, source_target_pairs={{0,8},{4,12},{8,0},{12,4},{16,24},{20,28},{24,16},{28,20},{1,9},{5... | collective-permute-start | bytes 1081352 | tf_op jit(solution)/shard_map/ppermute | solution.py:846
  154.4 26.9 %copy-start.4 = (bf16[4,256,256]{2,1,0:T(8,128)(2,1)}, bf16[4,256,256]{2,1,0:T(8,128)(2,1)S(1)}, u32[]{:S(2)}) copy-start(bf16[4,256,256]{2,1,0:T(8,128)(2,1)S(1)} %all-to-all-done.1.refs_0_.refs_3_) | copy-start | bytes 1572868
  154.4 1.9 collective-permute-start.14
  181.3 2.2 collective-permute-start.16
  187.5 19.6 %all-to-all-start.2 = ((bf16[4,256,256]{2,1,0:T(8,128)(2,1)}), bf16[4,256,256]{2,1,0:T(8,128)(2,1)S(1)}, u32[]{:S(2)}, u32[]{:S(2)}) async-start(bf16[4,256,256]{2,1,0:T(8,128)(2,1)} %get-tuple-element.132), calls=%async_computation.2 | async-start | bytes 1048576 | tf_op jit(solution)/shard_map/all_to_all | solution.py:951
  192.4 118.2 %reduce-scatter.3.cloned.1.call-start = ((), (), s32[]{:S(2)}) async-start(), calls=%async_computation.9 | async-start | bytes 2621440 | tf_op jit(solution)/shard_map/reduce_scatter | solution.py:999
  192.4 34.8 %collective-permute-start.18 = (bf16[512,1408]{1,0:T(8,128)(2,1)}, bf16[512,1408]{1,0:T(8,128)(2,1)}, u32[]{:S(2)}, u32[]{:S(2)}) collective-permute-start(bf16[512,1408]{1,0:T(8,128)(2,1)} %get-tuple-element.144), channel_id=1, source_target_pairs={{0,8},{4,12},{8,0},{12,4},{16,24},{20,28},{24,16},{28,20},{1,9},{5... | collective-permute-start | bytes 4325384 | tf_op jit(solution)/shard_map/ppermute | solution.py:846
  193.6 34.7 %collective-permute-start.19 = (bf16[512,1408]{1,0:T(8,128)(2,1)}, bf16[512,1408]{1,0:T(8,128)(2,1)S(1)}, u32[]{:S(2)}, u32[]{:S(2)}) collective-permute-start(bf16[512,1408]{1,0:T(8,128)(2,1)} %get-tuple-element.145), channel_id=1, source_target_pairs={{0,16},{4,20},{8,24},{12,28},{16,0},{20,4},{24,8},{28,12},{1,17},{... | collective-permute-start | bytes 4325384 | tf_op jit(solution)/shard_map/ppermute | solution.py:846
  205.6 37.0 %collective-permute-start.26 = (bf16[704,512]{1,0:T(8,128)(2,1)}, bf16[704,512]{1,0:T(8,128)(2,1)}, u32[]{:S(2)}, u32[]{:S(2)}) collective-permute-start(bf16[704,512]{1,0:T(8,128)(2,1)} %get-tuple-element.157), channel_id=1, source_target_pairs={{0,8},{4,12},{8,0},{12,4},{16,24},{20,28},{24,16},{28,20},{1,9},{5... | collective-permute-start | bytes 2162696 | tf_op jit(solution)/shard_map/ppermute | solution.py:846
  206.4 39.2 %collective-permute-start.28 = (bf16[704,512]{1,0:T(8,128)(2,1)}, bf16[704,512]{1,0:T(8,128)(2,1)S(1)}, u32[]{:S(2)}, u32[]{:S(2)}) collective-permute-start(bf16[704,512]{1,0:T(8,128)(2,1)} %get-tuple-element.159), channel_id=1, source_target_pairs={{0,16},{4,20},{8,24},{12,28},{16,0},{20,4},{24,8},{28,12},{1,17},{... | collective-permute-start | bytes 2162696 | tf_op jit(solution)/shard_map/ppermute | solution.py:846
  224.9 100.0 %reduce-scatter.5.cloned.1.call-start = ((), (), s32[]{:S(2)}) async-start(), calls=%async_computation.10 | async-start | bytes 2785280 | tf_op jit(solution)/shard_map/reduce_scatter | solution.py:993
  228.3 6.7 %copy-start.15 = (bf16[512,1408]{1,0:T(8,128)(2,1)S(1)}, bf16[512,1408]{1,0:T(8,128)(2,1)}, u32[]{:S(2)}) copy-start(bf16[512,1408]{1,0:T(8,128)(2,1)} %get-tuple-element.154) | copy-start | bytes 4325380
  236.8 22.4 %collective-permute-start.23 = (bf16[256,1408]{1,0:T(8,128)(2,1)S(1)}, bf16[256,1408]{1,0:T(8,128)(2,1)S(1)}, u32[]{:S(2)}, u32[]{:S(2)}) collective-permute-start(bf16[256,1408]{1,0:T(8,128)(2,1)S(1)} %slice.294), channel_id=1, source_target_pairs={{0,16},{4,20},{8,24},{12,28},{16,0},{20,4},{24,8},{28,12},{1,17},{... | collective-permute-start | bytes 2162696 | tf_op jit(solution)/shard_map/ppermute | solution.py:846
  238.9 3.7 %copy-start.19 = (bf16[704,512]{1,0:T(8,128)(2,1)S(1)}, bf16[704,512]{1,0:T(8,128)(2,1)}, u32[]{:S(2)}) copy-start(bf16[704,512]{1,0:T(8,128)(2,1)} %get-tuple-element.156) | copy-start | bytes 2162692
  239.0 6.7 %copy-start.18 = (bf16[704,512]{1,0:T(8,128)(2,1)S(1)}, bf16[704,512]{1,0:T(8,128)(2,1)}, u32[]{:S(2)}) copy-start(bf16[704,512]{1,0:T(8,128)(2,1)} %get-tuple-element.158) | copy-start | bytes 2162692
  239.0 20.4 %collective-permute-start.24 = (bf16[256,1408]{1,0:T(8,128)(2,1)S(1)}, bf16[256,1408]{1,0:T(8,128)(2,1)S(1)}, u32[]{:S(2)}, u32[]{:S(2)}) collective-permute-start(bf16[256,1408]{1,0:T(8,128)(2,1)S(1)} %slice.296), channel_id=1, source_target_pairs={{0,8},{4,12},{8,0},{12,4},{16,24},{20,28},{24,16},{28,20},{1,9},{5... | collective-permute-start | bytes 2162696 | tf_op jit(solution)/shard_map/ppermute | solution.py:846
  243.9 21.5 %collective-permute-start.27 = (bf16[352,512]{1,0:T(8,128)(2,1)S(1)}, bf16[352,512]{1,0:T(8,128)(2,1)S(1)}, u32[]{:S(2)}, u32[]{:S(2)}) collective-permute-start(bf16[352,512]{1,0:T(8,128)(2,1)S(1)} %slice.298), channel_id=1, source_target_pairs={{0,16},{4,20},{8,24},{12,28},{16,0},{20,4},{24,8},{28,12},{1,17},{... | collective-permute-start | bytes 1081352 | tf_op jit(solution)/shard_map/ppermute | solution.py:846
  245.9 19.7 %collective-permute-start.29 = (bf16[352,512]{1,0:T(8,128)(2,1)S(1)}, bf16[352,512]{1,0:T(8,128)(2,1)S(1)}, u32[]{:S(2)}, u32[]{:S(2)}) collective-permute-start(bf16[352,512]{1,0:T(8,128)(2,1)S(1)} %slice.300), channel_id=1, source_target_pairs={{0,8},{4,12},{8,0},{12,4},{16,24},{20,28},{24,16},{28,20},{1,9},{5... | collective-permute-start | bytes 1081352 | tf_op jit(solution)/shard_map/ppermute | solution.py:846
  259.8 7.1 %collective-permute-start.25 = (bf16[128,2816]{1,0:T(8,128)(2,1)S(1)}, bf16[128,2816]{1,0:T(8,128)(2,1)S(1)}, u32[]{:S(2)}, u32[]{:S(2)}) collective-permute-start(bf16[128,2816]{1,0:T(8,128)(2,1)S(1)} %pad_maximum_fusion.3), channel_id=1, source_target_pairs={{0,4},{4,0},{8,12},{12,8},{16,20},{20,16},{24,28},{28,24},{1,5},{5... | collective-permute-start | bytes 2162696 | tf_op jit(solution)/shard_map/ppermute | solution.py:846
  261.2 7.5 %collective-permute-start.20 = (bf16[512,1792]{1,0:T(8,128)(2,1)S(1)}, bf16[512,1792]{1,0:T(8,128)(2,1)}, u32[]{:S(2)}, u32[]{:S(2)}) collective-permute-start(bf16[512,1792]{1,0:T(8,128)(2,1)S(1)} %copy-done.40), channel_id=1, source_target_pairs={{0,4},{4,0},{8,12},{12,8},{16,20},{20,16},{24,28},{28,24},{1,5},{5... | collective-permute-start | bytes 5505032 | tf_op jit(solution)/shard_map/ppermute | solution.py:846
  271.2 2.5 copy-start.36
  271.3 22.4 %collective-permute-start.21 = (bf16[256,1792]{1,0:T(8,128)(2,1)S(1)}, bf16[256,1792]{1,0:T(8,128)(2,1)}, u32[]{:S(2)}, u32[]{:S(2)}) collective-permute-start(bf16[256,1792]{1,0:T(8,128)(2,1)S(1)} %slice.290), channel_id=1, source_target_pairs={{0,8},{4,12},{8,0},{12,4},{16,24},{20,28},{24,16},{28,20},{1,9},{5... | collective-permute-start | bytes 2752520 | tf_op jit(solution)/shard_map/ppermute | solution.py:846
  273.6 23.3 %collective-permute-start.17 = (bf16[256,1024]{1,0:T(8,128)(2,1)}, bf16[256,1024]{1,0:T(8,128)(2,1)}, u32[]{:S(2)}, u32[]{:S(2)}) collective-permute-start(bf16[256,1024]{1,0:T(8,128)(2,1)} %get-tuple-element.134), channel_id=1, source_target_pairs={{0,4},{4,0},{8,12},{12,8},{16,20},{20,16},{24,28},{28,24},{1,5},{5... | collective-permute-start | bytes 1572872 | tf_op jit(solution)/shard_map/ppermute | solution.py:846
  274.4 24.7 %all-to-all-start.4 = ((f32[32,8,128]{2,1,0:T(8,128)}), f32[32,8,128]{2,1,0:T(8,128)}, u32[]{:S(2)}, u32[]{:S(2)}) async-start(f32[32,8,128]{2,1,0:T(8,128)} %broadcast_in_dim.35), calls=%async_computation.6 | async-start | bytes 262144 | tf_op jit(solution)/shard_map/all_to_all | solution.py:995
  280.3 16.6 %copy-start.11 = (f32[256,1024]{1,0:T(8,128)S(1)}, f32[256,1024]{1,0:T(8,128)}, u32[]{:S(2)}) copy-start(f32[256,1024]{1,0:T(8,128)} %get-tuple-element.122.res_hbm) | copy-start | bytes 3145732
  280.3 16.6 %copy-start.16 = (f32[256,1024]{1,0:T(8,128)S(1)}, f32[256,1024]{1,0:T(8,128)}, u32[]{:S(2)}) copy-start(f32[256,1024]{1,0:T(8,128)} %get-tuple-element.131) | copy-start | bytes 3145732
  295.1 10.1 %collective-permute-start.22 = (bf16[128,1792]{1,0:T(8,128)(2,1)S(1)}, bf16[128,1792]{1,0:T(8,128)(2,1)S(1)}, u32[]{:S(2)}, u32[]{:S(2)}) collective-permute-start(bf16[128,1792]{1,0:T(8,128)(2,1)S(1)} %slice.292), channel_id=1, source_target_pairs={{0,16},{4,20},{8,24},{12,28},{16,0},{20,4},{24,8},{28,12},{1,17},{... | collective-permute-start | bytes 1376264 | tf_op jit(solution)/shard_map/ppermute | solution.py:846
  300.2 11.9 %copy-start.38 = (f32[16]{0:T(128)}, f32[16]{0:T(128)S(1)}, u32[]{:S(2)}) copy-start(f32[16]{0:T(128)S(1)} %reshape_squeeze.3) | copy-start | bytes 196
  300.2 11.9 %copy-start.39 = (f32[16]{0:T(128)}, f32[16]{0:T(128)S(1)}, u32[]{:S(2)}) copy-start(f32[16]{0:T(128)S(1)} %divide_sqrt_fusion) | copy-start | bytes 196
  306.1 22.9 %all-to-all-start.3 = ((bf16[4,32,1792]{2,1,0:T(8,128)(2,1)}), bf16[4,32,1792]{2,1,0:T(8,128)(2,1)S(1)}, u32[]{:S(2)}, u32[]{:S(2)}) async-start(bf16[4,32,1792]{2,1,0:T(8,128)(2,1)} %bitcast.26), calls=%async_computation.4 | async-start | bytes 917504 | tf_op jit(solution)/shard_map/all_to_all | solution.py:1006
  310.5 3.0 copy-start.10
  313.5 11.4 %copy-start = (bf16[32,2816]{1,0:T(8,128)(2,1)S(1)}, bf16[32,2816]{1,0:T(8,128)(2,1)}, u32[]{:S(2)}) copy-start(bf16[32,2816]{1,0:T(8,128)(2,1)} %wu.1) | copy-start | bytes 540676
  313.6 11.4 %copy-start.1 = (bf16[32,2816]{1,0:T(8,128)(2,1)S(1)}, bf16[32,2816]{1,0:T(8,128)(2,1)}, u32[]{:S(2)}) copy-start(bf16[32,2816]{1,0:T(8,128)(2,1)} %wg.1) | copy-start | bytes 540676
  313.6 11.4 %copy-start.5 = (f32[32,2816]{1,0:T(8,128)S(1)}, f32[32,2816]{1,0:T(8,128)}, u32[]{:S(2)}) copy-start(f32[32,2816]{1,0:T(8,128)} %mg.1) | copy-start | bytes 1081348
  313.6 11.4 %copy-start.6 = (f32[32,2816]{1,0:T(8,128)S(1)}, f32[32,2816]{1,0:T(8,128)}, u32[]{:S(2)}) copy-start(f32[32,2816]{1,0:T(8,128)} %mu.1) | copy-start | bytes 1081348
  313.6 11.3 %copy-start.7 = (f32[88,1024]{1,0:T(8,128)S(1)}, f32[88,1024]{1,0:T(8,128)}, u32[]{:S(2)}) copy-start(f32[88,1024]{1,0:T(8,128)} %md.1) | copy-start | bytes 1081348
  (18 other events, 28.2 us)
Sparse Core Ops, SparseCore 0:
  12.4 41.8 all-gather.4
  56.4 56.9 all-gather.2
  225.0 44.8 reduce-scatter.2
  272.2 52.6 reduce-scatter.4

commit v11 on v10

--- a/solution.py
+++ b/solution.py
@@ -902,9 +902,9 @@
     mine = jnp.where(flip, odd, even)
     other = swap(jnp.where(flip, even, odd), 1)
     out_rows = jnp.stack([w_out[:, :512], w_out[:, 512:]]).reshape(2, 32, 2, 256)
-    wide = jnp.stack([mine, other], axis=1)
-    wide = jnp.concatenate([wide, out_rows.transpose(0, 2, 1, 3)], axis=3)
-    wide = lax.all_gather(wide, "ctx", axis=2, tiled=True).reshape(2, 256, FF2 + 256)
+    wide = jnp.stack([mine, other], axis=0)
+    wide = jnp.concatenate([wide, out_rows.transpose(2, 0, 1, 3)], axis=3)
+    wide = lax.all_gather(wide, "ctx", axis=2, tiled=True).transpose(1, 0, 2, 3).reshape(2, 256, FF2 + 256)
     padded = jnp.concatenate([act, w_down], axis=0)
     rows_all = lax.all_gather(padded, "ctx", axis=0, tiled=True)
     heads = jnp.stack(

time: 341 us -> 341 us (level)
  no operation moved by 1% of the time
where the time goes in v11:
time: 341 us; the launch traced here: 338 us
  waiting for transfers between devices  135 us (40%)
  Pallas kernels  82.7 us (24%)
  starting transfers between devices  46.9 us (14%)
  other arithmetic  27.9 us (8%)
  between operations  16.1 us (5%)
  local copies, waits for them, and re-layouts  15.3 us (4%)
  blocking collectives  13.8 us (4%)
    ppermute x30, waiting for transfers between devices, swap(): return lax.ppermute(array, 'dp', [(i, i ^ bit) for i in range(8)])  102 us
    pallas_call x6, Pallas kernels, call(): pl.pallas_call(kernel, out_shape=tuple((pltpu.HBM(*o) for o in outs)), in...  80.9 us
    ppermute x30, starting transfers between devices, swap(): return lax.ppermute(array, 'dp', [(i, i ^ bit) for i in range(8)])  27.3 us
    all_to_all x1, blocking collectives, fast_device(): heads = lax.all_to_all(heads, 'ctx', 0, 0, tiled=True).reshape(128, 768)  13.8 us
    all_gather x1, waiting for transfers between devices, fast_device(): rows_all = lax.all_gather(padded, 'ctx', axis=0, tiled=True)  13.4 us
    all_gather x1, waiting for transfers between devices, fast_device(): lax.all_gather(wide, 'ctx', axis=2, tiled=True).transpose(1, 0, 2, 3)  9.74 us
    convert_element_type x11, other arithmetic, add_low(): return (left.astype(f32) + right.astype(f32)).astype(bf)  8.9 us
    reduce_scatter x1, waiting for transfers between devices, fast_device(): lax.psum_scatter(grad_wide, 'ctx', scatter_dimension=0, tiled=True)  8.6 us
  transfers between devices with their start and end apart: 38, of which 22 were waited for; matrix products, arithmetic and copies ran while one was open for 9% of the time, Pallas kernels for 16%

profile of v11, /device:TPU:0, one launch (start us, length us, event | category | flops | bytes accessed | tf_op | source)
XLA Modules:
  0.0 338.1 jit_solution(16655740255569338239)
XLA Ops:
  7.3 1.0 fusion.14
  8.3 1.0 fusion.15
  12.5 13.8 %all_to_all.25 = bf16[4,32,768]{2,1,0:T(8,128)(2,1)S(1)} all-to-all(bf16[4,32,768]{2,1,0:T(8,128)(2,1)S(1)} %pad_maximum_fusion.11), channel_id=1, replica_groups=mesh['dp'=8,'ctx'=4] {'ctx'}, dimensions={0} | all-to-all | bytes 393216 | tf_op jit(solution)/shard_map/all_to_all | solution.py:916
  26.3 1.5 collective-permute-start.3
  27.8 4.2 %collective-permute-done.3 = bf16[128,768]{1,0:T(8,128)(2,1)S(1)} collective-permute-done((bf16[128,768]{1,0:T(8,128)(2,1)S(1)}, bf16[128,768]{1,0:T(8,128)(2,1)S(1)}, u32[]{:S(2)}, u32[]{:S(2)}) %collective-permute-start.3) | collective-permute-done | bytes 196640 | tf_op jit(solution)/shard_map/ppermute | solution.py:846
  32.0 1.6 collective-permute-start.4
  35.0 5.4 %collective-permute-done.4 = bf16[256,768]{1,0:T(8,128)(2,1)S(1)} collective-permute-done((bf16[256,768]{1,0:T(8,128)(2,1)S(1)}, bf16[256,768]{1,0:T(8,128)(2,1)S(1)}, u32[]{:S(2)}, u32[]{:S(2)}) %collective-permute-start.4) | collective-permute-done | bytes 393248 | tf_op jit(solution)/shard_map/ppermute | solution.py:846
  40.6 1.9 fusion.7
  42.5 1.8 pad_maximum_fusion.7
  44.5 9.7 %all-gather.5.cloned.1.call-done = bf16[2,2,128,1664]{3,2,1,0:T(8,128)(2,1)} async-done(((bf16[2,2,32,1664]{3,2,1,0:T(8,128)(2,1)}), bf16[2,2,128,1664]{3,2,1,0:T(8,128)(2,1)}) %all-gather.5.cloned.1.call-update) | async-done | bytes 1703952 | tf_op jit(solution)/shard_map/all_gather | solution.py:907
  54.3 1.6 copy.55
  56.6 1.5 collective-permute-start.6
  58.0 1.5 collective-permute-start.7
  59.5 36.0 %collective-permute-done.6.refs_6_.refs_7_ = bf16[2,256,1664]{2,1,0:T(8,128)(2,1)S(1)} collective-permute-done((bf16[2,256,1664]{2,1,0:T(8,128)(2,1)S(1)}, bf16[2,256,1664]{2,1,0:T(8,128)(2,1)S(1)}, u32[]{:S(2)}, u32[]{:S(2)}) %collective-permute-start.6) | collective-permute-done | bytes 1703968 | tf_op jit(solution)/shard_map/ppermute | solution.py:846
  95.6 1.5 collective-permute-start.8
  97.1 1.3 copy-done.21
  98.4 1.5 collective-permute-start.9
  100.0 13.4 %all-gather.3.cloned.1.call-done.refs_0_ = bf16[1376,1024]{1,0:T(8,128)(2,1)} async-done(((bf16[344,1024]{1,0:T(8,128)(2,1)}), bf16[1376,1024]{1,0:T(8,128)(2,1)}) %all-gather.3.cloned.1.call-update) | async-done | bytes 2818064 | tf_op jit(solution)/shard_map/all_gather | solution.py:909
  113.4 1.2 fusion.12
  114.7 1.5 collective-permute-start.10
  116.3 1.5 collective-permute-start.11
  117.7 1.3 collective-permute-done.9.refs_9_.refs_10_
  119.0 17.2 %attend.1 = (bf16[1024,1024]{1,0:T(8,128)(2,1)}, bf16[1024,768]{1,0:T(8,128)(2,1)}, bf16[1024,256]{1,0:T(8,128)(2,1)}, f32[8,1024]{1,0:T(8,128)}, f32[8,128]{1,0:T(8,128)}, /*index=5*/bf16[8,256,256]{2,1,0:T(8,128)(2,1)}) custom-call(bf16[1376,1024]{1,0:T(8,128)(2,1)} %all-gather.3.cloned.1.call-done.refs_0_, bf16[1024,768]{1,0:T(8,128)(2,1)} %copy-done.12, ...), custom_call_target="tpu_custom_call" | custom-call | flops 4294967296 | bytes 8388608 | tf_op jit(solution)/shard_map/attend/pallas_call | solution.py:308
  138.0 4.0 %all-to-all-start.1 = ((bf16[4,256,256]{2,1,0:T(8,128)(2,1)}), bf16[4,256,256]{2,1,0:T(8,128)(2,1)S(1)}, u32[]{:S(2)}, u32[]{:S(2)}) async-start(bf16[4,256,256]{2,1,0:T(8,128)(2,1)} %bitcast.103), calls=%async_computation.1 | async-start | bytes 1048576 | tf_op jit(solution)/shard_map/all_to_all | solution.py:940
  142.0 1.0 slice.250
  143.5 1.0 collective-permute-start.13
  144.5 9.4 %collective-permute-done.12.refs_14_.refs_8_ = bf16[352,512]{1,0:T(8,128)(2,1)S(1)} collective-permute-done((bf16[352,512]{1,0:T(8,128)(2,1)S(1)}, bf16[352,512]{1,0:T(8,128)(2,1)S(1)}, u32[]{:S(2)}, u32[]{:S(2)}) %collective-permute-start.12) | collective-permute-done | bytes 360480 | tf_op jit(solution)/shard_map/ppermute | solution.py:846
  154.5 1.9 collective-permute-done.14.refs_1_
  156.4 24.9 %feed.1 = (bf16[256,1024]{1,0:T(8,128)(2,1)}, f32[256,1024]{1,0:T(8,128)}, f32[256,1024]{1,0:T(8,128)}, bf16[1024,1024]{1,0:T(8,128)(2,1)}, bf16[512,1408]{1,0:T...) custom-call(bf16[4,256,256]{2,1,0:T(8,128)(2,1)S(1)} %all-to-all-don, ...), custom_call_target="tpu_custom_call" | custom-call | flops 12884901888 | bytes 8388608 | tf_op jit(solution)/shard_map/feed/pallas_call | solution.py:308
  181.5 2.0 collective-permute-done.16.part_hbm
  183.5 4.0 %branch.1 = (f32[256,1024]{1,0:T(8,128)}, bf16[4,256,256]{2,1,0:T(8,128)(2,1)}) custom-call(bf16[256,1024]{1,0:T(8,128)(2,1)S(1)} %collective-permute-done.16.part_hbm, f32[256,1024]{1,0:T(8,128)} %get-tuple-element.128.gnown_hbm, f32[256,1024]{1,0:T(8,128)} %get-tuple-element.122.res_hbm, bf16[256,1024]{1,0:T(8,128)(2,1)} %bitcast.13.refs_4_.cot_hbm.refs_1_, ...), custom_call_target="tpu_custom_call" | custom-call | flops 1073741824 | bytes 8388608 | tf_op jit(solution)/shard_map/branch/pallas_call | solution.py:308
  187.5 4.8 %all-to-all-start.2 = ((bf16[4,256,256]{2,1,0:T(8,128)(2,1)}), bf16[4,256,256]{2,1,0:T(8,128)(2,1)S(1)}, u32[]{:S(2)}, u32[]{:S(2)}) async-start(bf16[4,256,256]{2,1,0:T(8,128)(2,1)} %get-tuple-element.132), calls=%async_computation.2 | async-start | bytes 1048576 | tf_op jit(solution)/shard_map/all_to_all | solution.py:951
  192.4 1.2 collective-permute-start.18
  193.6 1.7 collective-permute-start.19
  195.3 10.3 %finish.1 = (bf16[256,1024]{1,0:T(8,128)(2,1)}, f32[256,1024]{1,0:T(8,128)}, bf16[704,512]{1,0:T(8,128)(2,1)}, bf16[704,512]{1,0:T(8,128)(2,1)}, bf16[704,512]{1...) custom-call(bf16[512,1408]{1,0:T(8,128)(2,1)} %get-tuple-element.123.refs_0_, ...), custom_call_target="tpu_custom_call" | custom-call | flops 64424509440 | bytes 8388608 | tf_op jit(solution)/shard_map/finish/pallas_call | solution.py:308
  207.2 17.7 %attend_back.1 = (bf16[1024,768]{1,0:T(8,128)(2,1)}, bf16[1024,1024]{1,0:T(8,128)(2,1)}) custom-call(bf16[1024,256]{1,0:T(8,128)(2,1)S(1)} %bitcast.78, bf16[1024,768]{1,0:T(8,128)(2,1)} %get-tuple-element.136.mixed_hbm, f32[8,1024]{1,0:T(8,128)} %get-tuple-element.137.total_hbm, f32[1024,128]{1,0:T(8,128)} %get-tuple-element.106.refs_2_.cos_hbm, ...), custom_call_target="tpu_custom_call" | custom-call | bytes 8388608 | tf_op jit(solution)/shard_map/attend_back/pallas_call | solution.py:308
  225.2 1.9 collective-permute-done.18
  227.2 1.2 collective-permute-done.19
  228.3 6.7 %project_weights.1 = (bf16[512,1792]{1,0:T(8,128)(2,1)}, bf16[512,1792]{1,0:T(8,128)(2,1)}) custom-call(bf16[1024,768]{1,0:T(8,128)(2,1)} %get-tuple-element.146.gm_hbm, bf16[1024,1024]{1,0:T(8,128)(2,1)} %get-tuple-element.147.normed_hbm, bf16[512,1024]{1,0:T(8,128)(2,1)} %get-tuple-element.148.okeep_hbm, bf16[512,1024]{1,0:T(8,128)(2,1)} %get-tuple-element.149.osend_hbm), custom_call_target="tpu_custom_call" | custom-call | flops 1073741824 | bytes 8388608 | tf_op jit(solution)/shard_map/project_weights/pallas_call | solution.py:308
  235.0 1.7 add_convert_fusion.2
  236.8 1.8 collective-permute-start.23
  239.8 2.8 collective-permute-done.26
  242.6 1.3 add_convert_fusion.5
  243.9 1.7 collective-permute-start.27
  245.9 1.3 collective-permute-start.29
  247.2 12.0 %collective-permute-done.23 = bf16[256,1408]{1,0:T(8,128)(2,1)S(1)} collective-permute-done((bf16[256,1408]{1,0:T(8,128)(2,1)S(1)}, bf16[256,1408]{1,0:T(8,128)(2,1)S(1)}, u32[]{:S(2)}, u32[]{:S(2)}) %collective-permute-start.23) | collective-permute-done | bytes 720928 | tf_op jit(solution)/shard_map/ppermute | solution.py:846
  259.9 1.3 copy-done.40
  261.2 4.3 %collective-permute-done.27 = bf16[352,512]{1,0:T(8,128)(2,1)S(1)} collective-permute-done((bf16[352,512]{1,0:T(8,128)(2,1)S(1)}, bf16[352,512]{1,0:T(8,128)(2,1)S(1)}, u32[]{:S(2)}, u32[]{:S(2)}) %collective-permute-start.27) | collective-permute-done | bytes 360480 | tf_op jit(solution)/shard_map/ppermute | solution.py:846
  267.2 1.5 pad_maximum_fusion
  268.7 2.5 add_convert_fusion
  274.4 5.9 %all-to-all-start.4 = ((f32[32,8,128]{2,1,0:T(8,128)}), f32[32,8,128]{2,1,0:T(8,128)}, u32[]{:S(2)}, u32[]{:S(2)}) async-start(f32[32,8,128]{2,1,0:T(8,128)} %broadcast_in_dim.35), calls=%async_computation.6 | async-start | bytes 262144 | tf_op jit(solution)/shard_map/all_to_all | solution.py:995
  280.3 13.4 %collective-permute-done.21 = bf16[256,1792]{1,0:T(8,128)(2,1)} collective-permute-done((bf16[256,1792]{1,0:T(8,128)(2,1)S(1)}, bf16[256,1792]{1,0:T(8,128)(2,1)}, u32[]{:S(2)}, u32[]{:S(2)}) %collective-permute-start.21) | collective-permute-done | bytes 917536 | tf_op jit(solution)/shard_map/ppermute | solution.py:846
  293.7 1.4 add_convert_fusion.3
  295.1 1.8 collective-permute-start.22
  296.9 2.1 fusion.6
  300.3 4.9 %collective-permute-done.22 = bf16[128,1792]{1,0:T(8,128)(2,1)S(1)} collective-permute-done((bf16[128,1792]{1,0:T(8,128)(2,1)S(1)}, bf16[128,1792]{1,0:T(8,128)(2,1)S(1)}, u32[]{:S(2)}, u32[]{:S(2)}) %collective-permute-start.22) | collective-permute-done | bytes 458784 | tf_op jit(solution)/shard_map/ppermute | solution.py:846
  306.1 4.4 %all-to-all-start.3 = ((bf16[4,32,1792]{2,1,0:T(8,128)(2,1)}), bf16[4,32,1792]{2,1,0:T(8,128)(2,1)S(1)}, u32[]{:S(2)}, u32[]{:S(2)}) async-start(bf16[4,32,1792]{2,1,0:T(8,128)(2,1)} %bitcast.26), calls=%async_computation.4 | async-start | bytes 917504 | tf_op jit(solution)/shard_map/all_to_all | solution.py:1006
  310.5 1.5 fusion.3
  312.1 1.5 fusion.5
  313.6 2.7 add_bitcast_fusion
  316.3 8.6 %reduce-scatter.5.cloned.1.call-done.wide_ref = bf16[32,8704]{1,0:T(8,128)(2,1)} async-done(((bf16[128,8704]{1,0:T(8,128)(2,1)}), bf16[32,8704]{1,0:T(8,128)(2,1)}) %reduce-scatter.5.cloned.1.call-update) | async-done | bytes 557072 | tf_op jit(solution)/shard_map/reduce_scatter | solution.py:993
  324.9 1.0 copy-done.3
  326.0 1.8 update.1
  327.9 1.2 all-to-all-done.3
  (199 shorter events, 20.7 us)
Async XLA Ops:
  7.2 3.2 copy-start.27
  7.2 47.1 %all-gather.5.cloned.1.call-start = ((), (), s32[]{:S(2)}) async-start(), calls=%async_computation.8 | async-start | bytes 2129920 | tf_op jit(solution)/shard_map/all_gather | solution.py:907
  9.7 2.7 copy-start.25
  9.7 2.7 copy-start.23
  9.8 2.6 copy-start.22
  9.9 1.6 collective-permute-start
  12.2 21.3 %copy-start.8 = (bf16[1,256,1024]{2,1,0:T(8,128)(2,1)S(1)}, bf16[1,256,1024]{2,1,0:T(8,128)(2,1)}, u32[]{:S(2)}) copy-start(bf16[1,256,1024]{2,1,0:T(8,128)(2,1)} %param.19) | copy-start | bytes 1572868
  12.2 21.9 %copy-start.2 = (bf16[88,1024]{1,0:T(8,128)(2,1)S(1)}, bf16[88,1024]{1,0:T(8,128)(2,1)}, u32[]{:S(2)}) copy-start(bf16[88,1024]{1,0:T(8,128)(2,1)} %wd.1) | copy-start | bytes 540676
  12.3 101.2 %all-gather.3.cloned.1.call-start = ((), (), s32[]{:S(2)}) async-start(), calls=%async_computation.7 | async-start | bytes 3522560 | tf_op jit(solution)/shard_map/all_gather | solution.py:909
  26.3 5.7 %collective-permute-start.3 = (bf16[128,768]{1,0:T(8,128)(2,1)S(1)}, bf16[128,768]{1,0:T(8,128)(2,1)S(1)}, u32[]{:S(2)}, u32[]{:S(2)}) collective-permute-start(bf16[128,768]{1,0:T(8,128)(2,1)S(1)} %bitcast.84), channel_id=1, source_target_pairs={{0,8},{4,12},{8,0},{12,4},{16,24},{20,28},{24,16},{28,20},{1,9},{5... | collective-permute-start | bytes 589832 | tf_op jit(solution)/shard_map/ppermute | solution.py:846
  32.0 8.5 %collective-permute-start.4 = (bf16[256,768]{1,0:T(8,128)(2,1)S(1)}, bf16[256,768]{1,0:T(8,128)(2,1)S(1)}, u32[]{:S(2)}, u32[]{:S(2)}) collective-permute-start(bf16[256,768]{1,0:T(8,128)(2,1)S(1)} %pad_maximum_fusion.10), channel_id=1, source_target_pairs={{0,16},{4,20},{8,24},{12,28},{16,0},{20,4},{24,8},{28,12},{1,17},{... | collective-permute-start | bytes 1179656 | tf_op jit(solution)/shard_map/ppermute | solution.py:846
  33.6 22.3 %collective-permute-start.2 = (bf16[256,1024]{1,0:T(8,128)(2,1)}, bf16[256,1024]{1,0:T(8,128)(2,1)}, u32[]{:S(2)}, u32[]{:S(2)}) collective-permute-start(bf16[256,1024]{1,0:T(8,128)(2,1)} %bitcast.13.refs_4_.cot_hbm.refs_1_), channel_id=1, source_target_pairs={{0,4},{4,0},{8,12},{12,8},{16,20},{20,16},{24,28},{28,24},{1,5},{5... | collective-permute-start | bytes 1572872 | tf_op jit(solution)/shard_map/ppermute | solution.py:846
  33.6 22.3 %collective-permute-start.1 = (bf16[256,1024]{1,0:T(8,128)(2,1)S(1)}, bf16[256,1024]{1,0:T(8,128)(2,1)}, u32[]{:S(2)}, u32[]{:S(2)}) collective-permute-start(bf16[256,1024]{1,0:T(8,128)(2,1)S(1)} %bitcast.80), channel_id=1, source_target_pairs={{0,4},{4,0},{8,12},{12,8},{16,20},{20,16},{24,28},{28,24},{1,5},{5... | collective-permute-start | bytes 1572872 | tf_op jit(solution)/shard_map/ppermute | solution.py:846
  40.5 3.9 %collective-permute-start.5 = (bf16[512,768]{1,0:T(8,128)(2,1)S(1)}, bf16[512,768]{1,0:T(8,128)(2,1)S(1)}, u32[]{:S(2)}, u32[]{:S(2)}) collective-permute-start(bf16[512,768]{1,0:T(8,128)(2,1)S(1)} %pad_maximum_fusion.1), channel_id=1, source_target_pairs={{0,4},{4,0},{8,12},{12,8},{16,20},{20,16},{24,28},{28,24},{1,5},{5... | collective-permute-start | bytes 2359304 | tf_op jit(solution)/shard_map/ppermute | solution.py:846
  44.5 11.3 %copy-start.12 = (bf16[1024,768]{1,0:T(8,128)(2,1)}, bf16[1024,768]{1,0:T(8,128)(2,1)S(1)}, u32[]{:S(2)}) copy-start(bf16[1024,768]{1,0:T(8,128)(2,1)S(1)} %constant_dynamic-update-slice_fusion.refs_1_.weight_hbm) | copy-start | bytes 4718596
  55.9 42.6 %copy-start.13 = (bf16[2,2,128,1664]{3,2,1,0:T(8,128)(2,1)}, bf16[2,2,128,1664]{3,2,1,0:T(8,128)(2,1)S(1)}, u32[]{:S(2)}) copy-start(bf16[2,2,128,1664]{3,2,1,0:T(8,128)(2,1)S(1)} %copy.55) | copy-start | bytes 5111812
  56.6 38.9 %collective-permute-start.6 = (bf16[2,256,1664]{2,1,0:T(8,128)(2,1)S(1)}, bf16[2,256,1664]{2,1,0:T(8,128)(2,1)S(1)}, u32[]{:S(2)}, u32[]{:S(2)}) collective-permute-start(bf16[2,256,1664]{2,1,0:T(8,128)(2,1)S(1)} %bitcast.91), channel_id=1, source_target_pairs={{0,8},{4,12},{8,0},{12,4},{16,24},{20,28},{24,16},{28,20},{1,9},{5... | collective-permute-start | bytes 5111816 | tf_op jit(solution)/shard_map/ppermute | solution.py:846
  58.0 39.0 %collective-permute-start.7 = (bf16[2,256,1664]{2,1,0:T(8,128)(2,1)S(1)}, bf16[2,256,1664]{2,1,0:T(8,128)(2,1)S(1)}, u32[]{:S(2)}, u32[]{:S(2)}) collective-permute-start(bf16[2,256,1664]{2,1,0:T(8,128)(2,1)S(1)} %bitcast.92), channel_id=1, source_target_pairs={{0,16},{4,20},{8,24},{12,28},{16,0},{20,4},{24,8},{28,12},{1,17},{... | collective-permute-start | bytes 5111816 | tf_op jit(solution)/shard_map/ppermute | solution.py:846
  95.5 2.9 copy-start.20
  95.6 22.2 %collective-permute-start.8 = (bf16[256,1664]{1,0:T(8,128)(2,1)S(1)}, bf16[256,1664]{1,0:T(8,128)(2,1)}, u32[]{:S(2)}, u32[]{:S(2)}) collective-permute-start(bf16[256,1664]{1,0:T(8,128)(2,1)S(1)} %slice_bitcast_fusion.1), channel_id=1, source_target_pairs={{0,16},{4,20},{8,24},{12,28},{16,0},{20,4},{24,8},{28,12},{1,17},{... | collective-permute-start | bytes 2555912 | tf_op jit(solution)/shard_map/ppermute | solution.py:846
  98.4 20.6 %collective-permute-start.9 = (bf16[256,1664]{1,0:T(8,128)(2,1)S(1)}, bf16[256,1664]{1,0:T(8,128)(2,1)}, u32[]{:S(2)}, u32[]{:S(2)}) collective-permute-start(bf16[256,1664]{1,0:T(8,128)(2,1)S(1)} %slice_bitcast_fusion), channel_id=1, source_target_pairs={{0,8},{4,12},{8,0},{12,4},{16,24},{20,28},{24,16},{28,20},{1,9},{5... | collective-permute-start | bytes 2555912 | tf_op jit(solution)/shard_map/ppermute | solution.py:846
  114.7 21.5 %copy-start.17 = (bf16[352,1024]{1,0:T(8,128)(2,1)}, bf16[352,1024]{1,0:T(8,128)(2,1)S(1)}, u32[]{:S(2)}) copy-start(bf16[352,1024]{1,0:T(8,128)(2,1)S(1)} %pad_maximum_fusion.2.refs_11_.refs_5_) | copy-start | bytes 2162692
  114.7 21.5 %collective-permute-start.10 = (bf16[352,1024]{1,0:T(8,128)(2,1)S(1)}, bf16[352,1024]{1,0:T(8,128)(2,1)S(1)}, u32[]{:S(2)}, u32[]{:S(2)}) collective-permute-start(bf16[352,1024]{1,0:T(8,128)(2,1)S(1)} %pad_maximum_fusion.2.refs_11_.refs_5_), channel_id=1, source_target_pairs={{0,8},{4,12},{8,0},{12,4},{16,24},{20,28},{24,16},{28,20},{1,9},{5... | collective-permute-start | bytes 2162696 | tf_op jit(solution)/shard_map/ppermute | solution.py:846
  116.3 20.0 %collective-permute-start.11 = (bf16[352,1024]{1,0:T(8,128)(2,1)S(1)}, bf16[352,1024]{1,0:T(8,128)(2,1)S(1)}, u32[]{:S(2)}, u32[]{:S(2)}) collective-permute-start(bf16[352,1024]{1,0:T(8,128)(2,1)S(1)} %pad_maximum_fusion.2.refs_11_.refs_5_), channel_id=1, source_target_pairs={{0,16},{4,20},{8,24},{12,28},{16,0},{20,4},{24,8},{28,12},{1,17},{... | collective-permute-start | bytes 2162696 | tf_op jit(solution)/shard_map/ppermute | solution.py:846
  138.0 5.5 %copy-start.31 = (bf16[352,1024]{1,0:T(8,128)(2,1)S(1)}, bf16[352,1024]{1,0:T(8,128)(2,1)}, u32[]{:S(2)}) copy-start(bf16[352,1024]{1,0:T(8,128)(2,1)} %copy-done.30) | copy-start | bytes 2162692
  138.0 16.5 %all-to-all-start.1 = ((bf16[4,256,256]{2,1,0:T(8,128)(2,1)}), bf16[4,256,256]{2,1,0:T(8,128)(2,1)S(1)}, u32[]{:S(2)}, u32[]{:S(2)}) async-start(bf16[4,256,256]{2,1,0:T(8,128)(2,1)} %bitcast.103), calls=%async_computation.1 | async-start | bytes 1048576 | tf_op jit(solution)/shard_map/all_to_all | solution.py:940
  142.0 12.4 %collective-permute-start.15 = (bf16[8,256,256]{2,1,0:T(8,128)(2,1)}, bf16[8,256,256]{2,1,0:T(8,128)(2,1)S(1)}, u32[]{:S(2)}, u32[]{:S(2)}) collective-permute-start(bf16[8,256,256]{2,1,0:T(8,128)(2,1)} %get-tuple-element.121), channel_id=1, source_target_pairs={{0,4},{4,0},{8,12},{12,8},{16,20},{20,16},{24,28},{28,24},{1,5},{5... | collective-permute-start | bytes 3145736 | tf_op jit(solution)/shard_map/ppermute | solution.py:846
  143.0 10.9 %collective-permute-start.12 = (bf16[352,512]{1,0:T(8,128)(2,1)S(1)}, bf16[352,512]{1,0:T(8,128)(2,1)S(1)}, u32[]{:S(2)}, u32[]{:S(2)}) collective-permute-start(bf16[352,512]{1,0:T(8,128)(2,1)S(1)} %slice.250), channel_id=1, source_target_pairs={{0,16},{4,20},{8,24},{12,28},{16,0},{20,4},{24,8},{28,12},{1,17},{... | collective-permute-start | bytes 1081352 | tf_op jit(solution)/shard_map/ppermute | solution.py:846
  143.5 10.6 %collective-permute-start.13 = (bf16[352,512]{1,0:T(8,128)(2,1)S(1)}, bf16[352,512]{1,0:T(8,128)(2,1)S(1)}, u32[]{:S(2)}, u32[]{:S(2)}) collective-permute-start(bf16[352,512]{1,0:T(8,128)(2,1)S(1)} %slice.251), channel_id=1, source_target_pairs={{0,8},{4,12},{8,0},{12,4},{16,24},{20,28},{24,16},{28,20},{1,9},{5... | collective-permute-start | bytes 1081352 | tf_op jit(solution)/shard_map/ppermute | solution.py:846
  154.4 26.9 %copy-start.4 = (bf16[4,256,256]{2,1,0:T(8,128)(2,1)}, bf16[4,256,256]{2,1,0:T(8,128)(2,1)S(1)}, u32[]{:S(2)}) copy-start(bf16[4,256,256]{2,1,0:T(8,128)(2,1)S(1)} %all-to-all-done.1.refs_0_.refs_3_) | copy-start | bytes 1572868
  154.4 1.9 collective-permute-start.14
  181.3 2.2 collective-permute-start.16
  187.5 19.6 %all-to-all-start.2 = ((bf16[4,256,256]{2,1,0:T(8,128)(2,1)}), bf16[4,256,256]{2,1,0:T(8,128)(2,1)S(1)}, u32[]{:S(2)}, u32[]{:S(2)}) async-start(bf16[4,256,256]{2,1,0:T(8,128)(2,1)} %get-tuple-element.132), calls=%async_computation.2 | async-start | bytes 1048576 | tf_op jit(solution)/shard_map/all_to_all | solution.py:951
  192.4 118.2 %reduce-scatter.3.cloned.1.call-start = ((), (), s32[]{:S(2)}) async-start(), calls=%async_computation.9 | async-start | bytes 2621440 | tf_op jit(solution)/shard_map/reduce_scatter | solution.py:999
  192.4 34.8 %collective-permute-start.18 = (bf16[512,1408]{1,0:T(8,128)(2,1)}, bf16[512,1408]{1,0:T(8,128)(2,1)}, u32[]{:S(2)}, u32[]{:S(2)}) collective-permute-start(bf16[512,1408]{1,0:T(8,128)(2,1)} %get-tuple-element.144), channel_id=1, source_target_pairs={{0,8},{4,12},{8,0},{12,4},{16,24},{20,28},{24,16},{28,20},{1,9},{5... | collective-permute-start | bytes 4325384 | tf_op jit(solution)/shard_map/ppermute | solution.py:846
  193.6 34.7 %collective-permute-start.19 = (bf16[512,1408]{1,0:T(8,128)(2,1)}, bf16[512,1408]{1,0:T(8,128)(2,1)S(1)}, u32[]{:S(2)}, u32[]{:S(2)}) collective-permute-start(bf16[512,1408]{1,0:T(8,128)(2,1)} %get-tuple-element.145), channel_id=1, source_target_pairs={{0,16},{4,20},{8,24},{12,28},{16,0},{20,4},{24,8},{28,12},{1,17},{... | collective-permute-start | bytes 4325384 | tf_op jit(solution)/shard_map/ppermute | solution.py:846
  205.6 37.0 %collective-permute-start.26 = (bf16[704,512]{1,0:T(8,128)(2,1)}, bf16[704,512]{1,0:T(8,128)(2,1)}, u32[]{:S(2)}, u32[]{:S(2)}) collective-permute-start(bf16[704,512]{1,0:T(8,128)(2,1)} %get-tuple-element.157), channel_id=1, source_target_pairs={{0,8},{4,12},{8,0},{12,4},{16,24},{20,28},{24,16},{28,20},{1,9},{5... | collective-permute-start | bytes 2162696 | tf_op jit(solution)/shard_map/ppermute | solution.py:846
  206.4 39.2 %collective-permute-start.28 = (bf16[704,512]{1,0:T(8,128)(2,1)}, bf16[704,512]{1,0:T(8,128)(2,1)S(1)}, u32[]{:S(2)}, u32[]{:S(2)}) collective-permute-start(bf16[704,512]{1,0:T(8,128)(2,1)} %get-tuple-element.159), channel_id=1, source_target_pairs={{0,16},{4,20},{8,24},{12,28},{16,0},{20,4},{24,8},{28,12},{1,17},{... | collective-permute-start | bytes 2162696 | tf_op jit(solution)/shard_map/ppermute | solution.py:846
  224.9 100.0 %reduce-scatter.5.cloned.1.call-start = ((), (), s32[]{:S(2)}) async-start(), calls=%async_computation.10 | async-start | bytes 2785280 | tf_op jit(solution)/shard_map/reduce_scatter | solution.py:993
  228.3 6.7 %copy-start.15 = (bf16[512,1408]{1,0:T(8,128)(2,1)S(1)}, bf16[512,1408]{1,0:T(8,128)(2,1)}, u32[]{:S(2)}) copy-start(bf16[512,1408]{1,0:T(8,128)(2,1)} %get-tuple-element.154) | copy-start | bytes 4325380
  236.8 22.4 %collective-permute-start.23 = (bf16[256,1408]{1,0:T(8,128)(2,1)S(1)}, bf16[256,1408]{1,0:T(8,128)(2,1)S(1)}, u32[]{:S(2)}, u32[]{:S(2)}) collective-permute-start(bf16[256,1408]{1,0:T(8,128)(2,1)S(1)} %slice.294), channel_id=1, source_target_pairs={{0,16},{4,20},{8,24},{12,28},{16,0},{20,4},{24,8},{28,12},{1,17},{... | collective-permute-start | bytes 2162696 | tf_op jit(solution)/shard_map/ppermute | solution.py:846
  238.9 3.7 %copy-start.19 = (bf16[704,512]{1,0:T(8,128)(2,1)S(1)}, bf16[704,512]{1,0:T(8,128)(2,1)}, u32[]{:S(2)}) copy-start(bf16[704,512]{1,0:T(8,128)(2,1)} %get-tuple-element.156) | copy-start | bytes 2162692
  239.0 6.7 %copy-start.18 = (bf16[704,512]{1,0:T(8,128)(2,1)S(1)}, bf16[704,512]{1,0:T(8,128)(2,1)}, u32[]{:S(2)}) copy-start(bf16[704,512]{1,0:T(8,128)(2,1)} %get-tuple-element.158) | copy-start | bytes 2162692
  239.0 20.4 %collective-permute-start.24 = (bf16[256,1408]{1,0:T(8,128)(2,1)S(1)}, bf16[256,1408]{1,0:T(8,128)(2,1)S(1)}, u32[]{:S(2)}, u32[]{:S(2)}) collective-permute-start(bf16[256,1408]{1,0:T(8,128)(2,1)S(1)} %slice.296), channel_id=1, source_target_pairs={{0,8},{4,12},{8,0},{12,4},{16,24},{20,28},{24,16},{28,20},{1,9},{5... | collective-permute-start | bytes 2162696 | tf_op jit(solution)/shard_map/ppermute | solution.py:846
  243.9 21.5 %collective-permute-start.27 = (bf16[352,512]{1,0:T(8,128)(2,1)S(1)}, bf16[352,512]{1,0:T(8,128)(2,1)S(1)}, u32[]{:S(2)}, u32[]{:S(2)}) collective-permute-start(bf16[352,512]{1,0:T(8,128)(2,1)S(1)} %slice.298), channel_id=1, source_target_pairs={{0,16},{4,20},{8,24},{12,28},{16,0},{20,4},{24,8},{28,12},{1,17},{... | collective-permute-start | bytes 1081352 | tf_op jit(solution)/shard_map/ppermute | solution.py:846
  245.9 19.7 %collective-permute-start.29 = (bf16[352,512]{1,0:T(8,128)(2,1)S(1)}, bf16[352,512]{1,0:T(8,128)(2,1)S(1)}, u32[]{:S(2)}, u32[]{:S(2)}) collective-permute-start(bf16[352,512]{1,0:T(8,128)(2,1)S(1)} %slice.300), channel_id=1, source_target_pairs={{0,8},{4,12},{8,0},{12,4},{16,24},{20,28},{24,16},{28,20},{1,9},{5... | collective-permute-start | bytes 1081352 | tf_op jit(solution)/shard_map/ppermute | solution.py:846
  259.8 7.1 %collective-permute-start.25 = (bf16[128,2816]{1,0:T(8,128)(2,1)S(1)}, bf16[128,2816]{1,0:T(8,128)(2,1)S(1)}, u32[]{:S(2)}, u32[]{:S(2)}) collective-permute-start(bf16[128,2816]{1,0:T(8,128)(2,1)S(1)} %pad_maximum_fusion.3), channel_id=1, source_target_pairs={{0,4},{4,0},{8,12},{12,8},{16,20},{20,16},{24,28},{28,24},{1,5},{5... | collective-permute-start | bytes 2162696 | tf_op jit(solution)/shard_map/ppermute | solution.py:846
  261.2 7.5 %collective-permute-start.20 = (bf16[512,1792]{1,0:T(8,128)(2,1)S(1)}, bf16[512,1792]{1,0:T(8,128)(2,1)}, u32[]{:S(2)}, u32[]{:S(2)}) collective-permute-start(bf16[512,1792]{1,0:T(8,128)(2,1)S(1)} %copy-done.40), channel_id=1, source_target_pairs={{0,4},{4,0},{8,12},{12,8},{16,20},{20,16},{24,28},{28,24},{1,5},{5... | collective-permute-start | bytes 5505032 | tf_op jit(solution)/shard_map/ppermute | solution.py:846
  271.2 2.5 copy-start.36
  271.3 22.4 %collective-permute-start.21 = (bf16[256,1792]{1,0:T(8,128)(2,1)S(1)}, bf16[256,1792]{1,0:T(8,128)(2,1)}, u32[]{:S(2)}, u32[]{:S(2)}) collective-permute-start(bf16[256,1792]{1,0:T(8,128)(2,1)S(1)} %slice.290), channel_id=1, source_target_pairs={{0,8},{4,12},{8,0},{12,4},{16,24},{20,28},{24,16},{28,20},{1,9},{5... | collective-permute-start | bytes 2752520 | tf_op jit(solution)/shard_map/ppermute | solution.py:846
  273.6 23.3 %collective-permute-start.17 = (bf16[256,1024]{1,0:T(8,128)(2,1)}, bf16[256,1024]{1,0:T(8,128)(2,1)}, u32[]{:S(2)}, u32[]{:S(2)}) collective-permute-start(bf16[256,1024]{1,0:T(8,128)(2,1)} %get-tuple-element.134), channel_id=1, source_target_pairs={{0,4},{4,0},{8,12},{12,8},{16,20},{20,16},{24,28},{28,24},{1,5},{5... | collective-permute-start | bytes 1572872 | tf_op jit(solution)/shard_map/ppermute | solution.py:846
  274.4 24.7 %all-to-all-start.4 = ((f32[32,8,128]{2,1,0:T(8,128)}), f32[32,8,128]{2,1,0:T(8,128)}, u32[]{:S(2)}, u32[]{:S(2)}) async-start(f32[32,8,128]{2,1,0:T(8,128)} %broadcast_in_dim.35), calls=%async_computation.6 | async-start | bytes 262144 | tf_op jit(solution)/shard_map/all_to_all | solution.py:995
  280.3 16.6 %copy-start.11 = (f32[256,1024]{1,0:T(8,128)S(1)}, f32[256,1024]{1,0:T(8,128)}, u32[]{:S(2)}) copy-start(f32[256,1024]{1,0:T(8,128)} %get-tuple-element.122.res_hbm) | copy-start | bytes 3145732
  280.3 16.6 %copy-start.16 = (f32[256,1024]{1,0:T(8,128)S(1)}, f32[256,1024]{1,0:T(8,128)}, u32[]{:S(2)}) copy-start(f32[256,1024]{1,0:T(8,128)} %get-tuple-element.131) | copy-start | bytes 3145732
  295.1 10.1 %collective-permute-start.22 = (bf16[128,1792]{1,0:T(8,128)(2,1)S(1)}, bf16[128,1792]{1,0:T(8,128)(2,1)S(1)}, u32[]{:S(2)}, u32[]{:S(2)}) collective-permute-start(bf16[128,1792]{1,0:T(8,128)(2,1)S(1)} %slice.292), channel_id=1, source_target_pairs={{0,16},{4,20},{8,24},{12,28},{16,0},{20,4},{24,8},{28,12},{1,17},{... | collective-permute-start | bytes 1376264 | tf_op jit(solution)/shard_map/ppermute | solution.py:846
  300.2 11.9 %copy-start.38 = (f32[16]{0:T(128)}, f32[16]{0:T(128)S(1)}, u32[]{:S(2)}) copy-start(f32[16]{0:T(128)S(1)} %reshape_squeeze.3) | copy-start | bytes 196
  300.2 11.9 %copy-start.39 = (f32[16]{0:T(128)}, f32[16]{0:T(128)S(1)}, u32[]{:S(2)}) copy-start(f32[16]{0:T(128)S(1)} %divide_sqrt_fusion) | copy-start | bytes 196
  306.1 22.9 %all-to-all-start.3 = ((bf16[4,32,1792]{2,1,0:T(8,128)(2,1)}), bf16[4,32,1792]{2,1,0:T(8,128)(2,1)S(1)}, u32[]{:S(2)}, u32[]{:S(2)}) async-start(bf16[4,32,1792]{2,1,0:T(8,128)(2,1)} %bitcast.26), calls=%async_computation.4 | async-start | bytes 917504 | tf_op jit(solution)/shard_map/all_to_all | solution.py:1006
  310.5 3.0 copy-start.10
  313.5 11.4 %copy-start = (bf16[32,2816]{1,0:T(8,128)(2,1)S(1)}, bf16[32,2816]{1,0:T(8,128)(2,1)}, u32[]{:S(2)}) copy-start(bf16[32,2816]{1,0:T(8,128)(2,1)} %wu.1) | copy-start | bytes 540676
  313.6 11.4 %copy-start.1 = (bf16[32,2816]{1,0:T(8,128)(2,1)S(1)}, bf16[32,2816]{1,0:T(8,128)(2,1)}, u32[]{:S(2)}) copy-start(bf16[32,2816]{1,0:T(8,128)(2,1)} %wg.1) | copy-start | bytes 540676
  313.6 11.4 %copy-start.5 = (f32[32,2816]{1,0:T(8,128)S(1)}, f32[32,2816]{1,0:T(8,128)}, u32[]{:S(2)}) copy-start(f32[32,2816]{1,0:T(8,128)} %mg.1) | copy-start | bytes 1081348
  313.6 11.4 %copy-start.6 = (f32[32,2816]{1,0:T(8,128)S(1)}, f32[32,2816]{1,0:T(8,128)}, u32[]{:S(2)}) copy-start(f32[32,2816]{1,0:T(8,128)} %mu.1) | copy-start | bytes 1081348
  313.6 11.3 %copy-start.7 = (f32[88,1024]{1,0:T(8,128)S(1)}, f32[88,1024]{1,0:T(8,128)}, u32[]{:S(2)}) copy-start(f32[88,1024]{1,0:T(8,128)} %md.1) | copy-start | bytes 1081348
  (18 other events, 28.2 us)
Sparse Core Ops, SparseCore 0:
  12.4 41.8 all-gather.4
  56.4 56.9 all-gather.2
  225.0 44.8 reduce-scatter.2
  272.2 52.6 reduce-scatter.4
